TPU v7x, 32 devices: a whole 2x2x4 slice. The times are simulated.
32 devices in a mesh: grp: 4 (over x, core), seq: 4 (over z), tp: 2 (over y).
Axes of the slice: x: 2, y: 2, z: 4, core: 2. Of those that a mesh axis runs over, the one named last changes fastest.
Arguments:
- prompt_in: bfloat16 [4, 1536, 768], P('grp', 'seq'), may hold values from -6 to 6
- cont_in: bfloat16 [4, 4, 512, 768], P('grp', 'seq'), may hold values from -6 to 6
- prompt_cot: bfloat16 [4, 1536, 768], P('grp', 'seq'), may hold values from -6 to 6
- cont_cot: bfloat16 [4, 4, 512, 768], P('grp', 'seq'), may hold values from -6 to 6
- prompt_len: int32 [4, 4], P('grp', 'seq'), may hold values from 1 to 1536, as said below
- qkv_weight: bfloat16 [3, 768, 768], P(None, None, 'tp'), may hold values from -0.3125 to 0.3125
- out_weight: bfloat16 [768, 768], P('tp'), may hold values from -1.25 to 1.25
- ffn_in: bfloat16 [768, 3072], P(None, 'tp'), may hold values from -0.21875 to 0.21875
- ffn_out: bfloat16 [3072, 768], P('tp'), may hold values from -0.109375 to 0.109375
- norm_gain: bfloat16 [2, 768], replicated, may hold values from 0.5 to 1.5
- norm_shift: bfloat16 [2, 768], replicated, may hold values from -1.5 to 1.5
Outputs:
- prompt_out: bfloat16 [4, 1536, 768], P('grp', 'seq')
- cont_out: bfloat16 [4, 4, 512, 768], P('grp', 'seq')
- prompt_grad: bfloat16 [4, 1536, 768], P('grp', 'seq')
- cont_grad: bfloat16 [4, 4, 512, 768], P('grp', 'seq')
- qkv_weight_grad: float32 [3, 768, 768], P(None, 'seq', 'tp')
- out_weight_grad: float32 [768, 768], P('tp', 'seq')
- ffn_in_grad: float32 [768, 3072], P('seq', 'tp')
- ffn_out_grad: float32 [3072, 768], P('tp', 'seq')
- norm_gain_grad: float32 [2, 768], P(None, ('seq', 'tp'))
- norm_shift_grad: float32 [2, 768], P(None, ('seq', 'tp'))
Inputs may be any that keep to these rules, and one draw needn't show every extreme that they name: prompt_len[g, c] counts the leading prompt tokens of group g that continuation c sees; in every group some continuation sees all 1536.
All inputs are finite; a program needn't handle non-finite values.
Results may differ from a plain program's by a relative error of at most 0.02.
Values may be sent and summed in bfloat16 or wider, within the bound.
No kernel may reach another device: no remote copies, remote signals or barrier semaphores. Data moves between devices by JAX's collectives and lax.ppermute only.
A program may use at most 256 MiB of HBM per device.

v0:
```python
import jax
import jax.numpy as jnp
from jax import lax
from jax.sharding import PartitionSpec as P

HEAD = 64


norm_eps = 1e-05
hidden_value = -1e30


def layer_norm(tokens, gain, shift):
    mean = jnp.mean(tokens, axis=-1, keepdims=True)
    centred = tokens - mean
    variance = jnp.mean(centred * centred, axis=-1, keepdims=True)
    return centred * lax.rsqrt(variance + norm_eps) * gain + shift


def norm_terms(tokens, upstream):
    mean = jnp.mean(tokens, axis=-1, keepdims=True)
    centred = tokens - mean
    variance = jnp.mean(centred * centred, axis=-1, keepdims=True)
    scaled = centred * lax.rsqrt(variance + norm_eps)
    return jnp.stack([jnp.sum(upstream * scaled, axis=0), jnp.sum(upstream, axis=0)])


def exact_gelu(upper):
    return jax.nn.gelu(upper, approximate=False)


def head_scores(queries, keys, visible, scale):
    scores = jnp.einsum("ne,ke->nk", queries, keys, preferred_element_type=jnp.float32) * scale
    return jnp.where(visible, scores, hidden_value)


def body(
    prompt_in,
    cont_in,
    prompt_cot,
    cont_cot,
    prompt_len,
    qkv_weight,
    out_weight,
    ffn_in,
    ffn_out,
    norm_gain,
    norm_shift,
):
    prompt_rows = prompt_in.shape[1]
    width = prompt_in.shape[2]
    local_width = qkv_weight.shape[2]
    local_heads = local_width // HEAD
    scale = HEAD ** (-0.5)
    tokens = jnp.concatenate([prompt_in[0], cont_in[0, 0]], axis=0).astype(jnp.float32)
    row_count = tokens.shape[0]
    gains = norm_gain.astype(jnp.float32)
    shifts = norm_shift.astype(jnp.float32)
    nothing = jnp.zeros((), jnp.float32)
    tp_count = lax.axis_size("tp")
    half_rows = row_count // tp_count
    row_start = lax.axis_index("tp") * half_rows

    def own_rows(matrix):
        return lax.dynamic_slice_in_dim(matrix, row_start, half_rows, 0)

    normed, first_pull = jax.vjp(layer_norm, tokens, gains[0], shifts[0])
    normed_low = normed.astype(jnp.bfloat16)
    projected = jnp.einsum(
        "nd,cde->cne", normed_low, qkv_weight, preferred_element_type=jnp.float32
    ).astype(jnp.bfloat16)
    own_kv = projected[1:3, :prompt_rows]
    gathered = lax.all_gather(own_kv, "seq", axis=1, tiled=True)
    prompt_keys = gathered.shape[1]

    def split_heads(matrix):
        return matrix.reshape(matrix.shape[0], local_heads, HEAD).transpose(1, 0, 2)

    def join_heads(stacked):
        return stacked.transpose(1, 0, 2).reshape(stacked.shape[1], local_width)

    keyvals = jnp.concatenate([gathered, projected[1:3, prompt_rows:]], axis=1)
    key_count = keyvals.shape[1]
    row_index = jnp.arange(row_count, dtype=jnp.int32)[:, None]
    key_index = jnp.arange(key_count, dtype=jnp.int32)[None, :]
    limit = jnp.where(row_index < prompt_rows, prompt_keys, prompt_len[0, 0])
    visible = (key_index < limit) | (key_index >= prompt_keys) & (row_index >= prompt_rows)
    head_queries = split_heads(projected[0])

    def forward_head(carry, pieces):
        queries, keys, values = pieces
        scores = head_scores(queries, keys, visible, scale)
        largest = jnp.max(scores, axis=-1, keepdims=True)
        weights = jnp.exp(scores - largest)
        summed = jnp.sum(weights, axis=-1, keepdims=True)
        probs = (weights / summed).astype(jnp.bfloat16)
        output = jnp.dot(probs, values, preferred_element_type=jnp.float32)
        return (carry, (output, largest[:, 0] + jnp.log(summed[:, 0])))

    _, (head_out, log_sums) = lax.scan(
        forward_head, nothing, (head_queries, split_heads(keyvals[0]), split_heads(keyvals[1]))
    )
    attended = join_heads(head_out).astype(jnp.bfloat16)
    mixed_terms = jnp.dot(attended, out_weight, preferred_element_type=jnp.float32)
    resid = tokens + lax.psum(mixed_terms, "tp")
    second_low = layer_norm(resid, gains[1], shifts[1]).astype(jnp.bfloat16)
    upper = jnp.dot(second_low, ffn_in, preferred_element_type=jnp.float32)
    activated, gelu_pull = jax.vjp(exact_gelu, upper)
    act_low = activated.astype(jnp.bfloat16)
    ffn_terms = jnp.dot(act_low, ffn_out, preferred_element_type=jnp.float32)
    result = (resid + lax.psum(ffn_terms.astype(jnp.bfloat16), "tp").astype(jnp.float32)).astype(
        jnp.bfloat16
    )
    prompt_out = result[:prompt_rows][None]
    cont_out = result[prompt_rows:][None, None]
    cotangent = jnp.concatenate([prompt_cot[0], cont_cot[0, 0]], axis=0)
    down_grad = jnp.einsum("nf,nd->fd", act_low, cotangent, preferred_element_type=jnp.float32)
    act_grad = jnp.einsum("nd,fd->nf", cotangent, ffn_out, preferred_element_type=jnp.float32)
    upper_grad = gelu_pull(act_grad)[0].astype(jnp.bfloat16)
    in_grad = jnp.einsum("nd,nf->df", second_low, upper_grad, preferred_element_type=jnp.float32)
    second_terms = jnp.einsum("nf,df->nd", upper_grad, ffn_in, preferred_element_type=jnp.float32)
    second_grad = lax.psum(second_terms.astype(jnp.bfloat16), "tp").astype(jnp.float32)
    _, second_pull = jax.vjp(layer_norm, resid, gains[1], shifts[1])
    resid_grad = cotangent.astype(jnp.float32) + second_pull(second_grad)[0]
    norm_two = norm_terms(own_rows(resid), own_rows(second_grad))
    mixed_low = resid_grad.astype(jnp.bfloat16)
    mixing_grad = jnp.einsum("ne,nd->ed", attended, mixed_low, preferred_element_type=jnp.float32)
    attended_grad = jnp.einsum(
        "nd,ed->ne", mixed_low, out_weight, preferred_element_type=jnp.float32
    ).astype(jnp.bfloat16)

    def backward_head(carry, pieces):
        queries, keys, values, log_sum, head_grad = pieces
        scores = head_scores(queries, keys, visible, scale)
        probs = jnp.exp(scores - log_sum[:, None])
        prob_grad = jnp.einsum("ne,ke->nk", head_grad, values, preferred_element_type=jnp.float32)
        inner = jnp.sum(probs * prob_grad, axis=-1, keepdims=True)
        score_grad = (probs * (prob_grad - inner)).astype(jnp.bfloat16)
        query_grad = jnp.dot(score_grad, keys, preferred_element_type=jnp.float32) * scale
        key_grad = (
            jnp.einsum("nk,ne->ke", score_grad, queries, preferred_element_type=jnp.float32) * scale
        )
        value_grad = jnp.einsum(
            "nk,ne->ke", probs.astype(jnp.bfloat16), head_grad, preferred_element_type=jnp.float32
        )
        return (carry, (query_grad, key_grad, value_grad))

    _, (query_grads, key_grads, value_grads) = lax.scan(
        backward_head,
        nothing,
        (
            head_queries,
            split_heads(keyvals[0]),
            split_heads(keyvals[1]),
            log_sums,
            split_heads(attended_grad),
        ),
    )
    query_grad = join_heads(query_grads)
    key_grad = join_heads(key_grads)
    value_grad = join_heads(value_grads)
    shared_grad = lax.psum_scatter(
        jnp.stack([key_grad[:prompt_keys], value_grad[:prompt_keys]]).astype(jnp.bfloat16),
        "seq",
        scatter_dimension=1,
        tiled=True,
    ).astype(jnp.float32)
    key_full = jnp.concatenate([shared_grad[0], key_grad[prompt_keys:]], axis=0)
    value_full = jnp.concatenate([shared_grad[1], value_grad[prompt_keys:]], axis=0)
    proj_grad = jnp.stack([query_grad, key_full, value_full]).astype(jnp.bfloat16)
    qkv_grad = jnp.einsum("nd,cne->cde", normed_low, proj_grad, preferred_element_type=jnp.float32)
    first_terms = jnp.einsum(
        "cne,cde->nd", proj_grad, qkv_weight, preferred_element_type=jnp.float32
    )
    first_grad, norm_two_sum = (
        lax.psum(first_terms.astype(jnp.bfloat16), "tp").astype(jnp.float32),
        lax.psum(norm_two.astype(jnp.bfloat16), "tp").astype(jnp.float32),
    )
    token_back, gain_one, shift_one = first_pull(first_grad)
    token_grad = resid_grad + token_back
    prompt_grad = token_grad[:prompt_rows].astype(jnp.bfloat16)[None]
    cont_grad = token_grad[prompt_rows:].astype(jnp.bfloat16)[None, None]
    seq_count = lax.axis_size("seq")
    piece_width = width // (seq_count * tp_count)

    def own_part(vectors):
        arranged = vectors.reshape(2, seq_count, tp_count, piece_width)
        picked = lax.dynamic_index_in_dim(arranged, lax.axis_index("tp"), axis=2, keepdims=False)
        return picked.reshape(2, seq_count * piece_width)

    gain_grads = own_part(jnp.stack([gain_one, norm_two_sum[0]]))
    shift_grads = own_part(jnp.stack([shift_one, norm_two_sum[1]]))
    shards = (
        lax.psum_scatter(
            qkv_grad.astype(jnp.bfloat16), "seq", scatter_dimension=1, tiled=True
        ).astype(jnp.float32),
        lax.psum_scatter(
            mixing_grad.astype(jnp.bfloat16), "seq", scatter_dimension=1, tiled=True
        ).astype(jnp.float32),
        lax.psum_scatter(
            in_grad.astype(jnp.bfloat16), "seq", scatter_dimension=0, tiled=True
        ).astype(jnp.float32),
        lax.psum_scatter(
            down_grad.astype(jnp.bfloat16), "seq", scatter_dimension=1, tiled=True
        ).astype(jnp.float32),
        lax.psum_scatter(
            gain_grads.astype(jnp.bfloat16), "seq", scatter_dimension=1, tiled=True
        ).astype(jnp.float32),
        lax.psum_scatter(
            shift_grads.astype(jnp.bfloat16), "seq", scatter_dimension=1, tiled=True
        ).astype(jnp.float32),
    )
    summed = (
        lax.psum(shards[0].astype(jnp.bfloat16), "grp").astype(jnp.float32),
        lax.psum(shards[1].astype(jnp.bfloat16), "grp").astype(jnp.float32),
        lax.psum(shards[2].astype(jnp.bfloat16), "grp").astype(jnp.float32),
        lax.psum(shards[3].astype(jnp.bfloat16), "grp").astype(jnp.float32),
        lax.psum(shards[4].astype(jnp.bfloat16), "grp").astype(jnp.float32),
        lax.psum(shards[5].astype(jnp.bfloat16), "grp").astype(jnp.float32),
    )
    return (
        prompt_out,
        cont_out,
        prompt_grad,
        cont_grad,
        summed[0],
        summed[1],
        summed[2],
        summed[3],
        summed[4],
        summed[5],
    )


def solution(mesh):
    placed = (
        P("grp", "seq", None),
        P("grp", "seq", None, None),
        P("grp", "seq", None),
        P("grp", "seq", None, None),
        P("grp", "seq"),
        P(None, None, "tp"),
        P("tp", None),
        P(None, "tp"),
        P("tp", None),
        P(),
        P(),
    )
    return jax.shard_map(
        body,
        mesh=mesh,
        in_specs=placed,
        out_specs=(
            P("grp", "seq", None),
            P("grp", "seq", None, None),
            P("grp", "seq", None),
            P("grp", "seq", None, None),
            P(None, "seq", "tp"),
            P("tp", "seq"),
            P("seq", "tp"),
            P("tp", "seq"),
            P(None, ("seq", "tp")),
            P(None, ("seq", "tp")),
        ),
        check_vma=False,
    )
```

profile of v0, /device:TPU:0, one launch (start us, length us, event | category | flops | bytes accessed | tf_op | source)
XLA Modules:
  0.0 824.5 jit_solution(16898805846346654703)
XLA Ops:
  11.4 3.8 convert_bitcast_fusion
  24.6 45.9 %all-gather.2.cloned.1.call-done = bf16[2,1536,384]{1,2,0:T(8,128)(2,1)} async-done(((bf16[2,384,384]{1,2,0:T(8,128)(2,1)}), bf16[2,1536,384]{1,2,0:T(8,128)(2,1)}) %all-gather.2.cloned.1.call-update) | async-done | bytes 2359312 | tf_op jit(solution)/shard_map/all_gather | solution.py:73
  70.6 4.0 pad_maximum_fusion.2
  74.6 4.1 copy.59
  78.7 4.1 copy.60
  83.8 49.4 %while.28 = (s32[]{:T(128)}, bf16[6,896,64]{1,2,0:T(8,128)(2,1)}, f32[6,896]{1,0:T(8,128)S(1)}, bf16[6,896,64]{2,1,0:T(8,128)(2,1)}, bf16[6,2048,64]{2,1,0:T(8,1...) while((s32[]{:T(128)}, bf16[6,896,64]{1,2,0:T(8,128)(2,1)}, ...), condition=%wide.region_5.6_spmd.clone, body=%wide.region_2.5_spmd.clone.sunk | while | flops 489946240 | bytes 23579128 | solution.py:100
  83.8 3.6 fusion.124
  88.5 3.4 fusion.126
  92.0 3.6 fusion.124
  96.8 3.4 fusion.126
  100.3 3.6 fusion.124
  105.0 3.4 fusion.126
  108.5 3.6 fusion.124
  113.3 3.4 fusion.126
  116.7 3.6 fusion.124
  121.5 3.4 fusion.126
  125.0 3.6 fusion.124
  129.7 3.4 fusion.126
  133.2 3.7 fusion.88
  137.5 75.6 %all-reduce.8.cloned.1.call-done = f32[896,768]{1,0:T(8,128)} async-done(((f32[896,768]{1,0:T(8,128)}), f32[896,768]{1,0:T(8,128)}) %all-reduce.8.cloned.1.call-update) | async-done | bytes 2752528 | tf_op jit(solution)/shard_map/psum | solution.py:105
  215.9 14.8 %multiply_convert_fusion.1 = (bf16[896,1536]{1,0:T(8,128)(2,1)}, f32[896,1536]{1,0:T(8,128)S(1)}, f32[896,1536]{1,0:T(8,128)S(1)}) fusion(bf16[768,1536]{1,0:T(8,128)(2,1)S(1)} %copy-done, f32[896,768]{1,0:T(8,128)S(1)} %get-tuple-element.266, f32[768]{0:T(1024)S(1)} %get-tuple-element.209, f32[768]{0:T(1024)S(1)} %get-tuple-element.277, ...), kind=kOutput, calls=%fused_computation.59 | convolution fusion | flops 2206826496 | bytes 18887680 | tf_op jit(solution)/shard_map/dot_general | solution.py:107
  230.7 4.3 add_convert_fusion
  236.6 3.4 convolution_convert_fusion.2
  240.3 47.2 %all-reduce.10.cloned.1.call-done = bf16[896,768]{1,0:T(8,128)(2,1)} async-done(((bf16[896,768]{1,0:T(8,128)(2,1)}), bf16[896,768]{1,0:T(8,128)(2,1)}) %all-reduce.10.cloned.1.call-update) | async-done | bytes 1376272 | tf_op jit(solution)/shard_map/psum | solution.py:122
  287.4 2.9 multiply_reduce_fusion.1
  290.4 2.8 fusion.84
  296.9 122.4 %while.29 = (s32[]{:T(128)}, bf16[6,896,64]{1,2,0:T(8,128)(2,1)S(1)}, bf16[6,2048,64]{1,2,0:T(8,128)(2,1)}, bf16[6,2048,64]{1,2,0:T(8,128)(2,1)}, bf16[6,896,64]...) while((s32[]{:T(128)}, ...), condition=%wide.region_15.16_spmd.clone, body=%wide.region_13.15_spmd.clone.sunk | while | flops 1196612736 | bytes 115471480 | solution.py:148
  299.1 5.2 multiply_reduce_fusion.6
  304.3 5.8 multiply_convert_fusion.3
  312.2 2.6 fusion.136
  319.5 5.3 multiply_reduce_fusion.6
  324.7 5.8 multiply_convert_fusion.3
  339.9 5.2 multiply_reduce_fusion.6
  345.1 5.8 multiply_convert_fusion.3
  353.0 2.6 fusion.136
  360.3 5.2 multiply_reduce_fusion.6
  365.5 5.8 multiply_convert_fusion.3
  373.4 2.6 fusion.136
  380.7 5.2 multiply_reduce_fusion.6
  386.0 5.8 multiply_convert_fusion.3
  401.1 5.2 multiply_reduce_fusion.6
  406.4 5.8 multiply_convert_fusion.3
  425.8 5.9 convolution_convert_fusion.3
  434.6 38.8 %reduce-scatter.14.cloned.1.call-done = bf16[2,384,384]{2,1,0:T(8,128)(2,1)} async-done(((bf16[2,1536,384]{2,1,0:T(8,128)(2,1)}), bf16[2,384,384]{2,1,0:T(8,128)(2,1)}) %reduce-scatter.14.cloned.1.call-update) | async-done | bytes 589840 | tf_op jit(solution)/shard_map/reduce_scatter | solution.py:162
  475.6 3.1 bitcast_convert_fusion
  480.1 4.7 convert_bitcast_fusion.1
  484.8 5.2 copy.71
  490.0 3.3 copy.79
  493.3 3.2 convolution_convert_fusion.5
  496.6 7.1 convolution_convert_fusion.1
  504.0 5.7 convolution_convert_fusion
  515.0 4.9 psum.85
  520.1 35.5 %all-reduce.14.cloned.1.call-done = (bf16[896,768]{1,0:T(8,128)(2,1)}, bf16[896,768]{1,0:T(8,128)(2,1)}) async-done(((bf16[896,768]{1,0:T(8,128)(2,1)}, bf16[896,768]{1,0:T(8,128)(2,1)}), (bf16[896,768]{1,0:T(8,128)(2,1)}, bf16[896,768]{1,0:T(8,128)(2,1)})) %all-reduce.14.cloned.1.call-update) | async-done | bytes 2752528 | tf_op jit(solution)/shard_map/psum | solution.py:111
  558.0 2.9 fusion.66
  561.8 4.5 add_convert_fusion.1
  567.2 3.5 add_convert_fusion.2
  570.8 25.5 %reduce-scatter.22.cloned.1.call-done = bf16[192,1152]{1,0:T(8,128)(2,1)} async-done(((bf16[768,1152]{1,0:T(8,128)(2,1)}), bf16[192,1152]{1,0:T(8,128)(2,1)}) %reduce-scatter.22.cloned.1.call-update) | async-done | bytes 442384
  599.0 21.4 %reduce-scatter.16.cloned.1.call-done = bf16[384,192]{0,1:T(8,128)(2,1)} async-done(((bf16[384,768]{0,1:T(8,128)(2,1)}), bf16[384,192]{0,1:T(8,128)(2,1)}) %reduce-scatter.16.cloned.1.call-update) | async-done | bytes 147472 | tf_op jit(solution)/shard_map/reduce_scatter | solution.py:197
  620.4 48.3 %reduce-scatter.18.cloned.1.call-done = bf16[192,1536]{1,0:T(8,128)(2,1)} async-done(((bf16[768,1536]{1,0:T(8,128)(2,1)}), bf16[192,1536]{1,0:T(8,128)(2,1)}) %reduce-scatter.18.cloned.1.call-update) | async-done | bytes 589840 | tf_op jit(solution)/shard_map/reduce_scatter | solution.py:200
  668.7 49.4 %reduce-scatter.20.cloned.1.call-done = bf16[1536,192]{0,1:T(8,128)(2,1)} async-done(((bf16[1536,768]{0,1:T(8,128)(2,1)}), bf16[1536,192]{0,1:T(8,128)(2,1)}) %reduce-scatter.20.cloned.1.call-update) | async-done | bytes 589840 | tf_op jit(solution)/shard_map/reduce_scatter | solution.py:203
  722.8 16.8 %reduce-scatter.24.cloned.1.call-done = bf16[96,2]{1,0:T(8,128)(2,1)} async-done(((bf16[384,2]{1,0:T(8,128)(2,1)}), bf16[96,2]{1,0:T(8,128)(2,1)}) %reduce-scatter.24.cloned.1.call-update) | async-done | bytes 400
  740.6 19.4 %reduce-scatter.26.cloned.1.call-done = bf16[96,2]{1,0:T(8,128)(2,1)} async-done(((bf16[384,2]{1,0:T(8,128)(2,1)}), bf16[96,2]{1,0:T(8,128)(2,1)}) %reduce-scatter.26.cloned.1.call-update) | async-done | bytes 400
  760.8 5.7 all-reduce
  767.6 42.3 %all-reduce.12.cloned.1.call-done = (bf16[3,192,384]{1,2,0:T(8,128)(2,1)}, bf16[384,192]{0,1:T(8,128)(2,1)}, bf16[192,1536]{1,0:T(8,128)(2,1)}, bf16[1536,192]{0,1:T(8,128)(2,1)}) async-done(((bf16[3,192,384]{1,2,0:T(8,128)(2,1)}, bf16[384,192]{0,1:T(8,128)(2,1)}, bf16[192,1536]{1,0:T(8,128)(2,1)}, bf16[1536,192]{0,1:T(8,128)(2,1)}), (bf16[3,192,384]{1,2,0:T(8,128)(2,1)}, bf16[384,192]{0,1:T(8,128)(2,1)}, ...) | async-done | bytes 1769488 | tf_op jit(solution)/shard_map/psum | solution.py:214
  (284 shorter events, 118.3 us)
Async XLA Ops:
  7.2 208.6 %copy-start = (bf16[768,1536]{1,0:T(8,128)(2,1)S(1)}, bf16[768,1536]{1,0:T(8,128)(2,1)}, u32[]{:S(2)}) copy-start(bf16[768,1536]{1,0:T(8,128)(2,1)} %param.22) | copy-start | bytes 7077892
  7.2 4.2 copy-start.6
  7.2 3.7 copy-start.41
  7.2 3.7 copy-start.42
  7.2 63.3 %all-gather.2.cloned.1.call-start = ((), (), s32[]{:S(2)}) async-start(), calls=%async_computation.7 | async-start | bytes 2949120 | tf_op jit(solution)/shard_map/all_gather | solution.py:73
  7.3 4.2 copy-start.9
  9.0 6.2 copy-start.29
  10.9 4.3 copy-start.33
  11.0 4.3 copy-start.31
  11.0 4.3 copy-start.39
  11.0 204.8 %copy-start.37 = (f32[768]{0:T(1024)}, f32[768]{0:T(1024)S(1)}, u32[]{:S(2)}) copy-start(f32[768]{0:T(1024)S(1)} %get-tuple-element.209) | copy-start | bytes 9220
  17.4 195.6 %all-reduce.8.cloned.1.call-start = ((), (), s32[]{:S(2)}) async-start(), calls=%async_computation.8 | async-start | bytes 5505024 | tf_op jit(solution)/shard_map/psum | solution.py:105
  137.0 150.4 %all-reduce.10.cloned.1.call-start = ((), (), s32[]{:S(2)}) async-start(), calls=%async_computation.9 | async-start | bytes 2752512 | tf_op jit(solution)/shard_map/psum | solution.py:122
  215.3 15.3 %copy-start.4 = (f32[896,768]{1,0:T(8,128)}, f32[896,768]{1,0:T(8,128)S(1)}, u32[]{:S(2)}) copy-start(f32[896,768]{1,0:T(8,128)S(1)} %get-tuple-element.266) | copy-start | bytes 8257540
  215.8 14.8 %copy-start.14 = (bf16[1,1,512,768]{3,2,1,0:T(8,128)(2,1)S(1)}, bf16[1,1,512,768]{3,2,1,0:T(8,128)(2,1)}, u32[]{:S(2)}) copy-start(bf16[1,1,512,768]{3,2,1,0:T(8,128)(2,1)} %param.18) | copy-start | bytes 2359300
  215.8 14.8 %copy-start.19 = (bf16[1,384,768]{2,1,0:T(8,128)(2,1)S(1)}, bf16[1,384,768]{2,1,0:T(8,128)(2,1)}, u32[]{:S(2)}) copy-start(bf16[1,384,768]{2,1,0:T(8,128)(2,1)} %param.17) | copy-start | bytes 1769476
  215.8 14.8 %copy-start.43 = (bf16[1536,768]{1,0:T(8,128)(2,1)S(1)}, bf16[1536,768]{1,0:T(8,128)(2,1)}, u32[]{:S(2)}) copy-start(bf16[1536,768]{1,0:T(8,128)(2,1)} %param.23) | copy-start | bytes 7077892
  240.0 233.3 %reduce-scatter.14.cloned.1.call-start = ((), (), s32[]{:S(2)}) async-start(), calls=%async_computation.10 | async-start | bytes 2949120 | tf_op jit(solution)/shard_map/reduce_scatter | solution.py:162
  287.4 3.0 copy-start.11
  290.4 2.9 copy-start.20
  299.1 5.3 copy-start.2
  304.3 5.8 copy-start.23
  310.2 2.0 copy-start.3
  312.2 5.1 copy-start.24
  319.5 5.3 copy-start.2
  324.7 5.8 copy-start.23
  330.6 2.0 copy-start.3
  332.6 5.1 copy-start.24
  339.9 5.3 copy-start.2
  345.1 5.8 copy-start.23
  351.0 2.0 copy-start.3
  353.0 5.1 copy-start.24
  360.3 5.3 copy-start.2
  365.5 5.8 copy-start.23
  371.4 2.0 copy-start.3
  373.4 5.1 copy-start.24
  380.7 5.3 copy-start.2
  385.9 5.8 copy-start.23
  391.8 2.0 copy-start.3
  393.8 5.1 copy-start.24
  401.1 5.3 copy-start.2
  406.3 5.8 copy-start.23
  412.2 2.0 copy-start.3
  414.2 5.1 copy-start.24
  425.5 130.1 %all-reduce.14.cloned.1.call-start = ((), (), s32[]{:S(2)}) async-start(), calls=%async_computation.18 | async-start | bytes 5505024 | tf_op jit(solution)/shard_map/psum | solution.py:111
  425.8 8.0 copy-start.17
  473.4 2.3 copy-start.44
  478.8 117.5 %reduce-scatter.22.cloned.1.call-start = ((), (), s32[]{:S(2)}) async-start(), calls=%async_computation.14 | async-start | bytes 2211840
  490.0 3.3 copy-start.18
  493.2 3.3 copy-start.38
  493.3 127.2 %reduce-scatter.16.cloned.1.call-start = ((), (), s32[]{:S(2)}) async-start(), calls=%async_computation.11 | async-start | bytes 737280 | tf_op jit(solution)/shard_map/reduce_scatter | solution.py:197
  496.5 7.5 copy-start.15
  496.5 7.5 copy-start.21
  496.5 172.2 %reduce-scatter.18.cloned.1.call-start = ((), (), s32[]{:S(2)}) async-start(), calls=%async_computation.12 | async-start | bytes 2949120 | tf_op jit(solution)/shard_map/reduce_scatter | solution.py:200
  503.7 214.5 %reduce-scatter.20.cloned.1.call-start = ((), (), s32[]{:S(2)}) async-start(), calls=%async_computation.13 | async-start | bytes 2949120 | tf_op jit(solution)/shard_map/reduce_scatter | solution.py:203
  509.7 229.9 %reduce-scatter.24.cloned.1.call-start = ((), (), s32[]{:S(2)}) async-start(), calls=%async_computation.15 | async-start | bytes 122880
  511.2 3.4 copy-start.5
  514.6 43.4 %copy-start.36 = (f32[896]{0:T(1024)S(1)}, f32[896]{0:T(1024)}, u32[]{:S(2)}) copy-start(f32[896]{0:T(1024)} %copy-done.35) | copy-start | bytes 10756
  566.3 193.7 %reduce-scatter.26.cloned.1.call-start = ((), (), s32[]{:S(2)}) async-start(), calls=%async_computation.16 | async-start | bytes 122880
  567.2 242.8 %all-reduce.12.cloned.1.call-start = ((), (), s32[]{:S(2)}) async-start(), calls=%async_computation.17 | async-start | bytes 3833856 | tf_op jit(solution)/shard_map/psum | solution.py:214
  570.8 147.4 %copy-start.12 = (bf16[896,768]{1,0:T(8,128)(2,1)S(1)}, bf16[896,768]{1,0:T(8,128)(2,1)}, u32[]{:S(2)}) copy-start(bf16[896,768]{1,0:T(8,128)(2,1)} %add_convert_fusion.1) | copy-start | bytes 4128772
  718.2 3.7 copy-start.13
  739.6 77.6 %copy-start.1 = (bf16[768,1536]{1,0:T(8,128)(2,1)S(1)}, bf16[768,1536]{1,0:T(8,128)(2,1)}, u32[]{:S(2)}) copy-start(bf16[768,1536]{1,0:T(8,128)(2,1)} %param.22) | copy-start | bytes 7077892
  809.9 6.1 copy-start.27
  (14 other events, 17.8 us)
Sparse Core Ops, SparseCore 0:
  17.6 52.9 all-gather.1
  137.1 75.9 all-reduce.7
  240.2 47.2 all-reduce.9
  425.6 47.6 reduce-scatter.13
  478.9 76.6 all-reduce.13
  557.8 38.4 reduce-scatter.21
  599.2 21.2 reduce-scatter.15
  622.7 45.9 reduce-scatter.17
  671.0 47.0 reduce-scatter.19
  720.8 18.7 reduce-scatter.23
  742.4 17.5 reduce-scatter.25
  763.0 46.8 all-reduce.11
where the time goes:
time: 835 us; the launch traced here: 824 us
  waiting for transfers between devices  466 us (56%)
  matrix products  182 us (22%)
  other arithmetic  84.8 us (10%)
  local copies, waits for them, and re-layouts  62.9 us (8%)
  between operations  16 us (2%)
  blocking collectives  10.6 us (1%)
    psum x1, waiting for transfers between devices, body(): resid = tokens + lax.psum(mixed_terms, 'tp')  75.6 us
    unnamed x15, waiting for transfers between devices  62 us
    dot_general x12, matrix products, head_scores(): jnp.einsum('ne,ke->nk', queries, keys, preferred_element_type=jnp.float32)  53 us
    reduce_scatter x1, waiting for transfers between devices, body(): lax.psum_scatter(down_grad.astype(jnp.bfloat16), 'seq', scatter_dimension...  49.4 us
    reduce_scatter x1, waiting for transfers between devices, body(): lax.psum_scatter(in_grad.astype(jnp.bfloat16), 'seq', scatter_dimension=0...  48.3 us
    psum x1, waiting for transfers between devices, body(): lax.psum(second_terms.astype(jnp.bfloat16), 'tp').astype(jnp.float32)  47.2 us
    all_gather x1, waiting for transfers between devices, body(): gathered = lax.all_gather(own_kv, 'seq', axis=1, tiled=True)  45.9 us
    psum x1, waiting for transfers between devices, body(): lax.psum(shards[0].astype(jnp.bfloat16), 'grp').astype(jnp.float32)  42.3 us
  transfers between devices with their start and end apart: 12, of which 12 were waited for; matrix products, arithmetic and copies ran while one was open for 9% of the time, Pallas kernels for 0%

commit v1 on v0

v1 whole, which is shorter than its diff:
```python
import jax
import jax.numpy as jnp
from jax import lax
from jax.sharding import PartitionSpec as P

HEAD = 64
CORES = 2
norm_eps = 1e-05
hidden_value = -1e30
BF = jnp.bfloat16
F32 = jnp.float32


def pick(array, index, axis):
    return lax.dynamic_index_in_dim(array, index, axis, keepdims=False)


def shift_perm(count, step):
    return [(j, (j + step) % count) for j in range(count)]


def group_perm(count, core_flip, step):
    chips = count // CORES
    return [
        (x * CORES + c, ((x + step) % chips) * CORES + (c ^ core_flip))
        for x in range(chips)
        for c in range(CORES)
    ]


def tp_sum(part):
    low = lax.optimization_barrier(part.astype(BF))
    other = lax.ppermute(low, "tp", shift_perm(lax.axis_size("tp"), 1))
    return low.astype(F32) + other.astype(F32)


def spread_sum(grad):
    seq_n = lax.axis_size("seq")
    grp_n = lax.axis_size("grp")
    chips = grp_n // CORES
    seq_i = lax.axis_index("seq")
    grp_i = lax.axis_index("grp")
    core_i = grp_i % CORES
    chip_i = grp_i // CORES
    rows = grad.shape[0] // (seq_n * grp_n)
    width = grad.shape[1]
    low = grad.astype(BF).reshape(seq_n, CORES, chips, rows, width)
    got = lax.ppermute(pick(low, 1 - core_i, 1), "grp", group_perm(grp_n, 1, 0))
    half = (pick(low, core_i, 1).astype(F32) + got.astype(F32)).astype(BF)
    total = pick(half, chip_i, 1).astype(F32)
    for step in range(1, chips):
        sent = pick(half, (chip_i + step) % chips, 1)
        total += lax.ppermute(sent, "grp", group_perm(grp_n, 0, step)).astype(F32)
    part = total.astype(BF)
    total = pick(part, seq_i, 0).astype(F32)
    for step in range(1, seq_n):
        sent = pick(part, (seq_i + step) % seq_n, 0)
        total += lax.ppermute(sent, "seq", shift_perm(seq_n, step)).astype(F32)
    mine = lax.optimization_barrier(total.astype(BF))
    line = jnp.zeros((chips, rows, width), BF)
    line = lax.dynamic_update_index_in_dim(line, mine, chip_i, 0)
    for step in range(1, chips):
        came = lax.ppermute(mine, "grp", group_perm(grp_n, 0, step))
        line = lax.dynamic_update_index_in_dim(line, came, (chip_i - step) % chips, 0)
    other = lax.ppermute(line, "grp", group_perm(grp_n, 1, 0))
    first = core_i == 0
    both = jnp.stack([jnp.where(first, line, other), jnp.where(first, other, line)])
    return both.reshape(CORES * chips * rows, width).astype(F32)


def norm_parts(tokens):
    mean = jnp.mean(tokens, axis=-1, keepdims=True)
    centred = tokens - mean
    variance = jnp.mean(centred * centred, axis=-1, keepdims=True)
    inv = lax.rsqrt(variance + norm_eps)
    return centred * inv, inv


def norm_back(normed, inv, upstream, gain):
    scaled = upstream * gain
    mean = jnp.mean(scaled, axis=-1, keepdims=True)
    inner = jnp.mean(scaled * normed, axis=-1, keepdims=True)
    return inv * (scaled - mean - normed * inner)


def exact_gelu(upper):
    return jax.nn.gelu(upper, approximate=False)


def body(
    prompt_in,
    cont_in,
    prompt_cot,
    cont_cot,
    prompt_len,
    qkv_weight,
    out_weight,
    ffn_in,
    ffn_out,
    norm_gain,
    norm_shift,
):
    prompt_rows = prompt_in.shape[1]
    width = prompt_in.shape[2]
    local_width = qkv_weight.shape[2]
    local_heads = local_width // HEAD
    scale = HEAD ** (-0.5)
    seq_n = lax.axis_size("seq")
    seq_i = lax.axis_index("seq")
    tp_n = lax.axis_size("tp")
    tokens = jnp.concatenate([prompt_in[0], cont_in[0, 0]], axis=0).astype(F32)
    row_count = tokens.shape[0]
    gains = norm_gain.astype(F32)
    shifts = norm_shift.astype(F32)
    normed_one, inv_one = norm_parts(tokens)
    first_low = (normed_one * gains[0] + shifts[0]).astype(BF)
    projected = jnp.einsum(
        "nd,cde->cne", first_low, qkv_weight, preferred_element_type=F32
    ).astype(BF)
    own_kv = projected[1:3, :prompt_rows]
    blocks = [own_kv]
    places = [seq_i]
    for step in range(1, seq_n):
        blocks.append(lax.ppermute(own_kv, "seq", shift_perm(seq_n, step)))
        places.append((seq_i - step) % seq_n)
    prompt_keys = seq_n * prompt_rows

    def split_heads(matrix):
        return matrix.reshape(matrix.shape[0], local_heads, HEAD).transpose(1, 0, 2)

    def join_heads(stacked):
        return stacked.transpose(1, 0, 2).reshape(stacked.shape[1], local_width)

    keyvals = jnp.concatenate(blocks + [projected[1:3, prompt_rows:]], axis=1)
    key_count = keyvals.shape[1]
    inside = jnp.arange(prompt_rows, dtype=jnp.int32)
    position = (jnp.stack(places)[:, None] * prompt_rows + inside[None, :]).reshape(-1)
    position = jnp.concatenate(
        [position, jnp.full((key_count - prompt_keys,), prompt_keys, jnp.int32)]
    )[None, :]
    row_index = jnp.arange(row_count, dtype=jnp.int32)[:, None]
    limit = jnp.where(row_index < prompt_rows, prompt_keys, prompt_len[0, 0])
    visible = (position < limit) | (position >= prompt_keys) & (row_index >= prompt_rows)
    head_queries = split_heads(projected[0])
    nothing = jnp.zeros((), F32)

    def head_scores(queries, keys):
        scores = jnp.einsum("ne,ke->nk", queries, keys, preferred_element_type=F32) * scale
        return jnp.where(visible, scores, hidden_value)

    def forward_head(carry, pieces):
        queries, keys, values = pieces
        scores = head_scores(queries, keys)
        largest = jnp.max(scores, axis=-1, keepdims=True)
        weights = jnp.exp(scores - largest)
        summed = jnp.sum(weights, axis=-1, keepdims=True)
        probs = (weights / summed).astype(BF)
        output = jnp.dot(probs, values, preferred_element_type=F32)
        return (carry, (output, largest[:, 0] + jnp.log(summed[:, 0])))

    _, (head_out, log_sums) = lax.scan(
        forward_head, nothing, (head_queries, split_heads(keyvals[0]), split_heads(keyvals[1]))
    )
    attended = join_heads(head_out).astype(BF)
    resid = tokens + tp_sum(jnp.dot(attended, out_weight, preferred_element_type=F32))
    normed_two, inv_two = norm_parts(resid)
    second_low = (normed_two * gains[1] + shifts[1]).astype(BF)
    upper = jnp.dot(second_low, ffn_in, preferred_element_type=F32)
    activated, gelu_pull = jax.vjp(exact_gelu, upper)
    act_low = activated.astype(BF)
    cotangent = jnp.concatenate([prompt_cot[0], cont_cot[0, 0]], axis=0)
    act_grad = jnp.einsum("nd,fd->nf", cotangent, ffn_out, preferred_element_type=F32)
    upper_grad = gelu_pull(act_grad)[0].astype(BF)
    second_terms = jnp.einsum("nf,df->nd", upper_grad, ffn_in, preferred_element_type=F32)
    second_grad = tp_sum(second_terms)
    in_grad = jnp.einsum("nd,nf->df", second_low, upper_grad, preferred_element_type=F32)
    down_grad = jnp.einsum("nd,nf->df", cotangent, act_low, preferred_element_type=F32)
    in_sum = spread_sum(in_grad)
    down_sum = spread_sum(down_grad)
    ffn_terms = jnp.dot(act_low, ffn_out, preferred_element_type=F32)
    result = (resid + tp_sum(ffn_terms)).astype(BF)
    prompt_out = result[:prompt_rows][None]
    cont_out = result[prompt_rows:][None, None]
    resid_grad = cotangent.astype(F32) + norm_back(normed_two, inv_two, second_grad, gains[1])
    mixed_low = resid_grad.astype(BF)
    mixing_grad = jnp.einsum("nd,ne->de", mixed_low, attended, preferred_element_type=F32)
    mixing_sum = spread_sum(mixing_grad)
    attended_grad = jnp.einsum("nd,ed->ne", mixed_low, out_weight, preferred_element_type=F32).astype(
        BF
    )

    def backward_head(carry, pieces):
        queries, keys, values, log_sum, head_grad = pieces
        scores = head_scores(queries, keys)
        probs = jnp.exp(scores - log_sum[:, None])
        prob_grad = jnp.einsum("ne,ke->nk", head_grad, values, preferred_element_type=F32)
        inner = jnp.sum(probs * prob_grad, axis=-1, keepdims=True)
        score_grad = (probs * (prob_grad - inner)).astype(BF)
        query_grad = jnp.dot(score_grad, keys, preferred_element_type=F32) * scale
        key_grad = jnp.einsum("nk,ne->ke", score_grad, queries, preferred_element_type=F32) * scale
        value_grad = jnp.einsum(
            "nk,ne->ke", probs.astype(BF), head_grad, preferred_element_type=F32
        )
        return (carry, (query_grad, key_grad, value_grad))

    _, (query_grads, key_grads, value_grads) = lax.scan(
        backward_head,
        nothing,
        (
            head_queries,
            split_heads(keyvals[0]),
            split_heads(keyvals[1]),
            log_sums,
            split_heads(attended_grad),
        ),
    )
    query_grad = join_heads(query_grads)
    keyval_grad = jnp.stack([join_heads(key_grads), join_heads(value_grads)])
    shared = keyval_grad[:, :prompt_rows]
    for step in range(1, seq_n):
        block = keyval_grad[:, step * prompt_rows : (step + 1) * prompt_rows].astype(BF)
        shared += lax.ppermute(block, "seq", shift_perm(seq_n, -step)).astype(F32)
    full = jnp.concatenate([shared, keyval_grad[:, prompt_keys:]], axis=1)
    proj_grad = jnp.concatenate([query_grad[None], full]).astype(BF)
    first_terms = jnp.einsum("cne,cde->nd", proj_grad, qkv_weight, preferred_element_type=F32)
    first_grad = tp_sum(first_terms)
    qkv_grad = jnp.einsum("nd,cne->dce", first_low, proj_grad, preferred_element_type=F32)
    qkv_sum = spread_sum(qkv_grad.reshape(width, 3 * local_width))
    token_grad = resid_grad + norm_back(normed_one, inv_one, first_grad, gains[0])
    prompt_grad = token_grad[:prompt_rows].astype(BF)[None]
    cont_grad = token_grad[prompt_rows:].astype(BF)[None, None]
    norm_rows = jnp.stack(
        [
            jnp.sum(first_grad * normed_one, axis=0),
            jnp.sum(second_grad * normed_two, axis=0),
            jnp.sum(first_grad, axis=0),
            jnp.sum(second_grad, axis=0),
        ]
    )
    norm_blocks = norm_rows.reshape(4, seq_n, tp_n, -1)
    norm_own = pick(norm_blocks, lax.axis_index("tp"), 2)
    total = pick(norm_own, seq_i, 1)
    for step in range(1, seq_n):
        sent = pick(norm_own, (seq_i + step) % seq_n, 1)
        total += lax.ppermute(sent, "seq", shift_perm(seq_n, step))
    grp_n = lax.axis_size("grp")
    part = total
    for step in range(1, grp_n // CORES):
        total += lax.ppermute(part, "grp", group_perm(grp_n, 0, step))
    total = lax.optimization_barrier(total)
    total = total + lax.ppermute(total, "grp", group_perm(grp_n, 1, 0))
    seq_rows = width // seq_n
    return (
        prompt_out,
        cont_out,
        prompt_grad,
        cont_grad,
        qkv_sum.reshape(seq_rows, 3, local_width).transpose(1, 0, 2),
        mixing_sum.T,
        in_sum,
        down_sum.T,
        total[:2],
        total[2:],
    )


def solution(mesh):
    placed = (
        P("grp", "seq", None),
        P("grp", "seq", None, None),
        P("grp", "seq", None),
        P("grp", "seq", None, None),
        P("grp", "seq"),
        P(None, None, "tp"),
        P("tp", None),
        P(None, "tp"),
        P("tp", None),
        P(),
        P(),
    )
    return jax.shard_map(
        body,
        mesh=mesh,
        in_specs=placed,
        out_specs=(
            P("grp", "seq", None),
            P("grp", "seq", None, None),
            P("grp", "seq", None),
            P("grp", "seq", None, None),
            P(None, "seq", "tp"),
            P("tp", "seq"),
            P("seq", "tp"),
            P("tp", "seq"),
            P(None, ("seq", "tp")),
            P(None, ("seq", "tp")),
        ),
        check_vma=False,
    )
```

time: 835 us -> 594 us (0.71)
  waiting for transfers between devices: 466 us -> 208 us
  starting transfers between devices: 1.6 us -> 58.5 us
  matrix products: 182 us -> 166 us
  other arithmetic: 84.8 us -> 70.1 us
  local copies, waits for them, and re-layouts: 62.9 us -> 77.2 us
  between operations: 16 us -> 2.78 us
  blocking collectives: 10.6 us -> 0 us
    ppermute x0 -> x43, waiting for transfers between devices: none -> 208 us  [the longest x4 95.1 us: tp_sum(): other = lax.ppermute(low, 'tp', shift_perm(lax.axis_size('tp'), 1))]
    psum x4 -> x0, waiting for transfers between devices: 201 us -> none  [the longest x1 75.6 us: body(): resid = tokens + lax.psum(mixed_terms, 'tp')]
    reduce_scatter x4 -> x0, waiting for transfers between devices: 158 us -> none  [the longest x1 49.4 us: body(): lax.psum_scatter(down_grad.astype(jnp.bfloat16), 'seq', scatter_dimension...]
    unnamed x15 -> x0, waiting for transfers between devices: 62 us -> none
    ppermute x0 -> x43, starting transfers between devices: none -> 58.5 us  [the longest x12 20.5 us: spread_sum(): total += lax.ppermute(sent, 'seq', shift_perm(seq_n, step)).astype(F32)]
    all_gather x1 -> x0, waiting for transfers between devices: 45.9 us -> none  [body(): gathered = lax.all_gather(own_kv, 'seq', axis=1, tiled=True)]
    dot_general x54, matrix products: 182 us -> 166 us  [the longest x12 50.6 us: head_scores(): jnp.einsum('ne,ke->nk', queries, keys, preferred_element_type=F32) * scale]
    unnamed x93 -> x84, local copies, waits for them, and re-layouts: 23.7 us -> 9.66 us
  transfers between devices with their start and end apart: 12 -> 43, of which waited for: 12 -> 19; matrix products, arithmetic and copies ran while one was open for 9% -> 33% of each run, Pallas kernels for 0% -> 0%
where the time goes in v1:
time: 594 us; the launch traced here: 584 us
  waiting for transfers between devices  208 us (35%)
  matrix products  166 us (28%)
  local copies, waits for them, and re-layouts  77.2 us (13%)
  other arithmetic  70.1 us (12%)
  starting transfers between devices  58.5 us (10%)
    ppermute x4, waiting for transfers between devices, tp_sum(): other = lax.ppermute(low, 'tp', shift_perm(lax.axis_size('tp'), 1))  95.1 us
    dot_general x12, matrix products, head_scores(): jnp.einsum('ne,ke->nk', queries, keys, preferred_element_type=F32) * scale  50.6 us
    ppermute x3, waiting for transfers between devices, body(): blocks.append(lax.ppermute(own_kv, 'seq', shift_perm(seq_n, step)))  42.4 us
    ppermute x12, waiting for transfers between devices, spread_sum(): total += lax.ppermute(sent, 'seq', shift_perm(seq_n, step)).astype(F32)  40.7 us
    convert_element_type x6, other arithmetic, backward_head(): score_grad = (probs * (prob_grad - inner)).astype(BF)  34.2 us
    ppermute x12, starting transfers between devices, spread_sum(): total += lax.ppermute(sent, 'seq', shift_perm(seq_n, step)).astype(F32)  20.5 us
    dot_general x6, matrix products, forward_head(): output = jnp.dot(probs, values, preferred_element_type=F32)  20.2 us
    dot_general x6, matrix products, backward_head(): jnp.einsum('nk,ne->ke', score_grad, queries, preferred_element_type=F32)  15.3 us
  transfers between devices with their start and end apart: 43, of which 19 were waited for; matrix products, arithmetic and copies ran while one was open for 33% of the time, Pallas kernels for 0%

profile of v1, /device:TPU:0, one launch (start us, length us, event | category | flops | bytes accessed | tf_op | source)
XLA Modules:
  0.0 583.6 jit_solution(13909139882485190996)
XLA Ops:
  4.4 3.8 convert_bitcast_fusion
  10.7 5.1 collective-permute-start.2
  22.0 32.9 %collective-permute-done = bf16[2,384,384]{1,2,0:T(8,128)(2,1)} collective-permute-done((bf16[2,384,384]{1,2,0:T(8,128)(2,1)}, bf16[2,384,384]{1,2,0:T(8,128)(2,1)}, u32[]{:S(2)}, u32[]{:S(2)}) %collective-permute-start) | collective-permute-done | bytes 589856 | tf_op jit(solution)/shard_map/ppermute | solution.py:124
  57.0 9.5 %collective-permute-done.1 = bf16[2,384,384]{1,2,0:T(8,128)(2,1)} collective-permute-done((bf16[2,384,384]{1,2,0:T(8,128)(2,1)}, bf16[2,384,384]{1,2,0:T(8,128)(2,1)}, u32[]{:S(2)}, u32[]{:S(2)}) %collective-permute-start.1) | collective-permute-done | bytes 589856 | tf_op jit(solution)/shard_map/ppermute | solution.py:124
  72.6 4.0 fusion.124
  76.6 4.1 copy.32
  80.7 4.1 copy.33
  85.7 56.0 %while.28 = (s32[]{:T(128)}, bf16[6,896,64]{1,2,0:T(8,128)(2,1)}, f32[6,896]{1,0:T(8,128)}, bf16[6,896,64]{2,1,0:T(8,128)(2,1)}, bf16[6,2048,64]{2,1,0:T(8,128)(...) while((s32[]{:T(128)}, bf16[6,896,64]{1,2,0:T(8,128)(2,1)}, ...), condition=%wide.region_5.6_spmd.clone, body=%wide.region_2.5_spmd.clone.sunk | while | flops 489946240 | bytes 23587328 | solution.py:161
  85.7 3.4 fusion.160
  90.3 3.4 fusion.162
  95.0 3.4 fusion.160
  99.6 3.4 fusion.162
  104.3 3.4 fusion.160
  108.9 3.4 fusion.162
  113.6 3.4 fusion.160
  118.2 3.4 fusion.162
  122.9 3.4 fusion.160
  127.5 3.4 fusion.162
  132.2 3.4 fusion.160
  136.8 3.4 fusion.162
  141.7 3.4 convolution_convert_fusion.3
  146.6 29.9 %collective-permute-done.3 = bf16[896,768]{1,0:T(8,128)(2,1)} collective-permute-done((bf16[896,768]{1,0:T(8,128)(2,1)}, bf16[896,768]{1,0:T(8,128)(2,1)}, u32[]{:S(2)}, u32[]{:S(2)}) %collective-permute-start.3) | collective-permute-done | bytes 1376288 | tf_op jit(solution)/shard_map/ppermute | solution.py:33
  179.5 13.8 %multiply_convert_fusion.1 = (bf16[896,1536]{1,0:T(8,128)(2,1)S(1)}, f32[896,1536]{1,0:T(8,128)S(1)}, f32[896,1536]{1,0:T(8,128)S(1)}) fusion(bf16[768,1536]{1,0:T(8,128)(2,1)S(1)} %copy-done, f32[896,768]{1,0:T(8,128)S(1)} %get-tuple-element.236, f32[768]{0:T(1024)S(1)} %get-tuple-element.185, f32[768]{0:T(1024)S(1)} %get-tuple-element.277, ...), kind=kOutput, calls=%fused_computation.59 | convolution fusion | flops 2206826496 | bytes 18887680 | tf_op jit(solution)/shard_map/dot_general | solution.py:168
  193.4 4.5 add_convert_fusion
  200.2 3.2 convolution_convert_fusion.1
  203.5 3.0 convolution_convert_fusion
  216.2 55.0 %collective-permute-done.5 = bf16[896,768]{1,0:T(8,128)(2,1)S(1)} collective-permute-done((bf16[896,768]{1,0:T(8,128)(2,1)S(1)}, bf16[896,768]{1,0:T(8,128)(2,1)S(1)}, u32[]{:S(2)}, u32[]{:S(2)}) %collective-permute-start.5) | collective-permute-done | bytes 1376288 | tf_op jit(solution)/shard_map/ppermute | solution.py:33
  272.6 2.9 multiply_add_fusion
  279.5 125.0 %while.29 = (s32[]{:T(128)}, bf16[6,896,64]{1,2,0:T(8,128)(2,1)S(1)}, f32[6,2048,64]{1,2,0:T(8,128)}, f32[6,2048,64]{1,2,0:T(8,128)}, bf16[6,896,64]{2,1,0:T(8,1...) while((s32[]{:T(128)}, ...), condition=%wide.region_12.13_spmd.clone, body=%wide.region_10.12_spmd.clone.sunk | while | flops 1196612736 | bytes 102933120 | solution.py:206
  282.7 5.0 multiply_reduce_fusion.5
  287.8 5.7 multiply_convert_fusion.3
  298.0 2.6 fusion.173
  303.5 5.0 multiply_reduce_fusion.5
  308.6 5.7 multiply_convert_fusion.3
  324.3 5.0 multiply_reduce_fusion.5
  329.4 5.7 multiply_convert_fusion.3
  339.6 2.6 fusion.173
  345.1 5.0 multiply_reduce_fusion.5
  350.2 5.7 multiply_convert_fusion.3
  365.9 5.0 multiply_reduce_fusion.5
  371.0 5.7 multiply_convert_fusion.3
  386.7 5.0 multiply_reduce_fusion.5
  391.8 5.7 multiply_convert_fusion.3
  404.5 3.5 copy.36
  408.0 3.5 copy.35
  411.6 3.3 fusion.48
  420.0 3.2 collective-permute-start.8
  437.1 17.4 %collective-permute-done.19 = bf16[48,384]{1,0:T(8,128)(2,1)S(1)} collective-permute-done((bf16[48,384]{1,0:T(8,128)(2,1)S(1)}, bf16[48,384]{1,0:T(8,128)(2,1)S(1)}, u32[]{:S(2)}, u32[]{:S(2)}) %collective-permute-start.19) | collective-permute-done | bytes 36896 | tf_op jit(solution)/shard_map/ppermute | solution.py:58
  454.5 3.8 collective-permute-start.28
  463.0 4.0 collective-permute-start.35
  467.0 6.9 %collective-permute-done.27 = bf16[48,1536]{1,0:T(8,128)(2,1)S(1)} collective-permute-done((bf16[48,1536]{1,0:T(8,128)(2,1)S(1)}, bf16[48,1536]{1,0:T(8,128)(2,1)S(1)}, u32[]{:S(2)}, u32[]{:S(2)}) %collective-permute-start.27) | collective-permute-done | bytes 147488 | tf_op jit(solution)/shard_map/ppermute | solution.py:58
  474.0 6.2 %collective-permute-start.7 = (bf16[2,384,384]{2,1,0:T(8,128)(2,1)S(1)}, bf16[2,384,384]{2,1,0:T(8,128)(2,1)S(1)}, u32[]{:S(2)}, u32[]{:S(2)}) collective-permute-start(bf16[2,384,384]{2,1,0:T(8,128)(2,1)S(1)} %copy-done.24), channel_id=1, source_target_pairs={{0,4},{2,6},{4,0},{6,2},{1,5},{3,7},{5,1},{7,3},{8,12},{10,14},{12... | collective-permute-start | bytes 1769480 | tf_op jit(solution)/shard_map/ppermute | solution.py:222
  480.2 15.8 %collective-permute-done.34 = bf16[48,1536]{1,0:T(8,128)(2,1)S(1)} collective-permute-done((bf16[48,1536]{1,0:T(8,128)(2,1)S(1)}, bf16[48,1536]{1,0:T(8,128)(2,1)S(1)}, u32[]{:S(2)}, u32[]{:S(2)}) %collective-permute-start.34) | collective-permute-done | bytes 147488 | tf_op jit(solution)/shard_map/ppermute | solution.py:58
  498.4 9.0 %collective-permute-done.7 = bf16[2,384,384]{2,1,0:T(8,128)(2,1)S(1)} collective-permute-done((bf16[2,384,384]{2,1,0:T(8,128)(2,1)S(1)}, bf16[2,384,384]{2,1,0:T(8,128)(2,1)S(1)}, u32[]{:S(2)}, u32[]{:S(2)}) %collective-permute-start.7) | collective-permute-done | bytes 589856 | tf_op jit(solution)/shard_map/ppermute | solution.py:222
  507.8 3.1 bitcast_convert_fusion
  513.4 2.9 copy.39
  516.3 5.4 convert_element_type.343
  531.9 9.6 %collective-permute-done.11 = bf16[4,48,1152]{2,1,0:T(8,128)(2,1)S(1)} collective-permute-done((bf16[4,48,1152]{2,1,0:T(8,128)(2,1)S(1)}, bf16[4,48,1152]{2,1,0:T(8,128)(2,1)S(1)}, u32[]{:S(2)}, u32[]{:S(2)}) %collective-permute-start.11) | collective-permute-done | bytes 442400 | tf_op jit(solution)/shard_map/ppermute | solution.py:53
  541.7 3.8 collective-permute-start.14
  545.5 10.3 %collective-permute-done.9 = bf16[896,768]{1,0:T(8,128)(2,1)S(1)} collective-permute-done((bf16[896,768]{1,0:T(8,128)(2,1)}, bf16[896,768]{1,0:T(8,128)(2,1)S(1)}, u32[]{:S(2)}, u32[]{:S(2)}) %collective-permute-start.9) | collective-permute-done | bytes 1376288 | tf_op jit(solution)/shard_map/ppermute | solution.py:33
  557.7 3.8 collective-permute-start.40
  561.5 3.5 fusion.67
  565.0 3.0 collective-permute-start.13
  574.5 3.6 collective-permute-done.15
  (356 shorter events, 165.2 us)
Async XLA Ops:
  0.6 178.8 %copy-start = (bf16[768,1536]{1,0:T(8,128)(2,1)S(1)}, bf16[768,1536]{1,0:T(8,128)(2,1)}, u32[]{:S(2)}) copy-start(bf16[768,1536]{1,0:T(8,128)(2,1)} %param.22) | copy-start | bytes 7077892
  2.4 5.8 copy-start.26
  10.7 57.8 %collective-permute-start.2 = (bf16[2,384,384]{1,2,0:T(8,128)(2,1)}, bf16[2,384,384]{1,2,0:T(8,128)(2,1)}, u32[]{:S(2)}, u32[]{:S(2)}) collective-permute-start(bf16[2,384,384]{1,2,0:T(8,128)(2,1)} %get-tuple-element.248), channel_id=1, source_target_pairs={{0,6},{2,0},{4,2},{6,4},{1,7},{3,1},{5,3},{7,5},{8,14},{10,8},{12,... | collective-permute-start | bytes 1769480 | tf_op jit(solution)/shard_map/ppermute | solution.py:124
  15.8 50.7 %collective-permute-start.1 = (bf16[2,384,384]{1,2,0:T(8,128)(2,1)}, bf16[2,384,384]{1,2,0:T(8,128)(2,1)}, u32[]{:S(2)}, u32[]{:S(2)}) collective-permute-start(bf16[2,384,384]{1,2,0:T(8,128)(2,1)} %get-tuple-element.248), channel_id=1, source_target_pairs={{0,4},{2,6},{4,0},{6,2},{1,5},{3,7},{5,1},{7,3},{8,12},{10,14},{12... | collective-permute-start | bytes 1769480 | tf_op jit(solution)/shard_map/ppermute | solution.py:124
  15.8 39.2 %collective-permute-start = (bf16[2,384,384]{1,2,0:T(8,128)(2,1)}, bf16[2,384,384]{1,2,0:T(8,128)(2,1)}, u32[]{:S(2)}, u32[]{:S(2)}) collective-permute-start(bf16[2,384,384]{1,2,0:T(8,128)(2,1)} %get-tuple-element.248), channel_id=1, source_target_pairs={{0,2},{2,4},{4,6},{6,0},{1,3},{3,5},{5,7},{7,1},{8,10},{10,12},{12... | collective-permute-start | bytes 1769480 | tf_op jit(solution)/shard_map/ppermute | solution.py:124
  141.7 37.3 %copy-start.32 = (s32[2048]{0:T(1024)}, s32[2048]{0:T(1024)S(1)}, u32[]{:S(2)}) copy-start(s32[2048]{0:T(1024)S(1)} %get-tuple-element.571) | copy-start | bytes 24580
  141.7 37.3 %copy-start.38 = (pred[2048]{0:T(1024)(128)(4,1)}, pred[2048]{0:T(1024)(128)(4,1)S(1)}, u32[]{:S(2)}) copy-start(pred[2048]{0:T(1024)(128)(4,1)S(1)} %get-tuple-element.574) | copy-start | bytes 6148
  141.7 37.3 %copy-start.42 = (pred[896]{0:T(1024)(128)(4,1)}, pred[896]{0:T(1024)(128)(4,1)S(1)}, u32[]{:S(2)}) copy-start(pred[896]{0:T(1024)(128)(4,1)S(1)} %get-tuple-element.583) | copy-start | bytes 2692
  145.1 31.4 %collective-permute-start.3 = (bf16[896,768]{1,0:T(8,128)(2,1)}, bf16[896,768]{1,0:T(8,128)(2,1)}, u32[]{:S(2)}, u32[]{:S(2)}) collective-permute-start(bf16[896,768]{1,0:T(8,128)(2,1)} %convolution_convert_fusion.3), channel_id=1, source_target_pairs={{0,1},{1,0},{2,3},{3,2},{4,5},{5,4},{6,7},{7,6},{8,9},{9,8},{10,11... | collective-permute-start | bytes 4128776 | tf_op jit(solution)/shard_map/ppermute | solution.py:33
  179.5 13.9 %copy-start.20 = (bf16[1,1,512,768]{3,2,1,0:T(8,128)(2,1)S(1)}, bf16[1,1,512,768]{3,2,1,0:T(8,128)(2,1)}, u32[]{:S(2)}) copy-start(bf16[1,1,512,768]{3,2,1,0:T(8,128)(2,1)} %param.18) | copy-start | bytes 2359300
  179.5 13.9 %copy-start.23 = (bf16[1,384,768]{2,1,0:T(8,128)(2,1)S(1)}, bf16[1,384,768]{2,1,0:T(8,128)(2,1)}, u32[]{:S(2)}) copy-start(bf16[1,384,768]{2,1,0:T(8,128)(2,1)} %param.17) | copy-start | bytes 1769476
  179.5 13.9 %copy-start.40 = (bf16[1536,768]{1,0:T(8,128)(2,1)S(1)}, bf16[1536,768]{1,0:T(8,128)(2,1)}, u32[]{:S(2)}) copy-start(bf16[1536,768]{1,0:T(8,128)(2,1)} %param.23) | copy-start | bytes 7077892
  203.5 8.2 %collective-permute-start.24 = (bf16[4,2,48,1536]{3,2,1,0:T(8,128)(2,1)S(1)}, bf16[4,2,48,1536]{3,2,1,0:T(8,128)(2,1)S(1)}, u32[]{:S(2)}, u32[]{:S(2)}) collective-permute-start(bf16[4,2,48,1536]{3,2,1,0:T(8,128)(2,1)S(1)} %dynamic-slice_bitcast_fusion.1), channel_id=1, source_target_pairs={{0,8},{8,0},{16,24},{24,16},{1,9},{9,1},{17,25},{25,17},{2,10},{10... | collective-permute-start | bytes 3538952 | tf_op jit(solution)/shard_map/ppermute | solution.py:48
  206.7 7.7 %collective-permute-start.31 = (bf16[4,2,48,1536]{3,2,1,0:T(8,128)(2,1)S(1)}, bf16[4,2,48,1536]{3,2,1,0:T(8,128)(2,1)S(1)}, u32[]{:S(2)}, u32[]{:S(2)}) collective-permute-start(bf16[4,2,48,1536]{3,2,1,0:T(8,128)(2,1)S(1)} %dynamic-slice_bitcast_fusion), channel_id=1, source_target_pairs={{0,8},{8,0},{16,24},{24,16},{1,9},{9,1},{17,25},{25,17},{2,10},{10... | collective-permute-start | bytes 3538952 | tf_op jit(solution)/shard_map/ppermute | solution.py:48
  209.5 63.1 %collective-permute-start.4 = (bf16[896,768]{1,0:T(8,128)(2,1)S(1)}, bf16[896,768]{1,0:T(8,128)(2,1)S(1)}, u32[]{:S(2)}, u32[]{:S(2)}) collective-permute-start(bf16[896,768]{1,0:T(8,128)(2,1)S(1)} %convolution_convert_fusion.5), channel_id=1, source_target_pairs={{0,1},{1,0},{2,3},{3,2},{4,5},{5,4},{6,7},{7,6},{8,9},{9,8},{10,11... | collective-permute-start | bytes 4128776 | tf_op jit(solution)/shard_map/ppermute | solution.py:33
  211.1 60.1 %collective-permute-start.5 = (bf16[896,768]{1,0:T(8,128)(2,1)S(1)}, bf16[896,768]{1,0:T(8,128)(2,1)S(1)}, u32[]{:S(2)}, u32[]{:S(2)}) collective-permute-start(bf16[896,768]{1,0:T(8,128)(2,1)S(1)} %convolution_convert_fusion.4), channel_id=1, source_target_pairs={{0,1},{1,0},{2,3},{3,2},{4,5},{5,4},{6,7},{7,6},{8,9},{9,8},{10,11... | collective-permute-start | bytes 4128776 | tf_op jit(solution)/shard_map/ppermute | solution.py:33
  212.9 213.9 %collective-permute-start.25 = (bf16[4,48,1536]{2,1,0:T(8,128)(2,1)}, bf16[4,48,1536]{2,1,0:T(8,128)(2,1)}, u32[]{:S(2)}, u32[]{:S(2)}) collective-permute-start(bf16[4,48,1536]{2,1,0:T(8,128)(2,1)} %dynamic-slice_bitcast_fusion.4), channel_id=1, source_target_pairs={{0,16},{8,24},{16,0},{24,8},{1,17},{9,25},{17,1},{25,9},{2,18},{10... | collective-permute-start | bytes 1769480 | tf_op jit(solution)/shard_map/ppermute | solution.py:53
  214.7 57.9 %copy-start.15 = (bf16[4,2,48,1536]{3,2,1,0:T(8,128)(2,1)}, bf16[4,2,48,1536]{3,2,1,0:T(8,128)(2,1)S(1)}, u32[]{:S(2)}) copy-start(bf16[4,2,48,1536]{3,2,1,0:T(8,128)(2,1)S(1)} %fusion.74) | copy-start | bytes 3538948
  215.7 212.3 %collective-permute-start.32 = (bf16[4,48,1536]{2,1,0:T(8,128)(2,1)}, bf16[4,48,1536]{2,1,0:T(8,128)(2,1)}, u32[]{:S(2)}, u32[]{:S(2)}) collective-permute-start(bf16[4,48,1536]{2,1,0:T(8,128)(2,1)} %dynamic-slice_bitcast_fusion.3), channel_id=1, source_target_pairs={{0,16},{8,24},{16,0},{24,8},{1,17},{9,25},{17,1},{25,9},{2,18},{10... | collective-permute-start | bytes 1769480 | tf_op jit(solution)/shard_map/ppermute | solution.py:53
  278.6 145.5 %collective-permute-start.17 = (bf16[4,2,48,384]{3,2,1,0:T(8,128)(2,1)}, bf16[4,2,48,384]{3,2,1,0:T(8,128)(2,1)S(1)}, u32[]{:S(2)}, u32[]{:S(2)}) collective-permute-start(bf16[4,2,48,384]{3,2,1,0:T(8,128)(2,1)} %dynamic-slice_bitcast_fusion.6), channel_id=1, source_target_pairs={{0,8},{8,0},{16,24},{24,16},{1,9},{9,1},{17,25},{25,17},{2,10},{10... | collective-permute-start | bytes 884744 | tf_op jit(solution)/shard_map/ppermute | solution.py:48
  282.7 5.1 copy-start.2
  303.5 5.1 copy-start.2
  324.3 5.1 copy-start.2
  386.7 5.1 copy-start.2
  420.0 7.9 %copy-start.16 = (bf16[4,2,48,1536]{3,2,1,0:T(8,128)(2,1)S(1)}, bf16[4,2,48,1536]{3,2,1,0:T(8,128)(2,1)}, u32[]{:S(2)}) copy-start(bf16[4,2,48,1536]{3,2,1,0:T(8,128)(2,1)} %copy-done.15) | copy-start | bytes 3538948
  420.0 77.7 %collective-permute-start.6 = (bf16[2,384,384]{2,1,0:T(8,128)(2,1)}, bf16[2,384,384]{2,1,0:T(8,128)(2,1)S(1)}, u32[]{:S(2)}, u32[]{:S(2)}) collective-permute-start(bf16[2,384,384]{2,1,0:T(8,128)(2,1)} %get-tuple-element.241), channel_id=1, source_target_pairs={{0,6},{2,0},{4,2},{6,4},{1,7},{3,1},{5,3},{7,5},{8,14},{10,8},{12,... | collective-permute-start | bytes 1769480 | tf_op jit(solution)/shard_map/ppermute | solution.py:222
  420.0 78.3 %collective-permute-start.8 = (bf16[2,384,384]{2,1,0:T(8,128)(2,1)}, bf16[2,384,384]{2,1,0:T(8,128)(2,1)S(1)}, u32[]{:S(2)}, u32[]{:S(2)}) collective-permute-start(bf16[2,384,384]{2,1,0:T(8,128)(2,1)} %get-tuple-element.242), channel_id=1, source_target_pairs={{0,2},{2,4},{4,6},{6,0},{1,3},{3,5},{5,7},{7,1},{8,10},{10,12},{12... | collective-permute-start | bytes 1769480 | tf_op jit(solution)/shard_map/ppermute | solution.py:222
  425.2 6.0 %collective-permute-start.18 = (bf16[4,48,384]{2,1,0:T(8,128)(2,1)S(1)}, bf16[4,48,384]{2,1,0:T(8,128)(2,1)S(1)}, u32[]{:S(2)}, u32[]{:S(2)}) collective-permute-start(bf16[4,48,384]{2,1,0:T(8,128)(2,1)S(1)} %dynamic-slice_bitcast_fusion.13), channel_id=1, source_target_pairs={{0,16},{8,24},{16,0},{24,8},{1,17},{9,25},{17,1},{25,9},{2,18},{10... | collective-permute-start | bytes 442376 | tf_op jit(solution)/shard_map/ppermute | solution.py:53
  427.9 46.1 %copy-start.24 = (bf16[2,384,384]{2,1,0:T(8,128)(2,1)S(1)}, bf16[2,384,384]{2,1,0:T(8,128)(2,1)}, u32[]{:S(2)}) copy-start(bf16[2,384,384]{2,1,0:T(8,128)(2,1)} %get-tuple-element.243) | copy-start | bytes 1769476
  428.0 79.4 %copy-start.6 = (f32[1,2048,384]{2,1,0:T(8,128)S(1)}, f32[1,2048,384]{2,1,0:T(8,128)}, u32[]{:S(2)}) copy-start(f32[1,2048,384]{2,1,0:T(8,128)} %copy.35) | copy-start | bytes 9437188
  429.3 78.1 %copy-start.5 = (f32[1,2048,384]{2,1,0:T(8,128)S(1)}, f32[1,2048,384]{2,1,0:T(8,128)}, u32[]{:S(2)}) copy-start(f32[1,2048,384]{2,1,0:T(8,128)} %copy.36) | copy-start | bytes 9437188
  431.3 23.2 %collective-permute-start.19 = (bf16[48,384]{1,0:T(8,128)(2,1)S(1)}, bf16[48,384]{1,0:T(8,128)(2,1)S(1)}, u32[]{:S(2)}, u32[]{:S(2)}) collective-permute-start(bf16[48,384]{1,0:T(8,128)(2,1)S(1)} %get-tuple-element.267), channel_id=1, source_target_pairs={{0,2},{2,4},{4,6},{6,0},{1,3},{3,5},{5,7},{7,1},{8,10},{10,12},{12... | collective-permute-start | bytes 110600 | tf_op jit(solution)/shard_map/ppermute | solution.py:58
  433.8 20.6 %collective-permute-start.21 = (bf16[48,384]{1,0:T(8,128)(2,1)S(1)}, bf16[48,384]{1,0:T(8,128)(2,1)S(1)}, u32[]{:S(2)}, u32[]{:S(2)}) collective-permute-start(bf16[48,384]{1,0:T(8,128)(2,1)S(1)} %get-tuple-element.268), channel_id=1, source_target_pairs={{0,6},{2,0},{4,2},{6,4},{1,7},{3,1},{5,3},{7,5},{8,14},{10,8},{12,... | collective-permute-start | bytes 110600 | tf_op jit(solution)/shard_map/ppermute | solution.py:58
  435.2 23.1 %collective-permute-start.20 = (bf16[48,384]{1,0:T(8,128)(2,1)S(1)}, bf16[48,384]{1,0:T(8,128)(2,1)S(1)}, u32[]{:S(2)}, u32[]{:S(2)}) collective-permute-start(bf16[48,384]{1,0:T(8,128)(2,1)S(1)} %get-tuple-element.269), channel_id=1, source_target_pairs={{0,4},{2,6},{4,0},{6,2},{1,5},{3,7},{5,1},{7,3},{8,12},{10,14},{12... | collective-permute-start | bytes 110600 | tf_op jit(solution)/shard_map/ppermute | solution.py:58
  454.5 8.5 %collective-permute-start.26 = (bf16[48,1536]{1,0:T(8,128)(2,1)S(1)}, bf16[48,1536]{1,0:T(8,128)(2,1)S(1)}, u32[]{:S(2)}, u32[]{:S(2)}) collective-permute-start(bf16[48,1536]{1,0:T(8,128)(2,1)S(1)} %get-tuple-element.257), channel_id=1, source_target_pairs={{0,2},{2,4},{4,6},{6,0},{1,3},{3,5},{5,7},{7,1},{8,10},{10,12},{12... | collective-permute-start | bytes 442376 | tf_op jit(solution)/shard_map/ppermute | solution.py:58
  454.5 8.5 %collective-permute-start.28 = (bf16[48,1536]{1,0:T(8,128)(2,1)S(1)}, bf16[48,1536]{1,0:T(8,128)(2,1)S(1)}, u32[]{:S(2)}, u32[]{:S(2)}) collective-permute-start(bf16[48,1536]{1,0:T(8,128)(2,1)S(1)} %get-tuple-element.258), channel_id=1, source_target_pairs={{0,6},{2,0},{4,2},{6,4},{1,7},{3,1},{5,3},{7,5},{8,14},{10,8},{12,... | collective-permute-start | bytes 442376 | tf_op jit(solution)/shard_map/ppermute | solution.py:58
  458.3 4.0 collective-permute-start.22
  462.4 11.5 %collective-permute-start.27 = (bf16[48,1536]{1,0:T(8,128)(2,1)S(1)}, bf16[48,1536]{1,0:T(8,128)(2,1)S(1)}, u32[]{:S(2)}, u32[]{:S(2)}) collective-permute-start(bf16[48,1536]{1,0:T(8,128)(2,1)S(1)} %get-tuple-element.259), channel_id=1, source_target_pairs={{0,4},{2,6},{4,0},{6,2},{1,5},{3,7},{5,1},{7,3},{8,12},{10,14},{12... | collective-permute-start | bytes 442376 | tf_op jit(solution)/shard_map/ppermute | solution.py:58
  463.0 11.0 %collective-permute-start.33 = (bf16[48,1536]{1,0:T(8,128)(2,1)S(1)}, bf16[48,1536]{1,0:T(8,128)(2,1)S(1)}, u32[]{:S(2)}, u32[]{:S(2)}) collective-permute-start(bf16[48,1536]{1,0:T(8,128)(2,1)S(1)} %get-tuple-element.252), channel_id=1, source_target_pairs={{0,2},{2,4},{4,6},{6,0},{1,3},{3,5},{5,7},{7,1},{8,10},{10,12},{12... | collective-permute-start | bytes 442376 | tf_op jit(solution)/shard_map/ppermute | solution.py:58
  463.0 17.2 %collective-permute-start.35 = (bf16[48,1536]{1,0:T(8,128)(2,1)S(1)}, bf16[48,1536]{1,0:T(8,128)(2,1)S(1)}, u32[]{:S(2)}, u32[]{:S(2)}) collective-permute-start(bf16[48,1536]{1,0:T(8,128)(2,1)S(1)} %get-tuple-element.253), channel_id=1, source_target_pairs={{0,6},{2,0},{4,2},{6,4},{1,7},{3,1},{5,3},{7,5},{8,14},{10,8},{12,... | collective-permute-start | bytes 442376 | tf_op jit(solution)/shard_map/ppermute | solution.py:58
  473.9 22.1 %collective-permute-start.34 = (bf16[48,1536]{1,0:T(8,128)(2,1)S(1)}, bf16[48,1536]{1,0:T(8,128)(2,1)S(1)}, u32[]{:S(2)}, u32[]{:S(2)}) collective-permute-start(bf16[48,1536]{1,0:T(8,128)(2,1)S(1)} %get-tuple-element.254), channel_id=1, source_target_pairs={{0,4},{2,6},{4,0},{6,2},{1,5},{3,7},{5,1},{7,3},{8,12},{10,14},{12... | collective-permute-start | bytes 442376 | tf_op jit(solution)/shard_map/ppermute | solution.py:58
  474.0 33.4 %collective-permute-start.7 = (bf16[2,384,384]{2,1,0:T(8,128)(2,1)S(1)}, bf16[2,384,384]{2,1,0:T(8,128)(2,1)S(1)}, u32[]{:S(2)}, u32[]{:S(2)}) collective-permute-start(bf16[2,384,384]{2,1,0:T(8,128)(2,1)S(1)} %copy-done.24), channel_id=1, source_target_pairs={{0,4},{2,6},{4,0},{6,2},{1,5},{3,7},{5,1},{7,3},{8,12},{10,14},{12... | collective-permute-start | bytes 1769480 | tf_op jit(solution)/shard_map/ppermute | solution.py:222
  480.2 44.4 %collective-permute-start.23 = (bf16[2,48,384]{2,1,0:T(8,128)(2,1)S(1)}, bf16[2,48,384]{2,1,0:T(8,128)(2,1)S(1)}, u32[]{:S(2)}, u32[]{:S(2)}) collective-permute-start(bf16[2,48,384]{2,1,0:T(8,128)(2,1)S(1)} %bitcast_dynamic-update-slice_fusion.6), channel_id=1, source_target_pairs={{0,8},{8,0},{16,24},{24,16},{1,9},{9,1},{17,25},{25,17},{2,10},{10... | collective-permute-start | bytes 221192 | tf_op jit(solution)/shard_map/ppermute | solution.py:65
  496.0 29.4 %collective-permute-start.29 = (bf16[48,1536]{1,0:T(8,128)(2,1)S(1)}, bf16[48,1536]{1,0:T(8,128)(2,1)S(1)}, u32[]{:S(2)}, u32[]{:S(2)}) collective-permute-start(bf16[48,1536]{1,0:T(8,128)(2,1)S(1)} %fusion.99), channel_id=1, source_target_pairs={{0,16},{8,24},{16,0},{24,8},{1,17},{9,25},{17,1},{25,9},{2,18},{10... | collective-permute-start | bytes 442376 | tf_op jit(solution)/shard_map/ppermute | solution.py:63
  497.7 10.0 %copy-start.21 = (bf16[2,512,384]{2,1,0:T(8,128)(2,1)S(1)}, bf16[2,512,384]{2,1,0:T(8,128)(2,1)}, u32[]{:S(2)}) copy-start(bf16[2,512,384]{2,1,0:T(8,128)(2,1)} %slice.106) | copy-start | bytes 2359300
  497.7 10.0 %copy-start.22 = (bf16[1,896,384]{2,1,0:T(8,128)(2,1)S(1)}, bf16[1,896,384]{2,1,0:T(8,128)(2,1)}, u32[]{:S(2)}) copy-start(bf16[1,896,384]{2,1,0:T(8,128)(2,1)} %copy.37) | copy-start | bytes 2064388
  497.8 10.0 %copy-start.41 = (bf16[3,768,384]{2,1,0:T(8,128)(2,1)S(1)}, bf16[3,768,384]{2,1,0:T(8,128)(2,1)}, u32[]{:S(2)}) copy-start(bf16[3,768,384]{2,1,0:T(8,128)(2,1)} %param.20) | copy-start | bytes 5308420
  497.8 27.9 %collective-permute-start.36 = (bf16[48,1536]{1,0:T(8,128)(2,1)S(1)}, bf16[48,1536]{1,0:T(8,128)(2,1)S(1)}, u32[]{:S(2)}, u32[]{:S(2)}) collective-permute-start(bf16[48,1536]{1,0:T(8,128)(2,1)S(1)} %fusion.96), channel_id=1, source_target_pairs={{0,16},{8,24},{16,0},{24,8},{1,17},{9,25},{17,1},{25,9},{2,18},{10... | collective-permute-start | bytes 442376 | tf_op jit(solution)/shard_map/ppermute | solution.py:63
  522.9 5.9 %collective-permute-start.10 = (bf16[4,2,48,1152]{3,2,1,0:T(8,128)(2,1)S(1)}, bf16[4,2,48,1152]{3,2,1,0:T(8,128)(2,1)S(1)}, u32[]{:S(2)}, u32[]{:S(2)}) collective-permute-start(bf16[4,2,48,1152]{3,2,1,0:T(8,128)(2,1)S(1)} %dynamic-slice_bitcast_fusion.2), channel_id=1, source_target_pairs={{0,8},{8,0},{16,24},{24,16},{1,9},{9,1},{17,25},{25,17},{2,10},{10... | collective-permute-start | bytes 2654216 | tf_op jit(solution)/shard_map/ppermute | solution.py:48
  523.0 32.8 %collective-permute-start.9 = (bf16[896,768]{1,0:T(8,128)(2,1)}, bf16[896,768]{1,0:T(8,128)(2,1)S(1)}, u32[]{:S(2)}, u32[]{:S(2)}) collective-permute-start(bf16[896,768]{1,0:T(8,128)(2,1)} %bitcast_convert_fusion), channel_id=1, source_target_pairs={{0,1},{1,0},{2,3},{3,2},{4,5},{5,4},{6,7},{7,6},{8,9},{9,8},{10,11... | collective-permute-start | bytes 4128776 | tf_op jit(solution)/shard_map/ppermute | solution.py:33
  525.4 1.6 collective-permute-start.30
  525.7 1.8 collective-permute-start.37
  529.1 26.7 %copy-start.12 = (bf16[896,768]{1,0:T(8,128)(2,1)S(1)}, bf16[896,768]{1,0:T(8,128)(2,1)}, u32[]{:S(2)}) copy-start(bf16[896,768]{1,0:T(8,128)(2,1)} %bitcast_convert_fusion) | copy-start | bytes 4128772
  529.2 12.3 %collective-permute-start.11 = (bf16[4,48,1152]{2,1,0:T(8,128)(2,1)S(1)}, bf16[4,48,1152]{2,1,0:T(8,128)(2,1)S(1)}, u32[]{:S(2)}, u32[]{:S(2)}) collective-permute-start(bf16[4,48,1152]{2,1,0:T(8,128)(2,1)S(1)} %dynamic-slice_bitcast_fusion.5), channel_id=1, source_target_pairs={{0,16},{8,24},{16,0},{24,8},{1,17},{9,25},{17,1},{25,9},{2,18},{10... | collective-permute-start | bytes 1327112 | tf_op jit(solution)/shard_map/ppermute | solution.py:53
  541.6 31.2 %collective-permute-start.12 = (bf16[48,1152]{1,0:T(8,128)(2,1)S(1)}, bf16[48,1152]{1,0:T(8,128)(2,1)S(1)}, u32[]{:S(2)}, u32[]{:S(2)}) collective-permute-start(bf16[48,1152]{1,0:T(8,128)(2,1)S(1)} %get-tuple-element.262), channel_id=1, source_target_pairs={{0,2},{2,4},{4,6},{6,0},{1,3},{3,5},{5,7},{7,1},{8,10},{10,12},{12... | collective-permute-start | bytes 331784 | tf_op jit(solution)/shard_map/ppermute | solution.py:58
  541.7 31.1 %collective-permute-start.14 = (bf16[48,1152]{1,0:T(8,128)(2,1)S(1)}, bf16[48,1152]{1,0:T(8,128)(2,1)S(1)}, u32[]{:S(2)}, u32[]{:S(2)}) collective-permute-start(bf16[48,1152]{1,0:T(8,128)(2,1)S(1)} %get-tuple-element.263), channel_id=1, source_target_pairs={{0,6},{2,0},{4,2},{6,4},{1,7},{3,1},{5,3},{7,5},{8,14},{10,8},{12,... | collective-permute-start | bytes 331784 | tf_op jit(solution)/shard_map/ppermute | solution.py:58
  557.6 7.4 %collective-permute-start.38 = (f32[4,96]{1,0:T(4,128)S(1)}, f32[4,96]{1,0:T(4,128)S(1)}, u32[]{:S(2)}, u32[]{:S(2)}) collective-permute-start(f32[4,96]{1,0:T(4,128)S(1)} %get-tuple-element.270), channel_id=1, source_target_pairs={{0,2},{2,4},{4,6},{6,0},{1,3},{3,5},{5,7},{7,1},{8,10},{10,12},{12... | collective-permute-start | bytes 4616 | tf_op jit(solution)/shard_map/ppermute | solution.py:245
  557.7 10.3 %collective-permute-start.40 = (f32[4,96]{1,0:T(4,128)S(1)}, f32[4,96]{1,0:T(4,128)S(1)}, u32[]{:S(2)}, u32[]{:S(2)}) collective-permute-start(f32[4,96]{1,0:T(4,128)S(1)} %get-tuple-element.271), channel_id=1, source_target_pairs={{0,6},{2,0},{4,2},{6,4},{1,7},{3,1},{5,3},{7,5},{8,14},{10,8},{12,... | collective-permute-start | bytes 4616 | tf_op jit(solution)/shard_map/ppermute | solution.py:245
  561.5 6.5 %collective-permute-start.39 = (f32[4,96]{1,0:T(4,128)S(1)}, f32[4,96]{1,0:T(4,128)S(1)}, u32[]{:S(2)}, u32[]{:S(2)}) collective-permute-start(f32[4,96]{1,0:T(4,128)S(1)} %get-tuple-element.272), channel_id=1, source_target_pairs={{0,4},{2,6},{4,0},{6,2},{1,5},{3,7},{5,1},{7,3},{8,12},{10,14},{12... | collective-permute-start | bytes 4616 | tf_op jit(solution)/shard_map/ppermute | solution.py:245
  565.0 7.8 %collective-permute-start.13 = (bf16[48,1152]{1,0:T(8,128)(2,1)S(1)}, bf16[48,1152]{1,0:T(8,128)(2,1)S(1)}, u32[]{:S(2)}, u32[]{:S(2)}) collective-permute-start(bf16[48,1152]{1,0:T(8,128)(2,1)S(1)} %get-tuple-element.264), channel_id=1, source_target_pairs={{0,4},{2,6},{4,0},{6,2},{1,5},{3,7},{5,1},{7,3},{8,12},{10,14},{12... | collective-permute-start | bytes 331784 | tf_op jit(solution)/shard_map/ppermute | solution.py:58
  568.0 3.7 collective-permute-start.41
  571.6 1.2 collective-permute-start.42
  572.9 5.2 collective-permute-start.15
  578.2 1.5 collective-permute-start.16
  (43 other events, 115.7 us)

commit v2 on v1

v2 whole, which is shorter than its diff:
```python
import functools

import jax
import jax.numpy as jnp
from jax import lax
from jax.experimental import pallas as pl
from jax.experimental.pallas import tpu as pltpu
from jax.sharding import PartitionSpec as P

HEAD = 64
CORES = 2
LANES = 128
norm_eps = 1e-05
hidden_value = -1e30
BF = jnp.bfloat16
F32 = jnp.float32
BUDGET = 56 * 1024 * 1024


def nt(left, right):
    return lax.dot_general(left, right, (((1,), (1,)), ((), ())), preferred_element_type=F32)


def tn(left, right):
    return lax.dot_general(left, right, (((0,), (0,)), ((), ())), preferred_element_type=F32)


def nn(left, right):
    return lax.dot_general(left, right, (((1,), (0,)), ((), ())), preferred_element_type=F32)


def one_head(pair, which, factor=None):
    lane = lax.broadcasted_iota(jnp.int32, pair.shape, 1)
    wide = pair.astype(F32)
    if factor is not None:
        wide = wide * factor
    return jnp.where((lane // HEAD) == which, wide, 0.0).astype(BF)


def attend_kernel(*refs, masked, prompt_rows):
    if masked:
        q_ref, ko_ref, vo_ref, kf_ref, vf_ref, bo_ref, bf_ref, out_ref, log_ref = refs
    else:
        q_ref, ko_ref, vo_ref, kf_ref, vf_ref, out_ref, log_ref = refs
    queries = q_ref[0]
    rows = queries.shape[0]
    own_keys = ko_ref.shape[1] if masked else prompt_rows
    near_values = vo_ref[0, :own_keys]
    far_values = vf_ref[0]
    outs = []
    tops = []
    for which in range(2):
        mine = one_head(queries, which, HEAD ** (-0.5))
        near = nt(ko_ref[0, :own_keys], mine)
        far = nt(kf_ref[0], mine)
        if masked:
            near = near + jnp.concatenate([bo_ref[...]] * (rows // LANES), axis=1)
            far = far + jnp.concatenate([bf_ref[...]] * (rows // LANES), axis=1)
        top = jnp.maximum(
            jnp.max(near, axis=0, keepdims=True), jnp.max(far, axis=0, keepdims=True)
        )
        near = jnp.exp(near - top)
        far = jnp.exp(far - top)
        total = jnp.sum(near, axis=0, keepdims=True) + jnp.sum(far, axis=0, keepdims=True)
        mixed = tn(near.astype(BF), near_values) + tn(far.astype(BF), far_values)
        outs.append(mixed / jnp.transpose(jnp.broadcast_to(total, (LANES, rows))))
        log_ref[0, which : which + 1] = top + jnp.log(total)
    lane = lax.broadcasted_iota(jnp.int32, outs[0].shape, 1)
    out_ref[...] = jnp.where(lane < HEAD, outs[0], outs[1]).astype(BF)


def attend(own, far, bias, first_row, rows, prompt_rows, block):
    masked = bias is not None
    width = own.shape[2]
    q = own[0, first_row : first_row + rows][None]

    def kind_spec(array, kind):
        return pl.BlockSpec((1, array.shape[1], LANES), lambda p, r: (kind, 0, p))

    specs = [
        pl.BlockSpec((1, block, LANES), lambda p, r: (0, r, p)),
        kind_spec(own, 1),
        kind_spec(own, 2),
        kind_spec(far, 0),
        kind_spec(far, 1),
    ]
    args = [q, own, own, far, far]
    if masked:
        specs += [pl.BlockSpec(b.shape, lambda p, r: (0, 0)) for b in bias]
        args += list(bias)
    keys = far.shape[1] + (own.shape[1] if masked else prompt_rows)
    return pl.pallas_call(
        functools.partial(attend_kernel, masked=masked, prompt_rows=prompt_rows),
        grid=(width // LANES, rows // block),
        in_specs=specs,
        out_specs=[
            pl.BlockSpec((block, LANES), lambda p, r: (r, p)),
            pl.BlockSpec((1, 8, block), lambda p, r: (p, 0, r)),
        ],
        out_shape=[
            jax.ShapeDtypeStruct((rows, width), BF),
            jax.ShapeDtypeStruct((width // LANES, 8, rows), F32),
        ],
        compiler_params=pltpu.CompilerParams(vmem_limit_bytes=BUDGET),
        cost_estimate=pl.CostEstimate(
            flops=8 * rows * keys * width, transcendentals=rows * keys * width // HEAD, bytes_accessed=4 * keys * width
        ),
    )(*args)


def pull_kernel(*refs, masked, prompt_rows, chunk):
    if masked:
        (q_ref, ko_ref, vo_ref, kf_ref, vf_ref, bo_ref, bf_ref, do_ref, out_ref, lse_ref,
         dq_ref, dko_ref, dvo_ref, dkf_ref, dvf_ref, dkc_ref, dvc_ref) = refs
    else:
        (q_ref, ko_ref, vo_ref, kf_ref, vf_ref, do_ref, out_ref, lse_ref, pko_ref, pvo_ref, pkf_ref, pvf_ref,
         dq_ref, dko_ref, dvo_ref, dkf_ref, dvf_ref) = refs
    upstream = do_ref[...]
    inner = jnp.transpose(upstream.astype(F32) * out_ref[...].astype(F32))
    queries = q_ref[0]
    rows = upstream.shape[0]
    heads = []
    for which in range(2):
        heads.append(
            (
                one_head(queries, which, HEAD ** (-0.5)),
                one_head(upstream, which),
                jnp.sum(inner[which * HEAD : (which + 1) * HEAD], axis=0, keepdims=True),
                lse_ref[0, which : which + 1],
            )
        )

    def piece(keys, values, bias):
        key_grad = None
        query_grads = []
        for mine, grad, delta, log in heads:
            scores = nt(keys, mine)
            if bias is not None:
                scores = scores + jnp.concatenate([bias] * (rows // LANES), axis=1)
            probs = jnp.exp(scores - log)
            spread = probs * (nt(values, grad) - delta)
            low = spread.astype(BF)
            dv = nn(probs.astype(BF), grad)
            dk = nn(low, mine)
            key_grad = dk if key_grad is None else key_grad + dk
            value_grad = dv if len(query_grads) == 0 else value_grad + dv
            query_grads.append(tn(low, keys))
        return key_grad, value_grad, query_grads

    dk, dv, acc = piece(
        ko_ref[0, :prompt_rows], vo_ref[0, :prompt_rows], bo_ref[:prompt_rows] if masked else None
    )
    if masked:
        dko_ref[...] = dk
        dvo_ref[...] = dv
        dk, dv, more = piece(ko_ref[0, prompt_rows:], vo_ref[0, prompt_rows:], None)
        dkc_ref[...] = dk.astype(BF)
        dvc_ref[...] = dv.astype(BF)
        acc = [a + b for a, b in zip(acc, more)]
    else:
        dko_ref[...] = (dk + pko_ref[...]).astype(BF)
        dvo_ref[...] = (dv + pvo_ref[...]).astype(BF)

    def far_step(at, acc):
        span = pl.ds(at, chunk)
        dk, dv, more = piece(kf_ref[0, span], vf_ref[0, span], bf_ref[span] if masked else None)
        if masked:
            dkf_ref[span] = dk
            dvf_ref[span] = dv
        else:
            dkf_ref[span] = (dk + pkf_ref[span]).astype(BF)
            dvf_ref[span] = (dv + pvf_ref[span]).astype(BF)
        return [a + b for a, b in zip(acc, more)]

    count = kf_ref.shape[1] // chunk
    if count <= 4:
        for step in range(count):
            acc = far_step(step * chunk, acc)
    else:
        acc = lax.fori_loop(
            0, count, lambda i, a: far_step(pl.multiple_of(i * chunk, chunk), a), acc
        )
    lane = lax.broadcasted_iota(jnp.int32, acc[0].shape, 1)
    dq_ref[...] = (jnp.where(lane < HEAD, acc[0], acc[1]) * HEAD ** (-0.5)).astype(BF)


def pull(own, far, bias, first_row, rows, grad, out, lse, before, prompt_rows):
    masked = bias is not None
    width = own.shape[2]
    far_n = far.shape[1]
    q = own[0, first_row : first_row + rows][None]

    def full(array_rows):
        return pl.BlockSpec((array_rows, LANES), lambda p: (0, p))

    def kind_spec(array, kind):
        return pl.BlockSpec((1, array.shape[1], LANES), lambda p: (kind, 0, p))

    specs = [kind_spec(q, 0), kind_spec(own, 1), kind_spec(own, 2), kind_spec(far, 0), kind_spec(far, 1)]
    args = [q, own, own, far, far]
    if masked:
        specs += [pl.BlockSpec(b.shape, lambda p: (0, 0)) for b in bias]
        args += list(bias)
    specs += [full(rows)] * 2 + [pl.BlockSpec((1, 8, rows), lambda p: (p, 0, 0))]
    args += [grad, out, lse]
    kind = F32 if masked else BF
    outs = [(rows, BF), (prompt_rows, kind), (prompt_rows, kind), (far_n, kind), (far_n, kind)]
    if masked:
        outs += [(own.shape[1] - prompt_rows, BF)] * 2
    else:
        specs += [full(b.shape[0]) for b in before]
        args += list(before)
    keys = far_n + (own.shape[1] if masked else prompt_rows)
    return pl.pallas_call(
        functools.partial(pull_kernel, masked=masked, prompt_rows=prompt_rows, chunk=prompt_rows),
        grid=(width // LANES,),
        in_specs=specs,
        out_specs=[full(n) for n, _ in outs],
        out_shape=[jax.ShapeDtypeStruct((n, width), t) for n, t in outs],
        compiler_params=pltpu.CompilerParams(vmem_limit_bytes=BUDGET),
        cost_estimate=pl.CostEstimate(
            flops=20 * rows * keys * width, transcendentals=rows * keys * width // HEAD, bytes_accessed=12 * keys * width
        ),
    )(*args)
def pick(array, index, axis):
    return lax.dynamic_index_in_dim(array, index, axis, keepdims=False)


def shift_perm(count, step):
    return [(j, (j + step) % count) for j in range(count)]


def group_perm(count, core_flip, step):
    chips = count // CORES
    return [
        (x * CORES + c, ((x + step) % chips) * CORES + (c ^ core_flip))
        for x in range(chips)
        for c in range(CORES)
    ]


def tp_swap(array):
    return lax.ppermute(array, "tp", shift_perm(lax.axis_size("tp"), 1))


def tp_sum(part):
    low = lax.optimization_barrier(part.astype(BF))
    return low.astype(F32) + tp_swap(low).astype(F32)


def spread_sum(grad):
    seq_n = lax.axis_size("seq")
    grp_n = lax.axis_size("grp")
    chips = grp_n // CORES
    seq_i = lax.axis_index("seq")
    grp_i = lax.axis_index("grp")
    core_i = grp_i % CORES
    chip_i = grp_i // CORES
    rows = grad.shape[0] // (seq_n * grp_n)
    width = grad.shape[1]
    low = grad.astype(BF).reshape(seq_n, CORES, chips, rows, width)
    got = lax.ppermute(pick(low, 1 - core_i, 1), "grp", group_perm(grp_n, 1, 0))
    half = (pick(low, core_i, 1).astype(F32) + got.astype(F32)).astype(BF)
    total = pick(half, chip_i, 1).astype(F32)
    for step in range(1, chips):
        sent = pick(half, (chip_i + step) % chips, 1)
        total += lax.ppermute(sent, "grp", group_perm(grp_n, 0, step)).astype(F32)
    part = total.astype(BF)
    total = pick(part, seq_i, 0).astype(F32)
    for step in range(1, seq_n):
        sent = pick(part, (seq_i + step) % seq_n, 0)
        total += lax.ppermute(sent, "seq", shift_perm(seq_n, step)).astype(F32)
    mine = lax.optimization_barrier(total.astype(BF))
    line = jnp.zeros((chips, rows, width), BF)
    line = lax.dynamic_update_index_in_dim(line, mine, chip_i, 0)
    for step in range(1, chips):
        came = lax.ppermute(mine, "grp", group_perm(grp_n, 0, step))
        line = lax.dynamic_update_index_in_dim(line, came, (chip_i - step) % chips, 0)
    other = lax.ppermute(line, "grp", group_perm(grp_n, 1, 0))
    first = core_i == 0
    both = jnp.stack([jnp.where(first, line, other), jnp.where(first, other, line)])
    return both.reshape(CORES * chips * rows, width)


def norm_parts(tokens):
    mean = jnp.mean(tokens, axis=-1, keepdims=True)
    centred = tokens - mean
    variance = jnp.mean(centred * centred, axis=-1, keepdims=True)
    inv = lax.rsqrt(variance + norm_eps)
    return centred * inv, inv


def norm_back(normed, inv, upstream, gain):
    scaled = upstream * gain
    mean = jnp.mean(scaled, axis=-1, keepdims=True)
    inner = jnp.mean(scaled * normed, axis=-1, keepdims=True)
    return inv * (scaled - mean - normed * inner)


def exact_gelu(upper):
    return jax.nn.gelu(upper, approximate=False)


def in_order(earlier, later):
    return lax.optimization_barrier((earlier, later))[1]


def body(
    prompt_in,
    cont_in,
    prompt_cot,
    cont_cot,
    prompt_len,
    qkv_weight,
    out_weight,
    ffn_in,
    ffn_out,
    norm_gain,
    norm_shift,
):
    rows_p = prompt_in.shape[1]
    half = rows_p // 2
    width = prompt_in.shape[2]
    local_width = qkv_weight.shape[2]
    seq_n = lax.axis_size("seq")
    seq_i = lax.axis_index("seq")
    tp_n = lax.axis_size("tp")
    tp_i = lax.axis_index("tp")
    gains = norm_gain.astype(F32)
    shifts = norm_shift.astype(F32)

    sent = lax.dynamic_slice_in_dim(prompt_in[0], tp_i * half, half, 0)
    pieces = []
    starts = []
    for step in range(1, seq_n):
        came = lax.ppermute(sent, "seq", shift_perm(seq_n, step))
        pieces += [came, tp_swap(came)]
        block = (seq_i - step) % seq_n * rows_p
        starts += [block + tp_i * half, block + (1 - tp_i) * half]
    far_in = jnp.concatenate(pieces, axis=0)
    inside = jnp.arange(half, dtype=jnp.int32)
    limit = prompt_len[0, 0]
    place = (jnp.stack(starts)[:, None] + inside[None, :]).reshape(-1)
    bias_far = jnp.where(place < limit, 0.0, hidden_value).astype(F32)
    place = seq_i * rows_p + jnp.arange(rows_p, dtype=jnp.int32)
    bias_own = jnp.concatenate(
        [
            jnp.where(place < limit, 0.0, hidden_value).astype(F32),
            jnp.zeros((cont_in.shape[2],), F32),
        ]
    )
    bias = tuple(jnp.broadcast_to(b[:, None], (b.shape[0], LANES)) for b in (bias_own, bias_far))

    tokens = jnp.concatenate([prompt_in[0], cont_in[0, 0]], axis=0).astype(F32)
    count = tokens.shape[0]
    rows_c = count - rows_p
    normed_one, inv_one = norm_parts(tokens)
    first_low = (normed_one * gains[0] + shifts[0]).astype(BF)
    own = jnp.einsum("nd,cde->cne", first_low, qkv_weight, preferred_element_type=F32).astype(BF)
    first_far = (norm_parts(far_in.astype(F32))[0] * gains[0] + shifts[0]).astype(BF)
    far = jnp.einsum(
        "nd,cde->cne", first_far, qkv_weight[1:], preferred_element_type=F32
    ).astype(BF)

    att_c, log_c = attend(own, far, bias, rows_p, rows_c, rows_p, rows_c)
    mixed_c = jnp.dot(att_c, out_weight, preferred_element_type=F32)
    att_p, log_p = attend(own, far, None, 0, rows_p, rows_p, rows_p)
    mixed_p = jnp.dot(att_p, out_weight, preferred_element_type=F32)

    def feed(token_rows, mixed, cot):
        resid = token_rows + tp_sum(mixed)
        normed, inv = norm_parts(resid)
        low = (normed * gains[1] + shifts[1]).astype(BF)
        upper = jnp.dot(low, ffn_in, preferred_element_type=F32)
        activated, gelu_pull = jax.vjp(exact_gelu, upper)
        act_low = activated.astype(BF)
        act_grad = jnp.einsum("nd,fd->nf", cot, ffn_out, preferred_element_type=F32)
        upper_grad = gelu_pull(act_grad)[0].astype(BF)
        terms = jnp.einsum("nf,df->nd", upper_grad, ffn_in, preferred_element_type=F32)
        return resid, normed, inv, low, act_low, upper_grad, tp_sum(terms)

    cot_c = cont_cot[0, 0]
    cot_p = prompt_cot[0]
    resid_c, normed_c, inv_c, low_c, act_c, up_c, second_c = feed(tokens[rows_p:], mixed_c, cot_c)
    resid_p, normed_p, inv_p, low_p, act_p, up_p, second_p = feed(tokens[:rows_p], mixed_p, cot_p)

    def rows_grad(left_c, right_c, left_p, right_p):
        return jnp.einsum(
            "nd,nf->df",
            jnp.concatenate([left_p, left_c]),
            jnp.concatenate([right_p, right_c]),
            preferred_element_type=F32,
        ).astype(BF)

    in_grad = rows_grad(low_c, up_c, low_p, up_p)
    down_grad = rows_grad(cot_c, act_c, cot_p, act_p)

    def rest(cot, normed, inv, second):
        return cot.astype(F32) + norm_back(normed, inv, second, gains[1])

    grad_c = rest(cot_c, normed_c, inv_c, second_c)
    grad_p = rest(cot_p, normed_p, inv_p, second_p)
    dm_c = grad_c.astype(BF)
    dm_p = grad_p.astype(BF)
    do_c = jnp.einsum("nd,ed->ne", dm_c, out_weight, preferred_element_type=F32).astype(BF)
    do_p = jnp.einsum("nd,ed->ne", dm_p, out_weight, preferred_element_type=F32).astype(BF)
    mixing_grad = rows_grad(dm_c, att_c, dm_p, att_p)
    wide_sum = spread_sum(jnp.concatenate([in_grad, down_grad, mixing_grad], axis=1))

    dq_c, *partial, dk_c, dv_c = pull(
        own, far, bias, rows_p, rows_c, do_c, att_c, log_c, None, rows_p
    )
    proj_c = jnp.stack([dq_c, dk_c, dv_c])
    terms_c = jnp.einsum("cne,cde->nd", proj_c, qkv_weight, preferred_element_type=F32)
    first_c = tp_sum(terms_c)
    dq_p, dk_p, dv_p, dk_f, dv_f = pull(
        own, far, None, 0, rows_p, do_p, att_p, log_p, partial, rows_p
    )
    proj_p = jnp.stack([dq_p, dk_p, dv_p])
    proj_f = jnp.stack([dk_f, dv_f])
    terms_p = jnp.einsum("cne,cde->nd", proj_p, qkv_weight, preferred_element_type=F32)
    terms_f = jnp.einsum("cne,cde->nd", proj_f, qkv_weight[1:], preferred_element_type=F32)
    terms_f = terms_f.astype(BF).reshape(seq_n - 1, 2, half, width)
    terms_p = terms_p.astype(BF).reshape(2, half, width)
    total = pick(terms_p, tp_i, 0).astype(F32) + tp_swap(pick(terms_p, 1 - tp_i, 0)).astype(F32)
    for step in range(1, seq_n):
        mine = terms_f[step - 1, 0].astype(F32) + tp_swap(terms_f[step - 1, 1]).astype(F32)
        back = lax.ppermute(mine.astype(BF), "seq", shift_perm(seq_n, -step))
        total += back.astype(F32)
    mine = lax.optimization_barrier(total.astype(BF))
    other = tp_swap(mine)
    first = tp_i == 0
    first_p = jnp.concatenate([jnp.where(first, mine, other), jnp.where(first, other, mine)])
    first_p = first_p.astype(F32)

    qkv_grad = jnp.einsum(
        "nd,cne->dce", first_low, jnp.concatenate([proj_p, proj_c], axis=1), preferred_element_type=F32
    )
    far_grad = jnp.einsum("nd,cne->dce", first_far, proj_f, preferred_element_type=F32)
    qkv_grad = jnp.concatenate([qkv_grad[:, :1], qkv_grad[:, 1:] + far_grad], axis=1)
    qkv_sum = spread_sum(qkv_grad.reshape(width, 3 * local_width)).astype(F32)

    ffn_terms_c = tp_sum(jnp.dot(act_c, ffn_out, preferred_element_type=F32))
    ffn_terms_p = tp_sum(jnp.dot(act_p, ffn_out, preferred_element_type=F32))
    cont_out = (resid_c + ffn_terms_c).astype(BF)[None, None]
    prompt_out = (resid_p + ffn_terms_p).astype(BF)[None]

    one_p, one_c = normed_one[:rows_p], normed_one[rows_p:]
    cont_grad = (grad_c + norm_back(one_c, inv_one[rows_p:], first_c, gains[0])).astype(BF)[None, None]
    prompt_grad = (grad_p + norm_back(one_p, inv_one[:rows_p], first_p, gains[0])).astype(BF)[None]

    def sums(a, b):
        return jnp.sum(a, axis=0) + jnp.sum(b, axis=0)

    norm_rows = jnp.stack(
        [
            sums(first_p * one_p, first_c * one_c),
            sums(second_p * normed_p, second_c * normed_c),
            sums(first_p, first_c),
            sums(second_p, second_c),
        ]
    )
    norm_blocks = norm_rows.reshape(4, seq_n, tp_n, -1)
    norm_own = pick(norm_blocks, tp_i, 2)
    total = pick(norm_own, seq_i, 1)
    for step in range(1, seq_n):
        piece = pick(norm_own, (seq_i + step) % seq_n, 1)
        total += lax.ppermute(piece, "seq", shift_perm(seq_n, step))
    grp_n = lax.axis_size("grp")
    part = total
    for step in range(1, grp_n // CORES):
        total += lax.ppermute(part, "grp", group_perm(grp_n, 0, step))
    total = lax.optimization_barrier(total)
    total = total + lax.ppermute(total, "grp", group_perm(grp_n, 1, 0))
    seq_rows = width // seq_n
    hidden = ffn_in.shape[1]
    return (
        prompt_out,
        cont_out,
        prompt_grad,
        cont_grad,
        qkv_sum.reshape(seq_rows, 3, local_width).transpose(1, 0, 2),
        wide_sum[:, 2 * hidden :].astype(F32).T,
        wide_sum[:, :hidden].astype(F32),
        wide_sum[:, hidden : 2 * hidden].astype(F32).T,
        total[:2],
        total[2:],
    )


def solution(mesh):
    placed = (
        P("grp", "seq", None),
        P("grp", "seq", None, None),
        P("grp", "seq", None),
        P("grp", "seq", None, None),
        P("grp", "seq"),
        P(None, None, "tp"),
        P("tp", None),
        P(None, "tp"),
        P("tp", None),
        P(),
        P(),
    )
    return jax.shard_map(
        body,
        mesh=mesh,
        in_specs=placed,
        out_specs=(
            P("grp", "seq", None),
            P("grp", "seq", None, None),
            P("grp", "seq", None),
            P("grp", "seq", None, None),
            P(None, "seq", "tp"),
            P("tp", "seq"),
            P("seq", "tp"),
            P("tp", "seq"),
            P(None, ("seq", "tp")),
            P(None, ("seq", "tp")),
        ),
        check_vma=False,
    )
```

time: 594 us -> 404 us (0.68)
  matrix products: 166 us -> 55.6 us
  Pallas kernels: 0 us -> 59.2 us
  local copies, waits for them, and re-layouts: 77.2 us -> 25.5 us
  waiting for transfers between devices: 208 us -> 168 us
  other arithmetic: 70.1 us -> 37.3 us
  starting transfers between devices: 58.5 us -> 50.4 us
    dot_general x53 -> x21, matrix products: 162 us -> 52.1 us  [the longest x2 15.2 us: feed(): upper = jnp.dot(low, ffn_in, preferred_element_type=F32)]
    pallas_call x0 -> x4, Pallas kernels: none -> 59.2 us  [the longest x2 36.2 us: pull(): pl.pallas_call(functools.partial(pull_kernel, masked=masked, prompt_rows=...]
    ppermute x13 -> x24, waiting for transfers between devices: 147 us -> 101 us  [the longest x15 80 us: tp_swap(): return lax.ppermute(array, 'tp', shift_perm(lax.axis_size('tp'), 1))]
    convert_element_type x7, other arithmetic: 35.4 us -> 9.94 us  [the longest x1 2.81 us: body(): tokens = jnp.concatenate([prompt_in[0], cont_in[0, 0]], axis=0).astype(F32)]
    another operation x14 -> x1, local copies, waits for them, and re-layouts: 20.2 us -> 0.08 us  [body(): place = (jnp.stack(starts)[:, None] + inside[None, :]).reshape(-1)]
    ppermute x12 -> x6, starting transfers between devices: 20.5 us -> 8.63 us  [spread_sum(): total += lax.ppermute(sent, 'seq', shift_perm(seq_n, step)).astype(F32)]
    ppermute x13 -> x24, starting transfers between devices: 24.6 us -> 34.5 us  [the longest x15 15.4 us: tp_swap(): return lax.ppermute(array, 'tp', shift_perm(lax.axis_size('tp'), 1))]
    dynamic_update_slice x6 -> x0, local copies, waits for them, and re-layouts: 8.28 us -> none  [body(): lax.scan(forward_head, nothing, (head_queries, split_heads(keyvals[0]), s...]
  transfers between devices with their start and end apart: 43 -> 40, of which waited for: 19 -> 25; matrix products, arithmetic and copies ran while one was open for 33% -> 21% of each run, Pallas kernels for 0% -> 4%
where the time goes in v2:
time: 404 us; the launch traced here: 399 us
  waiting for transfers between devices  168 us (42%)
  Pallas kernels  59.2 us (15%)
  matrix products  55.6 us (14%)
  starting transfers between devices  50.4 us (12%)
  other arithmetic  37.3 us (9%)
  local copies, waits for them, and re-layouts  25.5 us (6%)
    ppermute x15, waiting for transfers between devices, tp_swap(): return lax.ppermute(array, 'tp', shift_perm(lax.axis_size('tp'), 1))  80 us
    ppermute x6, waiting for transfers between devices, spread_sum(): total += lax.ppermute(sent, 'seq', shift_perm(seq_n, step)).astype(F32)  36.9 us
    pallas_call x2, Pallas kernels, pull(): pl.pallas_call(functools.partial(pull_kernel, masked=masked, prompt_rows=...  36.2 us
    pallas_call x2, Pallas kernels, attend(): pl.pallas_call(functools.partial(attend_kernel, masked=masked, prompt_row...  23 us
    ppermute x2, waiting for transfers between devices, spread_sum(): total += lax.ppermute(sent, 'grp', group_perm(grp_n, 0, step)).astype(F32)  15.6 us
    ppermute x15, starting transfers between devices, tp_swap(): return lax.ppermute(array, 'tp', shift_perm(lax.axis_size('tp'), 1))  15.4 us
    dot_general x2, matrix products, feed(): upper = jnp.dot(low, ffn_in, preferred_element_type=F32)  15.2 us
    ppermute x3, waiting for transfers between devices, body(): back = lax.ppermute(mine.astype(BF), 'seq', shift_perm(seq_n, -step))  10.3 us
  transfers between devices with their start and end apart: 40, of which 25 were waited for; matrix products, arithmetic and copies ran while one was open for 21% of the time, Pallas kernels for 4%

profile of v2, /device:TPU:0, one launch (start us, length us, event | category | flops | bytes accessed | tf_op | source)
XLA Modules:
  0.0 398.5 jit_solution(16737013053155311730)
XLA Ops:
  0.7 1.9 dynamic-slice_bitcast_fusion.8
  2.6 5.1 %collective-permute-start.4 = (bf16[192,768]{1,0:T(8,128)(2,1)}, bf16[192,768]{1,0:T(8,128)(2,1)S(1)}, u32[]{:S(2)}, u32[]{:S(2)}) collective-permute-start(bf16[192,768]{1,0:T(8,128)(2,1)} %dynamic-slice_bitcast_fusion.8), channel_id=1, source_target_pairs={{0,6},{2,0},{4,2},{6,4},{1,7},{3,1},{5,3},{7,5},{8,14},{10,8},{12,... | collective-permute-start | bytes 884744 | tf_op jit(solution)/shard_map/ppermute | solution.py:336
  8.7 1.6 convert_reduce_fusion.1
  10.9 3.6 convert_bitcast_fusion.refs_1_.refs_2_
  14.5 2.0 subtract_multiply_fusion
  17.1 1.7 slice.121.refs_0_
  19.0 8.9 %collective-permute-done = bf16[192,768]{1,0:T(8,128)(2,1)} collective-permute-done((bf16[192,768]{1,0:T(8,128)(2,1)}, bf16[192,768]{1,0:T(8,128)(2,1)}, u32[]{:S(2)}, u32[]{:S(2)}) %collective-permute-start) | collective-permute-done | bytes 294944 | tf_op jit(solution)/shard_map/ppermute | solution.py:336
  29.4 2.8 fusion.138
  33.1 1.5 collective-permute-start.3
  38.0 5.3 %collective-permute-done.3 = bf16[192,768]{1,0:T(8,128)(2,1)S(1)} collective-permute-done((bf16[192,768]{1,0:T(8,128)(2,1)}, bf16[192,768]{1,0:T(8,128)(2,1)S(1)}, u32[]{:S(2)}, u32[]{:S(2)}) %collective-permute-start.3) | collective-permute-done | bytes 294944 | tf_op jit(solution)/shard_map/ppermute | solution.py:243
  43.4 5.2 %collective-permute-done.5 = bf16[192,768]{1,0:T(8,128)(2,1)S(1)} collective-permute-done((bf16[192,768]{1,0:T(8,128)(2,1)S(1)}, bf16[192,768]{1,0:T(8,128)(2,1)S(1)}, u32[]{:S(2)}, u32[]{:S(2)}) %collective-permute-start.5) | collective-permute-done | bytes 294944 | tf_op jit(solution)/shard_map/ppermute | solution.py:243
  49.9 3.1 fusion.14.refs_3_.refs_4_
  53.0 9.0 %shard_map.186 = (bf16[384,384]{1,0:T(8,128)(2,1)}, f32[3,8,384]{2,1,0:T(8,128)}) custom-call(bf16[1,384,384]{2,1,0:T(8,128)(2,1)} %slice.121.refs_0_, bf16[3,896,384]{2,1,0:T(8,128)(2,1)} %convert_bitcast_fusion.refs_1_.refs_2_, bf16[3,896,384]{2,1,0:T(8,128)(2,1)} %convert_bitcast_fusion.refs_1_.refs_2_, bf16[2,1152,384]{2,1,0:T(8,128)(2,1)} %fusion.14.refs_3_.refs_4_, ...), custom_call_target="tpu_custom_call" | custom-call | flops 1811939328 | bytes 2359296 | tf_op jit(solution)/shard_map/pallas_call | solution.py:92
  61.9 2.2 convolution_convert_fusion.8
  65.7 1.8 slice.125.refs_0_
  69.6 14.0 %shard_map.187 = (bf16[512,384]{1,0:T(8,128)(2,1)}, f32[3,8,512]{2,1,0:T(8,128)}) custom-call(bf16[1,512,384]{2,1,0:T(8,128)(2,1)} %slice.125.refs_0_, bf16[3,896,384]{2,1,0:T(8,128)(2,1)} %convert_bitcast_fusion.refs_1_.refs_2_, bf16[3,896,384]{2,1,0:T(8,128)(2,1)} %convert_bitcast_fusion.refs_1_.refs_2_, bf16[2,1152,384]{2,1,0:T(8,128)(2,1)} %fusion.14.refs_3_.refs_4_, ...), custom_call_target="tpu_custom_call" | custom-call | flops 3221225472 | bytes 3145728 | tf_op jit(solution)/shard_map/pallas_call | solution.py:92
  83.6 1.6 convolution_convert_fusion.5
  87.8 6.9 %multiply_convert_fusion.1 = (bf16[384,1536]{1,0:T(8,128)(2,1)S(1)}, f32[384,1536]{1,0:T(8,128)S(1)}, f32[384,1536]{1,0:T(8,128)S(1)}) fusion(bf16[384,768]{1,0:T(8,128)(2,1)S(1)} %add_convert_fusion.7, bf16[768,1536]{1,0:T(8,128)(2,1)S(1)} %copy-done), kind=kOutput, calls=%fused_computation.51 | convolution fusion | flops 944308224 | bytes 8847360 | tf_op jit(solution)/shard_map/dot_general | solution.py:374
  94.7 1.6 add_convert_fusion.2
  98.6 1.6 collective-permute-start.7
  100.7 4.9 %collective-permute-done.8 = bf16[512,768]{1,0:T(8,128)(2,1)S(1)} collective-permute-done((bf16[512,768]{1,0:T(8,128)(2,1)S(1)}, bf16[512,768]{1,0:T(8,128)(2,1)S(1)}, u32[]{:S(2)}, u32[]{:S(2)}) %collective-permute-start.8) | collective-permute-done | bytes 786464 | tf_op jit(solution)/shard_map/ppermute | solution.py:243
  106.6 8.3 %multiply_convert_fusion = (bf16[512,1536]{1,0:T(8,128)(2,1)S(1)}, f32[512,1536]{1,0:T(8,128)S(1)}, f32[512,1536]{1,0:T(8,128)S(1)}) fusion(bf16[512,768]{1,0:T(8,128)(2,1)S(1)} %add_convert_fusion.5, bf16[768,1536]{1,0:T(8,128)(2,1)S(1)} %copy-done), kind=kOutput, calls=%fused_computation.20 | convolution fusion | flops 1259077632 | bytes 11010048 | tf_op jit(solution)/shard_map/dot_general | solution.py:374
  114.9 2.2 add_convert_fusion
  122.0 2.9 convolution_convert_fusion.1
  124.9 4.2 %convolution_convert_fusion = bf16[768,1536]{1,0:T(8,128)(2,1)} fusion(bf16[512,1536]{1,0:T(8,128)(2,1)S(1)} %get-tuple-element.76, bf16[384,1536]{1,0:T(8,128)(2,1)S(1)} %get-tuple-element.80, bf16[512,768]{1,0:T(8,128)(2,1)S(1)} %bitcast.216, bf16[384,768]{1,0:T(8,128)(2,1)S(1)} %bitcast.217), kind=kOutput, calls=%fused_computation.14 | convolution fusion | flops 2123366400 | bytes 6488064 | tf_op jit(solution)/shard_map/nd,nf->df/dot_general | solution.py:388
  129.1 1.8 collective-permute-done.10
  131.6 1.8 fusion.140
  134.6 27.8 %collective-permute-done.11 = bf16[512,768]{1,0:T(8,128)(2,1)S(1)} collective-permute-done((bf16[512,768]{1,0:T(8,128)(2,1)S(1)}, bf16[512,768]{1,0:T(8,128)(2,1)S(1)}, u32[]{:S(2)}, u32[]{:S(2)}) %collective-permute-start.11) | collective-permute-done | bytes 786464 | tf_op jit(solution)/shard_map/ppermute | solution.py:243
  163.3 2.2 fusion.139
  167.9 21.9 %shard_map.188 = (bf16[512,384]{1,0:T(8,128)(2,1)}, f32[384,384]{1,0:T(8,128)}, f32[384,384]{1,0:T(8,128)}, f32[1152,384]{1,0:T(8,128)}, f32[1152,384]{1,0:T(8,1...) custom-call(bf16[1,512,384]{2,1,0:T(8,128)(2,1)} %slice.125.refs_0_, ...), custom_call_target="tpu_custom_call" | custom-call | flops 8053063680 | bytes 9437184 | tf_op jit(solution)/shard_map/pallas_call | solution.py:214
  189.8 14.4 %shard_map.189 = (bf16[384,384]{1,0:T(8,128)(2,1)}, bf16[384,384]{1,0:T(8,128)(2,1)}, bf16[384,384]{1,0:T(8,128)(2,1)}, bf16[1152,384]{1,0:T(8,128)(2,1)}, bf16[1152,384]{1,0:T(8,128)(2,1)}) custom-call(bf16[1,384,384]{2,1,0:T(8,128)(2,1)} %slice.121.refs_0_, bf16[3,896,384]{2,1,0:T(8,128)(2,1)} %convert_bitcast_fusion.refs_1_.refs_2_, ...), custom_call_target="tpu_custom_call" | custom-call | flops 4529848320 | bytes 7077888 | tf_op jit(solution)/shard_map/pallas_call | solution.py:214
  204.2 2.2 fusion.64
  206.5 2.1 bitcast_convert_fusion
  208.7 2.4 fusion.29
  211.2 2.2 fusion.23
  213.4 1.6 fusion.7
  220.5 2.4 copy-done.3
  222.9 1.8 dynamic-slice_bitcast_fusion
  224.7 23.6 %collective-permute-done.13 = bf16[192,768]{1,0:T(8,128)(2,1)S(1)} collective-permute-done((bf16[192,768]{1,0:T(8,128)(2,1)S(1)}, bf16[192,768]{1,0:T(8,128)(2,1)S(1)}, u32[]{:S(2)}, u32[]{:S(2)}) %collective-permute-start.13) | collective-permute-done | bytes 294944 | tf_op jit(solution)/shard_map/ppermute | solution.py:243
  248.2 6.3 %collective-permute-done.17 = bf16[192,768]{1,0:T(8,128)(2,1)S(1)} collective-permute-done((bf16[192,768]{1,0:T(8,128)(2,1)S(1)}, bf16[192,768]{1,0:T(8,128)(2,1)S(1)}, u32[]{:S(2)}, u32[]{:S(2)}) %collective-permute-start.17) | collective-permute-done | bytes 294944 | tf_op jit(solution)/shard_map/ppermute | solution.py:243
  254.5 3.3 collective-permute-done.15
  258.8 5.2 %collective-permute-start.18 = (bf16[192,768]{1,0:T(8,128)(2,1)}, bf16[192,768]{1,0:T(8,128)(2,1)}, u32[]{:S(2)}, u32[]{:S(2)}) collective-permute-start(bf16[192,768]{1,0:T(8,128)(2,1)} %get-tuple-element.85), channel_id=1, source_target_pairs={{0,2},{2,4},{4,6},{6,0},{1,3},{3,5},{5,7},{7,1},{8,10},{10,12},{12... | collective-permute-start | bytes 884744 | tf_op jit(solution)/shard_map/ppermute | solution.py:428
  264.0 3.9 collective-permute-start.16
  269.6 3.0 copy.26
  272.6 3.2 convert_element_type.382
  275.8 2.3 dynamic-slice_bitcast_fusion.2
  278.6 2.0 collective-permute-done.18
  280.6 8.3 %collective-permute-done.16 = bf16[192,768]{1,0:T(8,128)(2,1)} collective-permute-done((bf16[192,768]{1,0:T(8,128)(2,1)S(1)}, bf16[192,768]{1,0:T(8,128)(2,1)}, u32[]{:S(2)}, u32[]{:S(2)}) %collective-permute-start.16) | collective-permute-done | bytes 294944 | tf_op jit(solution)/shard_map/ppermute | solution.py:428
  291.2 2.0 multiply_reduce_fusion.2
  293.3 2.8 fusion.90
  298.1 3.7 collective-permute-start.37
  301.8 1.6 fusion.42
  307.7 4.8 %collective-permute-done.38 = f32[4,96]{1,0:T(4,128)S(1)} collective-permute-done((f32[4,96]{1,0:T(4,128)S(1)}, f32[4,96]{1,0:T(4,128)S(1)}, u32[]{:S(2)}, u32[]{:S(2)}) %collective-permute-start.38) | collective-permute-done | bytes 1568 | tf_op jit(solution)/shard_map/ppermute | solution.py:472
  313.9 3.2 fusion
  319.3 3.3 collective-permute-start.25
  323.6 2.9 collective-permute-done.23
  327.1 5.8 %collective-permute-done.24 = bf16[48,1152]{1,0:T(8,128)(2,1)S(1)} collective-permute-done((bf16[48,1152]{1,0:T(8,128)(2,1)S(1)}, bf16[48,1152]{1,0:T(8,128)(2,1)S(1)}, u32[]{:S(2)}, u32[]{:S(2)}) %collective-permute-start.24) | collective-permute-done | bytes 110624 | tf_op jit(solution)/shard_map/ppermute | solution.py:272
  333.6 15.6 %collective-permute-done.29 = bf16[4,48,3456]{2,1,0:T(8,128)(2,1)S(1)} collective-permute-done((bf16[4,48,3456]{2,1,0:T(8,128)(2,1)S(1)}, bf16[4,48,3456]{2,1,0:T(8,128)(2,1)S(1)}, u32[]{:S(2)}, u32[]{:S(2)}) %collective-permute-start.29) | collective-permute-done | bytes 1327136 | tf_op jit(solution)/shard_map/ppermute | solution.py:267
  350.3 3.3 collective-permute-start.32
  354.1 8.1 %collective-permute-done.30 = bf16[48,3456]{1,0:T(8,128)(2,1)S(1)} collective-permute-done((bf16[48,3456]{1,0:T(8,128)(2,1)S(1)}, bf16[48,3456]{1,0:T(8,128)(2,1)S(1)}, u32[]{:S(2)}, u32[]{:S(2)}) %collective-permute-start.30) | collective-permute-done | bytes 331808 | tf_op jit(solution)/shard_map/ppermute | solution.py:272
  362.3 4.3 %collective-permute-done.32 = bf16[48,3456]{1,0:T(8,128)(2,1)S(1)} collective-permute-done((bf16[48,3456]{1,0:T(8,128)(2,1)S(1)}, bf16[48,3456]{1,0:T(8,128)(2,1)S(1)}, u32[]{:S(2)}, u32[]{:S(2)}) %collective-permute-start.32) | collective-permute-done | bytes 331808 | tf_op jit(solution)/shard_map/ppermute | solution.py:272
  366.5 15.2 %collective-permute-done.31 = bf16[48,3456]{1,0:T(8,128)(2,1)S(1)} collective-permute-done((bf16[48,3456]{1,0:T(8,128)(2,1)S(1)}, bf16[48,3456]{1,0:T(8,128)(2,1)S(1)}, u32[]{:S(2)}, u32[]{:S(2)}) %collective-permute-start.31) | collective-permute-done | bytes 331808 | tf_op jit(solution)/shard_map/ppermute | solution.py:272
  383.6 8.2 %collective-permute-done.33 = bf16[48,3456]{1,0:T(8,128)(2,1)S(1)} collective-permute-done((bf16[48,3456]{1,0:T(8,128)(2,1)S(1)}, bf16[48,3456]{1,0:T(8,128)(2,1)S(1)}, u32[]{:S(2)}, u32[]{:S(2)}) %collective-permute-start.33) | collective-permute-done | bytes 331808 | tf_op jit(solution)/shard_map/ppermute | solution.py:277
  396.4 1.7 convert_bitcast_fusion.1
  (224 shorter events, 59.9 us)
Async XLA Ops:
  0.6 87.1 %copy-start = (bf16[768,1536]{1,0:T(8,128)(2,1)S(1)}, bf16[768,1536]{1,0:T(8,128)(2,1)}, u32[]{:S(2)}) copy-start(bf16[768,1536]{1,0:T(8,128)(2,1)} %param.18) | copy-start | bytes 7077892
  0.7 9.6 %copy-start.4 = (bf16[1,1,512,768]{3,2,1,0:T(8,128)(2,1)S(1)}, bf16[1,1,512,768]{3,2,1,0:T(8,128)(2,1)}, u32[]{:S(2)}) copy-start(bf16[1,1,512,768]{3,2,1,0:T(8,128)(2,1)} %param.12) | copy-start | bytes 2359300
  0.7 10.1 %copy-start.22 = (bf16[2,768]{1,0:T(2,128)(2,1)S(1)}, bf16[2,768]{1,0:T(2,128)(2,1)}, u32[]{:S(2)}) copy-start(bf16[2,768]{1,0:T(2,128)(2,1)} %param.20) | copy-start | bytes 9220
  0.7 10.2 %copy-start.23 = (bf16[2,768]{1,0:T(2,128)(2,1)S(1)}, bf16[2,768]{1,0:T(2,128)(2,1)}, u32[]{:S(2)}) copy-start(bf16[2,768]{1,0:T(2,128)(2,1)} %param.21) | copy-start | bytes 9220
  0.7 9.6 %copy-start.5 = (bf16[1,384,768]{2,1,0:T(8,128)(2,1)S(1)}, bf16[1,384,768]{2,1,0:T(8,128)(2,1)}, u32[]{:S(2)}) copy-start(bf16[1,384,768]{2,1,0:T(8,128)(2,1)} %param.11) | copy-start | bytes 1769476
  0.7 10.2 %copy-start.25 = (bf16[3,768,384]{2,1,0:T(8,128)(2,1)S(1)}, bf16[3,768,384]{2,1,0:T(8,128)(2,1)}, u32[]{:S(2)}) copy-start(bf16[3,768,384]{2,1,0:T(8,128)(2,1)} %param.16) | copy-start | bytes 5308420
  2.6 33.0 %collective-permute-start.4 = (bf16[192,768]{1,0:T(8,128)(2,1)}, bf16[192,768]{1,0:T(8,128)(2,1)S(1)}, u32[]{:S(2)}, u32[]{:S(2)}) collective-permute-start(bf16[192,768]{1,0:T(8,128)(2,1)} %dynamic-slice_bitcast_fusion.8), channel_id=1, source_target_pairs={{0,6},{2,0},{4,2},{6,4},{1,7},{3,1},{5,3},{7,5},{8,14},{10,8},{12,... | collective-permute-start | bytes 884744 | tf_op jit(solution)/shard_map/ppermute | solution.py:336
  7.7 25.4 %collective-permute-start.2 = (bf16[192,768]{1,0:T(8,128)(2,1)}, bf16[192,768]{1,0:T(8,128)(2,1)}, u32[]{:S(2)}, u32[]{:S(2)}) collective-permute-start(bf16[192,768]{1,0:T(8,128)(2,1)} %dynamic-slice_bitcast_fusion.8), channel_id=1, source_target_pairs={{0,4},{2,6},{4,0},{6,2},{1,5},{3,7},{5,1},{7,3},{8,12},{10,14},{12... | collective-permute-start | bytes 884744 | tf_op jit(solution)/shard_map/ppermute | solution.py:336
  7.7 20.2 %collective-permute-start = (bf16[192,768]{1,0:T(8,128)(2,1)}, bf16[192,768]{1,0:T(8,128)(2,1)}, u32[]{:S(2)}, u32[]{:S(2)}) collective-permute-start(bf16[192,768]{1,0:T(8,128)(2,1)} %dynamic-slice_bitcast_fusion.8), channel_id=1, source_target_pairs={{0,2},{2,4},{4,6},{6,0},{1,3},{3,5},{5,7},{7,1},{8,10},{10,12},{12... | collective-permute-start | bytes 884744 | tf_op jit(solution)/shard_map/ppermute | solution.py:336
  10.8 197.8 %copy-start.21 = (f32[896]{0:T(1024)}, f32[896]{0:T(1024)S(1)}, u32[]{:S(2)}) copy-start(f32[896]{0:T(1024)S(1)} %add_rsqrt_fusion.1) | copy-start | bytes 10756
  27.9 9.1 %collective-permute-start.1 = (bf16[192,768]{1,0:T(8,128)(2,1)}, bf16[192,768]{1,0:T(8,128)(2,1)S(1)}, u32[]{:S(2)}, u32[]{:S(2)}) collective-permute-start(bf16[192,768]{1,0:T(8,128)(2,1)} %collective-permute-done), channel_id=1, source_target_pairs={{0,1},{1,0},{2,3},{3,2},{4,5},{5,4},{6,7},{7,6},{8,9},{9,8},{10,11... | collective-permute-start | bytes 884744 | tf_op jit(solution)/shard_map/ppermute | solution.py:243
  33.1 10.2 %collective-permute-start.3 = (bf16[192,768]{1,0:T(8,128)(2,1)}, bf16[192,768]{1,0:T(8,128)(2,1)S(1)}, u32[]{:S(2)}, u32[]{:S(2)}) collective-permute-start(bf16[192,768]{1,0:T(8,128)(2,1)} %collective-permute-done.2), channel_id=1, source_target_pairs={{0,1},{1,0},{2,3},{3,2},{4,5},{5,4},{6,7},{7,6},{8,9},{9,8},{10,11... | collective-permute-start | bytes 884744 | tf_op jit(solution)/shard_map/ppermute | solution.py:243
  35.6 13.0 %collective-permute-start.5 = (bf16[192,768]{1,0:T(8,128)(2,1)S(1)}, bf16[192,768]{1,0:T(8,128)(2,1)S(1)}, u32[]{:S(2)}, u32[]{:S(2)}) collective-permute-start(bf16[192,768]{1,0:T(8,128)(2,1)S(1)} %collective-permute-done.4), channel_id=1, source_target_pairs={{0,1},{1,0},{2,3},{3,2},{4,5},{5,4},{6,7},{7,6},{8,9},{9,8},{10,11... | collective-permute-start | bytes 884744 | tf_op jit(solution)/shard_map/ppermute | solution.py:243
  43.3 6.5 %copy-start.26 = (bf16[3,768,384]{2,1,0:T(8,128)(2,1)S(1)}, bf16[3,768,384]{2,1,0:T(8,128)(2,1)}, u32[]{:S(2)}) copy-start(bf16[3,768,384]{2,1,0:T(8,128)(2,1)} %param.16) | copy-start | bytes 5308420
  53.0 9.0 %copy-start.11 = (bf16[384,768]{1,0:T(8,128)(2,1)S(1)}, bf16[384,768]{1,0:T(8,128)(2,1)}, u32[]{:S(2)}) copy-start(bf16[384,768]{1,0:T(8,128)(2,1)} %param.17) | copy-start | bytes 1769476
  64.2 21.5 %collective-permute-start.6 = (bf16[384,768]{1,0:T(8,128)(2,1)}, bf16[384,768]{1,0:T(8,128)(2,1)}, u32[]{:S(2)}, u32[]{:S(2)}) collective-permute-start(bf16[384,768]{1,0:T(8,128)(2,1)} %convolution_convert_fusion.8), channel_id=1, source_target_pairs={{0,1},{1,0},{2,3},{3,2},{4,5},{5,4},{6,7},{7,6},{8,9},{9,8},{10,11... | collective-permute-start | bytes 1769480 | tf_op jit(solution)/shard_map/ppermute | solution.py:243
  69.5 14.0 %copy-start.12 = (bf16[384,768]{1,0:T(8,128)(2,1)S(1)}, bf16[384,768]{1,0:T(8,128)(2,1)}, u32[]{:S(2)}) copy-start(bf16[384,768]{1,0:T(8,128)(2,1)} %param.17) | copy-start | bytes 1769476
  69.6 16.1 %copy-start.7 = (f32[896,768]{1,0:T(8,128)S(1)}, f32[896,768]{1,0:T(8,128)}, u32[]{:S(2)}) copy-start(f32[896,768]{1,0:T(8,128)} %fusion.138) | copy-start | bytes 8257540
  85.1 20.5 %collective-permute-start.8 = (bf16[512,768]{1,0:T(8,128)(2,1)S(1)}, bf16[512,768]{1,0:T(8,128)(2,1)S(1)}, u32[]{:S(2)}, u32[]{:S(2)}) collective-permute-start(bf16[512,768]{1,0:T(8,128)(2,1)S(1)} %convolution_convert_fusion.5), channel_id=1, source_target_pairs={{0,1},{1,0},{2,3},{3,2},{4,5},{5,4},{6,7},{7,6},{8,9},{9,8},{10,11... | collective-permute-start | bytes 2359304 | tf_op jit(solution)/shard_map/ppermute | solution.py:243
  87.8 7.0 %copy-start.17 = (bf16[1,384,768]{2,1,0:T(8,128)(2,1)S(1)}, bf16[1,384,768]{2,1,0:T(8,128)(2,1)}, u32[]{:S(2)}) copy-start(bf16[1,384,768]{2,1,0:T(8,128)(2,1)} %param.13) | copy-start | bytes 1769476
  87.8 6.9 %copy-start.24 = (bf16[1536,768]{1,0:T(8,128)(2,1)S(1)}, bf16[1536,768]{1,0:T(8,128)(2,1)}, u32[]{:S(2)}) copy-start(bf16[1536,768]{1,0:T(8,128)(2,1)} %param.19) | copy-start | bytes 7077892
  98.6 33.0 %collective-permute-start.7 = (bf16[384,768]{1,0:T(8,128)(2,1)S(1)}, bf16[384,768]{1,0:T(8,128)(2,1)S(1)}, u32[]{:S(2)}, u32[]{:S(2)}) collective-permute-start(bf16[384,768]{1,0:T(8,128)(2,1)S(1)} %convolution_convert_fusion.7), channel_id=1, source_target_pairs={{0,1},{1,0},{2,3},{3,2},{4,5},{5,4},{6,7},{7,6},{8,9},{9,8},{10,11... | collective-permute-start | bytes 1769480 | tf_op jit(solution)/shard_map/ppermute | solution.py:243
  100.2 30.7 %collective-permute-start.10 = (bf16[384,768]{1,0:T(8,128)(2,1)S(1)}, bf16[384,768]{1,0:T(8,128)(2,1)S(1)}, u32[]{:S(2)}, u32[]{:S(2)}) collective-permute-start(bf16[384,768]{1,0:T(8,128)(2,1)S(1)} %convolution_convert_fusion.6), channel_id=1, source_target_pairs={{0,1},{1,0},{2,3},{3,2},{4,5},{5,4},{6,7},{7,6},{8,9},{9,8},{10,11... | collective-permute-start | bytes 1769480 | tf_op jit(solution)/shard_map/ppermute | solution.py:243
  106.6 8.3 %copy-start.16 = (bf16[1,1,512,768]{3,2,1,0:T(8,128)(2,1)S(1)}, bf16[1,1,512,768]{3,2,1,0:T(8,128)(2,1)}, u32[]{:S(2)}) copy-start(bf16[1,1,512,768]{3,2,1,0:T(8,128)(2,1)} %param.14) | copy-start | bytes 2359300
  119.9 43.4 %collective-permute-start.9 = (bf16[512,768]{1,0:T(8,128)(2,1)S(1)}, bf16[512,768]{1,0:T(8,128)(2,1)S(1)}, u32[]{:S(2)}, u32[]{:S(2)}) collective-permute-start(bf16[512,768]{1,0:T(8,128)(2,1)S(1)} %convolution_convert_fusion.4), channel_id=1, source_target_pairs={{0,1},{1,0},{2,3},{3,2},{4,5},{5,4},{6,7},{7,6},{8,9},{9,8},{10,11... | collective-permute-start | bytes 2359304 | tf_op jit(solution)/shard_map/ppermute | solution.py:243
  120.5 41.9 %collective-permute-start.11 = (bf16[512,768]{1,0:T(8,128)(2,1)S(1)}, bf16[512,768]{1,0:T(8,128)(2,1)S(1)}, u32[]{:S(2)}, u32[]{:S(2)}) collective-permute-start(bf16[512,768]{1,0:T(8,128)(2,1)S(1)} %convolution_convert_fusion.3), channel_id=1, source_target_pairs={{0,1},{1,0},{2,3},{3,2},{4,5},{5,4},{6,7},{7,6},{8,9},{9,8},{10,11... | collective-permute-start | bytes 2359304 | tf_op jit(solution)/shard_map/ppermute | solution.py:243
  189.7 14.4 %copy-start.27 = (bf16[3,768,384]{2,1,0:T(8,128)(2,1)S(1)}, bf16[3,768,384]{2,1,0:T(8,128)(2,1)}, u32[]{:S(2)}) copy-start(bf16[3,768,384]{2,1,0:T(8,128)(2,1)} %param.16) | copy-start | bytes 5308420
  206.4 8.7 %copy-start.18 = (bf16[384,768]{1,0:T(8,128)(2,1)}, bf16[384,768]{1,0:T(8,128)(2,1)S(1)}, u32[]{:S(2)}) copy-start(bf16[384,768]{1,0:T(8,128)(2,1)S(1)} %fusion.64) | copy-start | bytes 1769476
  208.6 2.6 copy-start.9
  208.6 2.6 copy-start.29
  215.0 4.8 %copy-start.15 = (bf16[768,1536]{1,0:T(8,128)(2,1)S(1)}, bf16[768,1536]{1,0:T(8,128)(2,1)}, u32[]{:S(2)}) copy-start(bf16[768,1536]{1,0:T(8,128)(2,1)} %convolution_convert_fusion) | copy-start | bytes 7077892
  215.1 63.0 %collective-permute-start.12 = (bf16[192,768]{1,0:T(8,128)(2,1)S(1)}, bf16[192,768]{1,0:T(8,128)(2,1)}, u32[]{:S(2)}, u32[]{:S(2)}) collective-permute-start(bf16[192,768]{1,0:T(8,128)(2,1)S(1)} %dynamic-slice_bitcast_fusion.7), channel_id=1, source_target_pairs={{0,1},{1,0},{2,3},{3,2},{4,5},{5,4},{6,7},{7,6},{8,9},{9,8},{10,11... | collective-permute-start | bytes 884744 | tf_op jit(solution)/shard_map/ppermute | solution.py:243
  215.7 75.5 %collective-permute-start.20 = (bf16[512,768]{1,0:T(8,128)(2,1)}, bf16[512,768]{1,0:T(8,128)(2,1)}, u32[]{:S(2)}, u32[]{:S(2)}) collective-permute-start(bf16[512,768]{1,0:T(8,128)(2,1)} %bitcast_convert_fusion), channel_id=1, source_target_pairs={{0,1},{1,0},{2,3},{3,2},{4,5},{5,4},{6,7},{7,6},{8,9},{9,8},{10,11... | collective-permute-start | bytes 2359304 | tf_op jit(solution)/shard_map/ppermute | solution.py:243
  217.3 31.0 %collective-permute-start.13 = (bf16[192,768]{1,0:T(8,128)(2,1)S(1)}, bf16[192,768]{1,0:T(8,128)(2,1)S(1)}, u32[]{:S(2)}, u32[]{:S(2)}) collective-permute-start(bf16[192,768]{1,0:T(8,128)(2,1)S(1)} %get-tuple-element.87), channel_id=1, source_target_pairs={{0,1},{1,0},{2,3},{3,2},{4,5},{5,4},{6,7},{7,6},{8,9},{9,8},{10,11... | collective-permute-start | bytes 884744 | tf_op jit(solution)/shard_map/ppermute | solution.py:243
  217.8 36.7 %collective-permute-start.17 = (bf16[192,768]{1,0:T(8,128)(2,1)S(1)}, bf16[192,768]{1,0:T(8,128)(2,1)S(1)}, u32[]{:S(2)}, u32[]{:S(2)}) collective-permute-start(bf16[192,768]{1,0:T(8,128)(2,1)S(1)} %get-tuple-element.88), channel_id=1, source_target_pairs={{0,1},{1,0},{2,3},{3,2},{4,5},{5,4},{6,7},{7,6},{8,9},{9,8},{10,11... | collective-permute-start | bytes 884744 | tf_op jit(solution)/shard_map/ppermute | solution.py:243
  219.4 38.4 %collective-permute-start.15 = (bf16[192,768]{1,0:T(8,128)(2,1)S(1)}, bf16[192,768]{1,0:T(8,128)(2,1)S(1)}, u32[]{:S(2)}, u32[]{:S(2)}) collective-permute-start(bf16[192,768]{1,0:T(8,128)(2,1)S(1)} %get-tuple-element.89), channel_id=1, source_target_pairs={{0,1},{1,0},{2,3},{3,2},{4,5},{5,4},{6,7},{7,6},{8,9},{9,8},{10,11... | collective-permute-start | bytes 884744 | tf_op jit(solution)/shard_map/ppermute | solution.py:243
  258.8 19.3 %collective-permute-start.14 = (bf16[192,768]{1,0:T(8,128)(2,1)}, bf16[192,768]{1,0:T(8,128)(2,1)}, u32[]{:S(2)}, u32[]{:S(2)}) collective-permute-start(bf16[192,768]{1,0:T(8,128)(2,1)} %get-tuple-element.84), channel_id=1, source_target_pairs={{0,6},{2,0},{4,2},{6,4},{1,7},{3,1},{5,3},{7,5},{8,14},{10,8},{12,... | collective-permute-start | bytes 884744 | tf_op jit(solution)/shard_map/ppermute | solution.py:428
  258.8 21.7 %collective-permute-start.18 = (bf16[192,768]{1,0:T(8,128)(2,1)}, bf16[192,768]{1,0:T(8,128)(2,1)}, u32[]{:S(2)}, u32[]{:S(2)}) collective-permute-start(bf16[192,768]{1,0:T(8,128)(2,1)} %get-tuple-element.85), channel_id=1, source_target_pairs={{0,2},{2,4},{4,6},{6,0},{1,3},{3,5},{5,7},{7,1},{8,10},{10,12},{12... | collective-permute-start | bytes 884744 | tf_op jit(solution)/shard_map/ppermute | solution.py:428
  264.0 24.8 %collective-permute-start.16 = (bf16[192,768]{1,0:T(8,128)(2,1)S(1)}, bf16[192,768]{1,0:T(8,128)(2,1)}, u32[]{:S(2)}, u32[]{:S(2)}) collective-permute-start(bf16[192,768]{1,0:T(8,128)(2,1)S(1)} %get-tuple-element.86), channel_id=1, source_target_pairs={{0,4},{2,6},{4,0},{6,2},{1,5},{3,7},{5,1},{7,3},{8,12},{10,14},{12... | collective-permute-start | bytes 884744 | tf_op jit(solution)/shard_map/ppermute | solution.py:428
  275.8 15.4 %copy-start.2 = (f32[896,768]{1,0:T(8,128)S(1)}, f32[896,768]{1,0:T(8,128)}, u32[]{:S(2)}) copy-start(f32[896,768]{1,0:T(8,128)} %subtract_multiply_fusion) | copy-start | bytes 8257540
  278.1 15.2 %copy-start.10 = (f32[512,768]{1,0:T(8,128)S(1)}, f32[512,768]{1,0:T(8,128)}, u32[]{:S(2)}) copy-start(f32[512,768]{1,0:T(8,128)} %get-tuple-element.73) | copy-start | bytes 4718596
  278.1 35.8 %collective-permute-start.28 = (bf16[4,2,48,3456]{3,2,1,0:T(8,128)(2,1)}, bf16[4,2,48,3456]{3,2,1,0:T(8,128)(2,1)}, u32[]{:S(2)}, u32[]{:S(2)}) collective-permute-start(bf16[4,2,48,3456]{3,2,1,0:T(8,128)(2,1)} %dynamic-slice_bitcast_fusion), channel_id=1, source_target_pairs={{0,8},{8,0},{16,24},{24,16},{1,9},{9,1},{17,25},{25,17},{2,10},{10... | collective-permute-start | bytes 7962632 | tf_op jit(solution)/shard_map/ppermute | solution.py:262
  278.1 23.7 %collective-permute-start.21 = (bf16[4,2,48,1152]{3,2,1,0:T(8,128)(2,1)}, bf16[4,2,48,1152]{3,2,1,0:T(8,128)(2,1)}, u32[]{:S(2)}, u32[]{:S(2)}) collective-permute-start(bf16[4,2,48,1152]{3,2,1,0:T(8,128)(2,1)} %dynamic-slice_bitcast_fusion.2), channel_id=1, source_target_pairs={{0,8},{8,0},{16,24},{24,16},{1,9},{9,1},{17,25},{25,17},{2,10},{10... | collective-permute-start | bytes 2654216 | tf_op jit(solution)/shard_map/ppermute | solution.py:262
  290.4 6.8 %collective-permute-start.19 = (bf16[192,768]{1,0:T(8,128)(2,1)S(1)}, bf16[192,768]{1,0:T(8,128)(2,1)S(1)}, u32[]{:S(2)}, u32[]{:S(2)}) collective-permute-start(bf16[192,768]{1,0:T(8,128)(2,1)S(1)} %fusion.105), channel_id=1, source_target_pairs={{0,1},{1,0},{2,3},{3,2},{4,5},{5,4},{6,7},{7,6},{8,9},{9,8},{10,11... | collective-permute-start | bytes 884744 | tf_op jit(solution)/shard_map/ppermute | solution.py:243
  297.2 15.3 %slice-start = ((f32[896]{0:T(1024)}), f32[384]{0:T(512)S(1)}, s32[]{:S(2)}) async-start(f32[896]{0:T(1024)} %copy-done.21), calls=%async_computation | async-start | bytes 4096 | tf_op jit(solution)/shard_map/slice | solution.py:450
  297.8 14.7 %copy-start.13 = (f32[384,768]{1,0:T(8,128)S(1)}, f32[384,768]{1,0:T(8,128)}, u32[]{:S(2)}) copy-start(f32[384,768]{1,0:T(8,128)} %get-tuple-element.75) | copy-start | bytes 3538948
  297.9 7.1 %collective-permute-start.35 = (f32[4,96]{1,0:T(4,128)S(1)}, f32[4,96]{1,0:T(4,128)S(1)}, u32[]{:S(2)}, u32[]{:S(2)}) collective-permute-start(f32[4,96]{1,0:T(4,128)S(1)} %get-tuple-element.106), channel_id=1, source_target_pairs={{0,2},{2,4},{4,6},{6,0},{1,3},{3,5},{5,7},{7,1},{8,10},{10,12},{12... | collective-permute-start | bytes 4616 | tf_op jit(solution)/shard_map/ppermute | solution.py:468
  298.1 6.9 %collective-permute-start.37 = (f32[4,96]{1,0:T(4,128)S(1)}, f32[4,96]{1,0:T(4,128)S(1)}, u32[]{:S(2)}, u32[]{:S(2)}) collective-permute-start(f32[4,96]{1,0:T(4,128)S(1)} %get-tuple-element.107), channel_id=1, source_target_pairs={{0,6},{2,0},{4,2},{6,4},{1,7},{3,1},{5,3},{7,5},{8,14},{10,8},{12,... | collective-permute-start | bytes 4616 | tf_op jit(solution)/shard_map/ppermute | solution.py:468
  301.8 4.5 %collective-permute-start.36 = (f32[4,96]{1,0:T(4,128)S(1)}, f32[4,96]{1,0:T(4,128)S(1)}, u32[]{:S(2)}, u32[]{:S(2)}) collective-permute-start(f32[4,96]{1,0:T(4,128)S(1)} %get-tuple-element.108), channel_id=1, source_target_pairs={{0,4},{2,6},{4,0},{6,2},{1,5},{3,7},{5,1},{7,3},{8,12},{10,14},{12... | collective-permute-start | bytes 4616 | tf_op jit(solution)/shard_map/ppermute | solution.py:468
  303.5 10.3 %collective-permute-start.22 = (bf16[4,48,1152]{2,1,0:T(8,128)(2,1)S(1)}, bf16[4,48,1152]{2,1,0:T(8,128)(2,1)S(1)}, u32[]{:S(2)}, u32[]{:S(2)}) collective-permute-start(bf16[4,48,1152]{2,1,0:T(8,128)(2,1)S(1)} %dynamic-slice_bitcast_fusion.3), channel_id=1, source_target_pairs={{0,16},{8,24},{16,0},{24,8},{1,17},{9,25},{17,1},{25,9},{2,18},{10... | collective-permute-start | bytes 1327112 | tf_op jit(solution)/shard_map/ppermute | solution.py:267
  306.3 6.3 %collective-permute-start.38 = (f32[4,96]{1,0:T(4,128)S(1)}, f32[4,96]{1,0:T(4,128)S(1)}, u32[]{:S(2)}, u32[]{:S(2)}) collective-permute-start(f32[4,96]{1,0:T(4,128)S(1)} %fusion.117), channel_id=1, source_target_pairs={{0,16},{8,24},{16,0},{24,8},{1,17},{9,25},{17,1},{25,9},{2,18},{10... | collective-permute-start | bytes 4616 | tf_op jit(solution)/shard_map/ppermute | solution.py:472
  312.5 1.2 collective-permute-start.39
  317.2 32.1 %collective-permute-start.29 = (bf16[4,48,3456]{2,1,0:T(8,128)(2,1)S(1)}, bf16[4,48,3456]{2,1,0:T(8,128)(2,1)S(1)}, u32[]{:S(2)}, u32[]{:S(2)}) collective-permute-start(bf16[4,48,3456]{2,1,0:T(8,128)(2,1)S(1)} %dynamic-slice_bitcast_fusion.1), channel_id=1, source_target_pairs={{0,16},{8,24},{16,0},{24,8},{1,17},{9,25},{17,1},{25,9},{2,18},{10... | collective-permute-start | bytes 3981320 | tf_op jit(solution)/shard_map/ppermute | solution.py:267
  318.7 7.8 %collective-permute-start.23 = (bf16[48,1152]{1,0:T(8,128)(2,1)S(1)}, bf16[48,1152]{1,0:T(8,128)(2,1)S(1)}, u32[]{:S(2)}, u32[]{:S(2)}) collective-permute-start(bf16[48,1152]{1,0:T(8,128)(2,1)S(1)} %get-tuple-element.103), channel_id=1, source_target_pairs={{0,2},{2,4},{4,6},{6,0},{1,3},{3,5},{5,7},{7,1},{8,10},{10,12},{12... | collective-permute-start | bytes 331784 | tf_op jit(solution)/shard_map/ppermute | solution.py:272
  319.3 7.8 %collective-permute-start.25 = (bf16[48,1152]{1,0:T(8,128)(2,1)S(1)}, bf16[48,1152]{1,0:T(8,128)(2,1)S(1)}, u32[]{:S(2)}, u32[]{:S(2)}) collective-permute-start(bf16[48,1152]{1,0:T(8,128)(2,1)S(1)} %get-tuple-element.104), channel_id=1, source_target_pairs={{0,6},{2,0},{4,2},{6,4},{1,7},{3,1},{5,3},{7,5},{8,14},{10,8},{12,... | collective-permute-start | bytes 331784 | tf_op jit(solution)/shard_map/ppermute | solution.py:272
  322.6 10.3 %collective-permute-start.24 = (bf16[48,1152]{1,0:T(8,128)(2,1)S(1)}, bf16[48,1152]{1,0:T(8,128)(2,1)S(1)}, u32[]{:S(2)}, u32[]{:S(2)}) collective-permute-start(bf16[48,1152]{1,0:T(8,128)(2,1)S(1)} %get-tuple-element.105), channel_id=1, source_target_pairs={{0,4},{2,6},{4,0},{6,2},{1,5},{3,7},{5,1},{7,3},{8,12},{10,14},{12... | collective-permute-start | bytes 331784 | tf_op jit(solution)/shard_map/ppermute | solution.py:272
  332.9 21.1 %collective-permute-start.26 = (bf16[48,1152]{1,0:T(8,128)(2,1)S(1)}, bf16[48,1152]{1,0:T(8,128)(2,1)S(1)}, u32[]{:S(2)}, u32[]{:S(2)}) collective-permute-start(bf16[48,1152]{1,0:T(8,128)(2,1)S(1)} %fusion.110), channel_id=1, source_target_pairs={{0,16},{8,24},{16,0},{24,8},{1,17},{9,25},{17,1},{25,9},{2,18},{10... | collective-permute-start | bytes 331784 | tf_op jit(solution)/shard_map/ppermute | solution.py:277
  349.7 12.5 %collective-permute-start.30 = (bf16[48,3456]{1,0:T(8,128)(2,1)S(1)}, bf16[48,3456]{1,0:T(8,128)(2,1)S(1)}, u32[]{:S(2)}, u32[]{:S(2)}) collective-permute-start(bf16[48,3456]{1,0:T(8,128)(2,1)S(1)} %get-tuple-element.95), channel_id=1, source_target_pairs={{0,2},{2,4},{4,6},{6,0},{1,3},{3,5},{5,7},{7,1},{8,10},{10,12},{12... | collective-permute-start | bytes 995336 | tf_op jit(solution)/shard_map/ppermute | solution.py:272
  350.3 16.2 %collective-permute-start.32 = (bf16[48,3456]{1,0:T(8,128)(2,1)S(1)}, bf16[48,3456]{1,0:T(8,128)(2,1)S(1)}, u32[]{:S(2)}, u32[]{:S(2)}) collective-permute-start(bf16[48,3456]{1,0:T(8,128)(2,1)S(1)} %get-tuple-element.96), channel_id=1, source_target_pairs={{0,6},{2,0},{4,2},{6,4},{1,7},{3,1},{5,3},{7,5},{8,14},{10,8},{12,... | collective-permute-start | bytes 995336 | tf_op jit(solution)/shard_map/ppermute | solution.py:272
  353.6 28.2 %collective-permute-start.31 = (bf16[48,3456]{1,0:T(8,128)(2,1)S(1)}, bf16[48,3456]{1,0:T(8,128)(2,1)S(1)}, u32[]{:S(2)}, u32[]{:S(2)}) collective-permute-start(bf16[48,3456]{1,0:T(8,128)(2,1)S(1)} %get-tuple-element.97), channel_id=1, source_target_pairs={{0,4},{2,6},{4,0},{6,2},{1,5},{3,7},{5,1},{7,3},{8,12},{10,14},{12... | collective-permute-start | bytes 995336 | tf_op jit(solution)/shard_map/ppermute | solution.py:272
  354.1 37.8 %collective-permute-start.27 = (bf16[2,48,1152]{2,1,0:T(8,128)(2,1)S(1)}, bf16[2,48,1152]{2,1,0:T(8,128)(2,1)S(1)}, u32[]{:S(2)}, u32[]{:S(2)}) collective-permute-start(bf16[2,48,1152]{2,1,0:T(8,128)(2,1)S(1)} %bitcast_dynamic-update-slice_fusion.2), channel_id=1, source_target_pairs={{0,8},{8,0},{16,24},{24,16},{1,9},{9,1},{17,25},{25,17},{2,10},{10... | collective-permute-start | bytes 663560 | tf_op jit(solution)/shard_map/ppermute | solution.py:279
  382.0 9.8 %collective-permute-start.33 = (bf16[48,3456]{1,0:T(8,128)(2,1)S(1)}, bf16[48,3456]{1,0:T(8,128)(2,1)S(1)}, u32[]{:S(2)}, u32[]{:S(2)}) collective-permute-start(bf16[48,3456]{1,0:T(8,128)(2,1)S(1)} %fusion.96), channel_id=1, source_target_pairs={{0,16},{8,24},{16,0},{24,8},{1,17},{9,25},{17,1},{25,9},{2,18},{10... | collective-permute-start | bytes 995336 | tf_op jit(solution)/shard_map/ppermute | solution.py:277
  391.8 2.3 collective-permute-start.34
  395.5 2.6 copy-start.1
  (14 other events, 29.9 us)

commit v3 on v1

v3 whole, which is shorter than its diff:
```python
import functools

import jax
import jax.numpy as jnp
from jax import lax
from jax.experimental import pallas as pl
from jax.experimental.pallas import tpu as pltpu
from jax.sharding import PartitionSpec as P

HEAD = 64
CORES = 2
LANES = 128
norm_eps = 1e-05
hidden_value = -1e30
BF = jnp.bfloat16
F32 = jnp.float32
BUDGET = 56 * 1024 * 1024


def nt(left, right):
    return lax.dot_general(left, right, (((1,), (1,)), ((), ())), preferred_element_type=F32)


def tn(left, right):
    return lax.dot_general(left, right, (((0,), (0,)), ((), ())), preferred_element_type=F32)


def nn(left, right):
    return lax.dot_general(left, right, (((1,), (0,)), ((), ())), preferred_element_type=F32)


def one_head(pair, which, factor=None):
    lane = lax.broadcasted_iota(jnp.int32, pair.shape, 1)
    wide = pair.astype(F32)
    if factor is not None:
        wide = wide * factor
    return jnp.where((lane // HEAD) == which, wide, 0.0).astype(BF)


def lane_pair(pair):
    lane = lax.broadcasted_iota(jnp.int32, pair[0].shape, 1)
    return jnp.where(lane < HEAD, pair[0], pair[1])


def row_pair(pair):
    rows = pair[0].shape[1]
    return jnp.transpose(
        jnp.concatenate([jnp.broadcast_to(one, (HEAD, rows)) for one in pair], axis=0)
    )


def masked_scores(keys, mine, bias):
    scores = nt(keys, mine)
    if bias is None:
        return scores
    return scores + jnp.concatenate([bias] * (mine.shape[0] // LANES), axis=1)


def near_kernel(qp_ref, kp_ref, vp_ref, qc_ref, kc_ref, vc_ref, bias_ref, op_ref, sp_ref, oc_ref, sc_ref):
    parts = (
        (qp_ref, op_ref, sp_ref, [(kp_ref, vp_ref, None)]),
        (qc_ref, oc_ref, sc_ref, [(kp_ref, vp_ref, bias_ref), (kc_ref, vc_ref, None)]),
    )
    for q_ref, out_ref, stat_ref, sources in parts:
        outs = []
        for which in range(2):
            mine = one_head(q_ref[0], which, HEAD ** (-0.5))
            scores = [
                masked_scores(k_ref[0], mine, None if b_ref is None else b_ref[...])
                for k_ref, _, b_ref in sources
            ]
            top = functools.reduce(
                jnp.maximum, [jnp.max(s, axis=0, keepdims=True) for s in scores]
            )
            weights = [jnp.exp(s - top) for s in scores]
            stat_ref[0, which : which + 1] = top
            stat_ref[0, 2 + which : 3 + which] = sum(
                jnp.sum(w, axis=0, keepdims=True) for w in weights
            )
            outs.append(sum(tn(w.astype(BF), v_ref[0]) for w, (_, v_ref, _) in zip(weights, sources)))
        out_ref[...] = lane_pair(outs)


def kind_spec(array, kind):
    return pl.BlockSpec((1, array.shape[1], LANES), lambda p: (kind, 0, p))


def full_spec(rows):
    return pl.BlockSpec((rows, LANES), lambda p: (0, p))


def slab_spec(count, rows):
    return pl.BlockSpec((count, rows, LANES), lambda p: (0, 0, p))


def stat_spec(rows):
    return pl.BlockSpec((1, 8, rows), lambda p: (p, 0, 0))


def bias_spec(bias):
    return pl.BlockSpec(bias.shape, lambda p: (0, 0))


def params():
    return pltpu.CompilerParams(vmem_limit_bytes=BUDGET)


def cost(matmuls, pairs, width, moved):
    return pl.CostEstimate(flops=matmuls * pairs, transcendentals=0, bytes_accessed=moved)


def attend_near(own_p, own_c, bias):
    width = own_p.shape[2]
    outs = []
    for own in (own_p, own_c):
        rows = own.shape[1]
        outs += [
            jax.ShapeDtypeStruct((rows, width), F32),
            jax.ShapeDtypeStruct((width // LANES, 8, rows), F32),
        ]
    rows_p, rows_c = own_p.shape[1], own_c.shape[1]
    return pl.pallas_call(
        near_kernel,
        grid=(width // LANES,),
        in_specs=[kind_spec(own_p, c) for c in range(3)]
        + [kind_spec(own_c, c) for c in range(3)]
        + [bias_spec(bias)],
        out_specs=[full_spec(rows_p), stat_spec(rows_p), full_spec(rows_c), stat_spec(rows_c)],
        out_shape=outs,
        compiler_params=params(),
        cost_estimate=cost(2, rows_p * rows_p + rows_c * (rows_p + rows_c), width, 10 * rows_c),
    )(own_p, own_p, own_p, own_c, own_c, own_c, bias)


def far_kernel(*refs, masked):
    if masked:
        q_ref, k_ref, v_ref, bias_ref, part_ref, stat_ref, out_ref, log_ref = refs
    else:
        q_ref, k_ref, v_ref, part_ref, stat_ref, out_ref, log_ref = refs
    outs = []
    olds = []
    news = []
    for which in range(2):
        mine = one_head(q_ref[0], which, HEAD ** (-0.5))
        scores = masked_scores(k_ref[0], mine, bias_ref[...] if masked else None)
        old = stat_ref[0, which : which + 1]
        top = jnp.maximum(old, jnp.max(scores, axis=0, keepdims=True))
        weights = jnp.exp(scores - top)
        shrink = jnp.exp(old - top)
        total = shrink * stat_ref[0, 2 + which : 3 + which] + jnp.sum(
            weights, axis=0, keepdims=True
        )
        outs.append(tn(weights.astype(BF), v_ref[0]))
        olds.append(shrink / total)
        news.append(1.0 / total)
        log_ref[0, which : which + 1] = top + jnp.log(total)
    out = lane_pair(outs) * row_pair(news) + part_ref[...] * row_pair(olds)
    out_ref[...] = out.astype(BF)


def attend_far(own, far, bias, part, stat):
    masked = bias is not None
    rows = own.shape[1]
    width = own.shape[2]
    specs = [kind_spec(own, 0), kind_spec(far, 0), kind_spec(far, 1)]
    args = [own, far, far]
    if masked:
        specs.append(bias_spec(bias))
        args.append(bias)
    return pl.pallas_call(
        functools.partial(far_kernel, masked=masked),
        grid=(width // LANES,),
        in_specs=specs + [full_spec(rows), stat_spec(rows)],
        out_specs=[full_spec(rows), stat_spec(rows)],
        out_shape=[
            jax.ShapeDtypeStruct((rows, width), BF),
            jax.ShapeDtypeStruct((width // LANES, 8, rows), F32),
        ],
        compiler_params=params(),
        cost_estimate=cost(2, rows * far.shape[1], width, 4 * far.shape[1]),
    )(*args, part, stat)


def pull_heads(q_ref, do_ref, out_ref, log_ref):
    upstream = do_ref[...]
    inner = jnp.transpose(upstream.astype(F32) * out_ref[...].astype(F32))
    return [
        (
            one_head(q_ref[0], which, HEAD ** (-0.5)),
            one_head(upstream, which),
            jnp.sum(inner[which * HEAD : (which + 1) * HEAD], axis=0, keepdims=True),
            log_ref[0, which : which + 1],
        )
        for which in range(2)
    ]


def pull_piece(keys, values, bias, heads):
    key_grads = []
    value_grads = []
    query_grads = []
    for mine, grad, delta, log in heads:
        probs = jnp.exp(masked_scores(keys, mine, bias) - log)
        spread = probs * (nt(values, grad) - delta)
        low = spread.astype(BF)
        value_grads.append(nn(probs.astype(BF), grad))
        key_grads.append(nn(low, mine))
        query_grads.append(tn(low, keys))
    return key_grads[0] + key_grads[1], value_grads[0] + value_grads[1], query_grads


def pull_far_kernel(*refs, masked, chunk):
    if masked:
        q_ref, k_ref, v_ref, bias_ref, do_ref, out_ref, log_ref, dq_ref, dkv_ref = refs
    else:
        q_ref, k_ref, v_ref, do_ref, out_ref, log_ref, old_ref, dq_ref, dkv_ref = refs
    heads = pull_heads(q_ref, do_ref, out_ref, log_ref)

    def step(at, acc):
        span = pl.ds(at, chunk)
        bias = bias_ref[span] if masked else None
        dk, dv, more = pull_piece(k_ref[0, span], v_ref[0, span], bias, heads)
        if not masked:
            dk += old_ref[0, span]
            dv += old_ref[1, span]
        dkv_ref[0, span] = dk.astype(dkv_ref.dtype)
        dkv_ref[1, span] = dv.astype(dkv_ref.dtype)
        return more if acc is None else [a + b for a, b in zip(acc, more)]

    acc = step(0, None)
    count = k_ref.shape[1] // chunk
    if count <= 4:
        for i in range(1, count):
            acc = step(i * chunk, acc)
    else:
        acc = lax.fori_loop(
            1, count, lambda i, a: step(pl.multiple_of(i * chunk, chunk), a), acc
        )
    dq_ref[...] = lane_pair(acc) * HEAD ** (-0.5)


def pull_far(own, far, bias, grad, out, log, before, chunk):
    masked = bias is not None
    rows = own.shape[1]
    width = own.shape[2]
    keys = far.shape[1]
    specs = [kind_spec(own, 0), kind_spec(far, 0), kind_spec(far, 1)]
    args = [own, far, far]
    if masked:
        specs.append(bias_spec(bias))
        args.append(bias)
    specs += [full_spec(rows), full_spec(rows), stat_spec(rows)]
    args += [grad, out, log]
    if not masked:
        specs.append(slab_spec(2, keys))
        args.append(before)
    kind = F32 if masked else BF
    return pl.pallas_call(
        functools.partial(pull_far_kernel, masked=masked, chunk=chunk),
        grid=(width // LANES,),
        in_specs=specs,
        out_specs=[full_spec(rows), slab_spec(2, keys)],
        out_shape=[
            jax.ShapeDtypeStruct((rows, width), F32),
            jax.ShapeDtypeStruct((2, keys, width), kind),
        ],
        compiler_params=params(),
        cost_estimate=cost(5, rows * keys, width, 8 * keys),
    )(*args)


def pull_near_kernel(
    qp_ref, kp_ref, vp_ref, qc_ref, kc_ref, vc_ref, bias_ref,
    dop_ref, outp_ref, logp_ref, oldp_ref, doc_ref, outc_ref, logc_ref, oldc_ref,
    grad_ref,
):
    heads_p = pull_heads(qp_ref, dop_ref, outp_ref, logp_ref)
    heads_c = pull_heads(qc_ref, doc_ref, outc_ref, logc_ref)
    dk_p, dv_p, dq_p = pull_piece(kp_ref[0], vp_ref[0], None, heads_p)
    dk_pc, dv_pc, dq_pc = pull_piece(kp_ref[0], vp_ref[0], bias_ref[...], heads_c)
    dk_c, dv_c, dq_c = pull_piece(kc_ref[0], vc_ref[0], None, heads_c)
    split = qp_ref.shape[1]
    both = [a + b for a, b in zip(dq_pc, dq_c)]
    grad_ref[0, :split] = (lane_pair(dq_p) * HEAD ** (-0.5) + oldp_ref[...]).astype(BF)
    grad_ref[1, :split] = (dk_p + dk_pc).astype(BF)
    grad_ref[2, :split] = (dv_p + dv_pc).astype(BF)
    grad_ref[0, split:] = (lane_pair(both) * HEAD ** (-0.5) + oldc_ref[...]).astype(BF)
    grad_ref[1, split:] = dk_c.astype(BF)
    grad_ref[2, split:] = dv_c.astype(BF)


def pull_near(own_p, own_c, bias, part_p, part_c):
    width = own_p.shape[2]
    rows_p, rows_c = own_p.shape[1], own_c.shape[1]
    specs = [kind_spec(own_p, c) for c in range(3)] + [kind_spec(own_c, c) for c in range(3)]
    specs.append(bias_spec(bias))
    for rows in (rows_p, rows_c):
        specs += [full_spec(rows), full_spec(rows), stat_spec(rows), full_spec(rows)]
    return pl.pallas_call(
        pull_near_kernel,
        grid=(width // LANES,),
        in_specs=specs,
        out_specs=slab_spec(3, rows_p + rows_c),
        out_shape=jax.ShapeDtypeStruct((3, rows_p + rows_c, width), BF),
        compiler_params=params(),
        cost_estimate=cost(5, rows_p * rows_p + rows_c * (rows_p + rows_c), width, 10 * rows_c),
    )(own_p, own_p, own_p, own_c, own_c, own_c, bias, *part_p, *part_c)


def swap(array, axis, bit):
    count = lax.axis_size(axis)
    return lax.ppermute(array, axis, [(j, j ^ (1 << bit)) for j in range(count)])


def own_bit(axis, bit):
    return lax.axis_index(axis) // (1 << bit) % 2


def bits_of(count):
    return count.bit_length() - 1


def halve(part, axis, bit, dim):
    mine = own_bit(axis, bit)
    sent = lax.dynamic_index_in_dim(part, 1 - mine, dim, keepdims=False)
    kept = lax.dynamic_index_in_dim(part, mine, dim, keepdims=False)
    return kept, swap(sent, axis, bit)


def add_low(pair):
    return (pair[0].astype(F32) + pair[1].astype(F32)).astype(BF)


def double(mine, axis, bit, dim):
    other = swap(mine, axis, bit)
    first = own_bit(axis, bit) == 0
    return jnp.concatenate([jnp.where(first, mine, other), jnp.where(first, other, mine)], axis=dim)


def after(value, *earlier):
    return lax.optimization_barrier((value,) + earlier)[0]


def all_after(values, *earlier):
    return list(lax.optimization_barrier(tuple(values) + earlier)[: len(values)])


def tp_sum(low):
    return low.astype(F32) + swap(low, "tp", 0).astype(F32)


def wide_dot(left, right):
    return jnp.dot(left, right, preferred_element_type=F32)


def back_dot(left, right):
    return jnp.einsum("ne,de->nd", left, right, preferred_element_type=F32)


def rows_dot(left, right):
    return jnp.einsum("nd,nf->df", left, right, preferred_element_type=F32)


def cut(slabs):
    seq_bits = bits_of(lax.axis_size("seq"))
    grp_bits = bits_of(lax.axis_size("grp"))
    return slabs.reshape(
        (slabs.shape[0],) + (2,) * (seq_bits + grp_bits) + (-1, slabs.shape[2])
    )


def gather_group(mine):
    for bit in reversed(range(1, bits_of(lax.axis_size("grp")))):
        mine = double(lax.optimization_barrier(mine), "grp", bit, 1)
    return double(lax.optimization_barrier(mine), "grp", 0, 1)


def norm_parts(tokens):
    mean = jnp.mean(tokens, axis=-1, keepdims=True)
    centred = tokens - mean
    variance = jnp.mean(centred * centred, axis=-1, keepdims=True)
    inv = lax.rsqrt(variance + norm_eps)
    return centred * inv, inv


def norm_back(normed, inv, upstream, gain):
    scaled = upstream * gain
    mean = jnp.mean(scaled, axis=-1, keepdims=True)
    inner = jnp.mean(scaled * normed, axis=-1, keepdims=True)
    return inv * (scaled - mean - normed * inner)


def exact_gelu(upper):
    return jax.nn.gelu(upper, approximate=False)


def body(
    prompt_in,
    cont_in,
    prompt_cot,
    cont_cot,
    prompt_len,
    qkv_weight,
    out_weight,
    ffn_in,
    ffn_out,
    norm_gain,
    norm_shift,
):
    rows_p = prompt_in.shape[1]
    half = rows_p // 2
    width = prompt_in.shape[2]
    local_width = qkv_weight.shape[2]
    seq_n = lax.axis_size("seq")
    seq_i = lax.axis_index("seq")
    tp_n = lax.axis_size("tp")
    tp_i = lax.axis_index("tp")
    grp_n = lax.axis_size("grp")
    gains = norm_gain.astype(F32)
    shifts = norm_shift.astype(F32)

    seq_bits = bits_of(seq_n)
    grp_bits = bits_of(grp_n)
    held = lax.dynamic_slice_in_dim(prompt_in[0], tp_i * half, half, 0)
    direct = []
    for at in range(1, seq_n):
        direct.append(lax.ppermute(held, "seq", [(j, j ^ at) for j in range(seq_n)]))
    pieces = direct + [swap(came, "tp", 0) for came in direct]
    starts = [
        (seq_i ^ at) * rows_p + part * half for part in (tp_i, 1 - tp_i) for at in range(1, seq_n)
    ]
    inside = jnp.arange(half, dtype=jnp.int32)
    limit = prompt_len[0, 0]

    def bias_of(place):
        bias = jnp.where(place < limit, 0.0, hidden_value).astype(F32)
        return jnp.broadcast_to(bias[:, None], (place.shape[0], LANES))

    bias_far = bias_of((jnp.stack(starts)[:, None] + inside[None, :]).reshape(-1))
    bias_own = bias_of(seq_i * rows_p + jnp.arange(rows_p, dtype=jnp.int32))

    def project(rows):
        tokens = rows.astype(F32)
        normed, inv = norm_parts(tokens)
        return tokens, normed, inv, (normed * gains[0] + shifts[0]).astype(BF)

    def qkv(low, first):
        return jnp.einsum(
            "nd,cde->cne", low, qkv_weight[first:], preferred_element_type=F32
        ).astype(BF)

    tokens_c, one_c, inv_c, low_c = project(cont_in[0, 0])
    tokens_p, one_p, inv_p, low_p = project(prompt_in[0])
    own_c = qkv(low_c, 0)
    own_p = qkv(low_p, 0)
    part_p, stat_p, part_c, stat_c = attend_near(own_p, own_c, bias_own)
    _, one_f, _, low_f = project(after(jnp.concatenate(pieces, axis=0), part_c))
    far = qkv(low_f, 1)

    att_c, log_c = attend_far(own_c, far, bias_far, part_c, stat_c)
    mixed_c = wide_dot(att_c, out_weight).astype(BF)
    att_p, log_p = attend_far(own_p, far, None, after(part_p, mixed_c), stat_p)
    mixed_p = wide_dot(att_p, out_weight).astype(BF)

    def feed(tokens, mixed, cot):
        resid = tokens + tp_sum(mixed)
        normed, inv = norm_parts(resid)
        low = (normed * gains[1] + shifts[1]).astype(BF)
        upper = wide_dot(low, ffn_in)
        activated, gelu_pull = jax.vjp(exact_gelu, upper)
        act_grad = back_dot(cot, ffn_out)
        upper_grad = gelu_pull(act_grad)[0].astype(BF)
        terms = back_dot(upper_grad, ffn_in).astype(BF)
        return resid, normed, inv, low, activated.astype(BF), upper_grad, terms

    cot_c = cont_cot[0, 0]
    cot_p = prompt_cot[0]
    resid_c, two_c, inv_two_c, mid_c, act_c, up_c, terms_two_c = feed(tokens_c, mixed_c, cot_c)
    resid_p, two_p, inv_two_p, mid_p, act_p, up_p, terms_two_p = feed(
        after(tokens_p, terms_two_c), mixed_p, cot_p
    )
    second_other = swap(terms_two_c, "tp", 0)
    second_other_p = swap(terms_two_p, "tp", 0)

    def joined(first, second):
        return jnp.concatenate([first, second], axis=0)

    up_p = after(up_p, second_other)
    in_grad = rows_dot(joined(mid_p, mid_c), joined(up_p, up_c)).astype(BF)
    down_grad = rows_dot(joined(cot_p, cot_c), joined(act_p, act_c)).astype(BF)
    ffn_grad = cut(jnp.stack([in_grad, down_grad]))
    ffn_part = add_low(halve(ffn_grad, "grp", 0, seq_bits + 1))
    second_other = after(second_other, ffn_part)

    def rest(cot, normed, inv, second):
        grad = cot.astype(F32) + norm_back(normed, inv, second, gains[1])
        low = grad.astype(BF)
        return grad, low, back_dot(low, out_weight).astype(BF)

    second_c = terms_two_c.astype(F32) + second_other.astype(F32)
    grad_c, dm_c, do_c = rest(cot_c, two_c, inv_two_c, second_c)
    for bit in range(1, grp_bits):
        ffn_pair = halve(ffn_part, "grp", bit, seq_bits + 1)
        if bit + 1 < grp_bits:
            ffn_part = add_low(ffn_pair)
    dq_c, partial = pull_far(own_c, far, bias_far, do_c, att_c, log_c, None, rows_p)
    second_p = terms_two_p.astype(F32) + after(second_other_p, dq_c).astype(F32)
    grad_p, dm_p, do_p = rest(cot_p, two_p, inv_two_p, second_p)
    ffn_pair = all_after(ffn_pair, dq_c)
    ffn_part = add_low(ffn_pair)
    do_p = after(do_p, ffn_part)
    for bit in range(seq_bits - 1):
        ffn_pair = halve(ffn_part, "seq", bit, seq_bits - bit)
        if bit + 2 < seq_bits:
            ffn_part = add_low(ffn_pair)
    out_terms_c = wide_dot(after(act_c, dq_c), ffn_out).astype(BF)
    dq_p, dkv_f = pull_far(
        own_p, far, None, after(do_p, out_terms_c), att_p, log_p, partial, rows_p
    )

    def kv_terms(grads, weights):
        return jnp.einsum("cne,cde->nd", grads, weights, preferred_element_type=F32)

    terms_f = kv_terms(dkv_f, qkv_weight[1:])
    gain_f = jnp.sum(terms_f * one_f, axis=0)
    shift_f = jnp.sum(terms_f, axis=0)
    terms_f = lax.optimization_barrier(terms_f.astype(BF))
    away_rows = (seq_n - 1) * half
    swapped = swap(terms_f[away_rows:], "tp", 0)
    ffn_pair = all_after(ffn_pair, dkv_f)
    dq_p = after(dq_p, terms_f, *ffn_pair)
    ffn_part = add_low(ffn_pair)
    ffn_pair = halve(ffn_part, "seq", seq_bits - 1, 1)
    own_grads = pull_near(
        own_p, own_c, bias_own, (do_p, att_p, log_p, dq_p), (do_c, att_c, log_c, dq_c)
    )
    swapped, *ffn_pair, own_grads = all_after([swapped, *ffn_pair, own_grads])
    ffn_mine = add_low(ffn_pair)
    low_pc = joined(low_p, low_c)
    own_wide = jnp.einsum("nd,cne->cde", low_pc, own_grads, preferred_element_type=F32)
    far_wide = jnp.einsum("nd,cne->cde", low_f, dkv_f, preferred_element_type=F32)
    mixing_grad = rows_dot(joined(dm_p, dm_c), joined(att_p, att_c)).astype(BF)
    last_grad = jnp.concatenate(
        [
            own_wide[:1].astype(BF),
            (own_wide[1:] + far_wide).astype(BF),
            mixing_grad[None],
        ]
    )
    last_core = add_low(halve(cut(last_grad), "grp", 0, seq_bits + 1))
    last_part = last_core
    for bit in range(1, grp_bits):
        last_part = add_low(halve(last_part, "grp", bit, seq_bits + 1))

    terms = kv_terms(own_grads, qkv_weight)
    terms_p, terms_c = terms[:rows_p], terms[rows_p:]
    gain_one = gain_f + jnp.sum(terms_c * one_c, axis=0) + jnp.sum(terms_p * one_p, axis=0)
    shift_one = shift_f + jnp.sum(terms, axis=0)
    both = add_low((terms_f[:away_rows], swapped)).reshape(seq_n - 1, half, width)
    blocks = {at: both[at - 1] for at in range(1, seq_n)}
    for bit in range(seq_bits):
        away = [name for name in sorted(blocks) if name >> bit & 1]
        came = swap(jnp.stack([blocks.pop(name) for name in away]), "seq", bit)
        for i, name in enumerate(away):
            near = name ^ (1 << bit)
            blocks[near] = came[i] if near not in blocks else add_low((blocks[near], came[i]))
    halves_p = lax.optimization_barrier(terms_p.astype(BF)).reshape(2, half, width)
    first_p = halve(halves_p, "tp", 0, 0)
    first_p = first_p[0].astype(F32) + first_p[1].astype(F32) + blocks[0].astype(F32)
    first_c = tp_sum(lax.optimization_barrier(terms_c.astype(BF)))
    first_p = double(after(first_p.astype(BF), last_part), "tp", 0, 0).astype(F32)

    two = (terms_two_c.astype(F32), terms_two_p.astype(F32))
    norm_rows = jnp.stack(
        [
            gain_one,
            jnp.sum(two[0] * two_c, axis=0) + jnp.sum(two[1] * two_p, axis=0),
            shift_one,
            jnp.sum(two[0], axis=0) + jnp.sum(two[1], axis=0),
        ]
    )
    def norm_hops(axis):
        total = norm_rows
        for bit in range(bits_of(lax.axis_size(axis))):
            total = lax.optimization_barrier(total)
            total = total + swap(total, axis, bit)
        return total

    norm_rows = norm_hops("tp")
    norm_rows = norm_hops("seq")
    last_part = after(last_part, norm_rows)
    norm_rows = norm_hops("grp")
    columns = width // (seq_n * tp_n)
    norm_sum = lax.dynamic_slice_in_dim(norm_rows, (seq_i * tp_n + tp_i) * columns, columns, 1)

    ffn_sum = gather_group(ffn_mine).astype(F32)
    for bit in range(seq_bits):
        last_part = add_low(halve(last_part, "seq", bit, seq_bits - bit))
    out_terms_p = lax.optimization_barrier(wide_dot(after(act_p, last_core), ffn_out).astype(BF))
    out_other_p = swap(out_terms_p, "tp", 0)
    last_sum = gather_group(after(last_part, norm_rows, out_other_p)).astype(F32)
    cont_out = (resid_c + tp_sum(out_terms_c)).astype(BF)[None, None]
    out_p = out_terms_p.astype(F32) + out_other_p.astype(F32)
    prompt_out = (resid_p + out_p).astype(BF)[None]
    cont_grad = (grad_c + norm_back(one_c, inv_c, first_c, gains[0])).astype(BF)[None, None]
    prompt_grad = (grad_p + norm_back(one_p, inv_p, first_p, gains[0])).astype(BF)[None]
    return (
        prompt_out,
        cont_out,
        prompt_grad,
        cont_grad,
        last_sum[:3],
        last_sum[3].T,
        ffn_sum[0],
        ffn_sum[1].T,
        norm_sum[:2],
        norm_sum[2:],
    )


def solution(mesh):
    placed = (
        P("grp", "seq", None),
        P("grp", "seq", None, None),
        P("grp", "seq", None),
        P("grp", "seq", None, None),
        P("grp", "seq"),
        P(None, None, "tp"),
        P("tp", None),
        P(None, "tp"),
        P("tp", None),
        P(),
        P(),
    )
    return jax.shard_map(
        body,
        mesh=mesh,
        in_specs=placed,
        out_specs=(
            P("grp", "seq", None),
            P("grp", "seq", None, None),
            P("grp", "seq", None),
            P("grp", "seq", None, None),
            P(None, "seq", "tp"),
            P("tp", "seq"),
            P("seq", "tp"),
            P("tp", "seq"),
            P(None, ("seq", "tp")),
            P(None, ("seq", "tp")),
        ),
        check_vma=False,
    )
```

time: 594 us -> 314 us (0.53); the launches traced: 584 us -> 310 us
  waiting for transfers between devices: 208 us -> 73.9 us
  matrix products: 166 us -> 60.4 us
  Pallas kernels: 0 us -> 70.7 us
  local copies, waits for them, and re-layouts: 77.2 us -> 22 us
  other arithmetic: 70.1 us -> 39.5 us
  starting transfers between devices: 58.5 us -> 40.2 us
    ppermute x43 -> x35, waiting for transfers between devices: 208 us -> 73.9 us  [the longest x32 73.7 us: swap(): return lax.ppermute(array, axis, [(j, j ^ 1 << bit) for j in range(count)])]
    dot_general x54 -> x22, matrix products: 166 us -> 60.4 us  [the longest x6 22 us: wide_dot(): return jnp.dot(left, right, preferred_element_type=F32)]
    pallas_call x0 -> x6, Pallas kernels: none -> 70.7 us  [the longest x2 25.2 us: pull_far(): pl.pallas_call(functools.partial(pull_far_kernel, masked=masked, chunk=ch...]
    convert_element_type x19 -> x20, other arithmetic: 40.3 us -> 15.3 us  [the longest x10 6.85 us: add_low(): return (pair[0].astype(F32) + pair[1].astype(F32)).astype(BF)]
    another operation x14 -> x1, local copies, waits for them, and re-layouts: 20.2 us -> 0.08 us  [body(): jnp.stack(starts)[:, None] + inside[None, :]]
    ppermute x43 -> x35, starting transfers between devices: 58.5 us -> 40.2 us  [the longest x32 34.6 us: swap(): return lax.ppermute(array, axis, [(j, j ^ 1 << bit) for j in range(count)])]
    dynamic_update_slice x14 -> x0, local copies, waits for them, and re-layouts: 8.41 us -> none  [the longest x6 8.28 us: body(): lax.scan(forward_head, nothing, (head_queries, split_heads(keyvals[0]), s...]
    another operation x13 -> x2, other arithmetic: 7.4 us -> 0.89 us  [the longest x1 0.87 us: body(): came = swap(jnp.stack([blocks.pop(name) for name in away]), 'seq', bit)]
  transfers between devices with their start and end apart: 43 -> 35, of which waited for: 19 -> 22; matrix products, arithmetic and copies ran while one was open for 33% -> 28% of each run, Pallas kernels for 0% -> 19%
where the time goes in v3:
time: 314 us; the launch traced here: 310 us
  waiting for transfers between devices  73.9 us (24%)
  Pallas kernels  70.7 us (23%)
  matrix products  60.4 us (19%)
  starting transfers between devices  40.2 us (13%)
  other arithmetic  39.5 us (13%)
  local copies, waits for them, and re-layouts  22 us (7%)
  between operations  3.18 us (1%)
    ppermute x32, waiting for transfers between devices, swap(): return lax.ppermute(array, axis, [(j, j ^ 1 << bit) for j in range(count)])  73.7 us
    ppermute x32, starting transfers between devices, swap(): return lax.ppermute(array, axis, [(j, j ^ 1 << bit) for j in range(count)])  34.6 us
    pallas_call x2, Pallas kernels, pull_far(): pl.pallas_call(functools.partial(pull_far_kernel, masked=masked, chunk=ch...  25.2 us
    dot_general x6, matrix products, wide_dot(): return jnp.dot(left, right, preferred_element_type=F32)  22 us
    pallas_call x2, Pallas kernels, attend_far(): pl.pallas_call(functools.partial(far_kernel, masked=masked), grid=(width...  19.6 us
    pallas_call x1, Pallas kernels, pull_near(): pl.pallas_call(pull_near_kernel, grid=(width // LANES,), in_specs=specs,...  14.8 us
    pallas_call x1, Pallas kernels, attend_near(): pl.pallas_call(near_kernel, grid=(width // LANES,), in_specs=[kind_spec(o...  11.1 us
    dot_general x6, matrix products, back_dot(): return jnp.einsum('ne,de->nd', left, right, preferred_element_type=F32)  10.2 us
  transfers between devices with their start and end apart: 35, of which 22 were waited for; matrix products, arithmetic and copies ran while one was open for 28% of the time, Pallas kernels for 19%

profile of v3, /device:TPU:0, one launch (start us, length us, event | category | flops | bytes accessed | tf_op | source)
XLA Modules:
  0.0 309.9 jit_solution(15507144001970439758)
XLA Ops:
  0.7 1.8 dynamic-slice_bitcast_fusion.8
  2.5 5.1 %collective-permute-start.2 = (bf16[192,768]{1,0:T(8,128)(2,1)}, bf16[192,768]{1,0:T(8,128)(2,1)S(1)}, u32[]{:S(2)}, u32[]{:S(2)}) collective-permute-start(bf16[192,768]{1,0:T(8,128)(2,1)} %dynamic-slice_bitcast_fusion.8), channel_id=1, source_target_pairs={{0,6},{2,4},{4,2},{6,0},{1,7},{3,5},{5,3},{7,1},{8,14},{10,12},{12... | collective-permute-start | bytes 884744 | tf_op jit(solution)/shard_map/ppermute | solution.py:427
  13.5 1.9 fusion.67.qp_ref.kp_ref.vp_ref.refs_0_
  15.3 2.2 fusion.54.qc_ref.kc_ref.vc_ref.refs_0_
  18.5 11.1 %shard_map.186 = (f32[384,384]{1,0:T(8,128)}, f32[3,8,384]{2,1,0:T(8,128)}, f32[512,384]{1,0:T(8,128)}, f32[3,8,512]{2,1,0:T(8,128)}) custom-call(bf16[3,384,384]{2,1,0:T(8,128)(2,1)} %fusion.67.qp_ref.kp_ref.vp_ref.refs_0_, bf16[3,384,384]{2,1,0:T(8,128)(2,1)} %fusion.67.qp_ref.kp_ref.vp_ref.refs_0_, ...), custom_call_target="tpu_custom_call" | custom-call | flops 1212416 | bytes 5120 | tf_op jit(solution)/shard_map/pallas_call | solution.py:122
  29.7 1.8 collective-permute-start.3
  33.1 1.5 collective-permute-start.4
  35.6 4.2 %collective-permute-done.3 = bf16[192,768]{1,0:T(8,128)(2,1)S(1)} collective-permute-done((bf16[192,768]{1,0:T(8,128)(2,1)}, bf16[192,768]{1,0:T(8,128)(2,1)S(1)}, u32[]{:S(2)}, u32[]{:S(2)}) %collective-permute-start.3) | collective-permute-done | bytes 294944 | tf_op jit(solution)/shard_map/ppermute | solution.py:312
  39.8 10.9 %collective-permute-done.4 = bf16[192,768]{1,0:T(8,128)(2,1)S(1)} collective-permute-done((bf16[192,768]{1,0:T(8,128)(2,1)}, bf16[192,768]{1,0:T(8,128)(2,1)S(1)}, u32[]{:S(2)}, u32[]{:S(2)}) %collective-permute-start.4) | collective-permute-done | bytes 294944 | tf_op jit(solution)/shard_map/ppermute | solution.py:312
  52.9 3.2 %fusion.15.refs_1_.refs_2_ = bf16[2,1152,384]{2,1,0:T(8,128)(2,1)} fusion(bf16[3,768,384]{2,1,0:T(8,128)(2,1)S(1)} %copy-done.66, bf16[1152,768]{1,0:T(8,128)(2,1)S(1)} %constant_dynamic-update-slice_fusion, f32[768]{0:T(1024)S(1)} %get-tuple-element.97, f32[768]{0:T(1024)S(1)} %get-tuple-element.138, f32[1152]{0:T(1024)S(1)} %add_rsqrt_fusion, ...), kind=kOutput, calls=%fused_computation.38 | convolution fusion | flops 1365147648 | bytes 4743168 | tf_op jit(solution)/shard_map/nd,cde->cne/dot_general | solution.py:448
  57.1 10.8 %shard_map.187 = (bf16[512,384]{1,0:T(8,128)(2,1)}, f32[3,8,512]{2,1,0:T(8,128)}) custom-call(bf16[3,512,384]{2,1,0:T(8,128)(2,1)} %fusion.54.qc_ref.kc_ref.vc_ref.refs_0_, bf16[2,1152,384]{2,1,0:T(8,128)(2,1)} %fusion.15.refs_1_.refs_2_, bf16[2,1152,384]{2,1,0:T(8,128)(2,1)} %fusion.15.refs_1_.refs_2_, f32[1152,128]{1,0:T(8,128)} %broadcast_in_dim.33.refs_3_, ...), custom_call_target="tpu_custom_call" | custom-call | flops 1179648 | bytes 4608 | tf_op jit(solution)/shard_map/pallas_call | solution.py:170
  67.9 2.4 convolution_convert_fusion.7
  70.4 1.5 collective-permute-start.6
  73.0 8.8 %shard_map.188 = (bf16[384,384]{1,0:T(8,128)(2,1)}, f32[3,8,384]{2,1,0:T(8,128)}) custom-call(bf16[3,384,384]{2,1,0:T(8,128)(2,1)} %fusion.67.qp_ref.kp_ref.vp_ref.refs_0_, bf16[2,1152,384]{2,1,0:T(8,128)(2,1)} %fusion.15.refs_1_.refs_2_, bf16[2,1152,384]{2,1,0:T(8,128)(2,1)} %fusion.15.refs_1_.refs_2_, f32[384,384]{1,0:T(8,128)} %get-tuple-element.50.refs_3_, ...), custom_call_target="tpu_custom_call" | custom-call | flops 884736 | bytes 4608 | tf_op jit(solution)/shard_map/pallas_call | solution.py:170
  81.8 1.4 convolution_convert_fusion.10
  83.9 7.2 %collective-permute-done.6 = bf16[512,768]{1,0:T(8,128)(2,1)} collective-permute-done((bf16[512,768]{1,0:T(8,128)(2,1)}, bf16[512,768]{1,0:T(8,128)(2,1)}, u32[]{:S(2)}, u32[]{:S(2)}) %collective-permute-start.6) | collective-permute-done | bytes 786464 | tf_op jit(solution)/shard_map/ppermute | solution.py:312
  91.1 1.7 fusion.115
  94.4 8.3 %multiply_convert_fusion = (bf16[512,1536]{1,0:T(8,128)(2,1)S(1)}, f32[512,1536]{1,0:T(8,128)S(1)}, f32[512,1536]{1,0:T(8,128)S(1)}) fusion(bf16[512,768]{1,0:T(8,128)(2,1)S(1)} %add_convert_fusion.5, bf16[768,1536]{1,0:T(8,128)(2,1)S(1)} %copy-done), kind=kOutput, calls=%fused_computation.23 | convolution fusion | flops 1259077632 | bytes 11010048 | tf_op jit(solution)/shard_map/dot_general | solution.py:353
  102.7 2.1 add_convert_fusion
  104.8 1.4 convolution_convert_fusion.6
  106.3 1.6 collective-permute-start.9
  108.8 6.5 %multiply_convert_fusion.1 = (bf16[384,1536]{1,0:T(8,128)(2,1)S(1)}, f32[384,1536]{1,0:T(8,128)S(1)}, f32[384,1536]{1,0:T(8,128)S(1)}) fusion(bf16[384,768]{1,0:T(8,128)(2,1)S(1)} %add_convert_fusion.9, bf16[768,1536]{1,0:T(8,128)(2,1)S(1)} %copy-done), kind=kOutput, calls=%fused_computation.60 | convolution fusion | flops 944308224 | bytes 8847360 | tf_op jit(solution)/shard_map/dot_general | solution.py:353
  115.3 2.9 convolution_convert_fusion
  118.3 1.6 add_convert_fusion.2
  120.9 3.1 convolution_convert_fusion.1
  124.0 1.9 fusion.24
  126.3 2.5 convolution_convert_fusion.9
  131.2 2.3 fusion
  133.6 2.0 fusion.53
  136.9 3.0 fusion.111
  142.2 13.7 %shard_map.189 = (f32[512,384]{1,0:T(8,128)}, f32[2,1152,384]{2,1,0:T(8,128)}) custom-call(bf16[3,512,384]{2,1,0:T(8,128)(2,1)} %fusion.54.qc_ref.kc_ref.vc_ref.refs_0_, bf16[2,1152,384]{2,1,0:T(8,128)(2,1)} %fusion.15.refs_1_.refs_2_, bf16[2,1152,384]{2,1,0:T(8,128)(2,1)} %fusion.15.refs_1_.refs_2_, f32[1152,128]{1,0:T(8,128)} %broadcast_in_dim.33.refs_3_, ...), custom_call_target="tpu_custom_call" | custom-call | flops 2949120 | bytes 9216 | tf_op jit(solution)/shard_map/pallas_call | solution.py:258
  156.9 1.6 fusion.110
  159.8 2.3 convolution_convert_fusion.5
  162.0 1.8 collective-permute-done.11
  165.2 1.5 collective-permute-start.13
  166.6 1.8 fusion.68
  169.1 1.5 collective-permute-start.17
  170.6 11.6 %shard_map.190 = (f32[384,384]{1,0:T(8,128)}, bf16[2,1152,384]{2,1,0:T(8,128)(2,1)}) custom-call(bf16[3,384,384]{2,1,0:T(8,128)(2,1)} %fusion.67.qp_ref.kp_ref.vp_ref.refs_0_, bf16[2,1152,384]{2,1,0:T(8,128)(2,1)} %fusion.15.refs_1_.refs_2_, bf16[2,1152,384]{2,1,0:T(8,128)(2,1)} %fusion.15.refs_1_.refs_2_, ...), custom_call_target="tpu_custom_call" | custom-call | flops 2211840 | bytes 9216 | tf_op jit(solution)/shard_map/pallas_call | solution.py:258
  182.1 4.2 %fusion.7 = (f32[768]{0:T(1024)}, f32[768]{0:T(1024)S(1)}, bf16[1152,768]{1,0:T(8,128)(2,1)S(1)}) fusion(bf16[1152,768]{1,0:T(8,128)(2,1)S(1)} %copy-done.13, f32[1152]{0:T(1024)S(1)} %copy-done.58, f32[1152]{0:T(1024)S(1)} %copy-done.53, bf16[2,1152,384]{2,1,0:T(8,128)(2,1)} %get-tuple-element.65, bf16[3,768,384]{2,1,0:T(8,128)(2,1)} %param.16), kind=kOutput, calls=%fused_computation.16 | convolution fusion | flops 1365146112 | bytes 6503424 | tf_op jit(solution)/shard_map/cne,cde->nd/dot_general | solution.py:522
  188.1 2.1 collective-permute-start.14
  190.2 2.5 fusion.80
  192.7 14.8 %shard_map.191 = bf16[3,896,384]{2,1,0:T(8,128)(2,1)} custom-call(bf16[3,384,384]{2,1,0:T(8,128)(2,1)} %fusion.67.qp_ref.kp_ref.vp_ref.refs_0_, bf16[3,384,384]{2,1,0:T(8,128)(2,1)} %fusion.67.qp_ref.kp_ref.vp_ref.refs_0_, bf16[3,384,384]{2,1,0:T(8,128)(2,1)} %fusion.67.qp_ref.kp_ref.vp_ref.refs_0_, ...), custom_call_target="tpu_custom_call" | custom-call | flops 3031040 | bytes 5120 | tf_op jit(solution)/shard_map/pallas_call | solution.py:299
  208.0 3.8 %convolution_bitcast_fusion.1 = f32[3,768,384]{1,2,0:T(8,128)S(1)} fusion(bf16[3,896,384]{2,1,0:T(8,128)(2,1)} %shard_map.191, bf16[512,768]{1,0:T(8,128)(2,1)S(1)} %copy-done.29, bf16[384,768]{1,0:T(8,128)(2,1)S(1)} %copy-done.35), kind=kOutput, calls=%fused_computation.74 | convolution fusion | flops 1588199424 | bytes 6979584 | tf_op jit(solution)/shard_map/nd,cne->cde/dot_general | solution.py:540
  211.8 3.2 %fusion.27 = bf16[2,768,384]{1,2,0:T(8,128)(2,1)} fusion(f32[3,768,384]{1,2,0:T(8,128)S(1)} %convolution_bitcast_fusion.1, bf16[2,1152,384]{2,1,0:T(8,128)(2,1)S(1)} %copy-done.68, bf16[1152,768]{1,0:T(8,128)(2,1)S(1)} %copy-done.13, f32[768]{0:T(1024)S(1)} %copy-done.43, f32[768]{0:T(1024)S(1)} %get-tuple-element.138, f32[1152]{0:T(1024)S(1)} %copy-done.58, ...), kind=kOutput, calls=%fused_computation.54 | convolution fusion | flops 1365442560 | bytes 7093248 | tf_op jit(solution)/shard_map/nd,cne->cde/dot_general | solution.py:541
  215.1 2.0 fusion.118
  218.1 1.5 add_convert_fusion.3
  220.4 1.5 collective-permute-start.33
  224.7 2.0 copy.33
  229.8 1.6 pad_maximum_fusion
  233.4 2.6 collective-permute-done.19
  237.1 2.2 collective-permute-start.20
  239.3 11.9 %collective-permute-done.23 = bf16[512,768]{1,0:T(8,128)(2,1)S(1)} collective-permute-done((bf16[512,768]{1,0:T(8,128)(2,1)S(1)}, bf16[512,768]{1,0:T(8,128)(2,1)S(1)}, u32[]{:S(2)}, u32[]{:S(2)}) %collective-permute-start.23) | collective-permute-done | bytes 786464 | tf_op jit(solution)/shard_map/ppermute | solution.py:312
  253.4 1.6 fusion.82
  256.2 8.3 %collective-permute-done.21 = bf16[4,2,2,48,384]{4,3,2,1,0:T(8,128)(2,1)S(1)} collective-permute-done((bf16[4,2,2,48,384]{4,3,2,1,0:T(8,128)(2,1)S(1)}, bf16[4,2,2,48,384]{4,3,2,1,0:T(8,128)(2,1)S(1)}, u32[]{:S(2)}, u32[]{:S(2)}) %collective-permute-start.21) | collective-permute-done | bytes 589856 | tf_op jit(solution)/shard_map/ppermute | solution.py:312
  266.2 5.4 %collective-permute-done.22 = bf16[192,768]{1,0:T(8,128)(2,1)S(1)} collective-permute-done((bf16[192,768]{1,0:T(8,128)(2,1)S(1)}, bf16[192,768]{1,0:T(8,128)(2,1)S(1)}, u32[]{:S(2)}, u32[]{:S(2)}) %collective-permute-start.22) | collective-permute-done | bytes 294944 | tf_op jit(solution)/shard_map/ppermute | solution.py:312
  274.0 2.2 collective-permute-done.24
  277.9 1.9 collective-permute-start.16
  280.1 1.7 collective-permute-start.26
  281.7 1.6 slice_bitcast_fusion
  285.5 2.4 collective-permute-done.16
  291.6 1.7 collective-permute-start.28
  293.8 6.8 %collective-permute-done.28 = bf16[4,48,384]{2,1,0:T(8,128)(2,1)S(1)} collective-permute-done((bf16[4,48,384]{2,1,0:T(8,128)(2,1)S(1)}, bf16[4,48,384]{2,1,0:T(8,128)(2,1)S(1)}, u32[]{:S(2)}, u32[]{:S(2)}) %collective-permute-start.28) | collective-permute-done | bytes 147488 | tf_op jit(solution)/shard_map/ppermute | solution.py:312
  300.6 1.5 collective-permute-start.31
  303.4 2.4 collective-permute-done.31
  (300 shorter events, 60.9 us)
Async XLA Ops:
  0.6 93.7 %copy-start = (bf16[768,1536]{1,0:T(8,128)(2,1)S(1)}, bf16[768,1536]{1,0:T(8,128)(2,1)}, u32[]{:S(2)}) copy-start(bf16[768,1536]{1,0:T(8,128)(2,1)} %param.18) | copy-start | bytes 7077892
  0.7 10.8 %copy-start.4 = (bf16[1,1,512,768]{3,2,1,0:T(8,128)(2,1)S(1)}, bf16[1,1,512,768]{3,2,1,0:T(8,128)(2,1)}, u32[]{:S(2)}) copy-start(bf16[1,1,512,768]{3,2,1,0:T(8,128)(2,1)} %param.12) | copy-start | bytes 2359300
  0.7 11.5 %copy-start.60 = (bf16[2,768]{1,0:T(2,128)(2,1)S(1)}, bf16[2,768]{1,0:T(2,128)(2,1)}, u32[]{:S(2)}) copy-start(bf16[2,768]{1,0:T(2,128)(2,1)} %param.20) | copy-start | bytes 9220
  0.7 11.6 %copy-start.61 = (bf16[2,768]{1,0:T(2,128)(2,1)S(1)}, bf16[2,768]{1,0:T(2,128)(2,1)}, u32[]{:S(2)}) copy-start(bf16[2,768]{1,0:T(2,128)(2,1)} %param.21) | copy-start | bytes 9220
  2.5 29.9 %collective-permute-start.2 = (bf16[192,768]{1,0:T(8,128)(2,1)}, bf16[192,768]{1,0:T(8,128)(2,1)S(1)}, u32[]{:S(2)}, u32[]{:S(2)}) collective-permute-start(bf16[192,768]{1,0:T(8,128)(2,1)} %dynamic-slice_bitcast_fusion.8), channel_id=1, source_target_pairs={{0,6},{2,4},{4,2},{6,0},{1,7},{3,5},{5,3},{7,1},{8,14},{10,12},{12... | collective-permute-start | bytes 884744 | tf_op jit(solution)/shard_map/ppermute | solution.py:427
  7.6 25.4 %collective-permute-start.1 = (bf16[192,768]{1,0:T(8,128)(2,1)}, bf16[192,768]{1,0:T(8,128)(2,1)}, u32[]{:S(2)}, u32[]{:S(2)}) collective-permute-start(bf16[192,768]{1,0:T(8,128)(2,1)} %dynamic-slice_bitcast_fusion.8), channel_id=1, source_target_pairs={{0,4},{2,6},{4,0},{6,2},{1,5},{3,7},{5,1},{7,3},{8,12},{10,14},{12... | collective-permute-start | bytes 884744 | tf_op jit(solution)/shard_map/ppermute | solution.py:427
  7.6 22.0 %collective-permute-start = (bf16[192,768]{1,0:T(8,128)(2,1)}, bf16[192,768]{1,0:T(8,128)(2,1)}, u32[]{:S(2)}, u32[]{:S(2)}) collective-permute-start(bf16[192,768]{1,0:T(8,128)(2,1)} %dynamic-slice_bitcast_fusion.8), channel_id=1, source_target_pairs={{0,2},{2,0},{4,6},{6,4},{1,3},{3,1},{5,7},{7,5},{8,10},{10,8},{12,... | collective-permute-start | bytes 884744 | tf_op jit(solution)/shard_map/ppermute | solution.py:427
  12.3 39.6 %copy-start.42 = (f32[768]{0:T(1024)}, f32[768]{0:T(1024)S(1)}, u32[]{:S(2)}) copy-start(f32[768]{0:T(1024)S(1)} %get-tuple-element.97) | copy-start | bytes 9220
  12.3 80.9 %copy-start.44 = (f32[768]{0:T(1024)}, f32[768]{0:T(1024)S(1)}, u32[]{:S(2)}) copy-start(f32[768]{0:T(1024)S(1)} %get-tuple-element.96) | copy-start | bytes 9220
  29.7 10.2 %collective-permute-start.3 = (bf16[192,768]{1,0:T(8,128)(2,1)}, bf16[192,768]{1,0:T(8,128)(2,1)S(1)}, u32[]{:S(2)}, u32[]{:S(2)}) collective-permute-start(bf16[192,768]{1,0:T(8,128)(2,1)} %collective-permute-done), channel_id=1, source_target_pairs={{0,1},{1,0},{2,3},{3,2},{4,5},{5,4},{6,7},{7,6},{8,9},{9,8},{10,11... | collective-permute-start | bytes 884744 | tf_op jit(solution)/shard_map/ppermute | solution.py:312
  32.5 18.3 %collective-permute-start.5 = (bf16[192,768]{1,0:T(8,128)(2,1)S(1)}, bf16[192,768]{1,0:T(8,128)(2,1)S(1)}, u32[]{:S(2)}, u32[]{:S(2)}) collective-permute-start(bf16[192,768]{1,0:T(8,128)(2,1)S(1)} %collective-permute-done.2), channel_id=1, source_target_pairs={{0,1},{1,0},{2,3},{3,2},{4,5},{5,4},{6,7},{7,6},{8,9},{9,8},{10,11... | collective-permute-start | bytes 884744 | tf_op jit(solution)/shard_map/ppermute | solution.py:312
  33.1 17.7 %collective-permute-start.4 = (bf16[192,768]{1,0:T(8,128)(2,1)}, bf16[192,768]{1,0:T(8,128)(2,1)S(1)}, u32[]{:S(2)}, u32[]{:S(2)}) collective-permute-start(bf16[192,768]{1,0:T(8,128)(2,1)} %collective-permute-done.1), channel_id=1, source_target_pairs={{0,1},{1,0},{2,3},{3,2},{4,5},{5,4},{6,7},{7,6},{8,9},{9,8},{10,11... | collective-permute-start | bytes 884744 | tf_op jit(solution)/shard_map/ppermute | solution.py:312
  57.1 10.8 %copy-start.17 = (bf16[384,768]{1,0:T(8,128)(2,1)S(1)}, bf16[384,768]{1,0:T(8,128)(2,1)}, u32[]{:S(2)}) copy-start(bf16[384,768]{1,0:T(8,128)(2,1)} %param.17) | copy-start | bytes 1769476
  70.4 20.7 %collective-permute-start.6 = (bf16[512,768]{1,0:T(8,128)(2,1)}, bf16[512,768]{1,0:T(8,128)(2,1)}, u32[]{:S(2)}, u32[]{:S(2)}) collective-permute-start(bf16[512,768]{1,0:T(8,128)(2,1)} %convolution_convert_fusion.7), channel_id=1, source_target_pairs={{0,1},{1,0},{2,3},{3,2},{4,5},{5,4},{6,7},{7,6},{8,9},{9,8},{10,11... | collective-permute-start | bytes 2359304 | tf_op jit(solution)/shard_map/ppermute | solution.py:312
  73.0 8.8 %copy-start.18 = (bf16[384,768]{1,0:T(8,128)(2,1)S(1)}, bf16[384,768]{1,0:T(8,128)(2,1)}, u32[]{:S(2)}) copy-start(bf16[384,768]{1,0:T(8,128)(2,1)} %param.17) | copy-start | bytes 1769476
  83.3 24.6 %collective-permute-start.7 = (bf16[384,768]{1,0:T(8,128)(2,1)S(1)}, bf16[384,768]{1,0:T(8,128)(2,1)S(1)}, u32[]{:S(2)}, u32[]{:S(2)}) collective-permute-start(bf16[384,768]{1,0:T(8,128)(2,1)S(1)} %convolution_convert_fusion.10), channel_id=1, source_target_pairs={{0,1},{1,0},{2,3},{3,2},{4,5},{5,4},{6,7},{7,6},{8,9},{9,8},{10,11... | collective-permute-start | bytes 1769480 | tf_op jit(solution)/shard_map/ppermute | solution.py:312
  93.2 9.5 %copy-start.48 = (f32[512]{0:T(512)}, f32[512]{0:T(512)S(1)}, u32[]{:S(2)}) copy-start(f32[512]{0:T(512)S(1)} %add_rsqrt_fusion.2) | copy-start | bytes 6148
  94.3 8.3 %copy-start.30 = (bf16[1,1,512,768]{3,2,1,0:T(8,128)(2,1)S(1)}, bf16[1,1,512,768]{3,2,1,0:T(8,128)(2,1)}, u32[]{:S(2)}) copy-start(bf16[1,1,512,768]{3,2,1,0:T(8,128)(2,1)} %param.14) | copy-start | bytes 2359300
  94.4 8.3 %copy-start.62 = (bf16[1536,768]{1,0:T(8,128)(2,1)S(1)}, bf16[1536,768]{1,0:T(8,128)(2,1)}, u32[]{:S(2)}) copy-start(bf16[1536,768]{1,0:T(8,128)(2,1)} %param.19) | copy-start | bytes 7077892
  102.7 12.7 %copy-start.71 = (bf16[512,1536]{1,0:T(8,128)(2,1)}, bf16[512,1536]{1,0:T(8,128)(2,1)S(1)}, u32[]{:S(2)}) copy-start(bf16[512,1536]{1,0:T(8,128)(2,1)S(1)} %get-tuple-element.61) | copy-start | bytes 4718596
  106.3 14.6 %collective-permute-start.9 = (bf16[512,768]{1,0:T(8,128)(2,1)S(1)}, bf16[512,768]{1,0:T(8,128)(2,1)}, u32[]{:S(2)}, u32[]{:S(2)}) collective-permute-start(bf16[512,768]{1,0:T(8,128)(2,1)S(1)} %convolution_convert_fusion.6), channel_id=1, source_target_pairs={{0,1},{1,0},{2,3},{3,2},{4,5},{5,4},{6,7},{7,6},{8,9},{9,8},{10,11... | collective-permute-start | bytes 2359304 | tf_op jit(solution)/shard_map/ppermute | solution.py:312
  108.2 7.1 %copy-start.38 = (f32[384]{0:T(512)}, f32[384]{0:T(512)S(1)}, u32[]{:S(2)}) copy-start(f32[384]{0:T(512)S(1)} %broadcast_multiply_fusion.5) | copy-start | bytes 4612
  108.5 6.8 %copy-start.50 = (f32[384]{0:T(512)}, f32[384]{0:T(512)S(1)}, u32[]{:S(2)}) copy-start(f32[384]{0:T(512)S(1)} %add_rsqrt_fusion.1) | copy-start | bytes 4612
  108.8 6.6 %copy-start.36 = (bf16[1,384,768]{2,1,0:T(8,128)(2,1)S(1)}, bf16[1,384,768]{2,1,0:T(8,128)(2,1)}, u32[]{:S(2)}) copy-start(bf16[1,384,768]{2,1,0:T(8,128)(2,1)} %param.13) | copy-start | bytes 1769476
  126.3 4.9 %collective-permute-start.10 = (bf16[2,2,2,2,48,1536]{5,4,3,2,1,0:T(8,128)(2,1)}, bf16[2,2,2,2,48,1536]{5,4,3,2,1,0:T(8,128)(2,1)}, u32[]{:S(2)}, u32[]{:S(2)}) collective-permute-start(bf16[2,2,2,2,48,1536]{5,4,3,2,1,0:T(8,128)(2,1)} %fusion.24), channel_id=1, source_target_pairs={{0,8},{8,0},{16,24},{24,16},{1,9},{9,1},{17,25},{25,17},{2,10},{10... | collective-permute-start | bytes 7077896 | tf_op jit(solution)/shard_map/ppermute | solution.py:312
  128.8 27.0 %collective-permute-start.8 = (bf16[384,768]{1,0:T(8,128)(2,1)S(1)}, bf16[384,768]{1,0:T(8,128)(2,1)S(1)}, u32[]{:S(2)}, u32[]{:S(2)}) collective-permute-start(bf16[384,768]{1,0:T(8,128)(2,1)S(1)} %convolution_convert_fusion.9), channel_id=1, source_target_pairs={{0,1},{1,0},{2,3},{3,2},{4,5},{5,4},{6,7},{7,6},{8,9},{9,8},{10,11... | collective-permute-start | bytes 1769480 | tf_op jit(solution)/shard_map/ppermute | solution.py:312
  135.8 28.1 %collective-permute-start.11 = (bf16[2,2,2,48,1536]{4,3,2,1,0:T(8,128)(2,1)S(1)}, bf16[2,2,2,48,1536]{4,3,2,1,0:T(8,128)(2,1)S(1)}, u32[]{:S(2)}, u32[]{:S(2)}) collective-permute-start(bf16[2,2,2,48,1536]{4,3,2,1,0:T(8,128)(2,1)S(1)} %get-tuple-element.113), channel_id=1, source_target_pairs={{0,16},{8,24},{16,0},{24,8},{1,17},{9,25},{17,1},{25,9},{2,18},{10... | collective-permute-start | bytes 3538952 | tf_op jit(solution)/shard_map/ppermute | solution.py:312
  142.2 13.7 %copy-start.39 = (f32[384]{0:T(512)S(1)}, f32[384]{0:T(512)}, u32[]{:S(2)}) copy-start(f32[384]{0:T(512)} %copy-done.38) | copy-start | bytes 4612
  142.2 13.7 %copy-start.51 = (f32[384]{0:T(512)S(1)}, f32[384]{0:T(512)}, u32[]{:S(2)}) copy-start(f32[384]{0:T(512)} %copy-done.50) | copy-start | bytes 4612
  165.2 22.7 %collective-permute-start.13 = (bf16[2,2,48,1536]{3,2,0,1:T(8,128)(2,1)}, bf16[2,2,48,1536]{3,2,0,1:T(8,128)(2,1)S(1)}, u32[]{:S(2)}, u32[]{:S(2)}) collective-permute-start(bf16[2,2,48,1536]{3,2,0,1:T(8,128)(2,1)} %bitcast.214), channel_id=1, source_target_pairs={{0,2},{2,0},{4,6},{6,4},{1,3},{3,1},{5,7},{7,5},{8,10},{10,8},{12,... | collective-permute-start | bytes 1769480 | tf_op jit(solution)/shard_map/ppermute | solution.py:312
  169.1 21.1 %collective-permute-start.17 = (bf16[512,768]{1,0:T(8,128)(2,1)}, bf16[512,768]{1,0:T(8,128)(2,1)}, u32[]{:S(2)}, u32[]{:S(2)}) collective-permute-start(bf16[512,768]{1,0:T(8,128)(2,1)} %convolution_convert_fusion.5), channel_id=1, source_target_pairs={{0,1},{1,0},{2,3},{3,2},{4,5},{5,4},{6,7},{7,6},{8,9},{9,8},{10,11... | collective-permute-start | bytes 2359304 | tf_op jit(solution)/shard_map/ppermute | solution.py:312
  170.6 11.6 %copy-start.13 = (bf16[1152,768]{1,0:T(8,128)(2,1)S(1)}, bf16[1152,768]{1,0:T(8,128)(2,1)}, u32[]{:S(2)}) copy-start(bf16[1152,768]{1,0:T(8,128)(2,1)} %copy-done.12) | copy-start | bytes 5308420
  170.6 11.6 %copy-start.53 = (f32[1152]{0:T(1024)S(1)}, f32[1152]{0:T(1024)}, u32[]{:S(2)}) copy-start(f32[1152]{0:T(1024)} %copy-done.52) | copy-start | bytes 13828
  170.6 11.6 %copy-start.58 = (f32[1152]{0:T(1024)S(1)}, f32[1152]{0:T(1024)}, u32[]{:S(2)}) copy-start(f32[1152]{0:T(1024)} %copy-done.57) | copy-start | bytes 13828
  187.3 20.6 %collective-permute-start.12 = (bf16[576,768]{1,0:T(8,128)(2,1)}, bf16[576,768]{1,0:T(8,128)(2,1)}, u32[]{:S(2)}, u32[]{:S(2)}) collective-permute-start(bf16[576,768]{1,0:T(8,128)(2,1)} %slice.113), channel_id=1, source_target_pairs={{0,1},{1,0},{2,3},{3,2},{4,5},{5,4},{6,7},{7,6},{8,9},{9,8},{10,11... | collective-permute-start | bytes 2654216 | tf_op jit(solution)/shard_map/ppermute | solution.py:312
  188.1 19.5 %collective-permute-start.14 = (bf16[2,48,1536]{2,1,0:T(8,128)(2,1)S(1)}, bf16[2,48,1536]{2,1,0:T(8,128)(2,1)S(1)}, u32[]{:S(2)}, u32[]{:S(2)}) collective-permute-start(bf16[2,48,1536]{2,1,0:T(8,128)(2,1)S(1)} %get-tuple-element.127), channel_id=1, source_target_pairs={{0,4},{2,6},{4,0},{6,2},{1,5},{3,7},{5,1},{7,3},{8,12},{10,14},{12... | collective-permute-start | bytes 884744 | tf_op jit(solution)/shard_map/ppermute | solution.py:312
  192.7 15.2 %copy-start.29 = (bf16[512,768]{1,0:T(8,128)(2,1)S(1)}, bf16[512,768]{1,0:T(8,128)(2,1)}, u32[]{:S(2)}) copy-start(bf16[512,768]{1,0:T(8,128)(2,1)} %copy-done.28) | copy-start | bytes 2359300
  192.7 15.2 %copy-start.35 = (bf16[384,768]{1,0:T(8,128)(2,1)S(1)}, bf16[384,768]{1,0:T(8,128)(2,1)}, u32[]{:S(2)}) copy-start(bf16[384,768]{1,0:T(8,128)(2,1)} %copy-done.34) | copy-start | bytes 1769476
  220.4 11.2 %collective-permute-start.33 = (bf16[2,48,1536]{2,1,0:T(8,128)(2,1)}, bf16[2,48,1536]{2,1,0:T(8,128)(2,1)}, u32[]{:S(2)}, u32[]{:S(2)}) collective-permute-start(bf16[2,48,1536]{2,1,0:T(8,128)(2,1)} %add_convert_fusion.11), channel_id=1, source_target_pairs={{0,16},{8,24},{16,0},{24,8},{1,17},{9,25},{17,1},{25,9},{2,18},{10... | collective-permute-start | bytes 884744 | tf_op jit(solution)/shard_map/ppermute | solution.py:312
  222.8 13.1 %collective-permute-start.19 = (bf16[2,192,768]{2,1,0:T(8,128)(2,1)}, bf16[2,192,768]{2,1,0:T(8,128)(2,1)}, u32[]{:S(2)}, u32[]{:S(2)}) collective-permute-start(bf16[2,192,768]{2,1,0:T(8,128)(2,1)} %pad_maximum_fusion.1), channel_id=1, source_target_pairs={{0,2},{2,0},{4,6},{6,4},{1,3},{3,1},{5,7},{7,5},{8,10},{10,8},{12,... | collective-permute-start | bytes 1769480 | tf_op jit(solution)/shard_map/ppermute | solution.py:312
  227.7 27.3 %collective-permute-start.18 = (bf16[192,768]{1,0:T(8,128)(2,1)S(1)}, bf16[192,768]{1,0:T(8,128)(2,1)S(1)}, u32[]{:S(2)}, u32[]{:S(2)}) collective-permute-start(bf16[192,768]{1,0:T(8,128)(2,1)S(1)} %dynamic-slice_bitcast_fusion.5), channel_id=1, source_target_pairs={{0,1},{1,0},{2,3},{3,2},{4,5},{5,4},{6,7},{7,6},{8,9},{9,8},{10,11... | collective-permute-start | bytes 884744 | tf_op jit(solution)/shard_map/ppermute | solution.py:312
  229.0 22.1 %collective-permute-start.23 = (bf16[512,768]{1,0:T(8,128)(2,1)S(1)}, bf16[512,768]{1,0:T(8,128)(2,1)S(1)}, u32[]{:S(2)}, u32[]{:S(2)}) collective-permute-start(bf16[512,768]{1,0:T(8,128)(2,1)S(1)} %slice.153), channel_id=1, source_target_pairs={{0,1},{1,0},{2,3},{3,2},{4,5},{5,4},{6,7},{7,6},{8,9},{9,8},{10,11... | collective-permute-start | bytes 2359304 | tf_op jit(solution)/shard_map/ppermute | solution.py:312
  231.4 19.7 %copy-start.16 = (f32[896,768]{1,0:T(8,128)S(1)}, f32[896,768]{1,0:T(8,128)}, u32[]{:S(2)}) copy-start(f32[896,768]{1,0:T(8,128)} %copy-done.15) | copy-start | bytes 8257540
  231.5 19.6 %copy-start.5 = (bf16[1,1,512,768]{3,2,1,0:T(8,128)(2,1)S(1)}, bf16[1,1,512,768]{3,2,1,0:T(8,128)(2,1)}, u32[]{:S(2)}) copy-start(bf16[1,1,512,768]{3,2,1,0:T(8,128)(2,1)} %param.12) | copy-start | bytes 2359300
  231.6 19.6 %copy-start.47 = (f32[512]{0:T(512)S(1)}, f32[512]{0:T(512)}, u32[]{:S(2)}) copy-start(f32[512]{0:T(512)} %copy-done.46) | copy-start | bytes 6148
  231.6 20.5 %collective-permute-start.15 = (bf16[4,2,2,2,48,384]{5,4,3,2,1,0:T(8,128)(2,1)S(1)}, bf16[4,2,2,2,48,384]{5,4,3,2,1,0:T(8,128)(2,1)S(1)}, u32[]{:S(2)}, u32[]{:S(2)}) collective-permute-start(bf16[4,2,2,2,48,384]{5,4,3,2,1,0:T(8,128)(2,1)S(1)} %dynamic-slice_bitcast_fusion), channel_id=1, source_target_pairs={{0,8},{8,0},{16,24},{24,16},{1,9},{9,1},{17,25},{25,17},{2,10},{10... | collective-permute-start | bytes 3538952 | tf_op jit(solution)/shard_map/ppermute | solution.py:312
  233.0 33.1 %collective-permute-start.34 = (bf16[2,96,1536]{2,1,0:T(8,128)(2,1)S(1)}, bf16[2,96,1536]{2,1,0:T(8,128)(2,1)S(1)}, u32[]{:S(2)}, u32[]{:S(2)}) collective-permute-start(bf16[2,96,1536]{2,1,0:T(8,128)(2,1)S(1)} %pad_maximum_fusion.3), channel_id=1, source_target_pairs={{0,8},{8,0},{16,24},{24,16},{1,9},{9,1},{17,25},{25,17},{2,10},{10... | collective-permute-start | bytes 1769480 | tf_op jit(solution)/shard_map/ppermute | solution.py:312
  237.1 17.9 %collective-permute-start.20 = (bf16[1,192,768]{2,1,0:T(8,128)(2,1)S(1)}, bf16[1,192,768]{2,1,0:T(8,128)(2,1)S(1)}, u32[]{:S(2)}, u32[]{:S(2)}) collective-permute-start(bf16[1,192,768]{2,1,0:T(8,128)(2,1)S(1)} %fusion.90), channel_id=1, source_target_pairs={{0,4},{2,6},{4,0},{6,2},{1,5},{3,7},{5,1},{7,3},{8,12},{10,14},{12... | collective-permute-start | bytes 884744 | tf_op jit(solution)/shard_map/ppermute | solution.py:312
  252.4 12.0 %collective-permute-start.21 = (bf16[4,2,2,48,384]{4,3,2,1,0:T(8,128)(2,1)S(1)}, bf16[4,2,2,48,384]{4,3,2,1,0:T(8,128)(2,1)S(1)}, u32[]{:S(2)}, u32[]{:S(2)}) collective-permute-start(bf16[4,2,2,48,384]{4,3,2,1,0:T(8,128)(2,1)S(1)} %dynamic-slice_bitcast_fusion.3), channel_id=1, source_target_pairs={{0,16},{8,24},{16,0},{24,8},{1,17},{9,25},{17,1},{25,9},{2,18},{10... | collective-permute-start | bytes 1769480 | tf_op jit(solution)/shard_map/ppermute | solution.py:312
  264.6 7.0 %copy-start.7 = (bf16[1,384,768]{2,1,0:T(8,128)(2,1)S(1)}, bf16[1,384,768]{2,1,0:T(8,128)(2,1)}, u32[]{:S(2)}) copy-start(bf16[1,384,768]{2,1,0:T(8,128)(2,1)} %param.11) | copy-start | bytes 1769476
  264.6 7.0 %copy-start.41 = (f32[384]{0:T(512)S(1)}, f32[384]{0:T(512)}, u32[]{:S(2)}) copy-start(f32[384]{0:T(512)} %copy-done.40) | copy-start | bytes 4612
  264.7 7.0 %copy-start.55 = (f32[384]{0:T(512)S(1)}, f32[384]{0:T(512)}, u32[]{:S(2)}) copy-start(f32[384]{0:T(512)} %copy-done.54) | copy-start | bytes 4612
  264.7 6.9 %collective-permute-start.22 = (bf16[192,768]{1,0:T(8,128)(2,1)S(1)}, bf16[192,768]{1,0:T(8,128)(2,1)S(1)}, u32[]{:S(2)}, u32[]{:S(2)}) collective-permute-start(bf16[192,768]{1,0:T(8,128)(2,1)S(1)} %fusion.89), channel_id=1, source_target_pairs={{0,1},{1,0},{2,3},{3,2},{4,5},{5,4},{6,7},{7,6},{8,9},{9,8},{10,11... | collective-permute-start | bytes 884744 | tf_op jit(solution)/shard_map/ppermute | solution.py:312
  272.3 3.9 %collective-permute-start.24 = (f32[4,768]{1,0:T(4,128)S(1)}, f32[4,768]{1,0:T(4,128)S(1)}, u32[]{:S(2)}, u32[]{:S(2)}) collective-permute-start(f32[4,768]{1,0:T(4,128)S(1)} %pad_maximum_fusion.5), channel_id=1, source_target_pairs={{0,1},{1,0},{2,3},{3,2},{4,5},{5,4},{6,7},{7,6},{8,9},{9,8},{10,11... | collective-permute-start | bytes 36872 | tf_op jit(solution)/shard_map/ppermute | solution.py:312
  276.2 3.8 %collective-permute-start.25 = (f32[4,768]{1,0:T(4,128)S(1)}, f32[4,768]{1,0:T(4,128)S(1)}, u32[]{:S(2)}, u32[]{:S(2)}) collective-permute-start(f32[4,768]{1,0:T(4,128)S(1)} %add.472), channel_id=1, source_target_pairs={{0,2},{2,0},{4,6},{6,4},{1,3},{3,1},{5,7},{7,5},{8,10},{10,8},{12,... | collective-permute-start | bytes 36872 | tf_op jit(solution)/shard_map/ppermute | solution.py:312
  277.9 9.9 %collective-permute-start.16 = (bf16[384,768]{1,0:T(8,128)(2,1)S(1)}, bf16[384,768]{1,0:T(8,128)(2,1)S(1)}, u32[]{:S(2)}, u32[]{:S(2)}) collective-permute-start(bf16[384,768]{1,0:T(8,128)(2,1)S(1)} %convolution_convert_fusion.8), channel_id=1, source_target_pairs={{0,1},{1,0},{2,3},{3,2},{4,5},{5,4},{6,7},{7,6},{8,9},{9,8},{10,11... | collective-permute-start | bytes 1769480 | tf_op jit(solution)/shard_map/ppermute | solution.py:312
  280.1 4.6 %collective-permute-start.26 = (f32[4,768]{1,0:T(4,128)S(1)}, f32[4,768]{1,0:T(4,128)S(1)}, u32[]{:S(2)}, u32[]{:S(2)}) collective-permute-start(f32[4,768]{1,0:T(4,128)S(1)} %add.473), channel_id=1, source_target_pairs={{0,4},{2,6},{4,0},{6,2},{1,5},{3,7},{5,1},{7,3},{8,12},{10,14},{12... | collective-permute-start | bytes 36872 | tf_op jit(solution)/shard_map/ppermute | solution.py:312
  284.7 17.4 %copy-start.20 = (f32[384,768]{1,0:T(8,128)S(1)}, f32[384,768]{1,0:T(8,128)}, u32[]{:S(2)}) copy-start(f32[384,768]{1,0:T(8,128)} %get-tuple-element.99) | copy-start | bytes 3538948
  284.7 6.8 %collective-permute-start.27 = (bf16[4,2,48,384]{3,2,1,0:T(8,128)(2,1)S(1)}, bf16[4,2,48,384]{3,2,1,0:T(8,128)(2,1)S(1)}, u32[]{:S(2)}, u32[]{:S(2)}) collective-permute-start(bf16[4,2,48,384]{3,2,1,0:T(8,128)(2,1)S(1)} %dynamic-slice_bitcast_fusion.4), channel_id=1, source_target_pairs={{0,2},{2,0},{4,6},{6,4},{1,3},{3,1},{5,7},{7,5},{8,10},{10,8},{12,... | collective-permute-start | bytes 884744 | tf_op jit(solution)/shard_map/ppermute | solution.py:312
  288.9 1.2 collective-permute-start.29
  290.1 3.7 %collective-permute-start.30 = (f32[4,768]{1,0:T(4,128)S(1)}, f32[4,768]{1,0:T(4,128)S(1)}, u32[]{:S(2)}, u32[]{:S(2)}) collective-permute-start(f32[4,768]{1,0:T(4,128)S(1)} %add.477), channel_id=1, source_target_pairs={{0,16},{8,24},{16,0},{24,8},{1,17},{9,25},{17,1},{25,9},{2,18},{10... | collective-permute-start | bytes 36872 | tf_op jit(solution)/shard_map/ppermute | solution.py:312
  291.6 8.9 %collective-permute-start.28 = (bf16[4,48,384]{2,1,0:T(8,128)(2,1)S(1)}, bf16[4,48,384]{2,1,0:T(8,128)(2,1)S(1)}, u32[]{:S(2)}, u32[]{:S(2)}) collective-permute-start(bf16[4,48,384]{2,1,0:T(8,128)(2,1)S(1)} %dynamic-slice_bitcast_fusion.9), channel_id=1, source_target_pairs={{0,4},{2,6},{4,0},{6,2},{1,5},{3,7},{5,1},{7,3},{8,12},{10,14},{12... | collective-permute-start | bytes 442376 | tf_op jit(solution)/shard_map/ppermute | solution.py:312
  300.6 5.2 %collective-permute-start.31 = (bf16[4,48,384]{2,1,0:T(8,128)(2,1)S(1)}, bf16[4,48,384]{2,1,0:T(8,128)(2,1)S(1)}, u32[]{:S(2)}, u32[]{:S(2)}) collective-permute-start(bf16[4,48,384]{2,1,0:T(8,128)(2,1)S(1)} %fusion.95), channel_id=1, source_target_pairs={{0,16},{8,24},{16,0},{24,8},{1,17},{9,25},{17,1},{25,9},{2,18},{10... | collective-permute-start | bytes 442376 | tf_op jit(solution)/shard_map/ppermute | solution.py:312
  305.9 1.6 collective-permute-start.32
  (45 other events, 146.7 us)

commit v4 on v3

--- a/solution.py
+++ b/solution.py
@@ -375,6 +375,31 @@
     return double(lax.optimization_barrier(mine), "grp", 0, 1)
 
 
+def gather_last(mine, slab_rows, slabs, hold):
+    grp_n = lax.axis_size("grp")
+    mine = lax.optimization_barrier(mine)
+
+    def slabs_of(rows):
+        return rows[:slab_rows].reshape(slabs, -1, rows.shape[1])
+
+    if grp_n != 2 * CORES:
+        total = mine[slab_rows:].astype(F32)
+        for bit in range(bits_of(grp_n)):
+            total = total + swap(total, "grp", bit)
+        return gather_group(slabs_of(mine)).astype(F32), total
+    came = [mine] + [
+        lax.ppermute(mine, "grp", [(j, j ^ at) for j in range(grp_n)]) for at in range(1, grp_n)
+    ]
+    came = all_after(came, *hold)
+    total = sum(rows[slab_rows:].astype(F32) for rows in came)
+    came = [slabs_of(rows) for rows in came]
+    swapped_core = lax.axis_index("grp") % CORES == 1
+    swapped_chip = lax.axis_index("grp") // CORES == 1
+    came = [jnp.where(swapped_core, came[at ^ 1], came[at]) for at in range(grp_n)]
+    came = [jnp.where(swapped_chip, came[at ^ 2], came[at]) for at in range(grp_n)]
+    return jnp.concatenate([came[0], came[2], came[1], came[3]], axis=1).astype(F32), total
+
+
 def norm_parts(tokens):
     mean = jnp.mean(tokens, axis=-1, keepdims=True)
     centred = tokens - mean
@@ -408,6 +433,7 @@
     norm_shift,
 ):
     rows_p = prompt_in.shape[1]
+    rows_c = cont_in.shape[2]
     half = rows_p // 2
     width = prompt_in.shape[2]
     local_width = qkv_weight.shape[2]
@@ -504,16 +530,17 @@
         if bit + 1 < grp_bits:
             ffn_part = add_low(ffn_pair)
     dq_c, partial = pull_far(own_c, far, bias_far, do_c, att_c, log_c, None, rows_p)
-    second_p = terms_two_p.astype(F32) + after(second_other_p, dq_c).astype(F32)
-    grad_p, dm_p, do_p = rest(cot_p, two_p, inv_two_p, second_p)
     ffn_pair = all_after(ffn_pair, dq_c)
     ffn_part = add_low(ffn_pair)
-    do_p = after(do_p, ffn_part)
+    second_other_p = after(second_other_p, ffn_part)
+    second_p = terms_two_p.astype(F32) + second_other_p.astype(F32)
+    grad_p, dm_p, do_p = rest(cot_p, two_p, inv_two_p, second_p)
     for bit in range(seq_bits - 1):
         ffn_pair = halve(ffn_part, "seq", bit, seq_bits - bit)
         if bit + 2 < seq_bits:
             ffn_part = add_low(ffn_pair)
     out_terms_c = wide_dot(after(act_c, dq_c), ffn_out).astype(BF)
+    out_other_c = swap(out_terms_c, "tp", 0)
     dq_p, dkv_f = pull_far(
         own_p, far, None, after(do_p, out_terms_c), att_p, log_p, partial, rows_p
     )
@@ -528,48 +555,59 @@
     away_rows = (seq_n - 1) * half
     swapped = swap(terms_f[away_rows:], "tp", 0)
     ffn_pair = all_after(ffn_pair, dkv_f)
-    dq_p = after(dq_p, terms_f, *ffn_pair)
+    out_other_c = after(out_other_c, dkv_f)
+    dq_p = after(dq_p, terms_f, out_other_c, *ffn_pair)
     ffn_part = add_low(ffn_pair)
     ffn_pair = halve(ffn_part, "seq", seq_bits - 1, 1)
     own_grads = pull_near(
         own_p, own_c, bias_own, (do_p, att_p, log_p, dq_p), (do_c, att_c, log_c, dq_c)
     )
     swapped, *ffn_pair, own_grads = all_after([swapped, *ffn_pair, own_grads])
-    ffn_mine = add_low(ffn_pair)
+    ffn_mine = lax.optimization_barrier(add_low(ffn_pair))
+    for bit in reversed(range(1, grp_bits)):
+        ffn_mine = lax.optimization_barrier(double(ffn_mine, "grp", bit, 1))
     low_pc = joined(low_p, low_c)
-    own_wide = jnp.einsum("nd,cne->cde", low_pc, own_grads, preferred_element_type=F32)
-    far_wide = jnp.einsum("nd,cne->cde", low_f, dkv_f, preferred_element_type=F32)
-    mixing_grad = rows_dot(joined(dm_p, dm_c), joined(att_p, att_c)).astype(BF)
-    last_grad = jnp.concatenate(
-        [
-            own_wide[:1].astype(BF),
-            (own_wide[1:] + far_wide).astype(BF),
-            mixing_grad[None],
-        ]
-    )
-    last_core = add_low(halve(cut(last_grad), "grp", 0, seq_bits + 1))
+    last_grads = [rows_dot(low_pc, own_grads[0])]
+    for c in range(2):
+        last_grads.append(rows_dot(low_pc, own_grads[1 + c]) + rows_dot(low_f, dkv_f[c]))
+    mixing_grad = rows_dot(joined(dm_p, dm_c), joined(att_p, att_c))
+    last_cut = [cut(grad.astype(BF)[None]) for grad in last_grads + [mixing_grad]]
+    core_i = own_bit("grp", 0)
+
+    def core_half(which):
+        return jnp.concatenate(
+            [lax.dynamic_index_in_dim(g, which, seq_bits + 1, keepdims=False) for g in last_cut]
+        )
+
+    sent = lax.optimization_barrier(core_half(1 - core_i))
+    last_core = add_low((core_half(core_i), swap(sent, "grp", 0)))
+    ffn_mine = after(ffn_mine, sent)
+    ffn_other = swap(ffn_mine, "grp", 0)
+    out_other_c = after(out_other_c, last_core)
+    out_c = out_terms_c.astype(F32) + out_other_c.astype(F32)
+    cont_out = (resid_c + out_c).astype(BF)[None, None]
     last_part = last_core
     for bit in range(1, grp_bits):
-        last_part = add_low(halve(last_part, "grp", bit, seq_bits + 1))
-
-    terms = kv_terms(own_grads, qkv_weight)
+        last_pair = halve(last_part, "grp", bit, seq_bits + 1)
+        if bit + 1 < grp_bits:
+            last_part = add_low(last_pair)
+
+    terms = kv_terms(after(own_grads, sent), qkv_weight)
     terms_p, terms_c = terms[:rows_p], terms[rows_p:]
-    gain_one = gain_f + jnp.sum(terms_c * one_c, axis=0) + jnp.sum(terms_p * one_p, axis=0)
+    gain_one = gain_f + jnp.sum(terms * joined(one_p, one_c), axis=0)
     shift_one = shift_f + jnp.sum(terms, axis=0)
     both = add_low((terms_f[:away_rows], swapped)).reshape(seq_n - 1, half, width)
     blocks = {at: both[at - 1] for at in range(1, seq_n)}
     for bit in range(seq_bits):
         away = [name for name in sorted(blocks) if name >> bit & 1]
         came = swap(jnp.stack([blocks.pop(name) for name in away]), "seq", bit)
+        if bit == 0:
+            came = after(came, last_core)
         for i, name in enumerate(away):
             near = name ^ (1 << bit)
             blocks[near] = came[i] if near not in blocks else add_low((blocks[near], came[i]))
     halves_p = lax.optimization_barrier(terms_p.astype(BF)).reshape(2, half, width)
-    first_p = halve(halves_p, "tp", 0, 0)
-    first_p = first_p[0].astype(F32) + first_p[1].astype(F32) + blocks[0].astype(F32)
-    first_c = tp_sum(lax.optimization_barrier(terms_c.astype(BF)))
-    first_p = double(after(first_p.astype(BF), last_part), "tp", 0, 0).astype(F32)
-
+    mine_p, other_p = halve(halves_p, "tp", 0, 0)
     two = (terms_two_c.astype(F32), terms_two_p.astype(F32))
     norm_rows = jnp.stack(
         [
@@ -579,31 +617,59 @@
             jnp.sum(two[0], axis=0) + jnp.sum(two[1], axis=0),
         ]
     )
-    def norm_hops(axis):
-        total = norm_rows
-        for bit in range(bits_of(lax.axis_size(axis))):
-            total = lax.optimization_barrier(total)
-            total = total + swap(total, axis, bit)
-        return total
-
-    norm_rows = norm_hops("tp")
-    norm_rows = norm_hops("seq")
-    last_part = after(last_part, norm_rows)
-    norm_rows = norm_hops("grp")
-    columns = width // (seq_n * tp_n)
-    norm_sum = lax.dynamic_slice_in_dim(norm_rows, (seq_i * tp_n + tp_i) * columns, columns, 1)
-
-    ffn_sum = gather_group(ffn_mine).astype(F32)
-    for bit in range(seq_bits):
-        last_part = add_low(halve(last_part, "seq", bit, seq_bits - bit))
-    out_terms_p = lax.optimization_barrier(wide_dot(after(act_p, last_core), ffn_out).astype(BF))
+    low_norm = jnp.pad(norm_rows.astype(BF), ((0, 12), (0, 0)))
+    low_terms_c = lax.optimization_barrier(joined(terms_c.astype(BF), low_norm))
+    other_c = swap(low_terms_c, "tp", 0)
+
+    last_pair = all_after(last_pair, cont_out)
+    last_part = add_low(last_pair)
+    late = [other_p, other_c, blocks[0], ffn_mine, ffn_other]
+    other_p, other_c, home, ffn_mine, ffn_other = all_after(late, last_part)
+    first = core_i == 0
+    ffn_sum = jnp.concatenate(
+        [jnp.where(first, ffn_mine, ffn_other), jnp.where(first, ffn_other, ffn_mine)], axis=1
+    ).astype(F32)
+    ffn_sums = lax.optimization_barrier((ffn_sum[0], ffn_sum[1].T))
+    norm_rows = norm_rows + other_c[rows_c : rows_c + 4].astype(F32)
+    norm_cut = norm_rows.reshape(4, seq_n, tp_n, -1)
+    norm_cut = lax.dynamic_index_in_dim(norm_cut, tp_i, 2, keepdims=False)
+    columns = norm_cut.shape[2]
+    norm_cut = norm_cut.transpose(1, 0, 2).reshape(seq_n, -1)
+    norm_pad = jnp.pad(norm_cut, ((0, 0), (0, 16 * local_width - norm_cut.shape[1])))
+    norm_pad = norm_pad.astype(BF).reshape(seq_n, 16, local_width)
+    slab_rows = last_part.shape[0] * last_part.shape[-2]
+    last_part = last_part.reshape(last_part.shape[0], seq_n, -1, local_width)
+
+    def block(at):
+        slabs = lax.dynamic_index_in_dim(last_part, at, 1, keepdims=False)
+        norms = lax.dynamic_index_in_dim(norm_pad, at, 0, keepdims=False)
+        return jnp.concatenate([slabs.reshape(slab_rows, local_width), norms])
+
+    last_pieces = [block(seq_i)] + [
+        lax.ppermute(block(seq_i ^ at), "seq", [(j, j ^ at) for j in range(seq_n)])
+        for at in range(1, seq_n)
+    ]
+
+    first_p = mine_p.astype(F32) + other_p.astype(F32) + home.astype(F32)
+    first_p = lax.optimization_barrier(first_p.astype(BF))
+    gathered_p = swap(first_p, "tp", 0)
+    first_c = low_terms_c[:rows_c].astype(F32) + other_c[:rows_c].astype(F32)
+    out_terms_p = lax.optimization_barrier(wide_dot(after(act_p, first_p), ffn_out).astype(BF))
     out_other_p = swap(out_terms_p, "tp", 0)
-    last_sum = gather_group(after(last_part, norm_rows, out_other_p)).astype(F32)
-    cont_out = (resid_c + tp_sum(out_terms_c)).astype(BF)[None, None]
+
+    last_pieces = all_after(last_pieces, *ffn_sums)
+    last_mine = sum(piece.astype(F32) for piece in last_pieces).astype(BF)
+    gathered_p, out_other_p = all_after([gathered_p, out_other_p], last_mine)
+    first = tp_i == 0
+    first_p = jnp.concatenate(
+        [jnp.where(first, first_p, gathered_p), jnp.where(first, gathered_p, first_p)]
+    ).astype(F32)
     out_p = out_terms_p.astype(F32) + out_other_p.astype(F32)
     prompt_out = (resid_p + out_p).astype(BF)[None]
     cont_grad = (grad_c + norm_back(one_c, inv_c, first_c, gains[0])).astype(BF)[None, None]
     prompt_grad = (grad_p + norm_back(one_p, inv_p, first_p, gains[0])).astype(BF)[None]
+    last_sum, norm_sum = gather_last(last_mine, slab_rows, last_part.shape[0], (prompt_grad, cont_grad))
+    norm_sum = norm_sum.reshape(-1)[: 4 * columns].reshape(4, columns)
     return (
         prompt_out,
         cont_out,
@@ -611,8 +677,7 @@
         cont_grad,
         last_sum[:3],
         last_sum[3].T,
-        ffn_sum[0],
-        ffn_sum[1].T,
+        *ffn_sums,
         norm_sum[:2],
         norm_sum[2:],
     )

time: 314 us -> 298 us (0.949)
  waiting for transfers between devices: 73.9 us -> 54.1 us
  starting transfers between devices: 40.2 us -> 36.4 us
  other arithmetic: 39.5 us -> 43.3 us
    ppermute x32 -> x23, waiting for transfers between devices: 73.7 us -> 48.6 us  [swap(): return lax.ppermute(array, axis, [(j, j ^ 1 << bit) for j in range(count)])]
    ppermute x32 -> x23, starting transfers between devices: 34.6 us -> 24.3 us  [swap(): return lax.ppermute(array, axis, [(j, j ^ 1 << bit) for j in range(count)])]
    dot_general x3 -> x8, matrix products: 7.85 us -> 14.9 us  [rows_dot(): return jnp.einsum('nd,nf->df', left, right, preferred_element_type=F32)]
    dot_general x2 -> x0, matrix products: 6.96 us -> none  [the longest x1 3.79 us: body(): jnp.einsum('nd,cne->cde', low_pc, own_grads, preferred_element_type=F32)]
    ppermute x0 -> x6, starting transfers between devices: none -> 6.49 us  [the longest x3 4.57 us: body(): lax.ppermute(block(seq_i ^ at), 'seq', [(j, j ^ at) for j in range(seq_n)])]
    ppermute x0 -> x6, waiting for transfers between devices: none -> 5.46 us  [the longest x3 4.84 us: body(): lax.ppermute(block(seq_i ^ at), 'seq', [(j, j ^ at) for j in range(seq_n)])]
    dot_general x6, matrix products: 22 us -> 25.4 us  [wide_dot(): return jnp.dot(left, right, preferred_element_type=F32)]
    unnamed x153 -> x162, local copies, waits for them, and re-layouts: 6.71 us -> 9.91 us
  transfers between devices with their start and end apart: 35 -> 32, of which waited for: 22 -> 12; matrix products, arithmetic and copies ran while one was open for 28% -> 31% of each run, Pallas kernels for 19% -> 20%
where the time goes in v4:
time: 298 us; the launch traced here: 293 us
  Pallas kernels  70.7 us (24%)
  matrix products  63 us (21%)
  waiting for transfers between devices  54.1 us (18%)
  other arithmetic  43.3 us (15%)
  starting transfers between devices  36.4 us (12%)
  local copies, waits for them, and re-layouts  22.5 us (8%)
  between operations  3.33 us (1%)
    ppermute x23, waiting for transfers between devices, swap(): return lax.ppermute(array, axis, [(j, j ^ 1 << bit) for j in range(count)])  48.6 us
    dot_general x6, matrix products, wide_dot(): return jnp.dot(left, right, preferred_element_type=F32)  25.4 us
    pallas_call x2, Pallas kernels, pull_far(): pl.pallas_call(functools.partial(pull_far_kernel, masked=masked, chunk=ch...  25.1 us
    ppermute x23, starting transfers between devices, swap(): return lax.ppermute(array, axis, [(j, j ^ 1 << bit) for j in range(count)])  24.3 us
    pallas_call x2, Pallas kernels, attend_far(): pl.pallas_call(functools.partial(far_kernel, masked=masked), grid=(width...  19.5 us
    pallas_call x1, Pallas kernels, pull_near(): pl.pallas_call(pull_near_kernel, grid=(width // LANES,), in_specs=specs,...  14.9 us
    dot_general x8, matrix products, rows_dot(): return jnp.einsum('nd,nf->df', left, right, preferred_element_type=F32)  14.9 us
    pallas_call x1, Pallas kernels, attend_near(): pl.pallas_call(near_kernel, grid=(width // LANES,), in_specs=[kind_spec(o...  11.1 us
  transfers between devices with their start and end apart: 32, of which 12 were waited for; matrix products, arithmetic and copies ran while one was open for 31% of the time, Pallas kernels for 20%

profile of v4, /device:TPU:0, one launch (start us, length us, event | category | flops | bytes accessed | tf_op | source)
XLA Modules:
  0.0 293.4 jit_solution(11229066662948691534)
XLA Ops:
  0.7 1.9 dynamic-slice_bitcast_fusion.7
  2.5 3.1 %collective-permute-start = (bf16[192,768]{1,0:T(8,128)(2,1)}, bf16[192,768]{1,0:T(8,128)(2,1)}, u32[]{:S(2)}, u32[]{:S(2)}) collective-permute-start(bf16[192,768]{1,0:T(8,128)(2,1)} %dynamic-slice_bitcast_fusion.7), channel_id=1, source_target_pairs={{0,2},{2,0},{4,6},{6,4},{1,3},{3,1},{5,7},{7,5},{8,10},{10,8},{12,... | collective-permute-start | bytes 884744 | tf_op jit(solution)/shard_map/ppermute | solution.py:453
  5.6 2.6 collective-permute-start.1
  11.9 1.5 fusion.35
  13.4 1.3 subtract_multiply_fusion.2
  15.6 2.2 fusion.42.qc_ref.kc_ref.vc_ref.refs_0_
  17.8 1.8 fusion.53.qp_ref.kp_ref.vp_ref.refs_0_
  21.4 11.1 %shard_map.186 = (f32[384,384]{1,0:T(8,128)}, f32[3,8,384]{2,1,0:T(8,128)}, f32[512,384]{1,0:T(8,128)}, f32[3,8,512]{2,1,0:T(8,128)}) custom-call(bf16[3,384,384]{2,1,0:T(8,128)(2,1)} %fusion.53.qp_ref.kp_ref.vp_ref.refs_0_, bf16[3,384,384]{2,1,0:T(8,128)(2,1)} %fusion.53.qp_ref.kp_ref.vp_ref.refs_0_, ...), custom_call_target="tpu_custom_call" | custom-call | flops 1212416 | bytes 5120 | tf_op jit(solution)/shard_map/pallas_call | solution.py:122
  32.5 1.8 collective-permute-start.3
  36.7 1.8 collective-permute-start.5
  38.5 4.1 %collective-permute-done.3 = bf16[192,768]{1,0:T(8,128)(2,1)S(1)} collective-permute-done((bf16[192,768]{1,0:T(8,128)(2,1)}, bf16[192,768]{1,0:T(8,128)(2,1)S(1)}, u32[]{:S(2)}, u32[]{:S(2)}) %collective-permute-start.3) | collective-permute-done | bytes 294944 | tf_op jit(solution)/shard_map/ppermute | solution.py:312
  42.7 6.3 %collective-permute-done.4 = bf16[192,768]{1,0:T(8,128)(2,1)S(1)} collective-permute-done((bf16[192,768]{1,0:T(8,128)(2,1)}, bf16[192,768]{1,0:T(8,128)(2,1)S(1)}, u32[]{:S(2)}, u32[]{:S(2)}) %collective-permute-start.4) | collective-permute-done | bytes 294944 | tf_op jit(solution)/shard_map/ppermute | solution.py:312
  49.0 4.6 %collective-permute-done.5 = bf16[192,768]{1,0:T(8,128)(2,1)S(1)} collective-permute-done((bf16[192,768]{1,0:T(8,128)(2,1)S(1)}, bf16[192,768]{1,0:T(8,128)(2,1)S(1)}, u32[]{:S(2)}, u32[]{:S(2)}) %collective-permute-start.5) | collective-permute-done | bytes 294944 | tf_op jit(solution)/shard_map/ppermute | solution.py:312
  56.4 2.8 fusion.15.refs_1_.refs_2_
  60.2 10.8 %shard_map.187 = (bf16[512,384]{1,0:T(8,128)(2,1)}, f32[3,8,512]{2,1,0:T(8,128)}) custom-call(bf16[3,512,384]{2,1,0:T(8,128)(2,1)} %fusion.42.qc_ref.kc_ref.vc_ref.refs_0_, bf16[2,1152,384]{2,1,0:T(8,128)(2,1)} %fusion.15.refs_1_.refs_2_, bf16[2,1152,384]{2,1,0:T(8,128)(2,1)} %fusion.15.refs_1_.refs_2_, f32[1152,128]{1,0:T(8,128)} %broadcast_in_dim.33.refs_3_, ...), custom_call_target="tpu_custom_call" | custom-call | flops 1179648 | bytes 4608 | tf_op jit(solution)/shard_map/pallas_call | solution.py:170
  71.0 2.4 convolution_convert_fusion.7
  73.4 1.5 collective-permute-start.6
  76.1 8.8 %shard_map.188 = (bf16[384,384]{1,0:T(8,128)(2,1)}, f32[3,8,384]{2,1,0:T(8,128)}) custom-call(bf16[3,384,384]{2,1,0:T(8,128)(2,1)} %fusion.53.qp_ref.kp_ref.vp_ref.refs_0_, bf16[2,1152,384]{2,1,0:T(8,128)(2,1)} %fusion.15.refs_1_.refs_2_, bf16[2,1152,384]{2,1,0:T(8,128)(2,1)} %fusion.15.refs_1_.refs_2_, f32[384,384]{1,0:T(8,128)} %get-tuple-element.70.refs_3_, ...), custom_call_target="tpu_custom_call" | custom-call | flops 884736 | bytes 4608 | tf_op jit(solution)/shard_map/pallas_call | solution.py:170
  84.9 1.4 convolution_convert_fusion.11
  86.9 7.2 %collective-permute-done.6 = bf16[512,768]{1,0:T(8,128)(2,1)} collective-permute-done((bf16[512,768]{1,0:T(8,128)(2,1)}, bf16[512,768]{1,0:T(8,128)(2,1)}, u32[]{:S(2)}, u32[]{:S(2)}) %collective-permute-start.6) | collective-permute-done | bytes 786464 | tf_op jit(solution)/shard_map/ppermute | solution.py:312
  94.2 1.7 fusion.115
  97.4 8.3 %multiply_convert_fusion = (bf16[512,1536]{1,0:T(8,128)(2,1)S(1)}, f32[512,1536]{1,0:T(8,128)S(1)}, f32[512,1536]{1,0:T(8,128)S(1)}) fusion(bf16[512,768]{1,0:T(8,128)(2,1)S(1)} %add_convert_fusion.7, bf16[768,1536]{1,0:T(8,128)(2,1)S(1)} %copy-done), kind=kOutput, calls=%fused_computation.23 | convolution fusion | flops 1259077632 | bytes 11010048 | tf_op jit(solution)/shard_map/dot_general | solution.py:353
  105.7 2.2 add_convert_fusion
  107.9 1.4 convolution_convert_fusion.6
  109.4 1.6 collective-permute-start.9
  112.1 6.5 %multiply_convert_fusion.1 = (bf16[384,1536]{1,0:T(8,128)(2,1)S(1)}, f32[384,1536]{1,0:T(8,128)S(1)}, f32[384,1536]{1,0:T(8,128)S(1)}) fusion(bf16[384,768]{1,0:T(8,128)(2,1)S(1)} %add_convert_fusion.13, bf16[768,1536]{1,0:T(8,128)(2,1)S(1)} %copy-done), kind=kOutput, calls=%fused_computation.60 | convolution fusion | flops 944308224 | bytes 8847360 | tf_op jit(solution)/shard_map/dot_general | solution.py:353
  118.7 2.9 convolution_convert_fusion
  121.7 1.6 add_convert_fusion.3
  124.0 3.1 %convolution_convert_fusion.1 = bf16[768,1536]{1,0:T(8,128)(2,1)S(1)} fusion(bf16[512,1536]{1,0:T(8,128)(2,1)S(1)} %add_convert_fusion, bf16[384,1536]{1,0:T(8,128)(2,1)S(1)} %add_convert_fusion.3, bf16[512,768]{1,0:T(8,128)(2,1)S(1)} %add_convert_fusion.7, bf16[384,768]{1,0:T(8,128)(2,1)S(1)} %add_convert_fusion.13), kind=kOutput, calls=%fused_computation.20 | convolution fusion | flops 2123366400 | bytes 6488064 | tf_op jit(solution)/shard_map/nd,nf->df/dot_general | solution.py:361
  127.1 1.9 fusion.25
  129.4 2.5 convolution_convert_fusion.9
  134.3 2.3 fusion
  136.7 2.0 fusion.41
  140.0 3.1 %fusion.111 = (bf16[512,768]{1,0:T(8,128)(2,1)S(1)}, f32[512,768]{1,0:T(8,128)}) fusion(f32[512]{0:T(512)S(1)} %broadcast_multiply_fusion.9, f32[512,768]{1,0:T(8,128)S(1)} %copy-done.3, f32[512]{0:T(512)S(1)} %copy-done.53, f32[512]{0:T(512)S(1)} %broadcast_multiply_fusion.10, f32[768]{0:T(1024)S(1)} %get-tuple-element.201, ...), kind=kLoop, calls=%fused_computation.303 | loop fusion | flops 5111808 | bytes 6302720 | tf_op jit(solution)/shard_map/convert_element_type | solution.py:523
  144.0 1.4 convolution_convert_fusion.12.refs_4_.doc_ref
  145.4 13.6 %shard_map.189 = (f32[512,384]{1,0:T(8,128)}, f32[2,1152,384]{2,1,0:T(8,128)}) custom-call(bf16[3,512,384]{2,1,0:T(8,128)(2,1)} %fusion.42.qc_ref.kc_ref.vc_ref.refs_0_, bf16[2,1152,384]{2,1,0:T(8,128)(2,1)} %fusion.15.refs_1_.refs_2_, bf16[2,1152,384]{2,1,0:T(8,128)(2,1)} %fusion.15.refs_1_.refs_2_, f32[1152,128]{1,0:T(8,128)} %broadcast_in_dim.33.refs_3_, ...), custom_call_target="tpu_custom_call" | custom-call | flops 2949120 | bytes 9216 | tf_op jit(solution)/shard_map/pallas_call | solution.py:258
  159.0 4.4 %convolution_convert_fusion.5 = bf16[512,768]{1,0:T(8,128)(2,1)} fusion(bf16[512,1536]{1,0:T(8,128)(2,1)} %copy-done.76, bf16[1536,768]{1,0:T(8,128)(2,1)} %param.19), kind=kOutput, calls=%fused_computation.107 | convolution fusion | flops 1208352768 | bytes 4718592 | tf_op jit(solution)/shard_map/dot_general | solution.py:353
  163.4 1.5 collective-permute-start.15
  164.9 2.1 collective-permute-done.11
  169.4 1.6 fusion.110
  172.2 11.6 %shard_map.190 = (f32[384,384]{1,0:T(8,128)}, bf16[2,1152,384]{2,1,0:T(8,128)(2,1)}) custom-call(bf16[3,384,384]{2,1,0:T(8,128)(2,1)} %fusion.53.qp_ref.kp_ref.vp_ref.refs_0_, bf16[2,1152,384]{2,1,0:T(8,128)(2,1)} %fusion.15.refs_1_.refs_2_, bf16[2,1152,384]{2,1,0:T(8,128)(2,1)} %fusion.15.refs_1_.refs_2_, ...), custom_call_target="tpu_custom_call" | custom-call | flops 2211840 | bytes 9216 | tf_op jit(solution)/shard_map/pallas_call | solution.py:258
  183.8 3.6 %fusion.7 = (f32[768]{0:T(1024)S(1)}, f32[768]{0:T(1024)S(1)}, bf16[1152,768]{1,0:T(8,128)(2,1)S(1)}) fusion(bf16[1152,768]{1,0:T(8,128)(2,1)S(1)} %copy-done.9, f32[1152]{0:T(1024)S(1)} %copy-done.65, f32[1152]{0:T(1024)S(1)} %broadcast_multiply_fusion, bf16[2,1152,384]{2,1,0:T(8,128)(2,1)} %get-tuple-element.84, bf16[3,768,384]{2,1,0:T(8,128)(2,1)} %param.16), kind=kOutput, calls=%fused_computation.16 | convolution fusion | flops 1365146112 | bytes 6503424 | tf_op jit(solution)/shard_map/cne,cde->nd/dot_general | solution.py:549
  190.6 3.1 %collective-permute-start.14 = (bf16[2,48,1536]{2,1,0:T(8,128)(2,1)}, bf16[2,48,1536]{2,1,0:T(8,128)(2,1)}, u32[]{:S(2)}, u32[]{:S(2)}) collective-permute-start(bf16[2,48,1536]{2,1,0:T(8,128)(2,1)} %get-tuple-element.189), channel_id=1, source_target_pairs={{0,4},{2,6},{4,0},{6,2},{1,5},{3,7},{5,1},{7,3},{8,12},{10,14},{12... | collective-permute-start | bytes 884744 | tf_op jit(solution)/shard_map/ppermute | solution.py:312
  193.8 2.3 fusion.54
  196.3 14.9 %shard_map.191 = bf16[3,896,384]{2,1,0:T(8,128)(2,1)} custom-call(bf16[3,384,384]{2,1,0:T(8,128)(2,1)} %fusion.53.qp_ref.kp_ref.vp_ref.refs_0_, bf16[3,384,384]{2,1,0:T(8,128)(2,1)} %fusion.53.qp_ref.kp_ref.vp_ref.refs_0_, bf16[3,384,384]{2,1,0:T(8,128)(2,1)} %fusion.53.qp_ref.kp_ref.vp_ref.refs_0_, ...), custom_call_target="tpu_custom_call" | custom-call | flops 3031040 | bytes 5120 | tf_op jit(solution)/shard_map/pallas_call | solution.py:299
  211.3 2.2 fusion.80
  221.2 1.6 collective-permute-start.21
  222.8 1.4 add_convert_fusion.4
  225.7 2.0 bitcast_convert_fusion
  229.2 1.6 collective-permute-start.16
  232.3 7.0 %collective-permute-done.18 = bf16[2,192,768]{2,1,0:T(8,128)(2,1)S(1)} collective-permute-done((bf16[2,192,768]{2,1,0:T(8,128)(2,1)S(1)}, bf16[2,192,768]{2,1,0:T(8,128)(2,1)S(1)}, u32[]{:S(2)}, u32[]{:S(2)}) %collective-permute-start.18) | collective-permute-done | bytes 589856 | tf_op jit(solution)/shard_map/ppermute | solution.py:312
  240.2 2.5 fusion.72
  242.7 11.6 %collective-permute-done.20 = bf16[1,192,768]{2,1,0:T(8,128)(2,1)S(1)} collective-permute-done((bf16[1,192,768]{2,1,0:T(8,128)(2,1)S(1)}, bf16[1,192,768]{2,1,0:T(8,128)(2,1)S(1)}, u32[]{:S(2)}, u32[]{:S(2)}) %collective-permute-start.20) | collective-permute-done | bytes 294944 | tf_op jit(solution)/shard_map/ppermute | solution.py:312
  258.4 1.6 slice_bitcast_fusion
  260.4 2.5 collective-permute-start.28
  263.0 2.0 collective-permute-start.26
  265.0 2.3 convolution_convert_fusion.8
  267.4 1.6 collective-permute-start.25
  269.0 1.6 fusion.73
  270.7 4.8 %collective-permute-done.27 = bf16[208,384]{1,0:T(8,128)(2,1)S(1)} collective-permute-done((bf16[208,384]{1,0:T(8,128)(2,1)S(1)}, bf16[208,384]{1,0:T(8,128)(2,1)S(1)}, u32[]{:S(2)}, u32[]{:S(2)}) %collective-permute-start.27) | collective-permute-done | bytes 159776 | tf_op jit(solution)/shard_map/ppermute | solution.py:649
  277.5 3.8 %collective-permute-done.25 = bf16[384,768]{1,0:T(8,128)(2,1)S(1)} collective-permute-done((bf16[384,768]{1,0:T(8,128)(2,1)S(1)}, bf16[384,768]{1,0:T(8,128)(2,1)S(1)}, u32[]{:S(2)}, u32[]{:S(2)}) %collective-permute-start.25) | collective-permute-done | bytes 589856 | tf_op jit(solution)/shard_map/ppermute | solution.py:312
  281.3 1.3 broadcast_select_fusion.3
  288.4 2.3 slice.192
  290.7 2.2 fusion.86
  (323 shorter events, 53.9 us)
Async XLA Ops:
  0.6 96.7 %copy-start = (bf16[768,1536]{1,0:T(8,128)(2,1)S(1)}, bf16[768,1536]{1,0:T(8,128)(2,1)}, u32[]{:S(2)}) copy-start(bf16[768,1536]{1,0:T(8,128)(2,1)} %param.18) | copy-start | bytes 7077892
  0.7 10.2 %copy-start.4 = (bf16[1,1,512,768]{3,2,1,0:T(8,128)(2,1)S(1)}, bf16[1,1,512,768]{3,2,1,0:T(8,128)(2,1)}, u32[]{:S(2)}) copy-start(bf16[1,1,512,768]{3,2,1,0:T(8,128)(2,1)} %param.12) | copy-start | bytes 2359300
  2.5 29.9 %collective-permute-start = (bf16[192,768]{1,0:T(8,128)(2,1)}, bf16[192,768]{1,0:T(8,128)(2,1)}, u32[]{:S(2)}, u32[]{:S(2)}) collective-permute-start(bf16[192,768]{1,0:T(8,128)(2,1)} %dynamic-slice_bitcast_fusion.7), channel_id=1, source_target_pairs={{0,2},{2,0},{4,6},{6,4},{1,3},{3,1},{5,7},{7,5},{8,10},{10,8},{12,... | collective-permute-start | bytes 884744 | tf_op jit(solution)/shard_map/ppermute | solution.py:453
  5.6 29.7 %collective-permute-start.1 = (bf16[192,768]{1,0:T(8,128)(2,1)}, bf16[192,768]{1,0:T(8,128)(2,1)}, u32[]{:S(2)}, u32[]{:S(2)}) collective-permute-start(bf16[192,768]{1,0:T(8,128)(2,1)} %dynamic-slice_bitcast_fusion.7), channel_id=1, source_target_pairs={{0,4},{2,6},{4,0},{6,2},{1,5},{3,7},{5,1},{7,3},{8,12},{10,14},{12... | collective-permute-start | bytes 884744 | tf_op jit(solution)/shard_map/ppermute | solution.py:453
  8.2 28.5 %collective-permute-start.2 = (bf16[192,768]{1,0:T(8,128)(2,1)}, bf16[192,768]{1,0:T(8,128)(2,1)S(1)}, u32[]{:S(2)}, u32[]{:S(2)}) collective-permute-start(bf16[192,768]{1,0:T(8,128)(2,1)} %dynamic-slice_bitcast_fusion.7), channel_id=1, source_target_pairs={{0,6},{2,4},{4,2},{6,0},{1,7},{3,5},{5,3},{7,1},{8,14},{10,12},{12... | collective-permute-start | bytes 884744 | tf_op jit(solution)/shard_map/ppermute | solution.py:453
  11.9 84.4 %copy-start.56 = (f32[768]{0:T(1024)}, f32[768]{0:T(1024)S(1)}, u32[]{:S(2)}) copy-start(f32[768]{0:T(1024)S(1)} %get-tuple-element.138) | copy-start | bytes 9220
  32.5 10.2 %collective-permute-start.3 = (bf16[192,768]{1,0:T(8,128)(2,1)}, bf16[192,768]{1,0:T(8,128)(2,1)S(1)}, u32[]{:S(2)}, u32[]{:S(2)}) collective-permute-start(bf16[192,768]{1,0:T(8,128)(2,1)} %collective-permute-done), channel_id=1, source_target_pairs={{0,1},{1,0},{2,3},{3,2},{4,5},{5,4},{6,7},{7,6},{8,9},{9,8},{10,11... | collective-permute-start | bytes 884744 | tf_op jit(solution)/shard_map/ppermute | solution.py:312
  35.3 13.6 %collective-permute-start.4 = (bf16[192,768]{1,0:T(8,128)(2,1)}, bf16[192,768]{1,0:T(8,128)(2,1)S(1)}, u32[]{:S(2)}, u32[]{:S(2)}) collective-permute-start(bf16[192,768]{1,0:T(8,128)(2,1)} %collective-permute-done.1), channel_id=1, source_target_pairs={{0,1},{1,0},{2,3},{3,2},{4,5},{5,4},{6,7},{7,6},{8,9},{9,8},{10,11... | collective-permute-start | bytes 884744 | tf_op jit(solution)/shard_map/ppermute | solution.py:312
  36.7 16.9 %collective-permute-start.5 = (bf16[192,768]{1,0:T(8,128)(2,1)S(1)}, bf16[192,768]{1,0:T(8,128)(2,1)S(1)}, u32[]{:S(2)}, u32[]{:S(2)}) collective-permute-start(bf16[192,768]{1,0:T(8,128)(2,1)S(1)} %collective-permute-done.2), channel_id=1, source_target_pairs={{0,1},{1,0},{2,3},{3,2},{4,5},{5,4},{6,7},{7,6},{8,9},{9,8},{10,11... | collective-permute-start | bytes 884744 | tf_op jit(solution)/shard_map/ppermute | solution.py:312
  60.2 10.8 %copy-start.18 = (bf16[384,768]{1,0:T(8,128)(2,1)S(1)}, bf16[384,768]{1,0:T(8,128)(2,1)}, u32[]{:S(2)}) copy-start(bf16[384,768]{1,0:T(8,128)(2,1)} %param.17) | copy-start | bytes 1769476
  73.4 20.7 %collective-permute-start.6 = (bf16[512,768]{1,0:T(8,128)(2,1)}, bf16[512,768]{1,0:T(8,128)(2,1)}, u32[]{:S(2)}, u32[]{:S(2)}) collective-permute-start(bf16[512,768]{1,0:T(8,128)(2,1)} %convolution_convert_fusion.7), channel_id=1, source_target_pairs={{0,1},{1,0},{2,3},{3,2},{4,5},{5,4},{6,7},{7,6},{8,9},{9,8},{10,11... | collective-permute-start | bytes 2359304 | tf_op jit(solution)/shard_map/ppermute | solution.py:312
  76.1 8.8 %copy-start.19 = (bf16[384,768]{1,0:T(8,128)(2,1)S(1)}, bf16[384,768]{1,0:T(8,128)(2,1)}, u32[]{:S(2)}) copy-start(bf16[384,768]{1,0:T(8,128)(2,1)} %param.17) | copy-start | bytes 1769476
  86.3 24.6 %collective-permute-start.7 = (bf16[384,768]{1,0:T(8,128)(2,1)S(1)}, bf16[384,768]{1,0:T(8,128)(2,1)S(1)}, u32[]{:S(2)}, u32[]{:S(2)}) collective-permute-start(bf16[384,768]{1,0:T(8,128)(2,1)S(1)} %convolution_convert_fusion.11), channel_id=1, source_target_pairs={{0,1},{1,0},{2,3},{3,2},{4,5},{5,4},{6,7},{7,6},{8,9},{9,8},{10,11... | collective-permute-start | bytes 1769480 | tf_op jit(solution)/shard_map/ppermute | solution.py:312
  96.2 9.5 %copy-start.62 = (f32[512]{0:T(512)}, f32[512]{0:T(512)S(1)}, u32[]{:S(2)}) copy-start(f32[512]{0:T(512)S(1)} %add_rsqrt_fusion.2) | copy-start | bytes 6148
  97.4 8.3 %copy-start.39 = (bf16[1,1,512,768]{3,2,1,0:T(8,128)(2,1)S(1)}, bf16[1,1,512,768]{3,2,1,0:T(8,128)(2,1)}, u32[]{:S(2)}) copy-start(bf16[1,1,512,768]{3,2,1,0:T(8,128)(2,1)} %param.14) | copy-start | bytes 2359300
  97.4 8.3 %copy-start.69 = (bf16[1536,768]{1,0:T(8,128)(2,1)S(1)}, bf16[1536,768]{1,0:T(8,128)(2,1)}, u32[]{:S(2)}) copy-start(bf16[1536,768]{1,0:T(8,128)(2,1)} %param.19) | copy-start | bytes 7077892
  105.7 13.0 %copy-start.76 = (bf16[512,1536]{1,0:T(8,128)(2,1)}, bf16[512,1536]{1,0:T(8,128)(2,1)S(1)}, u32[]{:S(2)}) copy-start(bf16[512,1536]{1,0:T(8,128)(2,1)S(1)} %get-tuple-element.80) | copy-start | bytes 4718596
  109.4 14.6 %collective-permute-start.9 = (bf16[512,768]{1,0:T(8,128)(2,1)S(1)}, bf16[512,768]{1,0:T(8,128)(2,1)}, u32[]{:S(2)}, u32[]{:S(2)}) collective-permute-start(bf16[512,768]{1,0:T(8,128)(2,1)S(1)} %convolution_convert_fusion.6), channel_id=1, source_target_pairs={{0,1},{1,0},{2,3},{3,2},{4,5},{5,4},{6,7},{7,6},{8,9},{9,8},{10,11... | collective-permute-start | bytes 2359304 | tf_op jit(solution)/shard_map/ppermute | solution.py:312
  111.9 6.8 %copy-start.60 = (f32[384]{0:T(512)}, f32[384]{0:T(512)S(1)}, u32[]{:S(2)}) copy-start(f32[384]{0:T(512)S(1)} %add_rsqrt_fusion.1) | copy-start | bytes 4612
  112.1 6.6 %copy-start.42 = (bf16[1,384,768]{2,1,0:T(8,128)(2,1)S(1)}, bf16[1,384,768]{2,1,0:T(8,128)(2,1)}, u32[]{:S(2)}) copy-start(bf16[1,384,768]{2,1,0:T(8,128)(2,1)} %param.13) | copy-start | bytes 1769476
  121.6 5.5 %copy-start.10 = (bf16[768,1536]{1,0:T(8,128)(2,1)}, bf16[768,1536]{1,0:T(8,128)(2,1)S(1)}, u32[]{:S(2)}) copy-start(bf16[768,1536]{1,0:T(8,128)(2,1)S(1)} %convolution_convert_fusion) | copy-start | bytes 7077892
  129.4 4.9 %collective-permute-start.10 = (bf16[2,2,2,2,48,1536]{5,4,3,2,1,0:T(8,128)(2,1)}, bf16[2,2,2,2,48,1536]{5,4,3,2,1,0:T(8,128)(2,1)}, u32[]{:S(2)}, u32[]{:S(2)}) collective-permute-start(bf16[2,2,2,2,48,1536]{5,4,3,2,1,0:T(8,128)(2,1)} %fusion.25), channel_id=1, source_target_pairs={{0,8},{8,0},{16,24},{24,16},{1,9},{9,1},{17,25},{25,17},{2,10},{10... | collective-permute-start | bytes 7077896 | tf_op jit(solution)/shard_map/ppermute | solution.py:312
  129.4 4.9 %copy-start.11 = (bf16[768,1536]{1,0:T(8,128)(2,1)S(1)}, bf16[768,1536]{1,0:T(8,128)(2,1)}, u32[]{:S(2)}) copy-start(bf16[768,1536]{1,0:T(8,128)(2,1)} %copy-done.10) | copy-start | bytes 7077892
  129.4 4.9 %copy-start.13 = (bf16[768,1536]{1,0:T(8,128)(2,1)S(1)}, bf16[768,1536]{1,0:T(8,128)(2,1)}, u32[]{:S(2)}) copy-start(bf16[768,1536]{1,0:T(8,128)(2,1)} %copy-done.12) | copy-start | bytes 7077892
  132.0 35.3 %collective-permute-start.8 = (bf16[384,768]{1,0:T(8,128)(2,1)S(1)}, bf16[384,768]{1,0:T(8,128)(2,1)S(1)}, u32[]{:S(2)}, u32[]{:S(2)}) collective-permute-start(bf16[384,768]{1,0:T(8,128)(2,1)S(1)} %convolution_convert_fusion.9), channel_id=1, source_target_pairs={{0,1},{1,0},{2,3},{3,2},{4,5},{5,4},{6,7},{7,6},{8,9},{9,8},{10,11... | collective-permute-start | bytes 1769480 | tf_op jit(solution)/shard_map/ppermute | solution.py:312
  138.9 28.1 %collective-permute-start.11 = (bf16[2,2,2,48,1536]{4,3,2,1,0:T(8,128)(2,1)S(1)}, bf16[2,2,2,48,1536]{4,3,2,1,0:T(8,128)(2,1)S(1)}, u32[]{:S(2)}, u32[]{:S(2)}) collective-permute-start(bf16[2,2,2,48,1536]{4,3,2,1,0:T(8,128)(2,1)S(1)} %get-tuple-element.155), channel_id=1, source_target_pairs={{0,16},{8,24},{16,0},{24,8},{1,17},{9,25},{17,1},{25,9},{2,18},{10... | collective-permute-start | bytes 3538952 | tf_op jit(solution)/shard_map/ppermute | solution.py:312
  163.4 30.4 %collective-permute-start.15 = (bf16[512,768]{1,0:T(8,128)(2,1)}, bf16[512,768]{1,0:T(8,128)(2,1)}, u32[]{:S(2)}, u32[]{:S(2)}) collective-permute-start(bf16[512,768]{1,0:T(8,128)(2,1)} %convolution_convert_fusion.5), channel_id=1, source_target_pairs={{0,1},{1,0},{2,3},{3,2},{4,5},{5,4},{6,7},{7,6},{8,9},{9,8},{10,11... | collective-permute-start | bytes 2359304 | tf_op jit(solution)/shard_map/ppermute | solution.py:312
  168.5 21.1 %collective-permute-start.13 = (bf16[2,2,48,1536]{3,2,0,1:T(8,128)(2,1)S(1)}, bf16[2,2,48,1536]{3,2,0,1:T(8,128)(2,1)S(1)}, u32[]{:S(2)}, u32[]{:S(2)}) collective-permute-start(bf16[2,2,48,1536]{3,2,0,1:T(8,128)(2,1)S(1)} %bitcast.266), channel_id=1, source_target_pairs={{0,2},{2,0},{4,6},{6,4},{1,3},{3,1},{5,7},{7,5},{8,10},{10,8},{12,... | collective-permute-start | bytes 1769480 | tf_op jit(solution)/shard_map/ppermute | solution.py:312
  172.2 11.6 %copy-start.9 = (bf16[1152,768]{1,0:T(8,128)(2,1)S(1)}, bf16[1152,768]{1,0:T(8,128)(2,1)}, u32[]{:S(2)}) copy-start(bf16[1152,768]{1,0:T(8,128)(2,1)} %copy-done.8) | copy-start | bytes 5308420
  172.2 11.6 %copy-start.65 = (f32[1152]{0:T(1024)S(1)}, f32[1152]{0:T(1024)}, u32[]{:S(2)}) copy-start(f32[1152]{0:T(1024)} %copy-done.64) | copy-start | bytes 13828
  188.5 5.3 %copy-start.23 = (bf16[512,384]{1,0:T(8,128)(2,1)S(1)}, bf16[512,384]{1,0:T(8,128)(2,1)}, u32[]{:S(2)}) copy-start(bf16[512,384]{1,0:T(8,128)(2,1)} %get-tuple-element.67.refs_5_.outc_ref) | copy-start | bytes 1179652
  188.5 5.3 %copy-start.28 = (bf16[384,384]{1,0:T(8,128)(2,1)S(1)}, bf16[384,384]{1,0:T(8,128)(2,1)}, u32[]{:S(2)}) copy-start(bf16[384,384]{1,0:T(8,128)(2,1)} %get-tuple-element.72.refs_4_.outp_ref) | copy-start | bytes 884740
  188.5 22.7 %collective-permute-start.12 = (bf16[576,768]{1,0:T(8,128)(2,1)}, bf16[576,768]{1,0:T(8,128)(2,1)}, u32[]{:S(2)}, u32[]{:S(2)}) collective-permute-start(bf16[576,768]{1,0:T(8,128)(2,1)} %slice.182), channel_id=1, source_target_pairs={{0,1},{1,0},{2,3},{3,2},{4,5},{5,4},{6,7},{7,6},{8,9},{9,8},{10,11... | collective-permute-start | bytes 2654216 | tf_op jit(solution)/shard_map/ppermute | solution.py:312
  190.6 20.6 %collective-permute-start.14 = (bf16[2,48,1536]{2,1,0:T(8,128)(2,1)}, bf16[2,48,1536]{2,1,0:T(8,128)(2,1)}, u32[]{:S(2)}, u32[]{:S(2)}) collective-permute-start(bf16[2,48,1536]{2,1,0:T(8,128)(2,1)} %get-tuple-element.189), channel_id=1, source_target_pairs={{0,4},{2,6},{4,0},{6,2},{1,5},{3,7},{5,1},{7,3},{8,12},{10,14},{12... | collective-permute-start | bytes 884744 | tf_op jit(solution)/shard_map/ppermute | solution.py:312
  196.3 15.0 %copy-start.38 = (bf16[512,768]{1,0:T(8,128)(2,1)S(1)}, bf16[512,768]{1,0:T(8,128)(2,1)}, u32[]{:S(2)}) copy-start(bf16[512,768]{1,0:T(8,128)(2,1)} %copy-done.37) | copy-start | bytes 2359300
  196.3 15.0 %copy-start.45 = (bf16[384,768]{1,0:T(8,128)(2,1)S(1)}, bf16[384,768]{1,0:T(8,128)(2,1)}, u32[]{:S(2)}) copy-start(bf16[384,768]{1,0:T(8,128)(2,1)} %copy-done.44) | copy-start | bytes 1769476
  219.5 11.5 %collective-permute-start.19 = (bf16[4,2,2,2,48,384]{5,4,2,1,0,3:T(8,128)(2,1)S(1)}, bf16[4,2,2,2,48,384]{5,4,2,1,0,3:T(8,128)(2,1)S(1)}, u32[]{:S(2)}, u32[]{:S(2)}) collective-permute-start(bf16[4,2,2,2,48,384]{5,4,2,1,0,3:T(8,128)(2,1)S(1)} %pad_maximum_fusion.1), channel_id=1, source_target_pairs={{0,8},{8,0},{16,24},{24,16},{1,9},{9,1},{17,25},{25,17},{2,10},{10... | collective-permute-start | bytes 3538952 | tf_op jit(solution)/shard_map/ppermute | solution.py:312
  221.2 9.6 %collective-permute-start.21 = (bf16[2,48,1536]{2,1,0:T(8,128)(2,1)S(1)}, bf16[2,48,1536]{2,1,0:T(8,128)(2,1)S(1)}, u32[]{:S(2)}, u32[]{:S(2)}) collective-permute-start(bf16[2,48,1536]{2,1,0:T(8,128)(2,1)S(1)} %add_convert_fusion.15), channel_id=1, source_target_pairs={{0,16},{8,24},{16,0},{24,8},{1,17},{9,25},{17,1},{25,9},{2,18},{10... | collective-permute-start | bytes 884744 | tf_op jit(solution)/shard_map/ppermute | solution.py:312
  224.4 14.9 %collective-permute-start.18 = (bf16[2,192,768]{2,1,0:T(8,128)(2,1)S(1)}, bf16[2,192,768]{2,1,0:T(8,128)(2,1)S(1)}, u32[]{:S(2)}, u32[]{:S(2)}) collective-permute-start(bf16[2,192,768]{2,1,0:T(8,128)(2,1)S(1)} %pad_maximum_fusion.2), channel_id=1, source_target_pairs={{0,2},{2,0},{4,6},{6,4},{1,3},{3,1},{5,7},{7,5},{8,10},{10,8},{12,... | collective-permute-start | bytes 1769480 | tf_op jit(solution)/shard_map/ppermute | solution.py:312
  228.6 26.7 %copy-start.14 = (bf16[528,768]{1,0:T(8,128)(2,1)}, bf16[528,768]{1,0:T(8,128)(2,1)S(1)}, u32[]{:S(2)}) copy-start(bf16[528,768]{1,0:T(8,128)(2,1)S(1)} %fusion.71) | copy-start | bytes 2433028
  228.6 26.7 %collective-permute-start.17 = (bf16[528,768]{1,0:T(8,128)(2,1)S(1)}, bf16[528,768]{1,0:T(8,128)(2,1)S(1)}, u32[]{:S(2)}, u32[]{:S(2)}) collective-permute-start(bf16[528,768]{1,0:T(8,128)(2,1)S(1)} %fusion.71), channel_id=1, source_target_pairs={{0,1},{1,0},{2,3},{3,2},{4,5},{5,4},{6,7},{7,6},{8,9},{9,8},{10,11... | collective-permute-start | bytes 2433032 | tf_op jit(solution)/shard_map/ppermute | solution.py:312
  229.2 26.1 %collective-permute-start.16 = (bf16[192,768]{1,0:T(8,128)(2,1)S(1)}, bf16[192,768]{1,0:T(8,128)(2,1)S(1)}, u32[]{:S(2)}, u32[]{:S(2)}) collective-permute-start(bf16[192,768]{1,0:T(8,128)(2,1)S(1)} %dynamic-slice_bitcast_fusion.4), channel_id=1, source_target_pairs={{0,1},{1,0},{2,3},{3,2},{4,5},{5,4},{6,7},{7,6},{8,9},{9,8},{10,11... | collective-permute-start | bytes 884744 | tf_op jit(solution)/shard_map/ppermute | solution.py:312
  230.9 24.4 %collective-permute-start.22 = (bf16[2,96,1536]{2,1,0:T(8,128)(2,1)S(1)}, bf16[2,96,1536]{2,1,0:T(8,128)(2,1)S(1)}, u32[]{:S(2)}, u32[]{:S(2)}) collective-permute-start(bf16[2,96,1536]{2,1,0:T(8,128)(2,1)S(1)} %pad_maximum_fusion.3), channel_id=1, source_target_pairs={{0,8},{8,0},{16,24},{24,16},{1,9},{9,1},{17,25},{25,17},{2,10},{10... | collective-permute-start | bytes 1769480 | tf_op jit(solution)/shard_map/ppermute | solution.py:312
  231.5 22.9 %collective-permute-start.23 = (bf16[4,2,2,48,384]{4,3,2,1,0:T(8,128)(2,1)S(1)}, bf16[4,2,2,48,384]{4,3,2,1,0:T(8,128)(2,1)S(1)}, u32[]{:S(2)}, u32[]{:S(2)}) collective-permute-start(bf16[4,2,2,48,384]{4,3,2,1,0:T(8,128)(2,1)S(1)} %get-tuple-element.159), channel_id=1, source_target_pairs={{0,16},{8,24},{16,0},{24,8},{1,17},{9,25},{17,1},{25,9},{2,18},{10... | collective-permute-start | bytes 1769480 | tf_op jit(solution)/shard_map/ppermute | solution.py:312
  239.3 14.9 %collective-permute-start.20 = (bf16[1,192,768]{2,1,0:T(8,128)(2,1)S(1)}, bf16[1,192,768]{2,1,0:T(8,128)(2,1)S(1)}, u32[]{:S(2)}, u32[]{:S(2)}) collective-permute-start(bf16[1,192,768]{2,1,0:T(8,128)(2,1)S(1)} %fusion.88), channel_id=1, source_target_pairs={{0,4},{2,6},{4,0},{6,2},{1,5},{3,7},{5,1},{7,3},{8,12},{10,14},{12... | collective-permute-start | bytes 884744 | tf_op jit(solution)/shard_map/ppermute | solution.py:312
  242.7 12.7 %copy-start.5 = (bf16[1,1,512,768]{3,2,1,0:T(8,128)(2,1)S(1)}, bf16[1,1,512,768]{3,2,1,0:T(8,128)(2,1)}, u32[]{:S(2)}) copy-start(bf16[1,1,512,768]{3,2,1,0:T(8,128)(2,1)} %param.12) | copy-start | bytes 2359300
  242.7 12.7 %copy-start.49 = (f32[512]{0:T(512)S(1)}, f32[512]{0:T(512)}, u32[]{:S(2)}) copy-start(f32[512]{0:T(512)} %copy-done.48) | copy-start | bytes 6148
  242.7 12.7 %copy-start.59 = (f32[512]{0:T(512)S(1)}, f32[512]{0:T(512)}, u32[]{:S(2)}) copy-start(f32[512]{0:T(512)} %copy-done.58) | copy-start | bytes 6148
  256.9 20.6 %collective-permute-start.24 = (bf16[192,768]{1,0:T(8,128)(2,1)}, bf16[192,768]{1,0:T(8,128)(2,1)}, u32[]{:S(2)}, u32[]{:S(2)}) collective-permute-start(bf16[192,768]{1,0:T(8,128)(2,1)} %fusion.90), channel_id=1, source_target_pairs={{0,1},{1,0},{2,3},{3,2},{4,5},{5,4},{6,7},{7,6},{8,9},{9,8},{10,11... | collective-permute-start | bytes 884744 | tf_op jit(solution)/shard_map/ppermute | solution.py:312
  260.4 10.3 %collective-permute-start.28 = (bf16[208,384]{1,0:T(8,128)(2,1)S(1)}, bf16[208,384]{1,0:T(8,128)(2,1)S(1)}, u32[]{:S(2)}, u32[]{:S(2)}) collective-permute-start(bf16[208,384]{1,0:T(8,128)(2,1)S(1)} %pad_maximum_fusion.11), channel_id=1, source_target_pairs={{0,6},{2,4},{4,2},{6,0},{1,7},{3,5},{5,3},{7,1},{8,14},{10,12},{12... | collective-permute-start | bytes 479240 | tf_op jit(solution)/shard_map/ppermute | solution.py:649
  262.8 12.6 %collective-permute-start.27 = (bf16[208,384]{1,0:T(8,128)(2,1)S(1)}, bf16[208,384]{1,0:T(8,128)(2,1)S(1)}, u32[]{:S(2)}, u32[]{:S(2)}) collective-permute-start(bf16[208,384]{1,0:T(8,128)(2,1)S(1)} %pad_maximum_fusion.10), channel_id=1, source_target_pairs={{0,4},{2,6},{4,0},{6,2},{1,5},{3,7},{5,1},{7,3},{8,12},{10,14},{12... | collective-permute-start | bytes 479240 | tf_op jit(solution)/shard_map/ppermute | solution.py:649
  262.9 6.1 %copy-start.15 = (bf16[528,768]{1,0:T(8,128)(2,1)S(1)}, bf16[528,768]{1,0:T(8,128)(2,1)}, u32[]{:S(2)}) copy-start(bf16[528,768]{1,0:T(8,128)(2,1)} %copy-done.14) | copy-start | bytes 2433028
  263.0 6.0 %copy-start.17 = (f32[512,768]{1,0:T(8,128)S(1)}, f32[512,768]{1,0:T(8,128)}, u32[]{:S(2)}) copy-start(f32[512,768]{1,0:T(8,128)} %get-tuple-element.143) | copy-start | bytes 4718596
  263.0 6.0 %copy-start.27 = (bf16[528,768]{1,0:T(8,128)(2,1)S(1)}, bf16[528,768]{1,0:T(8,128)(2,1)}, u32[]{:S(2)}) copy-start(bf16[528,768]{1,0:T(8,128)(2,1)} %copy-done.26) | copy-start | bytes 2433028
  263.0 6.0 %copy-start.68 = (f32[512]{0:T(512)S(1)}, f32[512]{0:T(512)}, u32[]{:S(2)}) copy-start(f32[512]{0:T(512)} %broadcast_multiply_fusion.8) | copy-start | bytes 6148
  263.0 12.5 %collective-permute-start.26 = (bf16[208,384]{1,0:T(8,128)(2,1)S(1)}, bf16[208,384]{1,0:T(8,128)(2,1)S(1)}, u32[]{:S(2)}, u32[]{:S(2)}) collective-permute-start(bf16[208,384]{1,0:T(8,128)(2,1)S(1)} %pad_maximum_fusion.9), channel_id=1, source_target_pairs={{0,2},{2,0},{4,6},{6,4},{1,3},{3,1},{5,7},{7,5},{8,10},{10,8},{12,... | collective-permute-start | bytes 479240 | tf_op jit(solution)/shard_map/ppermute | solution.py:649
  267.4 13.9 %collective-permute-start.25 = (bf16[384,768]{1,0:T(8,128)(2,1)S(1)}, bf16[384,768]{1,0:T(8,128)(2,1)S(1)}, u32[]{:S(2)}, u32[]{:S(2)}) collective-permute-start(bf16[384,768]{1,0:T(8,128)(2,1)S(1)} %convolution_convert_fusion.8), channel_id=1, source_target_pairs={{0,1},{1,0},{2,3},{3,2},{4,5},{5,4},{6,7},{7,6},{8,9},{9,8},{10,11... | collective-permute-start | bytes 1769480 | tf_op jit(solution)/shard_map/ppermute | solution.py:312
  270.6 12.0 %copy-start.7 = (bf16[1,384,768]{2,1,0:T(8,128)(2,1)S(1)}, bf16[1,384,768]{2,1,0:T(8,128)(2,1)}, u32[]{:S(2)}) copy-start(bf16[1,384,768]{2,1,0:T(8,128)(2,1)} %param.11) | copy-start | bytes 1769476
  270.6 12.1 %copy-start.55 = (f32[384]{0:T(512)S(1)}, f32[384]{0:T(512)}, u32[]{:S(2)}) copy-start(f32[384]{0:T(512)} %copy-done.54) | copy-start | bytes 4612
  270.6 12.1 %copy-start.67 = (f32[384]{0:T(512)S(1)}, f32[384]{0:T(512)}, u32[]{:S(2)}) copy-start(f32[384]{0:T(512)} %copy-done.66) | copy-start | bytes 4612
  270.6 12.5 %copy-start.22 = (f32[384,768]{1,0:T(8,128)S(1)}, f32[384,768]{1,0:T(8,128)}, u32[]{:S(2)}) copy-start(f32[384,768]{1,0:T(8,128)} %get-tuple-element.141) | copy-start | bytes 3538948
  275.6 8.9 %collective-permute-start.29 = (bf16[208,384]{1,0:T(8,128)(2,1)S(1)}, bf16[208,384]{1,0:T(8,128)(2,1)S(1)}, u32[]{:S(2)}, u32[]{:S(2)}) collective-permute-start(bf16[208,384]{1,0:T(8,128)(2,1)S(1)} %add_convert_fusion.17), channel_id=1, source_target_pairs={{0,8},{8,0},{16,24},{24,16},{1,9},{9,1},{17,25},{25,17},{2,10},{10... | collective-permute-start | bytes 479240 | tf_op jit(solution)/shard_map/ppermute | solution.py:391
  275.7 8.8 %collective-permute-start.30 = (bf16[208,384]{1,0:T(8,128)(2,1)S(1)}, bf16[208,384]{1,0:T(8,128)(2,1)S(1)}, u32[]{:S(2)}, u32[]{:S(2)}) collective-permute-start(bf16[208,384]{1,0:T(8,128)(2,1)S(1)} %add_convert_fusion.17), channel_id=1, source_target_pairs={{0,16},{8,24},{16,0},{24,8},{1,17},{9,25},{17,1},{25,9},{2,18},{10... | collective-permute-start | bytes 479240 | tf_op jit(solution)/shard_map/ppermute | solution.py:391
  276.3 8.8 %collective-permute-start.31 = (bf16[208,384]{1,0:T(8,128)(2,1)S(1)}, bf16[208,384]{1,0:T(8,128)(2,1)S(1)}, u32[]{:S(2)}, u32[]{:S(2)}) collective-permute-start(bf16[208,384]{1,0:T(8,128)(2,1)S(1)} %add_convert_fusion.17), channel_id=1, source_target_pairs={{0,24},{8,16},{16,8},{24,0},{1,25},{9,17},{17,9},{25,1},{2,26},{10... | collective-permute-start | bytes 479240 | tf_op jit(solution)/shard_map/ppermute | solution.py:391
  (46 other events, 112.0 us)

commit v5 on v4

--- a/solution.py
+++ b/solution.py
@@ -130,6 +130,58 @@
         compiler_params=params(),
         cost_estimate=cost(2, rows_p * rows_p + rows_c * (rows_p + rows_c), width, 10 * rows_c),
     )(own_p, own_p, own_p, own_c, own_c, own_c, bias)
+
+
+def middle_kernel(
+    k_ref, v_ref, bias_ref, qp_ref, partp_ref, statp_ref, qc_ref, partc_ref, statc_ref,
+    outp_ref, newp_ref, outc_ref, newc_ref,
+):
+    parts = (
+        (qp_ref, None, partp_ref, statp_ref, outp_ref, newp_ref),
+        (qc_ref, bias_ref, partc_ref, statc_ref, outc_ref, newc_ref),
+    )
+    for q_ref, b_ref, part_ref, stat_ref, out_ref, new_ref in parts:
+        outs = []
+        shrinks = []
+        for which in range(2):
+            mine = one_head(q_ref[0], which, HEAD ** (-0.5))
+            scores = masked_scores(k_ref[0], mine, None if b_ref is None else b_ref[...])
+            old = stat_ref[0, which : which + 1]
+            top = jnp.maximum(old, jnp.max(scores, axis=0, keepdims=True))
+            weights = jnp.exp(scores - top)
+            shrink = jnp.exp(old - top)
+            new_ref[0, which : which + 1] = top
+            new_ref[0, 2 + which : 3 + which] = shrink * stat_ref[
+                0, 2 + which : 3 + which
+            ] + jnp.sum(weights, axis=0, keepdims=True)
+            outs.append(tn(weights.astype(BF), v_ref[0]))
+            shrinks.append(shrink)
+        out_ref[...] = lane_pair(outs) + part_ref[...] * row_pair(shrinks)
+
+
+def attend_middle(own_p, own_c, far, bias, part_p, stat_p, part_c, stat_c):
+    width = own_p.shape[2]
+    specs = [kind_spec(far, 0), kind_spec(far, 1), bias_spec(bias)]
+    out_specs = []
+    outs = []
+    for own in (own_p, own_c):
+        rows = own.shape[1]
+        specs += [kind_spec(own, 0), full_spec(rows), stat_spec(rows)]
+        out_specs += [full_spec(rows), stat_spec(rows)]
+        outs += [
+            jax.ShapeDtypeStruct((rows, width), F32),
+            jax.ShapeDtypeStruct((width // LANES, 8, rows), F32),
+        ]
+    rows = own_p.shape[1] + own_c.shape[1]
+    return pl.pallas_call(
+        middle_kernel,
+        grid=(width // LANES,),
+        in_specs=specs,
+        out_specs=out_specs,
+        out_shape=outs,
+        compiler_params=params(),
+        cost_estimate=cost(2, rows * far.shape[1], width, 4 * far.shape[1]),
+    )(far, far, bias, own_p, part_p, stat_p, own_c, part_c, stat_c)
 
 
 def far_kernel(*refs, masked):
@@ -451,7 +503,8 @@
     direct = []
     for at in range(1, seq_n):
         direct.append(lax.ppermute(held, "seq", [(j, j ^ at) for j in range(seq_n)]))
-    pieces = direct + [swap(came, "tp", 0) for came in direct]
+    direct = lax.optimization_barrier(jnp.concatenate(direct, axis=0))
+    swapped = swap(direct, "tp", 0)
     starts = [
         (seq_i ^ at) * rows_p + part * half for part in (tp_i, 1 - tp_i) for at in range(1, seq_n)
     ]
@@ -463,6 +516,7 @@
         return jnp.broadcast_to(bias[:, None], (place.shape[0], LANES))
 
     bias_far = bias_of((jnp.stack(starts)[:, None] + inside[None, :]).reshape(-1))
+    away_rows = (seq_n - 1) * half
     bias_own = bias_of(seq_i * rows_p + jnp.arange(rows_p, dtype=jnp.int32))
 
     def project(rows):
@@ -480,30 +534,46 @@
     own_c = qkv(low_c, 0)
     own_p = qkv(low_p, 0)
     part_p, stat_p, part_c, stat_c = attend_near(own_p, own_c, bias_own)
-    _, one_f, _, low_f = project(after(jnp.concatenate(pieces, axis=0), part_c))
-    far = qkv(low_f, 1)
-
-    att_c, log_c = attend_far(own_c, far, bias_far, part_c, stat_c)
+    _, one_a, _, low_a = project(after(direct, part_c))
+    far_a = qkv(low_a, 1)
+    part_p, stat_p, part_c, stat_c = attend_middle(
+        own_p, own_c, far_a, bias_far[:away_rows], part_p, stat_p, part_c, stat_c
+    )
+    _, one_b, _, low_b = project(after(swapped, part_c))
+    far_b = qkv(low_b, 1)
+
+    att_c, log_c = attend_far(own_c, far_b, bias_far[away_rows:], part_c, stat_c)
     mixed_c = wide_dot(att_c, out_weight).astype(BF)
-    att_p, log_p = attend_far(own_p, far, None, after(part_p, mixed_c), stat_p)
+    att_p, log_p = attend_far(own_p, far_b, None, after(part_p, mixed_c), stat_p)
     mixed_p = wide_dot(att_p, out_weight).astype(BF)
-
-    def feed(tokens, mixed, cot):
-        resid = tokens + tp_sum(mixed)
+    cot_c = cont_cot[0, 0]
+    cot_p = prompt_cot[0]
+    mixed_other_c = swap(mixed_c, "tp", 0)
+    mixed_other_p = swap(mixed_p, "tp", 0)
+    held = [far_a, far_b, low_a, low_b, cot_c, cot_p]
+    far_a, far_b, low_a, low_b, early_c, early_p = all_after(held, mixed_p)
+    far = jnp.concatenate([far_a, far_b], axis=1)
+    low_f = jnp.concatenate([low_a, low_b], axis=0)
+    act_grad_c = back_dot(early_c, ffn_out)
+    act_grad_p = back_dot(early_p, ffn_out)
+    held = [mixed_other_c, far, low_f, act_grad_c, act_grad_p, bias_far]
+    mixed_other_c, far, low_f, act_grad_c, act_grad_p, bias_far = all_after(held)
+
+    def feed(tokens, mixed, mixed_other, act_grad):
+        resid = tokens + (mixed.astype(F32) + mixed_other.astype(F32))
         normed, inv = norm_parts(resid)
         low = (normed * gains[1] + shifts[1]).astype(BF)
         upper = wide_dot(low, ffn_in)
         activated, gelu_pull = jax.vjp(exact_gelu, upper)
-        act_grad = back_dot(cot, ffn_out)
         upper_grad = gelu_pull(act_grad)[0].astype(BF)
         terms = back_dot(upper_grad, ffn_in).astype(BF)
         return resid, normed, inv, low, activated.astype(BF), upper_grad, terms
 
-    cot_c = cont_cot[0, 0]
-    cot_p = prompt_cot[0]
-    resid_c, two_c, inv_two_c, mid_c, act_c, up_c, terms_two_c = feed(tokens_c, mixed_c, cot_c)
+    resid_c, two_c, inv_two_c, mid_c, act_c, up_c, terms_two_c = feed(
+        tokens_c, mixed_c, mixed_other_c, act_grad_c
+    )
     resid_p, two_p, inv_two_p, mid_p, act_p, up_p, terms_two_p = feed(
-        after(tokens_p, terms_two_c), mixed_p, cot_p
+        after(tokens_p, terms_two_c), mixed_p, mixed_other_p, act_grad_p
     )
     second_other = swap(terms_two_c, "tp", 0)
     second_other_p = swap(terms_two_p, "tp", 0)
@@ -549,10 +619,10 @@
         return jnp.einsum("cne,cde->nd", grads, weights, preferred_element_type=F32)
 
     terms_f = kv_terms(dkv_f, qkv_weight[1:])
-    gain_f = jnp.sum(terms_f * one_f, axis=0)
+    gain_f = jnp.sum(terms_f[:away_rows] * one_a, axis=0)
+    gain_f += jnp.sum(terms_f[away_rows:] * one_b, axis=0)
     shift_f = jnp.sum(terms_f, axis=0)
     terms_f = lax.optimization_barrier(terms_f.astype(BF))
-    away_rows = (seq_n - 1) * half
     swapped = swap(terms_f[away_rows:], "tp", 0)
     ffn_pair = all_after(ffn_pair, dkv_f)
     out_other_c = after(out_other_c, dkv_f)

time: 298 us -> 292 us (0.980)
  waiting for transfers between devices: 54.1 us -> 40.1 us
  Pallas kernels: 70.7 us -> 76.3 us
  other arithmetic: 43.3 us -> 46.5 us
    ppermute x23 -> x21, waiting for transfers between devices: 48.6 us -> 33.1 us  [swap(): return lax.ppermute(array, axis, [(j, j ^ 1 << bit) for j in range(count)])]
    pallas_call x0 -> x1, Pallas kernels: none -> 11.1 us  [attend_middle(): pl.pallas_call(middle_kernel, grid=(width // LANES,), in_specs=specs, out...]
    pallas_call x2, Pallas kernels: 19.5 us -> 13.7 us  [attend_far(): pl.pallas_call(functools.partial(far_kernel, masked=masked), grid=(width...]
    concatenate x0 -> x3, other arithmetic: none -> 3.93 us  [the longest x1 1.49 us: body(): far = jnp.concatenate([far_a, far_b], axis=1)]
    dot_general x3 -> x4, matrix products: 6.8 us -> 7.61 us  [qkv(): jnp.einsum('nd,cde->cne', low, qkv_weight[first:], preferred_element_type...]
    ppermute x23 -> x21, starting transfers between devices: 24.3 us -> 24.7 us  [swap(): return lax.ppermute(array, axis, [(j, j ^ 1 << bit) for j in range(count)])]
    unnamed x162 -> x173, local copies, waits for them, and re-layouts: 9.91 us -> 10.1 us
  transfers between devices with their start and end apart: 32 -> 30, of which waited for: 12 -> 13; matrix products, arithmetic and copies ran while one was open for 31% -> 32% of each run, Pallas kernels for 20% -> 24%
where the time goes in v5:
time: 292 us; the launch traced here: 287 us
  Pallas kernels  76.3 us (26%)
  matrix products  60.5 us (21%)
  other arithmetic  46.5 us (16%)
  waiting for transfers between devices  40.1 us (14%)
  starting transfers between devices  36.8 us (13%)
  local copies, waits for them, and re-layouts  24.1 us (8%)
  between operations  3.13 us (1%)
    ppermute x21, waiting for transfers between devices, swap(): return lax.ppermute(array, axis, [(j, j ^ 1 << bit) for j in range(count)])  33.1 us
    pallas_call x2, Pallas kernels, pull_far(): pl.pallas_call(functools.partial(pull_far_kernel, masked=masked, chunk=ch...  25.4 us
    dot_general x6, matrix products, wide_dot(): return jnp.dot(left, right, preferred_element_type=F32)  25 us
    ppermute x21, starting transfers between devices, swap(): return lax.ppermute(array, axis, [(j, j ^ 1 << bit) for j in range(count)])  24.7 us
    pallas_call x1, Pallas kernels, pull_near(): pl.pallas_call(pull_near_kernel, grid=(width // LANES,), in_specs=specs,...  14.8 us
    dot_general x8, matrix products, rows_dot(): return jnp.einsum('nd,nf->df', left, right, preferred_element_type=F32)  13.8 us
    pallas_call x2, Pallas kernels, attend_far(): pl.pallas_call(functools.partial(far_kernel, masked=masked), grid=(width...  13.7 us
    pallas_call x1, Pallas kernels, attend_near(): pl.pallas_call(near_kernel, grid=(width // LANES,), in_specs=[kind_spec(o...  11.4 us
  transfers between devices with their start and end apart: 30, of which 13 were waited for; matrix products, arithmetic and copies ran while one was open for 32% of the time, Pallas kernels for 24%

profile of v5, /device:TPU:0, one launch (start us, length us, event | category | flops | bytes accessed | tf_op | source)
XLA Modules:
  0.0 287.5 jit_solution(15102000876301482967)
XLA Ops:
  0.7 1.8 dynamic-slice_bitcast_fusion.7
  2.5 5.1 %collective-permute-start.2 = (bf16[192,768]{1,0:T(8,128)(2,1)}, bf16[192,768]{1,0:T(8,128)(2,1)S(1)}, u32[]{:S(2)}, u32[]{:S(2)}) collective-permute-start(bf16[192,768]{1,0:T(8,128)(2,1)} %dynamic-slice_bitcast_fusion.7), channel_id=1, source_target_pairs={{0,6},{2,4},{4,2},{6,0},{1,7},{3,5},{5,3},{7,1},{8,14},{10,12},{12... | collective-permute-start | bytes 884744 | tf_op jit(solution)/shard_map/ppermute | solution.py:505
  11.4 2.4 subtract_multiply_fusion.2
  13.7 1.5 fusion.34
  16.0 1.8 fusion.59.qp_ref.kp_ref.vp_ref.refs_0_
  17.8 2.2 fusion.48.qc_ref.kc_ref.vc_ref.refs_0_
  21.1 11.4 %shard_map.186 = (f32[384,384]{1,0:T(8,128)}, f32[3,8,384]{2,1,0:T(8,128)}, f32[512,384]{1,0:T(8,128)}, f32[3,8,512]{2,1,0:T(8,128)}) custom-call(bf16[3,384,384]{2,1,0:T(8,128)(2,1)} %fusion.59.qp_ref.kp_ref.vp_ref.refs_0_, bf16[3,384,384]{2,1,0:T(8,128)(2,1)} %fusion.59.qp_ref.kp_ref.vp_ref.refs_0_, ...), custom_call_target="tpu_custom_call" | custom-call | flops 1212416 | bytes 5120 | tf_op jit(solution)/shard_map/pallas_call | solution.py:122
  34.2 1.6 collective-permute-start.3
  37.2 1.8 fusion.65.k_ref.v_ref
  39.9 11.1 %shard_map.187 = (f32[384,384]{1,0:T(8,128)}, f32[3,8,384]{2,1,0:T(8,128)}, f32[512,384]{1,0:T(8,128)}, f32[3,8,512]{2,1,0:T(8,128)}) custom-call(bf16[2,576,384]{2,1,0:T(8,128)(2,1)} %fusion.65.k_ref.v_ref, bf16[2,576,384]{2,1,0:T(8,128)(2,1)} %fusion.65.k_ref.v_ref, f32[576,128]{1,0:T(8,128)} %broadcast_in_dim.37.bias_ref, ...), custom_call_target="tpu_custom_call" | custom-call | flops 1032192 | bytes 2304 | tf_op jit(solution)/shard_map/pallas_call | solution.py:176
  51.0 4.0 %collective-permute-done.3 = bf16[576,768]{1,0:T(8,128)(2,1)S(1)} collective-permute-done((bf16[576,768]{1,0:T(8,128)(2,1)S(1)}, bf16[576,768]{1,0:T(8,128)(2,1)S(1)}, u32[]{:S(2)}, u32[]{:S(2)}) %collective-permute-start.3) | collective-permute-done | bytes 884768 | tf_op jit(solution)/shard_map/ppermute | solution.py:364
  56.8 1.8 fusion.66.refs_1_.refs_2_
  59.4 7.5 %shard_map.188 = (bf16[512,384]{1,0:T(8,128)(2,1)}, f32[3,8,512]{2,1,0:T(8,128)}) custom-call(bf16[3,512,384]{2,1,0:T(8,128)(2,1)} %fusion.48.qc_ref.kc_ref.vc_ref.refs_0_, bf16[2,576,384]{2,1,0:T(8,128)(2,1)} %fusion.66.refs_1_.refs_2_, bf16[2,576,384]{2,1,0:T(8,128)(2,1)} %fusion.66.refs_1_.refs_2_, f32[576,128]{1,0:T(8,128)} %broadcast_in_dim.38.refs_3_, ...), custom_call_target="tpu_custom_call" | custom-call | flops 589824 | bytes 2304 | tf_op jit(solution)/shard_map/pallas_call | solution.py:222
  67.0 2.4 convolution_convert_fusion.8
  69.4 1.5 collective-permute-start.4
  71.0 6.2 %shard_map.189 = (bf16[384,384]{1,0:T(8,128)(2,1)}, f32[3,8,384]{2,1,0:T(8,128)}) custom-call(bf16[3,384,384]{2,1,0:T(8,128)(2,1)} %fusion.59.qp_ref.kp_ref.vp_ref.refs_0_, bf16[2,576,384]{2,1,0:T(8,128)(2,1)} %fusion.66.refs_1_.refs_2_, bf16[2,576,384]{2,1,0:T(8,128)(2,1)} %fusion.66.refs_1_.refs_2_, f32[384,384]{1,0:T(8,128)} %get-tuple-element.91.refs_3_, ...), custom_call_target="tpu_custom_call" | custom-call | flops 442368 | bytes 2304 | tf_op jit(solution)/shard_map/pallas_call | solution.py:222
  77.1 1.4 convolution_convert_fusion.12
  79.1 1.5 pad_maximum_fusion.refs_1_.refs_2_
  84.3 1.4 fusion.122
  85.7 4.5 %collective-permute-done.4 = bf16[512,768]{1,0:T(8,128)(2,1)} collective-permute-done((bf16[512,768]{1,0:T(8,128)(2,1)}, bf16[512,768]{1,0:T(8,128)(2,1)}, u32[]{:S(2)}, u32[]{:S(2)}) %collective-permute-start.4) | collective-permute-done | bytes 786464 | tf_op jit(solution)/shard_map/ppermute | solution.py:364
  91.2 1.7 fusion.118
  94.5 8.3 %multiply_convert_fusion = (bf16[512,1536]{1,0:T(8,128)(2,1)S(1)}, f32[512,1536]{1,0:T(8,128)S(1)}, f32[512,1536]{1,0:T(8,128)S(1)}) fusion(bf16[512,768]{1,0:T(8,128)(2,1)S(1)} %add_convert_fusion.7, bf16[768,1536]{1,0:T(8,128)(2,1)S(1)} %copy-done), kind=kOutput, calls=%fused_computation.12 | convolution fusion | flops 1259077632 | bytes 11010048 | tf_op jit(solution)/shard_map/dot_general | solution.py:405
  104.1 1.4 convolution_convert_fusion.7
  105.5 1.6 collective-permute-start.7
  108.0 6.5 %multiply_convert_fusion.1 = (bf16[384,1536]{1,0:T(8,128)(2,1)S(1)}, f32[384,1536]{1,0:T(8,128)S(1)}, f32[384,1536]{1,0:T(8,128)S(1)}) fusion(bf16[384,768]{1,0:T(8,128)(2,1)S(1)} %add_convert_fusion.13, bf16[768,1536]{1,0:T(8,128)(2,1)S(1)} %copy-done), kind=kOutput, calls=%fused_computation.48 | convolution fusion | flops 944308224 | bytes 8847360 | tf_op jit(solution)/shard_map/dot_general | solution.py:405
  114.5 3.2 %convolution_convert_fusion = bf16[768,1536]{1,0:T(8,128)(2,1)S(1)} fusion(bf16[512,1536]{1,0:T(8,128)(2,1)S(1)} %get-tuple-element.113, bf16[384,1536]{1,0:T(8,128)(2,1)S(1)} %get-tuple-element.136, bf16[512,768]{1,0:T(8,128)(2,1)S(1)} %bitcast.261, bf16[384,768]{1,0:T(8,128)(2,1)S(1)} %bitcast.271), kind=kOutput, calls=%fused_computation.9 | convolution fusion | flops 2123366400 | bytes 6488064 | tf_op jit(solution)/shard_map/nd,nf->df/dot_general | solution.py:413
  119.9 2.9 %convolution_convert_fusion.1 = bf16[768,1536]{1,0:T(8,128)(2,1)S(1)} fusion(bf16[512,1536]{1,0:T(8,128)(2,1)S(1)} %add_convert_fusion, bf16[384,1536]{1,0:T(8,128)(2,1)S(1)} %add_convert_fusion.3, bf16[512,768]{1,0:T(8,128)(2,1)S(1)} %add_convert_fusion.7, bf16[384,768]{1,0:T(8,128)(2,1)S(1)} %add_convert_fusion.13), kind=kOutput, calls=%fused_computation.10 | convolution fusion | flops 2123366400 | bytes 6488064 | tf_op jit(solution)/shard_map/nd,nf->df/dot_general | solution.py:413
  122.9 1.9 fusion.16
  125.2 2.5 convolution_convert_fusion.10
  127.7 1.6 collective-permute-start.6
  130.1 2.3 fusion
  132.4 2.0 fusion.47
  134.7 1.6 collective-permute-start.9
  136.2 3.0 %fusion.114 = (bf16[512,768]{1,0:T(8,128)(2,1)S(1)}, f32[512,768]{1,0:T(8,128)}) fusion(f32[512]{0:T(512)S(1)} %broadcast_multiply_fusion.10, f32[512,768]{1,0:T(8,128)S(1)} %copy-done.3, f32[512]{0:T(512)S(1)} %copy-done.56, f32[512]{0:T(512)S(1)} %broadcast_multiply_fusion.11, f32[768]{0:T(1024)S(1)} %get-tuple-element.238, ...), kind=kLoop, calls=%fused_computation.313 | loop fusion | flops 5111808 | bytes 6302720 | tf_op jit(solution)/shard_map/convert_element_type | solution.py:593
  140.2 1.4 convolution_convert_fusion.13.refs_4_.doc_ref
  141.6 14.0 %shard_map.190 = (f32[512,384]{1,0:T(8,128)}, f32[2,1152,384]{2,1,0:T(8,128)}) custom-call(bf16[3,512,384]{2,1,0:T(8,128)(2,1)} %fusion.48.qc_ref.kc_ref.vc_ref.refs_0_, bf16[2,1152,384]{2,1,0:T(8,128)(2,1)} %pad_maximum_fusion.refs_1_.refs_2_, bf16[2,1152,384]{2,1,0:T(8,128)(2,1)} %pad_maximum_fusion.refs_1_.refs_2_, f32[1152,128]{1,0:T(8,128)} %broadcast_in_dim.39.refs_3_, ...), custom_call_target="tpu_custom_call" | custom-call | flops 2949120 | bytes 9216 | tf_op jit(solution)/shard_map/pallas_call | solution.py:310
  155.6 4.4 %convolution_convert_fusion.6 = bf16[512,768]{1,0:T(8,128)(2,1)} fusion(bf16[512,1536]{1,0:T(8,128)(2,1)} %copy-done.85, bf16[1536,768]{1,0:T(8,128)(2,1)} %param.19), kind=kOutput, calls=%fused_computation.118 | convolution fusion | flops 1208352768 | bytes 4718592 | tf_op jit(solution)/shard_map/dot_general | solution.py:405
  160.0 1.5 collective-permute-start.13
  164.2 1.7 fusion.113
  170.5 11.4 %shard_map.191 = (f32[384,384]{1,0:T(8,128)}, bf16[2,1152,384]{2,1,0:T(8,128)(2,1)}) custom-call(bf16[3,384,384]{2,1,0:T(8,128)(2,1)} %fusion.59.qp_ref.kp_ref.vp_ref.refs_0_, bf16[2,1152,384]{2,1,0:T(8,128)(2,1)} %pad_maximum_fusion.refs_1_.refs_2_, bf16[2,1152,384]{2,1,0:T(8,128)(2,1)} %pad_maximum_fusion.refs_1_.refs_2_, ...), custom_call_target="tpu_custom_call" | custom-call | flops 2211840 | bytes 9216 | tf_op jit(solution)/shard_map/pallas_call | solution.py:310
  181.9 3.1 %fusion.120 = (f32[768]{0:T(1024)S(1)}, bf16[1152,768]{1,0:T(8,128)(2,1)S(1)}, f32[1152,768]{1,0:T(8,128)S(1)}) fusion(bf16[2,1152,384]{2,1,0:T(8,128)(2,1)} %get-tuple-element.117, bf16[3,768,384]{2,1,0:T(8,128)(2,1)S(1)} %copy-done.80), kind=kOutput, calls=%fused_computation.316 | convolution fusion | flops 1360723200 | bytes 8260608 | tf_op jit(solution)/shard_map/cne,cde->nd/dot_general | solution.py:619
  185.1 1.6 collective-permute-start.10
  187.6 2.1 collective-permute-start.12
  190.4 14.8 %shard_map.192 = bf16[3,896,384]{2,1,0:T(8,128)(2,1)} custom-call(bf16[3,384,384]{2,1,0:T(8,128)(2,1)} %fusion.59.qp_ref.kp_ref.vp_ref.refs_0_, bf16[3,384,384]{2,1,0:T(8,128)(2,1)} %fusion.59.qp_ref.kp_ref.vp_ref.refs_0_, bf16[3,384,384]{2,1,0:T(8,128)(2,1)} %fusion.59.qp_ref.kp_ref.vp_ref.refs_0_, ...), custom_call_target="tpu_custom_call" | custom-call | flops 3031040 | bytes 5120 | tf_op jit(solution)/shard_map/pallas_call | solution.py:351
  205.8 2.4 convolution_convert_fusion.11
  215.8 2.0 bitcast_convert_fusion
  219.4 1.6 collective-permute-start.19
  222.6 1.6 collective-permute-start.14
  224.7 3.0 %collective-permute-done.19 = bf16[2,48,1536]{2,1,0:T(8,128)(2,1)S(1)} collective-permute-done((bf16[2,48,1536]{2,1,0:T(8,128)(2,1)S(1)}, bf16[2,48,1536]{2,1,0:T(8,128)(2,1)S(1)}, u32[]{:S(2)}, u32[]{:S(2)}) %collective-permute-start.19) | collective-permute-done | bytes 294944 | tf_op jit(solution)/shard_map/ppermute | solution.py:364
  228.8 6.7 %collective-permute-done.16 = bf16[2,192,768]{2,1,0:T(8,128)(2,1)S(1)} collective-permute-done((bf16[2,192,768]{2,1,0:T(8,128)(2,1)S(1)}, bf16[2,192,768]{2,1,0:T(8,128)(2,1)S(1)}, u32[]{:S(2)}, u32[]{:S(2)}) %collective-permute-start.16) | collective-permute-done | bytes 589856 | tf_op jit(solution)/shard_map/ppermute | solution.py:364
  236.0 2.2 collective-permute-start.18
  238.2 2.5 fusion.83
  240.7 9.5 %collective-permute-done.18 = bf16[1,192,768]{2,1,0:T(8,128)(2,1)S(1)} collective-permute-done((bf16[1,192,768]{2,1,0:T(8,128)(2,1)S(1)}, bf16[1,192,768]{2,1,0:T(8,128)(2,1)S(1)}, u32[]{:S(2)}, u32[]{:S(2)}) %collective-permute-start.18) | collective-permute-done | bytes 294944 | tf_op jit(solution)/shard_map/ppermute | solution.py:364
  252.1 1.5 collective-permute-start.22
  253.6 1.9 convolution_convert_fusion.9
  256.1 3.0 %collective-permute-start.25 = (bf16[208,384]{1,0:T(8,128)(2,1)S(1)}, bf16[208,384]{1,0:T(8,128)(2,1)S(1)}, u32[]{:S(2)}, u32[]{:S(2)}) collective-permute-start(bf16[208,384]{1,0:T(8,128)(2,1)S(1)} %pad_maximum_fusion.13), channel_id=1, source_target_pairs={{0,4},{2,6},{4,0},{6,2},{1,5},{3,7},{5,1},{7,3},{8,12},{10,14},{12... | collective-permute-start | bytes 479240 | tf_op jit(solution)/shard_map/ppermute | solution.py:719
  259.1 1.5 collective-permute-start.26
  263.2 1.6 slice_bitcast_fusion
  265.9 1.6 fusion.84
  267.5 3.2 %collective-permute-done.25 = bf16[208,384]{1,0:T(8,128)(2,1)S(1)} collective-permute-done((bf16[208,384]{1,0:T(8,128)(2,1)S(1)}, bf16[208,384]{1,0:T(8,128)(2,1)S(1)}, u32[]{:S(2)}, u32[]{:S(2)}) %collective-permute-start.25) | collective-permute-done | bytes 159776 | tf_op jit(solution)/shard_map/ppermute | solution.py:719
  270.9 1.6 collective-permute-start.28
  272.7 1.8 collective-permute-done.23
  277.4 3.3 %collective-permute-done.28 = bf16[208,384]{1,0:T(8,128)(2,1)S(1)} collective-permute-done((bf16[208,384]{1,0:T(8,128)(2,1)S(1)}, bf16[208,384]{1,0:T(8,128)(2,1)S(1)}, u32[]{:S(2)}, u32[]{:S(2)}) %collective-permute-start.28) | collective-permute-done | bytes 159776 | tf_op jit(solution)/shard_map/ppermute | solution.py:443
  285.1 2.1 slice.227
  (347 shorter events, 60.6 us)
Async XLA Ops:
  0.6 93.8 %copy-start = (bf16[768,1536]{1,0:T(8,128)(2,1)S(1)}, bf16[768,1536]{1,0:T(8,128)(2,1)}, u32[]{:S(2)}) copy-start(bf16[768,1536]{1,0:T(8,128)(2,1)} %param.18) | copy-start | bytes 7077892
  0.7 9.5 %copy-start.4 = (bf16[1,1,512,768]{3,2,1,0:T(8,128)(2,1)S(1)}, bf16[1,1,512,768]{3,2,1,0:T(8,128)(2,1)}, u32[]{:S(2)}) copy-start(bf16[1,1,512,768]{3,2,1,0:T(8,128)(2,1)} %param.12) | copy-start | bytes 2359300
  0.7 10.4 %copy-start.73 = (bf16[2,768]{1,0:T(2,128)(2,1)S(1)}, bf16[2,768]{1,0:T(2,128)(2,1)}, u32[]{:S(2)}) copy-start(bf16[2,768]{1,0:T(2,128)(2,1)} %param.20) | copy-start | bytes 9220
  0.7 10.4 %copy-start.74 = (bf16[2,768]{1,0:T(2,128)(2,1)S(1)}, bf16[2,768]{1,0:T(2,128)(2,1)}, u32[]{:S(2)}) copy-start(bf16[2,768]{1,0:T(2,128)(2,1)} %param.21) | copy-start | bytes 9220
  2.5 30.0 %collective-permute-start.2 = (bf16[192,768]{1,0:T(8,128)(2,1)}, bf16[192,768]{1,0:T(8,128)(2,1)S(1)}, u32[]{:S(2)}, u32[]{:S(2)}) collective-permute-start(bf16[192,768]{1,0:T(8,128)(2,1)} %dynamic-slice_bitcast_fusion.7), channel_id=1, source_target_pairs={{0,6},{2,4},{4,2},{6,0},{1,7},{3,5},{5,3},{7,1},{8,14},{10,12},{12... | collective-permute-start | bytes 884744 | tf_op jit(solution)/shard_map/ppermute | solution.py:505
  7.6 25.4 %collective-permute-start.1 = (bf16[192,768]{1,0:T(8,128)(2,1)}, bf16[192,768]{1,0:T(8,128)(2,1)}, u32[]{:S(2)}, u32[]{:S(2)}) collective-permute-start(bf16[192,768]{1,0:T(8,128)(2,1)} %dynamic-slice_bitcast_fusion.7), channel_id=1, source_target_pairs={{0,4},{2,6},{4,0},{6,2},{1,5},{3,7},{5,1},{7,3},{8,12},{10,14},{12... | collective-permute-start | bytes 884744 | tf_op jit(solution)/shard_map/ppermute | solution.py:505
  7.6 25.4 %collective-permute-start = (bf16[192,768]{1,0:T(8,128)(2,1)}, bf16[192,768]{1,0:T(8,128)(2,1)}, u32[]{:S(2)}, u32[]{:S(2)}) collective-permute-start(bf16[192,768]{1,0:T(8,128)(2,1)} %dynamic-slice_bitcast_fusion.7), channel_id=1, source_target_pairs={{0,2},{2,0},{4,6},{6,4},{1,3},{3,1},{5,7},{7,5},{8,10},{10,8},{12,... | collective-permute-start | bytes 884744 | tf_op jit(solution)/shard_map/ppermute | solution.py:505
  11.3 82.0 %copy-start.59 = (f32[768]{0:T(1024)}, f32[768]{0:T(1024)S(1)}, u32[]{:S(2)}) copy-start(f32[768]{0:T(1024)S(1)} %get-tuple-element.172) | copy-start | bytes 9220
  21.1 11.4 %copy-start.7 = (bf16[1,384,768]{2,1,0:T(8,128)(2,1)S(1)}, bf16[1,384,768]{2,1,0:T(8,128)(2,1)}, u32[]{:S(2)}) copy-start(bf16[1,384,768]{2,1,0:T(8,128)(2,1)} %param.11) | copy-start | bytes 1769476
  34.2 20.8 %collective-permute-start.3 = (bf16[576,768]{1,0:T(8,128)(2,1)S(1)}, bf16[576,768]{1,0:T(8,128)(2,1)S(1)}, u32[]{:S(2)}, u32[]{:S(2)}) collective-permute-start(bf16[576,768]{1,0:T(8,128)(2,1)S(1)} %pad_maximum_fusion.4), channel_id=1, source_target_pairs={{0,1},{1,0},{2,3},{3,2},{4,5},{5,4},{6,7},{7,6},{8,9},{9,8},{10,11... | collective-permute-start | bytes 2654216 | tf_op jit(solution)/shard_map/ppermute | solution.py:364
  59.4 7.5 %copy-start.23 = (bf16[384,768]{1,0:T(8,128)(2,1)S(1)}, bf16[384,768]{1,0:T(8,128)(2,1)}, u32[]{:S(2)}) copy-start(bf16[384,768]{1,0:T(8,128)(2,1)} %param.17) | copy-start | bytes 1769476
  69.4 20.7 %collective-permute-start.4 = (bf16[512,768]{1,0:T(8,128)(2,1)}, bf16[512,768]{1,0:T(8,128)(2,1)}, u32[]{:S(2)}, u32[]{:S(2)}) collective-permute-start(bf16[512,768]{1,0:T(8,128)(2,1)} %convolution_convert_fusion.8), channel_id=1, source_target_pairs={{0,1},{1,0},{2,3},{3,2},{4,5},{5,4},{6,7},{7,6},{8,9},{9,8},{10,11... | collective-permute-start | bytes 2359304 | tf_op jit(solution)/shard_map/ppermute | solution.py:364
  70.9 8.2 %copy-start.9 = (bf16[2,576,384]{2,1,0:T(8,128)(2,1)S(1)}, bf16[2,576,384]{2,1,0:T(8,128)(2,1)}, u32[]{:S(2)}) copy-start(bf16[2,576,384]{2,1,0:T(8,128)(2,1)} %fusion.66.refs_1_.refs_2_) | copy-start | bytes 2654212
  71.0 8.2 %copy-start.18 = (bf16[2,576,384]{2,1,0:T(8,128)(2,1)S(1)}, bf16[2,576,384]{2,1,0:T(8,128)(2,1)}, u32[]{:S(2)}) copy-start(bf16[2,576,384]{2,1,0:T(8,128)(2,1)} %fusion.65.k_ref.v_ref) | copy-start | bytes 2654212
  78.5 28.6 %collective-permute-start.5 = (bf16[384,768]{1,0:T(8,128)(2,1)S(1)}, bf16[384,768]{1,0:T(8,128)(2,1)S(1)}, u32[]{:S(2)}, u32[]{:S(2)}) collective-permute-start(bf16[384,768]{1,0:T(8,128)(2,1)S(1)} %convolution_convert_fusion.12), channel_id=1, source_target_pairs={{0,1},{1,0},{2,3},{3,2},{4,5},{5,4},{6,7},{7,6},{8,9},{9,8},{10,11... | collective-permute-start | bytes 1769480 | tf_op jit(solution)/shard_map/ppermute | solution.py:364
  93.3 9.5 %copy-start.69 = (f32[512]{0:T(512)}, f32[512]{0:T(512)S(1)}, u32[]{:S(2)}) copy-start(f32[512]{0:T(512)S(1)} %add_rsqrt_fusion.3) | copy-start | bytes 6148
  102.8 11.8 %copy-start.85 = (bf16[512,1536]{1,0:T(8,128)(2,1)}, bf16[512,1536]{1,0:T(8,128)(2,1)S(1)}, u32[]{:S(2)}) copy-start(bf16[512,1536]{1,0:T(8,128)(2,1)S(1)} %get-tuple-element.113) | copy-start | bytes 4718596
  105.5 14.4 %collective-permute-start.7 = (bf16[512,768]{1,0:T(8,128)(2,1)S(1)}, bf16[512,768]{1,0:T(8,128)(2,1)}, u32[]{:S(2)}, u32[]{:S(2)}) collective-permute-start(bf16[512,768]{1,0:T(8,128)(2,1)S(1)} %convolution_convert_fusion.7), channel_id=1, source_target_pairs={{0,1},{1,0},{2,3},{3,2},{4,5},{5,4},{6,7},{7,6},{8,9},{9,8},{10,11... | collective-permute-start | bytes 2359304 | tf_op jit(solution)/shard_map/ppermute | solution.py:364
  107.4 7.1 %copy-start.53 = (f32[384]{0:T(512)}, f32[384]{0:T(512)S(1)}, u32[]{:S(2)}) copy-start(f32[384]{0:T(512)S(1)} %broadcast_multiply_fusion.6) | copy-start | bytes 4612
  107.7 6.8 %copy-start.67 = (f32[384]{0:T(512)}, f32[384]{0:T(512)S(1)}, u32[]{:S(2)}) copy-start(f32[384]{0:T(512)S(1)} %add_rsqrt_fusion.2) | copy-start | bytes 4612
  117.7 5.2 %copy-start.14 = (bf16[768,1536]{1,0:T(8,128)(2,1)}, bf16[768,1536]{1,0:T(8,128)(2,1)S(1)}, u32[]{:S(2)}) copy-start(bf16[768,1536]{1,0:T(8,128)(2,1)S(1)} %convolution_convert_fusion) | copy-start | bytes 7077892
  125.2 4.9 %collective-permute-start.8 = (bf16[2,2,2,2,48,1536]{5,4,3,2,1,0:T(8,128)(2,1)}, bf16[2,2,2,2,48,1536]{5,4,3,2,1,0:T(8,128)(2,1)}, u32[]{:S(2)}, u32[]{:S(2)}) collective-permute-start(bf16[2,2,2,2,48,1536]{5,4,3,2,1,0:T(8,128)(2,1)} %fusion.16), channel_id=1, source_target_pairs={{0,8},{8,0},{16,24},{24,16},{1,9},{9,1},{17,25},{25,17},{2,10},{10... | collective-permute-start | bytes 7077896 | tf_op jit(solution)/shard_map/ppermute | solution.py:364
  125.2 4.9 %copy-start.15 = (bf16[768,1536]{1,0:T(8,128)(2,1)S(1)}, bf16[768,1536]{1,0:T(8,128)(2,1)}, u32[]{:S(2)}) copy-start(bf16[768,1536]{1,0:T(8,128)(2,1)} %copy-done.14) | copy-start | bytes 7077892
  125.2 4.9 %copy-start.17 = (bf16[768,1536]{1,0:T(8,128)(2,1)S(1)}, bf16[768,1536]{1,0:T(8,128)(2,1)}, u32[]{:S(2)}) copy-start(bf16[768,1536]{1,0:T(8,128)(2,1)} %copy-done.16) | copy-start | bytes 7077892
  127.7 4.7 %copy-start.3 = (f32[512,768]{1,0:T(8,128)S(1)}, f32[512,768]{1,0:T(8,128)}, u32[]{:S(2)}) copy-start(f32[512,768]{1,0:T(8,128)} %copy-done.2) | copy-start | bytes 4718596
  127.7 4.7 %copy-start.31 = (bf16[512,768]{1,0:T(8,128)(2,1)S(1)}, bf16[512,768]{1,0:T(8,128)(2,1)}, u32[]{:S(2)}) copy-start(bf16[512,768]{1,0:T(8,128)(2,1)} %copy-done.30) | copy-start | bytes 2359300
  127.7 4.7 %copy-start.56 = (f32[512]{0:T(512)S(1)}, f32[512]{0:T(512)}, u32[]{:S(2)}) copy-start(f32[512]{0:T(512)} %copy-done.55) | copy-start | bytes 6148
  127.7 4.7 %copy-start.70 = (f32[512]{0:T(512)S(1)}, f32[512]{0:T(512)}, u32[]{:S(2)}) copy-start(f32[512]{0:T(512)} %copy-done.69) | copy-start | bytes 6148
  127.7 35.3 %collective-permute-start.6 = (bf16[384,768]{1,0:T(8,128)(2,1)S(1)}, bf16[384,768]{1,0:T(8,128)(2,1)S(1)}, u32[]{:S(2)}, u32[]{:S(2)}) collective-permute-start(bf16[384,768]{1,0:T(8,128)(2,1)S(1)} %convolution_convert_fusion.10), channel_id=1, source_target_pairs={{0,1},{1,0},{2,3},{3,2},{4,5},{5,4},{6,7},{7,6},{8,9},{9,8},{10,11... | collective-permute-start | bytes 1769480 | tf_op jit(solution)/shard_map/ppermute | solution.py:364
  134.7 28.1 %collective-permute-start.9 = (bf16[2,2,2,48,1536]{4,3,2,1,0:T(8,128)(2,1)S(1)}, bf16[2,2,2,48,1536]{4,3,2,1,0:T(8,128)(2,1)S(1)}, u32[]{:S(2)}, u32[]{:S(2)}) collective-permute-start(bf16[2,2,2,48,1536]{4,3,2,1,0:T(8,128)(2,1)S(1)} %get-tuple-element.190), channel_id=1, source_target_pairs={{0,16},{8,24},{16,0},{24,8},{1,17},{9,25},{17,1},{25,9},{2,18},{10... | collective-permute-start | bytes 3538952 | tf_op jit(solution)/shard_map/ppermute | solution.py:364
  160.0 21.8 %collective-permute-start.13 = (bf16[512,768]{1,0:T(8,128)(2,1)}, bf16[512,768]{1,0:T(8,128)(2,1)}, u32[]{:S(2)}, u32[]{:S(2)}) collective-permute-start(bf16[512,768]{1,0:T(8,128)(2,1)} %convolution_convert_fusion.6), channel_id=1, source_target_pairs={{0,1},{1,0},{2,3},{3,2},{4,5},{5,4},{6,7},{7,6},{8,9},{9,8},{10,11... | collective-permute-start | bytes 2359304 | tf_op jit(solution)/shard_map/ppermute | solution.py:364
  167.9 18.8 %collective-permute-start.11 = (bf16[2,2,48,1536]{3,2,0,1:T(8,128)(2,1)}, bf16[2,2,48,1536]{3,2,0,1:T(8,128)(2,1)S(1)}, u32[]{:S(2)}, u32[]{:S(2)}) collective-permute-start(bf16[2,2,48,1536]{3,2,0,1:T(8,128)(2,1)} %bitcast.223), channel_id=1, source_target_pairs={{0,2},{2,0},{4,6},{6,4},{1,3},{3,1},{5,7},{7,5},{8,10},{10,8},{12,... | collective-permute-start | bytes 1769480 | tf_op jit(solution)/shard_map/ppermute | solution.py:364
  170.5 11.4 %copy-start.80 = (bf16[3,768,384]{2,1,0:T(8,128)(2,1)S(1)}, bf16[3,768,384]{2,1,0:T(8,128)(2,1)}, u32[]{:S(2)}) copy-start(bf16[3,768,384]{2,1,0:T(8,128)(2,1)} %param.16) | copy-start | bytes 5308420
  185.1 4.7 %copy-start.11 = (bf16[576,768]{1,0:T(8,128)(2,1)S(1)}, bf16[576,768]{1,0:T(8,128)(2,1)}, u32[]{:S(2)}) copy-start(bf16[576,768]{1,0:T(8,128)(2,1)} %copy-done.10) | copy-start | bytes 2654212
  185.1 4.7 %copy-start.13 = (bf16[576,768]{1,0:T(8,128)(2,1)S(1)}, bf16[576,768]{1,0:T(8,128)(2,1)}, u32[]{:S(2)}) copy-start(bf16[576,768]{1,0:T(8,128)(2,1)} %copy-done.12) | copy-start | bytes 2654212
  185.1 20.6 %collective-permute-start.10 = (bf16[576,768]{1,0:T(8,128)(2,1)S(1)}, bf16[576,768]{1,0:T(8,128)(2,1)S(1)}, u32[]{:S(2)}, u32[]{:S(2)}) collective-permute-start(bf16[576,768]{1,0:T(8,128)(2,1)S(1)} %slice.215), channel_id=1, source_target_pairs={{0,1},{1,0},{2,3},{3,2},{4,5},{5,4},{6,7},{7,6},{8,9},{9,8},{10,11... | collective-permute-start | bytes 2654216 | tf_op jit(solution)/shard_map/ppermute | solution.py:364
  187.6 17.6 %collective-permute-start.12 = (bf16[2,48,1536]{2,1,0:T(8,128)(2,1)}, bf16[2,48,1536]{2,1,0:T(8,128)(2,1)}, u32[]{:S(2)}, u32[]{:S(2)}) collective-permute-start(bf16[2,48,1536]{2,1,0:T(8,128)(2,1)} %get-tuple-element.224), channel_id=1, source_target_pairs={{0,4},{2,6},{4,0},{6,2},{1,5},{3,7},{5,1},{7,3},{8,12},{10,14},{12... | collective-permute-start | bytes 884744 | tf_op jit(solution)/shard_map/ppermute | solution.py:364
  190.4 15.3 %copy-start.40 = (bf16[512,768]{1,0:T(8,128)(2,1)S(1)}, bf16[512,768]{1,0:T(8,128)(2,1)}, u32[]{:S(2)}) copy-start(bf16[512,768]{1,0:T(8,128)(2,1)} %copy-done.39) | copy-start | bytes 2359300
  214.6 13.3 %collective-permute-start.17 = (bf16[4,2,2,2,48,384]{5,4,2,1,0,3:T(8,128)(2,1)S(1)}, bf16[4,2,2,2,48,384]{5,4,2,1,0,3:T(8,128)(2,1)S(1)}, u32[]{:S(2)}, u32[]{:S(2)}) collective-permute-start(bf16[4,2,2,2,48,384]{5,4,2,1,0,3:T(8,128)(2,1)S(1)} %pad_maximum_fusion.3), channel_id=1, source_target_pairs={{0,8},{8,0},{16,24},{24,16},{1,9},{9,1},{17,25},{25,17},{2,10},{10... | collective-permute-start | bytes 3538952 | tf_op jit(solution)/shard_map/ppermute | solution.py:364
  219.4 8.4 %collective-permute-start.19 = (bf16[2,48,1536]{2,1,0:T(8,128)(2,1)S(1)}, bf16[2,48,1536]{2,1,0:T(8,128)(2,1)S(1)}, u32[]{:S(2)}, u32[]{:S(2)}) collective-permute-start(bf16[2,48,1536]{2,1,0:T(8,128)(2,1)S(1)} %add_convert_fusion.15), channel_id=1, source_target_pairs={{0,16},{8,24},{16,0},{24,8},{1,17},{9,25},{17,1},{25,9},{2,18},{10... | collective-permute-start | bytes 884744 | tf_op jit(solution)/shard_map/ppermute | solution.py:364
  221.0 14.4 %collective-permute-start.16 = (bf16[2,192,768]{2,1,0:T(8,128)(2,1)S(1)}, bf16[2,192,768]{2,1,0:T(8,128)(2,1)S(1)}, u32[]{:S(2)}, u32[]{:S(2)}) collective-permute-start(bf16[2,192,768]{2,1,0:T(8,128)(2,1)S(1)} %pad_maximum_fusion.5), channel_id=1, source_target_pairs={{0,2},{2,0},{4,6},{6,4},{1,3},{3,1},{5,7},{7,5},{8,10},{10,8},{12,... | collective-permute-start | bytes 1769480 | tf_op jit(solution)/shard_map/ppermute | solution.py:364
  222.6 27.9 %copy-start.19 = (bf16[528,768]{1,0:T(8,128)(2,1)}, bf16[528,768]{1,0:T(8,128)(2,1)S(1)}, u32[]{:S(2)}) copy-start(bf16[528,768]{1,0:T(8,128)(2,1)S(1)} %fusion.82) | copy-start | bytes 2433028
  222.6 27.8 %collective-permute-start.14 = (bf16[192,768]{1,0:T(8,128)(2,1)S(1)}, bf16[192,768]{1,0:T(8,128)(2,1)S(1)}, u32[]{:S(2)}, u32[]{:S(2)}) collective-permute-start(bf16[192,768]{1,0:T(8,128)(2,1)S(1)} %dynamic-slice_bitcast_fusion.4), channel_id=1, source_target_pairs={{0,1},{1,0},{2,3},{3,2},{4,5},{5,4},{6,7},{7,6},{8,9},{9,8},{10,11... | collective-permute-start | bytes 884744 | tf_op jit(solution)/shard_map/ppermute | solution.py:364
  224.2 26.2 %collective-permute-start.15 = (bf16[528,768]{1,0:T(8,128)(2,1)S(1)}, bf16[528,768]{1,0:T(8,128)(2,1)S(1)}, u32[]{:S(2)}, u32[]{:S(2)}) collective-permute-start(bf16[528,768]{1,0:T(8,128)(2,1)S(1)} %fusion.82), channel_id=1, source_target_pairs={{0,1},{1,0},{2,3},{3,2},{4,5},{5,4},{6,7},{7,6},{8,9},{9,8},{10,11... | collective-permute-start | bytes 2433032 | tf_op jit(solution)/shard_map/ppermute | solution.py:364
  227.8 22.6 %collective-permute-start.20 = (bf16[2,96,1536]{2,1,0:T(8,128)(2,1)S(1)}, bf16[2,96,1536]{2,1,0:T(8,128)(2,1)S(1)}, u32[]{:S(2)}, u32[]{:S(2)}) collective-permute-start(bf16[2,96,1536]{2,1,0:T(8,128)(2,1)S(1)} %pad_maximum_fusion.6), channel_id=1, source_target_pairs={{0,8},{8,0},{16,24},{24,16},{1,9},{9,1},{17,25},{25,17},{2,10},{10... | collective-permute-start | bytes 1769480 | tf_op jit(solution)/shard_map/ppermute | solution.py:364
  235.4 14.9 %collective-permute-start.21 = (bf16[4,2,2,48,384]{4,3,2,1,0:T(8,128)(2,1)S(1)}, bf16[4,2,2,48,384]{4,3,2,1,0:T(8,128)(2,1)S(1)}, u32[]{:S(2)}, u32[]{:S(2)}) collective-permute-start(bf16[4,2,2,48,384]{4,3,2,1,0:T(8,128)(2,1)S(1)} %get-tuple-element.194), channel_id=1, source_target_pairs={{0,16},{8,24},{16,0},{24,8},{1,17},{9,25},{17,1},{25,9},{2,18},{10... | collective-permute-start | bytes 1769480 | tf_op jit(solution)/shard_map/ppermute | solution.py:364
  236.0 14.2 %collective-permute-start.18 = (bf16[1,192,768]{2,1,0:T(8,128)(2,1)S(1)}, bf16[1,192,768]{2,1,0:T(8,128)(2,1)S(1)}, u32[]{:S(2)}, u32[]{:S(2)}) collective-permute-start(bf16[1,192,768]{2,1,0:T(8,128)(2,1)S(1)} %fusion.99), channel_id=1, source_target_pairs={{0,4},{2,6},{4,0},{6,2},{1,5},{3,7},{5,1},{7,3},{8,12},{10,14},{12... | collective-permute-start | bytes 884744 | tf_op jit(solution)/shard_map/ppermute | solution.py:364
  240.7 9.8 %copy-start.5 = (bf16[1,1,512,768]{3,2,1,0:T(8,128)(2,1)S(1)}, bf16[1,1,512,768]{3,2,1,0:T(8,128)(2,1)}, u32[]{:S(2)}) copy-start(bf16[1,1,512,768]{3,2,1,0:T(8,128)(2,1)} %param.12) | copy-start | bytes 2359300
  240.7 9.9 %copy-start.52 = (f32[512]{0:T(512)S(1)}, f32[512]{0:T(512)}, u32[]{:S(2)}) copy-start(f32[512]{0:T(512)} %copy-done.51) | copy-start | bytes 6148
  240.7 9.9 %copy-start.66 = (f32[512]{0:T(512)S(1)}, f32[512]{0:T(512)}, u32[]{:S(2)}) copy-start(f32[512]{0:T(512)} %copy-done.65) | copy-start | bytes 6148
  252.1 20.6 %collective-permute-start.22 = (bf16[192,768]{1,0:T(8,128)(2,1)}, bf16[192,768]{1,0:T(8,128)(2,1)}, u32[]{:S(2)}, u32[]{:S(2)}) collective-permute-start(bf16[192,768]{1,0:T(8,128)(2,1)} %fusion.101), channel_id=1, source_target_pairs={{0,1},{1,0},{2,3},{3,2},{4,5},{5,4},{6,7},{7,6},{8,9},{9,8},{10,11... | collective-permute-start | bytes 884744 | tf_op jit(solution)/shard_map/ppermute | solution.py:364
  255.8 4.8 %copy-start.50 = (bf16[384,768]{1,0:T(8,128)(2,1)S(1)}, bf16[384,768]{1,0:T(8,128)(2,1)}, u32[]{:S(2)}) copy-start(bf16[384,768]{1,0:T(8,128)(2,1)} %convolution_convert_fusion.9) | copy-start | bytes 1769476
  256.0 11.5 %collective-permute-start.24 = (bf16[208,384]{1,0:T(8,128)(2,1)S(1)}, bf16[208,384]{1,0:T(8,128)(2,1)S(1)}, u32[]{:S(2)}, u32[]{:S(2)}) collective-permute-start(bf16[208,384]{1,0:T(8,128)(2,1)S(1)} %pad_maximum_fusion.12), channel_id=1, source_target_pairs={{0,2},{2,0},{4,6},{6,4},{1,3},{3,1},{5,7},{7,5},{8,10},{10,8},{12,... | collective-permute-start | bytes 479240 | tf_op jit(solution)/shard_map/ppermute | solution.py:719
  256.1 14.7 %collective-permute-start.25 = (bf16[208,384]{1,0:T(8,128)(2,1)S(1)}, bf16[208,384]{1,0:T(8,128)(2,1)S(1)}, u32[]{:S(2)}, u32[]{:S(2)}) collective-permute-start(bf16[208,384]{1,0:T(8,128)(2,1)S(1)} %pad_maximum_fusion.13), channel_id=1, source_target_pairs={{0,4},{2,6},{4,0},{6,2},{1,5},{3,7},{5,1},{7,3},{8,12},{10,14},{12... | collective-permute-start | bytes 479240 | tf_op jit(solution)/shard_map/ppermute | solution.py:719
  259.1 11.7 %collective-permute-start.26 = (bf16[208,384]{1,0:T(8,128)(2,1)S(1)}, bf16[208,384]{1,0:T(8,128)(2,1)S(1)}, u32[]{:S(2)}, u32[]{:S(2)}) collective-permute-start(bf16[208,384]{1,0:T(8,128)(2,1)S(1)} %pad_maximum_fusion.14), channel_id=1, source_target_pairs={{0,6},{2,4},{4,2},{6,0},{1,7},{3,5},{5,3},{7,1},{8,14},{10,12},{12... | collective-permute-start | bytes 479240 | tf_op jit(solution)/shard_map/ppermute | solution.py:719
  260.6 13.9 %collective-permute-start.23 = (bf16[384,768]{1,0:T(8,128)(2,1)S(1)}, bf16[384,768]{1,0:T(8,128)(2,1)S(1)}, u32[]{:S(2)}, u32[]{:S(2)}) collective-permute-start(bf16[384,768]{1,0:T(8,128)(2,1)S(1)} %copy-done.50), channel_id=1, source_target_pairs={{0,1},{1,0},{2,3},{3,2},{4,5},{5,4},{6,7},{7,6},{8,9},{9,8},{10,11... | collective-permute-start | bytes 1769480 | tf_op jit(solution)/shard_map/ppermute | solution.py:364
  267.4 8.2 %copy-start.8 = (bf16[1,384,768]{2,1,0:T(8,128)(2,1)S(1)}, bf16[1,384,768]{2,1,0:T(8,128)(2,1)}, u32[]{:S(2)}) copy-start(bf16[1,384,768]{2,1,0:T(8,128)(2,1)} %param.11) | copy-start | bytes 1769476
  267.4 8.2 %copy-start.58 = (f32[384]{0:T(512)S(1)}, f32[384]{0:T(512)}, u32[]{:S(2)}) copy-start(f32[384]{0:T(512)} %copy-done.57) | copy-start | bytes 4612
  267.4 8.2 %copy-start.72 = (f32[384]{0:T(512)S(1)}, f32[384]{0:T(512)}, u32[]{:S(2)}) copy-start(f32[384]{0:T(512)} %copy-done.71) | copy-start | bytes 4612
  267.4 8.7 %copy-start.26 = (f32[384,768]{1,0:T(8,128)S(1)}, f32[384,768]{1,0:T(8,128)}, u32[]{:S(2)}) copy-start(f32[384,768]{1,0:T(8,128)} %get-tuple-element.175) | copy-start | bytes 3538948
  270.8 6.6 %collective-permute-start.29 = (bf16[208,384]{1,0:T(8,128)(2,1)S(1)}, bf16[208,384]{1,0:T(8,128)(2,1)S(1)}, u32[]{:S(2)}, u32[]{:S(2)}) collective-permute-start(bf16[208,384]{1,0:T(8,128)(2,1)S(1)} %add_convert_fusion.17), channel_id=1, source_target_pairs={{0,24},{8,16},{16,8},{24,0},{1,25},{9,17},{17,9},{25,1},{2,26},{10... | collective-permute-start | bytes 479240 | tf_op jit(solution)/shard_map/ppermute | solution.py:443
  270.9 9.8 %collective-permute-start.28 = (bf16[208,384]{1,0:T(8,128)(2,1)S(1)}, bf16[208,384]{1,0:T(8,128)(2,1)S(1)}, u32[]{:S(2)}, u32[]{:S(2)}) collective-permute-start(bf16[208,384]{1,0:T(8,128)(2,1)S(1)} %add_convert_fusion.17), channel_id=1, source_target_pairs={{0,16},{8,24},{16,0},{24,8},{1,17},{9,25},{17,1},{25,9},{2,18},{10... | collective-permute-start | bytes 479240 | tf_op jit(solution)/shard_map/ppermute | solution.py:443
  272.5 8.2 %collective-permute-start.27 = (bf16[208,384]{1,0:T(8,128)(2,1)S(1)}, bf16[208,384]{1,0:T(8,128)(2,1)S(1)}, u32[]{:S(2)}, u32[]{:S(2)}) collective-permute-start(bf16[208,384]{1,0:T(8,128)(2,1)S(1)} %add_convert_fusion.17), channel_id=1, source_target_pairs={{0,8},{8,0},{16,24},{24,16},{1,9},{9,1},{17,25},{25,17},{2,10},{10... | collective-permute-start | bytes 479240 | tf_op jit(solution)/shard_map/ppermute | solution.py:443
  281.6 5.7 %copy-start.1 = (bf16[768,1536]{1,0:T(8,128)(2,1)S(1)}, bf16[768,1536]{1,0:T(8,128)(2,1)}, u32[]{:S(2)}) copy-start(bf16[768,1536]{1,0:T(8,128)(2,1)} %param.18) | copy-start | bytes 7077892
  (52 other events, 122.4 us)

commit v6 on v5

--- a/solution.py
+++ b/solution.py
@@ -467,8 +467,10 @@
     return inv * (scaled - mean - normed * inner)
 
 
-def exact_gelu(upper):
-    return jax.nn.gelu(upper, approximate=False)
+def gelu_parts(upper):
+    half = 0.5 + 0.5 * lax.erf(upper * 0.5**0.5)
+    bell = jnp.exp(-0.5 * upper * upper) * (2.0 * jnp.pi) ** -0.5
+    return upper * half, half + upper * bell
 
 
 def body(
@@ -564,8 +566,8 @@
         normed, inv = norm_parts(resid)
         low = (normed * gains[1] + shifts[1]).astype(BF)
         upper = wide_dot(low, ffn_in)
-        activated, gelu_pull = jax.vjp(exact_gelu, upper)
-        upper_grad = gelu_pull(act_grad)[0].astype(BF)
+        activated, slope = gelu_parts(upper)
+        upper_grad = (act_grad * slope).astype(BF)
         terms = back_dot(upper_grad, ffn_in).astype(BF)
         return resid, normed, inv, low, activated.astype(BF), upper_grad, terms
 
@@ -581,9 +583,9 @@
     def joined(first, second):
         return jnp.concatenate([first, second], axis=0)
 
-    up_p = after(up_p, second_other)
     in_grad = rows_dot(joined(mid_p, mid_c), joined(up_p, up_c)).astype(BF)
     down_grad = rows_dot(joined(cot_p, cot_c), joined(act_p, act_c)).astype(BF)
+    in_grad = after(in_grad, second_other, terms_two_p)
     ffn_grad = cut(jnp.stack([in_grad, down_grad]))
     ffn_part = add_low(halve(ffn_grad, "grp", 0, seq_bits + 1))
     second_other = after(second_other, ffn_part)

time: 292 us -> 288 us (0.986)
  matrix products: 60.5 us -> 48.4 us
  waiting for transfers between devices: 40.1 us -> 51.1 us
    dot_general x6, matrix products: 25 us -> 13 us  [wide_dot(): return jnp.dot(left, right, preferred_element_type=F32)]
    ppermute x21, waiting for transfers between devices: 33.1 us -> 43.9 us  [swap(): return lax.ppermute(array, axis, [(j, j ^ 1 << bit) for j in range(count)])]
    unnamed x173 -> x175, local copies, waits for them, and re-layouts: 10.1 us -> 8.44 us
  transfers between devices with their start and end apart: 30 -> 30, of which waited for: 13 -> 13; matrix products, arithmetic and copies ran while one was open for 32% -> 29% of each run, Pallas kernels for 24% -> 24%
where the time goes in v6:
time: 288 us; the launch traced here: 284 us
  Pallas kernels  76.2 us (26%)
  waiting for transfers between devices  51.1 us (18%)
  matrix products  48.4 us (17%)
  other arithmetic  47.1 us (16%)
  starting transfers between devices  35.1 us (12%)
  local copies, waits for them, and re-layouts  22.4 us (8%)
  between operations  3.38 us (1%)
    ppermute x21, waiting for transfers between devices, swap(): return lax.ppermute(array, axis, [(j, j ^ 1 << bit) for j in range(count)])  43.9 us
    pallas_call x2, Pallas kernels, pull_far(): pl.pallas_call(functools.partial(pull_far_kernel, masked=masked, chunk=ch...  25.2 us
    ppermute x21, starting transfers between devices, swap(): return lax.ppermute(array, axis, [(j, j ^ 1 << bit) for j in range(count)])  22.9 us
    pallas_call x1, Pallas kernels, pull_near(): pl.pallas_call(pull_near_kernel, grid=(width // LANES,), in_specs=specs,...  14.8 us
    pallas_call x2, Pallas kernels, attend_far(): pl.pallas_call(functools.partial(far_kernel, masked=masked), grid=(width...  14 us
    dot_general x8, matrix products, rows_dot(): return jnp.einsum('nd,nf->df', left, right, preferred_element_type=F32)  13.8 us
    dot_general x6, matrix products, wide_dot(): return jnp.dot(left, right, preferred_element_type=F32)  13 us
    pallas_call x1, Pallas kernels, attend_near(): pl.pallas_call(near_kernel, grid=(width // LANES,), in_specs=[kind_spec(o...  11.1 us
  transfers between devices with their start and end apart: 30, of which 13 were waited for; matrix products, arithmetic and copies ran while one was open for 29% of the time, Pallas kernels for 24%

profile of v6, /device:TPU:0, one launch (start us, length us, event | category | flops | bytes accessed | tf_op | source)
XLA Modules:
  0.0 283.7 jit_solution(3009308593415737880)
XLA Ops:
  0.7 1.9 dynamic-slice_bitcast_fusion.7
  2.5 5.1 %collective-permute-start.2 = (bf16[192,768]{1,0:T(8,128)(2,1)}, bf16[192,768]{1,0:T(8,128)(2,1)S(1)}, u32[]{:S(2)}, u32[]{:S(2)}) collective-permute-start(bf16[192,768]{1,0:T(8,128)(2,1)} %dynamic-slice_bitcast_fusion.7), channel_id=1, source_target_pairs={{0,6},{2,4},{4,2},{6,0},{1,7},{3,5},{5,3},{7,1},{8,14},{10,12},{12... | collective-permute-start | bytes 884744 | tf_op jit(solution)/shard_map/ppermute | solution.py:507
  11.4 2.4 subtract_multiply_fusion.2
  13.7 1.5 fusion.34
  16.0 1.8 fusion.59.qp_ref.kp_ref.vp_ref.refs_0_
  17.8 2.2 fusion.48.qc_ref.kc_ref.vc_ref.refs_0_
  21.1 11.1 %shard_map.186 = (f32[384,384]{1,0:T(8,128)}, f32[3,8,384]{2,1,0:T(8,128)}, f32[512,384]{1,0:T(8,128)}, f32[3,8,512]{2,1,0:T(8,128)}) custom-call(bf16[3,384,384]{2,1,0:T(8,128)(2,1)} %fusion.59.qp_ref.kp_ref.vp_ref.refs_0_, bf16[3,384,384]{2,1,0:T(8,128)(2,1)} %fusion.59.qp_ref.kp_ref.vp_ref.refs_0_, ...), custom_call_target="tpu_custom_call" | custom-call | flops 1212416 | bytes 5120 | tf_op jit(solution)/shard_map/pallas_call | solution.py:122
  34.2 1.6 collective-permute-start.3
  37.3 1.8 fusion.65.k_ref.v_ref
  39.9 11.1 %shard_map.187 = (f32[384,384]{1,0:T(8,128)}, f32[3,8,384]{2,1,0:T(8,128)}, f32[512,384]{1,0:T(8,128)}, f32[3,8,512]{2,1,0:T(8,128)}) custom-call(bf16[2,576,384]{2,1,0:T(8,128)(2,1)} %fusion.65.k_ref.v_ref, bf16[2,576,384]{2,1,0:T(8,128)(2,1)} %fusion.65.k_ref.v_ref, f32[576,128]{1,0:T(8,128)} %broadcast_in_dim.37.bias_ref, ...), custom_call_target="tpu_custom_call" | custom-call | flops 1032192 | bytes 2304 | tf_op jit(solution)/shard_map/pallas_call | solution.py:176
  51.0 4.0 %collective-permute-done.3 = bf16[576,768]{1,0:T(8,128)(2,1)S(1)} collective-permute-done((bf16[576,768]{1,0:T(8,128)(2,1)S(1)}, bf16[576,768]{1,0:T(8,128)(2,1)S(1)}, u32[]{:S(2)}, u32[]{:S(2)}) %collective-permute-start.3) | collective-permute-done | bytes 884768 | tf_op jit(solution)/shard_map/ppermute | solution.py:364
  56.8 1.8 fusion.66.refs_1_.refs_2_
  59.4 7.6 %shard_map.188 = (bf16[512,384]{1,0:T(8,128)(2,1)}, f32[3,8,512]{2,1,0:T(8,128)}) custom-call(bf16[3,512,384]{2,1,0:T(8,128)(2,1)} %fusion.48.qc_ref.kc_ref.vc_ref.refs_0_, bf16[2,576,384]{2,1,0:T(8,128)(2,1)} %fusion.66.refs_1_.refs_2_, bf16[2,576,384]{2,1,0:T(8,128)(2,1)} %fusion.66.refs_1_.refs_2_, f32[576,128]{1,0:T(8,128)} %broadcast_in_dim.38.refs_3_, ...), custom_call_target="tpu_custom_call" | custom-call | flops 589824 | bytes 2304 | tf_op jit(solution)/shard_map/pallas_call | solution.py:222
  67.0 2.4 convolution_convert_fusion.8
  69.4 1.5 collective-permute-start.4
  71.0 6.4 %shard_map.189 = (bf16[384,384]{1,0:T(8,128)(2,1)}, f32[3,8,384]{2,1,0:T(8,128)}) custom-call(bf16[3,384,384]{2,1,0:T(8,128)(2,1)} %fusion.59.qp_ref.kp_ref.vp_ref.refs_0_, bf16[2,576,384]{2,1,0:T(8,128)(2,1)} %fusion.66.refs_1_.refs_2_, bf16[2,576,384]{2,1,0:T(8,128)(2,1)} %fusion.66.refs_1_.refs_2_, f32[384,384]{1,0:T(8,128)} %get-tuple-element.91.refs_3_, ...), custom_call_target="tpu_custom_call" | custom-call | flops 442368 | bytes 2304 | tf_op jit(solution)/shard_map/pallas_call | solution.py:222
  77.4 1.4 convolution_convert_fusion.12
  79.4 1.5 pad_maximum_fusion.refs_1_.refs_2_
  85.9 4.2 %collective-permute-done.4 = bf16[512,768]{1,0:T(8,128)(2,1)} collective-permute-done((bf16[512,768]{1,0:T(8,128)(2,1)}, bf16[512,768]{1,0:T(8,128)(2,1)}, u32[]{:S(2)}, u32[]{:S(2)}) %collective-permute-start.4) | collective-permute-done | bytes 786464 | tf_op jit(solution)/shard_map/ppermute | solution.py:364
  91.2 1.7 fusion.116
  95.5 1.5 multiply_convert_fusion
  98.5 1.6 collective-permute-start.7
  100.1 2.7 collective-permute-done.5
  103.6 1.9 multiply_convert_fusion.1
  105.5 2.9 %convolution_convert_fusion.1 = bf16[768,1536]{1,0:T(8,128)(2,1)S(1)} fusion(bf16[512,1536]{1,0:T(8,128)(2,1)S(1)} %get-tuple-element.185, bf16[384,1536]{1,0:T(8,128)(2,1)S(1)} %get-tuple-element.191, bf16[512,768]{1,0:T(8,128)(2,1)S(1)} %add_convert_fusion.5, bf16[384,768]{1,0:T(8,128)(2,1)S(1)} %add_convert_fusion.11), kind=kOutput, calls=%fused_computation.10 | convolution fusion | flops 2123366400 | bytes 6488064 | tf_op jit(solution)/shard_map/nd,nf->df/dot_general | solution.py:413
  108.5 3.1 %convolution_convert_fusion = bf16[768,1536]{1,0:T(8,128)(2,1)S(1)} fusion(bf16[512,1536]{1,0:T(8,128)(2,1)S(1)} %get-tuple-element.113, bf16[384,1536]{1,0:T(8,128)(2,1)S(1)} %get-tuple-element.136, bf16[512,768]{1,0:T(8,128)(2,1)S(1)} %bitcast.261, bf16[384,768]{1,0:T(8,128)(2,1)S(1)} %bitcast.271), kind=kOutput, calls=%fused_computation.9 | convolution fusion | flops 2123366400 | bytes 6488064 | tf_op jit(solution)/shard_map/nd,nf->df/dot_general | solution.py:413
  111.6 1.9 convolution_convert_fusion.10
  113.5 3.4 %collective-permute-done.7 = bf16[512,768]{1,0:T(8,128)(2,1)S(1)} collective-permute-done((bf16[512,768]{1,0:T(8,128)(2,1)S(1)}, bf16[512,768]{1,0:T(8,128)(2,1)S(1)}, u32[]{:S(2)}, u32[]{:S(2)}) %collective-permute-start.7) | collective-permute-done | bytes 786464 | tf_op jit(solution)/shard_map/ppermute | solution.py:364
  116.9 1.7 fusion.21
  118.7 1.6 collective-permute-start.6
  120.3 3.2 %collective-permute-done.8 = bf16[2,2,2,2,48,1536]{5,4,3,2,1,0:T(8,128)(2,1)} collective-permute-done((bf16[2,2,2,2,48,1536]{5,4,3,2,1,0:T(8,128)(2,1)}, bf16[2,2,2,2,48,1536]{5,4,3,2,1,0:T(8,128)(2,1)}, u32[]{:S(2)}, u32[]{:S(2)}) %collective-permute-start.8) | collective-permute-done | bytes 2359328 | tf_op jit(solution)/shard_map/ppermute | solution.py:364
  123.5 3.0 %fusion = bf16[2,2,2,2,48,1536]{5,4,3,2,1,0:T(8,128)(2,1)S(1)} fusion(bf16[2,2,2,2,48,1536]{5,4,3,2,1,0:T(8,128)(2,1)} %collective-permute-done.8, s32[]{:T(128)S(6)} %select_n.236, bf16[1,2,2,2,2,48,1536]{6,5,4,3,2,1,0:T(8,128)(2,1)} %bitcast.237, bf16[1,2,2,2,2,48,1536]{6,5,4,3,2,1,0:T(8,128)(2,1)} %bitcast.239), kind=kLoop, calls=%fused_computation.6 | loop fusion | flops 5898240 | bytes 9437188 | tf_op jit(solution)/shard_map/convert_element_type | solution.py:383
  127.7 1.6 collective-permute-start.9
  129.2 1.8 fusion.114
  132.4 13.7 %shard_map.190 = (f32[512,384]{1,0:T(8,128)}, f32[2,1152,384]{2,1,0:T(8,128)}) custom-call(bf16[3,512,384]{2,1,0:T(8,128)(2,1)} %fusion.48.qc_ref.kc_ref.vc_ref.refs_0_, bf16[2,1152,384]{2,1,0:T(8,128)(2,1)} %pad_maximum_fusion.refs_1_.refs_2_, bf16[2,1152,384]{2,1,0:T(8,128)(2,1)} %pad_maximum_fusion.refs_1_.refs_2_, f32[1152,128]{1,0:T(8,128)} %broadcast_in_dim.39.refs_3_, ...), custom_call_target="tpu_custom_call" | custom-call | flops 2949120 | bytes 9216 | tf_op jit(solution)/shard_map/pallas_call | solution.py:310
  146.2 3.9 %convolution_convert_fusion.6 = bf16[512,768]{1,0:T(8,128)(2,1)} fusion(bf16[512,1536]{1,0:T(8,128)(2,1)S(1)} %copy-done.39, bf16[1536,768]{1,0:T(8,128)(2,1)} %param.19), kind=kOutput, calls=%fused_computation.102 | convolution fusion | flops 1208352768 | bytes 4718592 | tf_op jit(solution)/shard_map/dot_general | solution.py:405
  150.1 1.5 collective-permute-start.13
  151.6 4.2 %collective-permute-done.9 = bf16[2,2,2,48,1536]{4,3,2,1,0:T(8,128)(2,1)} collective-permute-done((bf16[2,2,2,48,1536]{4,3,2,1,0:T(8,128)(2,1)S(1)}, bf16[2,2,2,48,1536]{4,3,2,1,0:T(8,128)(2,1)}, u32[]{:S(2)}, u32[]{:S(2)}) %collective-permute-start.9) | collective-permute-done | bytes 1179680 | tf_op jit(solution)/shard_map/ppermute | solution.py:364
  155.9 1.6 add_convert_fusion.1
  157.5 1.8 fusion.70
  159.4 2.8 fusion.113
  166.4 11.5 %shard_map.191 = (f32[384,384]{1,0:T(8,128)}, bf16[2,1152,384]{2,1,0:T(8,128)(2,1)}) custom-call(bf16[3,384,384]{2,1,0:T(8,128)(2,1)} %fusion.59.qp_ref.kp_ref.vp_ref.refs_0_, bf16[2,1152,384]{2,1,0:T(8,128)(2,1)} %pad_maximum_fusion.refs_1_.refs_2_, bf16[2,1152,384]{2,1,0:T(8,128)(2,1)} %pad_maximum_fusion.refs_1_.refs_2_, ...), custom_call_target="tpu_custom_call" | custom-call | flops 2211840 | bytes 9216 | tf_op jit(solution)/shard_map/pallas_call | solution.py:310
  178.0 3.7 %fusion.118 = (f32[768]{0:T(1024)S(1)}, bf16[1152,768]{1,0:T(8,128)(2,1)S(1)}, f32[1152,768]{1,0:T(8,128)S(1)}) fusion(bf16[2,1152,384]{2,1,0:T(8,128)(2,1)} %get-tuple-element.117, bf16[3,768,384]{2,1,0:T(8,128)(2,1)} %param.16), kind=kOutput, calls=%fused_computation.300 | convolution fusion | flops 1360723200 | bytes 8260608 | tf_op jit(solution)/shard_map/cne,cde->nd/dot_general | solution.py:621
  181.7 1.6 collective-permute-start.10
  185.3 2.3 collective-permute-start.12
  188.3 14.8 %shard_map.192 = bf16[3,896,384]{2,1,0:T(8,128)(2,1)} custom-call(bf16[3,384,384]{2,1,0:T(8,128)(2,1)} %fusion.59.qp_ref.kp_ref.vp_ref.refs_0_, bf16[3,384,384]{2,1,0:T(8,128)(2,1)} %fusion.59.qp_ref.kp_ref.vp_ref.refs_0_, bf16[3,384,384]{2,1,0:T(8,128)(2,1)} %fusion.59.qp_ref.kp_ref.vp_ref.refs_0_, ...), custom_call_target="tpu_custom_call" | custom-call | flops 3031040 | bytes 5120 | tf_op jit(solution)/shard_map/pallas_call | solution.py:351
  203.2 2.4 convolution_convert_fusion.11
  213.4 2.0 bitcast_convert_fusion
  215.8 1.6 collective-permute-start.19
  221.0 3.1 %collective-permute-done.19 = bf16[2,48,1536]{2,1,0:T(8,128)(2,1)S(1)} collective-permute-done((bf16[2,48,1536]{2,1,0:T(8,128)(2,1)S(1)}, bf16[2,48,1536]{2,1,0:T(8,128)(2,1)S(1)}, u32[]{:S(2)}, u32[]{:S(2)}) %collective-permute-start.19) | collective-permute-done | bytes 294944 | tf_op jit(solution)/shard_map/ppermute | solution.py:364
  225.1 6.7 %collective-permute-done.16 = bf16[2,192,768]{2,1,0:T(8,128)(2,1)S(1)} collective-permute-done((bf16[2,192,768]{2,1,0:T(8,128)(2,1)S(1)}, bf16[2,192,768]{2,1,0:T(8,128)(2,1)S(1)}, u32[]{:S(2)}, u32[]{:S(2)}) %collective-permute-start.16) | collective-permute-done | bytes 589856 | tf_op jit(solution)/shard_map/ppermute | solution.py:364
  232.4 1.5 collective-permute-start.18
  234.0 2.2 fusion.83
  236.2 10.3 %collective-permute-done.18 = bf16[1,192,768]{2,1,0:T(8,128)(2,1)S(1)} collective-permute-done((bf16[1,192,768]{2,1,0:T(8,128)(2,1)S(1)}, bf16[1,192,768]{2,1,0:T(8,128)(2,1)S(1)}, u32[]{:S(2)}, u32[]{:S(2)}) %collective-permute-start.18) | collective-permute-done | bytes 294944 | tf_op jit(solution)/shard_map/ppermute | solution.py:364
  249.4 1.9 convolution_convert_fusion.9
  251.8 2.7 collective-permute-start.25
  254.5 1.8 collective-permute-start.26
  259.1 1.6 slice_bitcast_fusion
  261.7 1.6 fusion.84
  263.4 3.3 %collective-permute-done.25 = bf16[208,384]{1,0:T(8,128)(2,1)S(1)} collective-permute-done((bf16[208,384]{1,0:T(8,128)(2,1)S(1)}, bf16[208,384]{1,0:T(8,128)(2,1)S(1)}, u32[]{:S(2)}, u32[]{:S(2)}) %collective-permute-start.25) | collective-permute-done | bytes 159776 | tf_op jit(solution)/shard_map/ppermute | solution.py:721
  266.8 1.6 collective-permute-start.28
  268.7 2.1 collective-permute-done.23
  273.6 3.0 %collective-permute-done.28 = bf16[208,384]{1,0:T(8,128)(2,1)S(1)} collective-permute-done((bf16[208,384]{1,0:T(8,128)(2,1)S(1)}, bf16[208,384]{1,0:T(8,128)(2,1)S(1)}, u32[]{:S(2)}, u32[]{:S(2)}) %collective-permute-start.28) | collective-permute-done | bytes 159776 | tf_op jit(solution)/shard_map/ppermute | solution.py:443
  281.1 2.1 slice.227
  (348 shorter events, 60.5 us)
Async XLA Ops:
  0.6 93.5 %copy-start = (bf16[768,1536]{1,0:T(8,128)(2,1)S(1)}, bf16[768,1536]{1,0:T(8,128)(2,1)}, u32[]{:S(2)}) copy-start(bf16[768,1536]{1,0:T(8,128)(2,1)} %param.18) | copy-start | bytes 7077892
  0.7 9.5 %copy-start.4 = (bf16[1,1,512,768]{3,2,1,0:T(8,128)(2,1)S(1)}, bf16[1,1,512,768]{3,2,1,0:T(8,128)(2,1)}, u32[]{:S(2)}) copy-start(bf16[1,1,512,768]{3,2,1,0:T(8,128)(2,1)} %param.12) | copy-start | bytes 2359300
  0.7 10.4 %copy-start.76 = (bf16[2,768]{1,0:T(2,128)(2,1)S(1)}, bf16[2,768]{1,0:T(2,128)(2,1)}, u32[]{:S(2)}) copy-start(bf16[2,768]{1,0:T(2,128)(2,1)} %param.20) | copy-start | bytes 9220
  0.7 10.4 %copy-start.77 = (bf16[2,768]{1,0:T(2,128)(2,1)S(1)}, bf16[2,768]{1,0:T(2,128)(2,1)}, u32[]{:S(2)}) copy-start(bf16[2,768]{1,0:T(2,128)(2,1)} %param.21) | copy-start | bytes 9220
  2.5 29.7 %collective-permute-start.2 = (bf16[192,768]{1,0:T(8,128)(2,1)}, bf16[192,768]{1,0:T(8,128)(2,1)S(1)}, u32[]{:S(2)}, u32[]{:S(2)}) collective-permute-start(bf16[192,768]{1,0:T(8,128)(2,1)} %dynamic-slice_bitcast_fusion.7), channel_id=1, source_target_pairs={{0,6},{2,4},{4,2},{6,0},{1,7},{3,5},{5,3},{7,1},{8,14},{10,12},{12... | collective-permute-start | bytes 884744 | tf_op jit(solution)/shard_map/ppermute | solution.py:507
  7.6 25.4 %collective-permute-start.1 = (bf16[192,768]{1,0:T(8,128)(2,1)}, bf16[192,768]{1,0:T(8,128)(2,1)}, u32[]{:S(2)}, u32[]{:S(2)}) collective-permute-start(bf16[192,768]{1,0:T(8,128)(2,1)} %dynamic-slice_bitcast_fusion.7), channel_id=1, source_target_pairs={{0,4},{2,6},{4,0},{6,2},{1,5},{3,7},{5,1},{7,3},{8,12},{10,14},{12... | collective-permute-start | bytes 884744 | tf_op jit(solution)/shard_map/ppermute | solution.py:507
  7.6 25.4 %collective-permute-start = (bf16[192,768]{1,0:T(8,128)(2,1)}, bf16[192,768]{1,0:T(8,128)(2,1)}, u32[]{:S(2)}, u32[]{:S(2)}) collective-permute-start(bf16[192,768]{1,0:T(8,128)(2,1)} %dynamic-slice_bitcast_fusion.7), channel_id=1, source_target_pairs={{0,2},{2,0},{4,6},{6,4},{1,3},{3,1},{5,7},{7,5},{8,10},{10,8},{12,... | collective-permute-start | bytes 884744 | tf_op jit(solution)/shard_map/ppermute | solution.py:507
  11.3 82.0 %copy-start.62 = (f32[768]{0:T(1024)}, f32[768]{0:T(1024)S(1)}, u32[]{:S(2)}) copy-start(f32[768]{0:T(1024)S(1)} %get-tuple-element.172) | copy-start | bytes 9220
  21.0 11.1 %copy-start.7 = (bf16[1,384,768]{2,1,0:T(8,128)(2,1)S(1)}, bf16[1,384,768]{2,1,0:T(8,128)(2,1)}, u32[]{:S(2)}) copy-start(bf16[1,384,768]{2,1,0:T(8,128)(2,1)} %param.11) | copy-start | bytes 1769476
  34.2 20.8 %collective-permute-start.3 = (bf16[576,768]{1,0:T(8,128)(2,1)S(1)}, bf16[576,768]{1,0:T(8,128)(2,1)S(1)}, u32[]{:S(2)}, u32[]{:S(2)}) collective-permute-start(bf16[576,768]{1,0:T(8,128)(2,1)S(1)} %pad_maximum_fusion.4), channel_id=1, source_target_pairs={{0,1},{1,0},{2,3},{3,2},{4,5},{5,4},{6,7},{7,6},{8,9},{9,8},{10,11... | collective-permute-start | bytes 2654216 | tf_op jit(solution)/shard_map/ppermute | solution.py:364
  59.4 7.6 %copy-start.21 = (bf16[384,768]{1,0:T(8,128)(2,1)S(1)}, bf16[384,768]{1,0:T(8,128)(2,1)}, u32[]{:S(2)}) copy-start(bf16[384,768]{1,0:T(8,128)(2,1)} %param.17) | copy-start | bytes 1769476
  69.4 20.7 %collective-permute-start.4 = (bf16[512,768]{1,0:T(8,128)(2,1)}, bf16[512,768]{1,0:T(8,128)(2,1)}, u32[]{:S(2)}, u32[]{:S(2)}) collective-permute-start(bf16[512,768]{1,0:T(8,128)(2,1)} %convolution_convert_fusion.8), channel_id=1, source_target_pairs={{0,1},{1,0},{2,3},{3,2},{4,5},{5,4},{6,7},{7,6},{8,9},{9,8},{10,11... | collective-permute-start | bytes 2359304 | tf_op jit(solution)/shard_map/ppermute | solution.py:364
  71.0 8.4 %copy-start.9 = (bf16[2,576,384]{2,1,0:T(8,128)(2,1)S(1)}, bf16[2,576,384]{2,1,0:T(8,128)(2,1)}, u32[]{:S(2)}) copy-start(bf16[2,576,384]{2,1,0:T(8,128)(2,1)} %fusion.66.refs_1_.refs_2_) | copy-start | bytes 2654212
  71.0 8.4 %copy-start.16 = (bf16[2,576,384]{2,1,0:T(8,128)(2,1)S(1)}, bf16[2,576,384]{2,1,0:T(8,128)(2,1)}, u32[]{:S(2)}) copy-start(bf16[2,576,384]{2,1,0:T(8,128)(2,1)} %fusion.65.k_ref.v_ref) | copy-start | bytes 2654212
  78.8 23.9 %collective-permute-start.5 = (bf16[384,768]{1,0:T(8,128)(2,1)S(1)}, bf16[384,768]{1,0:T(8,128)(2,1)S(1)}, u32[]{:S(2)}, u32[]{:S(2)}) collective-permute-start(bf16[384,768]{1,0:T(8,128)(2,1)S(1)} %convolution_convert_fusion.12), channel_id=1, source_target_pairs={{0,1},{1,0},{2,3},{3,2},{4,5},{5,4},{6,7},{7,6},{8,9},{9,8},{10,11... | collective-permute-start | bytes 1769480 | tf_op jit(solution)/shard_map/ppermute | solution.py:364
  97.0 11.4 %copy-start.38 = (bf16[512,1536]{1,0:T(8,128)(2,1)}, bf16[512,1536]{1,0:T(8,128)(2,1)S(1)}, u32[]{:S(2)}) copy-start(bf16[512,1536]{1,0:T(8,128)(2,1)S(1)} %get-tuple-element.113) | copy-start | bytes 4718596
  98.5 4.8 %copy-start.63 = (f32[768]{0:T(1024)S(1)}, f32[768]{0:T(1024)}, u32[]{:S(2)}) copy-start(f32[768]{0:T(1024)} %copy-done.62) | copy-start | bytes 9220
  98.5 18.4 %collective-permute-start.7 = (bf16[512,768]{1,0:T(8,128)(2,1)S(1)}, bf16[512,768]{1,0:T(8,128)(2,1)S(1)}, u32[]{:S(2)}, u32[]{:S(2)}) collective-permute-start(bf16[512,768]{1,0:T(8,128)(2,1)S(1)} %convolution_convert_fusion.7), channel_id=1, source_target_pairs={{0,1},{1,0},{2,3},{3,2},{4,5},{5,4},{6,7},{7,6},{8,9},{9,8},{10,11... | collective-permute-start | bytes 2359304 | tf_op jit(solution)/shard_map/ppermute | solution.py:364
  108.4 8.5 %copy-start.14 = (bf16[768,1536]{1,0:T(8,128)(2,1)}, bf16[768,1536]{1,0:T(8,128)(2,1)S(1)}, u32[]{:S(2)}) copy-start(bf16[768,1536]{1,0:T(8,128)(2,1)S(1)} %convolution_convert_fusion.1) | copy-start | bytes 7077892
  111.6 5.3 %copy-start.15 = (bf16[768,1536]{1,0:T(8,128)(2,1)}, bf16[768,1536]{1,0:T(8,128)(2,1)S(1)}, u32[]{:S(2)}) copy-start(bf16[768,1536]{1,0:T(8,128)(2,1)S(1)} %convolution_convert_fusion) | copy-start | bytes 7077892
  118.6 4.9 %collective-permute-start.8 = (bf16[2,2,2,2,48,1536]{5,4,3,2,1,0:T(8,128)(2,1)}, bf16[2,2,2,2,48,1536]{5,4,3,2,1,0:T(8,128)(2,1)}, u32[]{:S(2)}, u32[]{:S(2)}) collective-permute-start(bf16[2,2,2,2,48,1536]{5,4,3,2,1,0:T(8,128)(2,1)} %fusion.21), channel_id=1, source_target_pairs={{0,8},{8,0},{16,24},{24,16},{1,9},{9,1},{17,25},{25,17},{2,10},{10... | collective-permute-start | bytes 7077896 | tf_op jit(solution)/shard_map/ppermute | solution.py:364
  118.6 7.9 %copy-start.3 = (f32[512,768]{1,0:T(8,128)S(1)}, f32[512,768]{1,0:T(8,128)}, u32[]{:S(2)}) copy-start(f32[512,768]{1,0:T(8,128)} %copy-done.2) | copy-start | bytes 4718596
  118.6 7.9 %copy-start.29 = (bf16[512,768]{1,0:T(8,128)(2,1)S(1)}, bf16[512,768]{1,0:T(8,128)(2,1)}, u32[]{:S(2)}) copy-start(bf16[512,768]{1,0:T(8,128)(2,1)} %copy-done.28) | copy-start | bytes 2359300
  118.7 7.9 %copy-start.31 = (bf16[512,768]{1,0:T(8,128)(2,1)S(1)}, bf16[512,768]{1,0:T(8,128)(2,1)}, u32[]{:S(2)}) copy-start(bf16[512,768]{1,0:T(8,128)(2,1)} %copy-done.30) | copy-start | bytes 2359300
  118.7 7.9 %copy-start.59 = (f32[512]{0:T(512)S(1)}, f32[512]{0:T(512)}, u32[]{:S(2)}) copy-start(f32[512]{0:T(512)} %copy-done.58) | copy-start | bytes 6148
  118.7 7.9 %copy-start.73 = (f32[512]{0:T(512)S(1)}, f32[512]{0:T(512)}, u32[]{:S(2)}) copy-start(f32[512]{0:T(512)} %copy-done.72) | copy-start | bytes 6148
  118.7 38.8 %collective-permute-start.6 = (bf16[384,768]{1,0:T(8,128)(2,1)}, bf16[384,768]{1,0:T(8,128)(2,1)S(1)}, u32[]{:S(2)}, u32[]{:S(2)}) collective-permute-start(bf16[384,768]{1,0:T(8,128)(2,1)} %convolution_convert_fusion.10), channel_id=1, source_target_pairs={{0,1},{1,0},{2,3},{3,2},{4,5},{5,4},{6,7},{7,6},{8,9},{9,8},{10,11... | collective-permute-start | bytes 1769480 | tf_op jit(solution)/shard_map/ppermute | solution.py:364
  127.7 28.2 %collective-permute-start.9 = (bf16[2,2,2,48,1536]{4,3,2,1,0:T(8,128)(2,1)S(1)}, bf16[2,2,2,48,1536]{4,3,2,1,0:T(8,128)(2,1)}, u32[]{:S(2)}, u32[]{:S(2)}) collective-permute-start(bf16[2,2,2,48,1536]{4,3,2,1,0:T(8,128)(2,1)S(1)} %get-tuple-element.188), channel_id=1, source_target_pairs={{0,16},{8,24},{16,0},{24,8},{1,17},{9,25},{17,1},{25,9},{2,18},{10... | collective-permute-start | bytes 3538952 | tf_op jit(solution)/shard_map/ppermute | solution.py:364
  132.4 13.7 %copy-start.39 = (bf16[512,1536]{1,0:T(8,128)(2,1)S(1)}, bf16[512,1536]{1,0:T(8,128)(2,1)}, u32[]{:S(2)}) copy-start(bf16[512,1536]{1,0:T(8,128)(2,1)} %copy-done.38) | copy-start | bytes 4718596
  150.1 27.8 %collective-permute-start.13 = (bf16[512,768]{1,0:T(8,128)(2,1)}, bf16[512,768]{1,0:T(8,128)(2,1)S(1)}, u32[]{:S(2)}, u32[]{:S(2)}) collective-permute-start(bf16[512,768]{1,0:T(8,128)(2,1)} %convolution_convert_fusion.6), channel_id=1, source_target_pairs={{0,1},{1,0},{2,3},{3,2},{4,5},{5,4},{6,7},{7,6},{8,9},{9,8},{10,11... | collective-permute-start | bytes 2359304 | tf_op jit(solution)/shard_map/ppermute | solution.py:364
  164.3 19.0 %collective-permute-start.11 = (bf16[2,2,48,1536]{3,2,0,1:T(8,128)(2,1)}, bf16[2,2,48,1536]{3,2,0,1:T(8,128)(2,1)}, u32[]{:S(2)}, u32[]{:S(2)}) collective-permute-start(bf16[2,2,48,1536]{3,2,0,1:T(8,128)(2,1)} %bitcast.223), channel_id=1, source_target_pairs={{0,2},{2,0},{4,6},{6,4},{1,3},{3,1},{5,7},{7,5},{8,10},{10,8},{12,... | collective-permute-start | bytes 1769480 | tf_op jit(solution)/shard_map/ppermute | solution.py:364
  181.7 5.9 %copy-start.11 = (bf16[576,768]{1,0:T(8,128)(2,1)S(1)}, bf16[576,768]{1,0:T(8,128)(2,1)}, u32[]{:S(2)}) copy-start(bf16[576,768]{1,0:T(8,128)(2,1)} %copy-done.10) | copy-start | bytes 2654212
  181.7 5.9 %copy-start.13 = (bf16[576,768]{1,0:T(8,128)(2,1)S(1)}, bf16[576,768]{1,0:T(8,128)(2,1)}, u32[]{:S(2)}) copy-start(bf16[576,768]{1,0:T(8,128)(2,1)} %copy-done.12) | copy-start | bytes 2654212
  181.7 5.9 %copy-start.65 = (f32[576]{0:T(1024)S(1)}, f32[576]{0:T(1024)}, u32[]{:S(2)}) copy-start(f32[576]{0:T(1024)} %copy-done.64) | copy-start | bytes 6916
  181.7 5.9 %copy-start.67 = (f32[576]{0:T(1024)S(1)}, f32[576]{0:T(1024)}, u32[]{:S(2)}) copy-start(f32[576]{0:T(1024)} %copy-done.66) | copy-start | bytes 6916
  181.7 21.5 %collective-permute-start.10 = (bf16[576,768]{1,0:T(8,128)(2,1)S(1)}, bf16[576,768]{1,0:T(8,128)(2,1)S(1)}, u32[]{:S(2)}, u32[]{:S(2)}) collective-permute-start(bf16[576,768]{1,0:T(8,128)(2,1)S(1)} %slice.215), channel_id=1, source_target_pairs={{0,1},{1,0},{2,3},{3,2},{4,5},{5,4},{6,7},{7,6},{8,9},{9,8},{10,11... | collective-permute-start | bytes 2654216 | tf_op jit(solution)/shard_map/ppermute | solution.py:364
  185.3 17.9 %collective-permute-start.12 = (bf16[2,48,1536]{2,1,0:T(8,128)(2,1)}, bf16[2,48,1536]{2,1,0:T(8,128)(2,1)S(1)}, u32[]{:S(2)}, u32[]{:S(2)}) collective-permute-start(bf16[2,48,1536]{2,1,0:T(8,128)(2,1)} %get-tuple-element.224), channel_id=1, source_target_pairs={{0,4},{2,6},{4,0},{6,2},{1,5},{3,7},{5,1},{7,3},{8,12},{10,14},{12... | collective-permute-start | bytes 884744 | tf_op jit(solution)/shard_map/ppermute | solution.py:364
  188.3 14.9 %copy-start.41 = (bf16[512,768]{1,0:T(8,128)(2,1)S(1)}, bf16[512,768]{1,0:T(8,128)(2,1)}, u32[]{:S(2)}) copy-start(bf16[512,768]{1,0:T(8,128)(2,1)} %copy-done.40) | copy-start | bytes 2359300
  212.1 12.2 %collective-permute-start.17 = (bf16[4,2,2,2,48,384]{5,4,2,1,0,3:T(8,128)(2,1)S(1)}, bf16[4,2,2,2,48,384]{5,4,2,1,0,3:T(8,128)(2,1)S(1)}, u32[]{:S(2)}, u32[]{:S(2)}) collective-permute-start(bf16[4,2,2,2,48,384]{5,4,2,1,0,3:T(8,128)(2,1)S(1)} %pad_maximum_fusion.3), channel_id=1, source_target_pairs={{0,8},{8,0},{16,24},{24,16},{1,9},{9,1},{17,25},{25,17},{2,10},{10... | collective-permute-start | bytes 3538952 | tf_op jit(solution)/shard_map/ppermute | solution.py:364
  215.8 8.3 %collective-permute-start.19 = (bf16[2,48,1536]{2,1,0:T(8,128)(2,1)S(1)}, bf16[2,48,1536]{2,1,0:T(8,128)(2,1)S(1)}, u32[]{:S(2)}, u32[]{:S(2)}) collective-permute-start(bf16[2,48,1536]{2,1,0:T(8,128)(2,1)S(1)} %add_convert_fusion.13), channel_id=1, source_target_pairs={{0,16},{8,24},{16,0},{24,8},{1,17},{9,25},{17,1},{25,9},{2,18},{10... | collective-permute-start | bytes 884744 | tf_op jit(solution)/shard_map/ppermute | solution.py:364
  217.5 14.4 %collective-permute-start.16 = (bf16[2,192,768]{2,1,0:T(8,128)(2,1)S(1)}, bf16[2,192,768]{2,1,0:T(8,128)(2,1)S(1)}, u32[]{:S(2)}, u32[]{:S(2)}) collective-permute-start(bf16[2,192,768]{2,1,0:T(8,128)(2,1)S(1)} %pad_maximum_fusion.5), channel_id=1, source_target_pairs={{0,2},{2,0},{4,6},{6,4},{1,3},{3,1},{5,7},{7,5},{8,10},{10,8},{12,... | collective-permute-start | bytes 1769480 | tf_op jit(solution)/shard_map/ppermute | solution.py:364
  218.9 28.0 %copy-start.17 = (bf16[528,768]{1,0:T(8,128)(2,1)}, bf16[528,768]{1,0:T(8,128)(2,1)S(1)}, u32[]{:S(2)}) copy-start(bf16[528,768]{1,0:T(8,128)(2,1)S(1)} %fusion.82) | copy-start | bytes 2433028
  218.9 27.9 %collective-permute-start.14 = (bf16[192,768]{1,0:T(8,128)(2,1)S(1)}, bf16[192,768]{1,0:T(8,128)(2,1)S(1)}, u32[]{:S(2)}, u32[]{:S(2)}) collective-permute-start(bf16[192,768]{1,0:T(8,128)(2,1)S(1)} %dynamic-slice_bitcast_fusion.4), channel_id=1, source_target_pairs={{0,1},{1,0},{2,3},{3,2},{4,5},{5,4},{6,7},{7,6},{8,9},{9,8},{10,11... | collective-permute-start | bytes 884744 | tf_op jit(solution)/shard_map/ppermute | solution.py:364
  220.2 26.6 %collective-permute-start.15 = (bf16[528,768]{1,0:T(8,128)(2,1)S(1)}, bf16[528,768]{1,0:T(8,128)(2,1)S(1)}, u32[]{:S(2)}, u32[]{:S(2)}) collective-permute-start(bf16[528,768]{1,0:T(8,128)(2,1)S(1)} %fusion.82), channel_id=1, source_target_pairs={{0,1},{1,0},{2,3},{3,2},{4,5},{5,4},{6,7},{7,6},{8,9},{9,8},{10,11... | collective-permute-start | bytes 2433032 | tf_op jit(solution)/shard_map/ppermute | solution.py:364
  224.2 22.6 %collective-permute-start.20 = (bf16[2,96,1536]{2,1,0:T(8,128)(2,1)S(1)}, bf16[2,96,1536]{2,1,0:T(8,128)(2,1)S(1)}, u32[]{:S(2)}, u32[]{:S(2)}) collective-permute-start(bf16[2,96,1536]{2,1,0:T(8,128)(2,1)S(1)} %pad_maximum_fusion.6), channel_id=1, source_target_pairs={{0,8},{8,0},{16,24},{24,16},{1,9},{9,1},{17,25},{25,17},{2,10},{10... | collective-permute-start | bytes 1769480 | tf_op jit(solution)/shard_map/ppermute | solution.py:364
  225.0 8.9 %copy-start.45 = (bf16[512,768]{1,0:T(8,128)(2,1)S(1)}, bf16[512,768]{1,0:T(8,128)(2,1)}, u32[]{:S(2)}) copy-start(bf16[512,768]{1,0:T(8,128)(2,1)} %copy-done.44) | copy-start | bytes 2359300
  231.8 14.8 %collective-permute-start.21 = (bf16[4,2,2,48,384]{4,3,2,1,0:T(8,128)(2,1)S(1)}, bf16[4,2,2,48,384]{4,3,2,1,0:T(8,128)(2,1)S(1)}, u32[]{:S(2)}, u32[]{:S(2)}) collective-permute-start(bf16[4,2,2,48,384]{4,3,2,1,0:T(8,128)(2,1)S(1)} %get-tuple-element.194), channel_id=1, source_target_pairs={{0,16},{8,24},{16,0},{24,8},{1,17},{9,25},{17,1},{25,9},{2,18},{10... | collective-permute-start | bytes 1769480 | tf_op jit(solution)/shard_map/ppermute | solution.py:364
  232.4 14.1 %collective-permute-start.18 = (bf16[1,192,768]{2,1,0:T(8,128)(2,1)S(1)}, bf16[1,192,768]{2,1,0:T(8,128)(2,1)S(1)}, u32[]{:S(2)}, u32[]{:S(2)}) collective-permute-start(bf16[1,192,768]{2,1,0:T(8,128)(2,1)S(1)} %fusion.99), channel_id=1, source_target_pairs={{0,4},{2,6},{4,0},{6,2},{1,5},{3,7},{5,1},{7,3},{8,12},{10,14},{12... | collective-permute-start | bytes 884744 | tf_op jit(solution)/shard_map/ppermute | solution.py:364
  236.2 10.7 %copy-start.5 = (bf16[1,1,512,768]{3,2,1,0:T(8,128)(2,1)S(1)}, bf16[1,1,512,768]{3,2,1,0:T(8,128)(2,1)}, u32[]{:S(2)}) copy-start(bf16[1,1,512,768]{3,2,1,0:T(8,128)(2,1)} %param.12) | copy-start | bytes 2359300
  236.2 10.7 %copy-start.55 = (f32[512]{0:T(512)S(1)}, f32[512]{0:T(512)}, u32[]{:S(2)}) copy-start(f32[512]{0:T(512)} %copy-done.54) | copy-start | bytes 6148
  236.2 10.7 %copy-start.69 = (f32[512]{0:T(512)S(1)}, f32[512]{0:T(512)}, u32[]{:S(2)}) copy-start(f32[512]{0:T(512)} %copy-done.68) | copy-start | bytes 6148
  248.4 20.2 %collective-permute-start.22 = (bf16[192,768]{1,0:T(8,128)(2,1)}, bf16[192,768]{1,0:T(8,128)(2,1)}, u32[]{:S(2)}, u32[]{:S(2)}) collective-permute-start(bf16[192,768]{1,0:T(8,128)(2,1)} %fusion.101), channel_id=1, source_target_pairs={{0,1},{1,0},{2,3},{3,2},{4,5},{5,4},{6,7},{7,6},{8,9},{9,8},{10,11... | collective-permute-start | bytes 884744 | tf_op jit(solution)/shard_map/ppermute | solution.py:364
  251.5 4.8 %copy-start.53 = (bf16[384,768]{1,0:T(8,128)(2,1)S(1)}, bf16[384,768]{1,0:T(8,128)(2,1)}, u32[]{:S(2)}) copy-start(bf16[384,768]{1,0:T(8,128)(2,1)} %convolution_convert_fusion.9) | copy-start | bytes 1769476
  251.7 11.6 %collective-permute-start.24 = (bf16[208,384]{1,0:T(8,128)(2,1)S(1)}, bf16[208,384]{1,0:T(8,128)(2,1)S(1)}, u32[]{:S(2)}, u32[]{:S(2)}) collective-permute-start(bf16[208,384]{1,0:T(8,128)(2,1)S(1)} %pad_maximum_fusion.12), channel_id=1, source_target_pairs={{0,2},{2,0},{4,6},{6,4},{1,3},{3,1},{5,7},{7,5},{8,10},{10,8},{12,... | collective-permute-start | bytes 479240 | tf_op jit(solution)/shard_map/ppermute | solution.py:721
  251.8 14.8 %collective-permute-start.25 = (bf16[208,384]{1,0:T(8,128)(2,1)S(1)}, bf16[208,384]{1,0:T(8,128)(2,1)S(1)}, u32[]{:S(2)}, u32[]{:S(2)}) collective-permute-start(bf16[208,384]{1,0:T(8,128)(2,1)S(1)} %pad_maximum_fusion.13), channel_id=1, source_target_pairs={{0,4},{2,6},{4,0},{6,2},{1,5},{3,7},{5,1},{7,3},{8,12},{10,14},{12... | collective-permute-start | bytes 479240 | tf_op jit(solution)/shard_map/ppermute | solution.py:721
  254.5 12.1 %collective-permute-start.26 = (bf16[208,384]{1,0:T(8,128)(2,1)S(1)}, bf16[208,384]{1,0:T(8,128)(2,1)S(1)}, u32[]{:S(2)}, u32[]{:S(2)}) collective-permute-start(bf16[208,384]{1,0:T(8,128)(2,1)S(1)} %pad_maximum_fusion.14), channel_id=1, source_target_pairs={{0,6},{2,4},{4,2},{6,0},{1,7},{3,5},{5,3},{7,1},{8,14},{10,12},{12... | collective-permute-start | bytes 479240 | tf_op jit(solution)/shard_map/ppermute | solution.py:721
  256.3 14.4 %collective-permute-start.23 = (bf16[384,768]{1,0:T(8,128)(2,1)S(1)}, bf16[384,768]{1,0:T(8,128)(2,1)S(1)}, u32[]{:S(2)}, u32[]{:S(2)}) collective-permute-start(bf16[384,768]{1,0:T(8,128)(2,1)S(1)} %copy-done.53), channel_id=1, source_target_pairs={{0,1},{1,0},{2,3},{3,2},{4,5},{5,4},{6,7},{7,6},{8,9},{9,8},{10,11... | collective-permute-start | bytes 1769480 | tf_op jit(solution)/shard_map/ppermute | solution.py:364
  263.3 8.5 %copy-start.8 = (bf16[1,384,768]{2,1,0:T(8,128)(2,1)S(1)}, bf16[1,384,768]{2,1,0:T(8,128)(2,1)}, u32[]{:S(2)}) copy-start(bf16[1,384,768]{2,1,0:T(8,128)(2,1)} %param.11) | copy-start | bytes 1769476
  263.3 8.5 %copy-start.61 = (f32[384]{0:T(512)S(1)}, f32[384]{0:T(512)}, u32[]{:S(2)}) copy-start(f32[384]{0:T(512)} %copy-done.60) | copy-start | bytes 4612
  263.3 8.5 %copy-start.75 = (f32[384]{0:T(512)S(1)}, f32[384]{0:T(512)}, u32[]{:S(2)}) copy-start(f32[384]{0:T(512)} %copy-done.74) | copy-start | bytes 4612
  263.3 9.0 %copy-start.24 = (f32[384,768]{1,0:T(8,128)S(1)}, f32[384,768]{1,0:T(8,128)}, u32[]{:S(2)}) copy-start(f32[384,768]{1,0:T(8,128)} %get-tuple-element.175) | copy-start | bytes 3538948
  266.7 6.9 %collective-permute-start.29 = (bf16[208,384]{1,0:T(8,128)(2,1)S(1)}, bf16[208,384]{1,0:T(8,128)(2,1)S(1)}, u32[]{:S(2)}, u32[]{:S(2)}) collective-permute-start(bf16[208,384]{1,0:T(8,128)(2,1)S(1)} %add_convert_fusion.15), channel_id=1, source_target_pairs={{0,24},{8,16},{16,8},{24,0},{1,25},{9,17},{17,9},{25,1},{2,26},{10... | collective-permute-start | bytes 479240 | tf_op jit(solution)/shard_map/ppermute | solution.py:443
  266.8 9.8 %collective-permute-start.28 = (bf16[208,384]{1,0:T(8,128)(2,1)S(1)}, bf16[208,384]{1,0:T(8,128)(2,1)S(1)}, u32[]{:S(2)}, u32[]{:S(2)}) collective-permute-start(bf16[208,384]{1,0:T(8,128)(2,1)S(1)} %add_convert_fusion.15), channel_id=1, source_target_pairs={{0,16},{8,24},{16,0},{24,8},{1,17},{9,25},{17,1},{25,9},{2,18},{10... | collective-permute-start | bytes 479240 | tf_op jit(solution)/shard_map/ppermute | solution.py:443
  268.4 8.2 %collective-permute-start.27 = (bf16[208,384]{1,0:T(8,128)(2,1)S(1)}, bf16[208,384]{1,0:T(8,128)(2,1)S(1)}, u32[]{:S(2)}, u32[]{:S(2)}) collective-permute-start(bf16[208,384]{1,0:T(8,128)(2,1)S(1)} %add_convert_fusion.15), channel_id=1, source_target_pairs={{0,8},{8,0},{16,24},{24,16},{1,9},{9,1},{17,25},{25,17},{2,10},{10... | collective-permute-start | bytes 479240 | tf_op jit(solution)/shard_map/ppermute | solution.py:443
  (53 other events, 121.4 us)

commit v7 on v6

--- a/solution.py
+++ b/solution.py
@@ -602,10 +602,10 @@
         if bit + 1 < grp_bits:
             ffn_part = add_low(ffn_pair)
     dq_c, partial = pull_far(own_c, far, bias_far, do_c, att_c, log_c, None, rows_p)
-    ffn_pair = all_after(ffn_pair, dq_c)
+    second_p = terms_two_p.astype(F32) + after(second_other_p, dq_c).astype(F32)
+    second_p = lax.optimization_barrier(second_p)
+    ffn_pair = all_after(ffn_pair, second_p)
     ffn_part = add_low(ffn_pair)
-    second_other_p = after(second_other_p, ffn_part)
-    second_p = terms_two_p.astype(F32) + second_other_p.astype(F32)
     grad_p, dm_p, do_p = rest(cot_p, two_p, inv_two_p, second_p)
     for bit in range(seq_bits - 1):
         ffn_pair = halve(ffn_part, "seq", bit, seq_bits - bit)

time: 288 us -> 282 us (0.979)
  waiting for transfers between devices: 51.1 us -> 44.1 us
    ppermute x21, waiting for transfers between devices: 43.9 us -> 38 us  [swap(): return lax.ppermute(array, axis, [(j, j ^ 1 << bit) for j in range(count)])]
  transfers between devices with their start and end apart: 30 -> 30, of which waited for: 13 -> 13; matrix products, arithmetic and copies ran while one was open for 29% -> 29% of each run, Pallas kernels for 24% -> 25%
where the time goes in v7:
time: 282 us; the launch traced here: 278 us
  Pallas kernels  76.2 us (27%)
  other arithmetic  47.3 us (17%)
  matrix products  46.2 us (16%)
  waiting for transfers between devices  44.1 us (16%)
  starting transfers between devices  36.1 us (13%)
  local copies, waits for them, and re-layouts  24.3 us (9%)
  between operations  3.38 us (1%)
    ppermute x21, waiting for transfers between devices, swap(): return lax.ppermute(array, axis, [(j, j ^ 1 << bit) for j in range(count)])  38 us
    pallas_call x2, Pallas kernels, pull_far(): pl.pallas_call(functools.partial(pull_far_kernel, masked=masked, chunk=ch...  25.2 us
    ppermute x21, starting transfers between devices, swap(): return lax.ppermute(array, axis, [(j, j ^ 1 << bit) for j in range(count)])  24 us
    pallas_call x1, Pallas kernels, pull_near(): pl.pallas_call(pull_near_kernel, grid=(width // LANES,), in_specs=specs,...  14.8 us
    pallas_call x2, Pallas kernels, attend_far(): pl.pallas_call(functools.partial(far_kernel, masked=masked), grid=(width...  14 us
    dot_general x8, matrix products, rows_dot(): return jnp.einsum('nd,nf->df', left, right, preferred_element_type=F32)  13.8 us
    dot_general x6, matrix products, wide_dot(): return jnp.dot(left, right, preferred_element_type=F32)  11.3 us
    pallas_call x1, Pallas kernels, attend_near(): pl.pallas_call(near_kernel, grid=(width // LANES,), in_specs=[kind_spec(o...  11.1 us
  transfers between devices with their start and end apart: 30, of which 13 were waited for; matrix products, arithmetic and copies ran while one was open for 29% of the time, Pallas kernels for 25%

profile of v7, /device:TPU:0, one launch (start us, length us, event | category | flops | bytes accessed | tf_op | source)
XLA Modules:
  0.0 277.6 jit_solution(12418659948826377458)
XLA Ops:
  0.7 1.9 dynamic-slice_bitcast_fusion.7
  2.5 5.1 %collective-permute-start.2 = (bf16[192,768]{1,0:T(8,128)(2,1)}, bf16[192,768]{1,0:T(8,128)(2,1)S(1)}, u32[]{:S(2)}, u32[]{:S(2)}) collective-permute-start(bf16[192,768]{1,0:T(8,128)(2,1)} %dynamic-slice_bitcast_fusion.7), channel_id=1, source_target_pairs={{0,6},{2,4},{4,2},{6,0},{1,7},{3,5},{5,3},{7,1},{8,14},{10,12},{12... | collective-permute-start | bytes 884744 | tf_op jit(solution)/shard_map/ppermute | solution.py:507
  11.4 2.4 subtract_multiply_fusion.2
  13.7 1.5 fusion.34
  16.0 1.8 fusion.59.qp_ref.kp_ref.vp_ref.refs_0_
  17.8 2.2 fusion.48.qc_ref.kc_ref.vc_ref.refs_0_
  21.1 11.1 %shard_map.186 = (f32[384,384]{1,0:T(8,128)}, f32[3,8,384]{2,1,0:T(8,128)}, f32[512,384]{1,0:T(8,128)}, f32[3,8,512]{2,1,0:T(8,128)}) custom-call(bf16[3,384,384]{2,1,0:T(8,128)(2,1)} %fusion.59.qp_ref.kp_ref.vp_ref.refs_0_, bf16[3,384,384]{2,1,0:T(8,128)(2,1)} %fusion.59.qp_ref.kp_ref.vp_ref.refs_0_, ...), custom_call_target="tpu_custom_call" | custom-call | flops 1212416 | bytes 5120 | tf_op jit(solution)/shard_map/pallas_call | solution.py:122
  34.2 1.6 collective-permute-start.3
  37.3 1.8 fusion.65.k_ref.v_ref
  39.9 11.1 %shard_map.187 = (f32[384,384]{1,0:T(8,128)}, f32[3,8,384]{2,1,0:T(8,128)}, f32[512,384]{1,0:T(8,128)}, f32[3,8,512]{2,1,0:T(8,128)}) custom-call(bf16[2,576,384]{2,1,0:T(8,128)(2,1)} %fusion.65.k_ref.v_ref, bf16[2,576,384]{2,1,0:T(8,128)(2,1)} %fusion.65.k_ref.v_ref, f32[576,128]{1,0:T(8,128)} %broadcast_in_dim.37.bias_ref, ...), custom_call_target="tpu_custom_call" | custom-call | flops 1032192 | bytes 2304 | tf_op jit(solution)/shard_map/pallas_call | solution.py:176
  51.0 4.0 %collective-permute-done.3 = bf16[576,768]{1,0:T(8,128)(2,1)S(1)} collective-permute-done((bf16[576,768]{1,0:T(8,128)(2,1)S(1)}, bf16[576,768]{1,0:T(8,128)(2,1)S(1)}, u32[]{:S(2)}, u32[]{:S(2)}) %collective-permute-start.3) | collective-permute-done | bytes 884768 | tf_op jit(solution)/shard_map/ppermute | solution.py:364
  56.8 1.8 fusion.66.refs_1_.refs_2_
  59.4 7.6 %shard_map.188 = (bf16[512,384]{1,0:T(8,128)(2,1)}, f32[3,8,512]{2,1,0:T(8,128)}) custom-call(bf16[3,512,384]{2,1,0:T(8,128)(2,1)} %fusion.48.qc_ref.kc_ref.vc_ref.refs_0_, bf16[2,576,384]{2,1,0:T(8,128)(2,1)} %fusion.66.refs_1_.refs_2_, bf16[2,576,384]{2,1,0:T(8,128)(2,1)} %fusion.66.refs_1_.refs_2_, f32[576,128]{1,0:T(8,128)} %broadcast_in_dim.38.refs_3_, ...), custom_call_target="tpu_custom_call" | custom-call | flops 589824 | bytes 2304 | tf_op jit(solution)/shard_map/pallas_call | solution.py:222
  67.0 2.4 convolution_convert_fusion.8
  69.4 1.5 collective-permute-start.4
  71.0 6.4 %shard_map.189 = (bf16[384,384]{1,0:T(8,128)(2,1)}, f32[3,8,384]{2,1,0:T(8,128)}) custom-call(bf16[3,384,384]{2,1,0:T(8,128)(2,1)} %fusion.59.qp_ref.kp_ref.vp_ref.refs_0_, bf16[2,576,384]{2,1,0:T(8,128)(2,1)} %fusion.66.refs_1_.refs_2_, bf16[2,576,384]{2,1,0:T(8,128)(2,1)} %fusion.66.refs_1_.refs_2_, f32[384,384]{1,0:T(8,128)} %get-tuple-element.91.refs_3_, ...), custom_call_target="tpu_custom_call" | custom-call | flops 442368 | bytes 2304 | tf_op jit(solution)/shard_map/pallas_call | solution.py:222
  77.4 1.4 convolution_convert_fusion.12
  79.4 1.5 pad_maximum_fusion.refs_1_.refs_2_
  84.5 1.4 fusion.118
  85.9 4.2 %collective-permute-done.4 = bf16[512,768]{1,0:T(8,128)(2,1)} collective-permute-done((bf16[512,768]{1,0:T(8,128)(2,1)}, bf16[512,768]{1,0:T(8,128)(2,1)}, u32[]{:S(2)}, u32[]{:S(2)}) %collective-permute-start.4) | collective-permute-done | bytes 786464 | tf_op jit(solution)/shard_map/ppermute | solution.py:364
  91.2 1.7 fusion.114
  94.1 1.4 fusion.120
  95.5 1.5 multiply_convert_fusion
  97.0 1.4 convolution_convert_fusion.7
  98.5 1.6 collective-permute-start.7
  100.1 2.7 collective-permute-done.5
  103.6 1.9 multiply_convert_fusion.1
  105.5 2.9 %convolution_convert_fusion.1 = bf16[768,1536]{1,0:T(8,128)(2,1)S(1)} fusion(bf16[512,1536]{1,0:T(8,128)(2,1)S(1)} %get-tuple-element.185, bf16[384,1536]{1,0:T(8,128)(2,1)S(1)} %get-tuple-element.191, bf16[512,768]{1,0:T(8,128)(2,1)S(1)} %add_convert_fusion.5, bf16[384,768]{1,0:T(8,128)(2,1)S(1)} %add_convert_fusion.11), kind=kOutput, calls=%fused_computation.10 | convolution fusion | flops 2123366400 | bytes 6488064 | tf_op jit(solution)/shard_map/nd,nf->df/dot_general | solution.py:413
  108.5 3.1 %convolution_convert_fusion = bf16[768,1536]{1,0:T(8,128)(2,1)S(1)} fusion(bf16[512,1536]{1,0:T(8,128)(2,1)S(1)} %get-tuple-element.111, bf16[384,1536]{1,0:T(8,128)(2,1)S(1)} %get-tuple-element.136, bf16[512,768]{1,0:T(8,128)(2,1)S(1)} %bitcast.261, bf16[384,768]{1,0:T(8,128)(2,1)S(1)} %bitcast.271), kind=kOutput, calls=%fused_computation.9 | convolution fusion | flops 2123366400 | bytes 6488064 | tf_op jit(solution)/shard_map/nd,nf->df/dot_general | solution.py:413
  111.6 1.9 convolution_convert_fusion.10
  113.5 3.4 %collective-permute-done.7 = bf16[512,768]{1,0:T(8,128)(2,1)S(1)} collective-permute-done((bf16[512,768]{1,0:T(8,128)(2,1)S(1)}, bf16[512,768]{1,0:T(8,128)(2,1)S(1)}, u32[]{:S(2)}, u32[]{:S(2)}) %collective-permute-start.7) | collective-permute-done | bytes 786464 | tf_op jit(solution)/shard_map/ppermute | solution.py:364
  116.9 1.7 fusion.21
  118.7 1.6 collective-permute-start.6
  120.3 3.2 %collective-permute-done.8 = bf16[2,2,2,2,48,1536]{5,4,3,2,1,0:T(8,128)(2,1)} collective-permute-done((bf16[2,2,2,2,48,1536]{5,4,3,2,1,0:T(8,128)(2,1)}, bf16[2,2,2,2,48,1536]{5,4,3,2,1,0:T(8,128)(2,1)}, u32[]{:S(2)}, u32[]{:S(2)}) %collective-permute-start.8) | collective-permute-done | bytes 2359328 | tf_op jit(solution)/shard_map/ppermute | solution.py:364
  123.5 3.0 %fusion = bf16[2,2,2,2,48,1536]{5,4,3,2,1,0:T(8,128)(2,1)S(1)} fusion(bf16[2,2,2,2,48,1536]{5,4,3,2,1,0:T(8,128)(2,1)} %collective-permute-done.8, s32[]{:T(128)S(6)} %select_n.236, bf16[1,2,2,2,2,48,1536]{6,5,4,3,2,1,0:T(8,128)(2,1)} %bitcast.237, bf16[1,2,2,2,2,48,1536]{6,5,4,3,2,1,0:T(8,128)(2,1)} %bitcast.239), kind=kLoop, calls=%fused_computation.6 | loop fusion | flops 5898240 | bytes 9437188 | tf_op jit(solution)/shard_map/convert_element_type | solution.py:383
  127.7 1.6 collective-permute-start.10
  129.3 1.8 fusion.112
  132.5 13.6 %shard_map.190 = (f32[512,384]{1,0:T(8,128)}, f32[2,1152,384]{2,1,0:T(8,128)}) custom-call(bf16[3,512,384]{2,1,0:T(8,128)(2,1)} %fusion.48.qc_ref.kc_ref.vc_ref.refs_0_, bf16[2,1152,384]{2,1,0:T(8,128)(2,1)} %pad_maximum_fusion.refs_1_.refs_2_, bf16[2,1152,384]{2,1,0:T(8,128)(2,1)} %pad_maximum_fusion.refs_1_.refs_2_, f32[1152,128]{1,0:T(8,128)} %broadcast_in_dim.39.refs_3_, ...), custom_call_target="tpu_custom_call" | custom-call | flops 2949120 | bytes 9216 | tf_op jit(solution)/shard_map/pallas_call | solution.py:310
  147.3 1.7 fusion.69
  149.2 1.5 fusion.111
  153.3 2.3 convolution_convert_fusion.6
  155.5 1.5 collective-permute-start.13
  157.1 1.6 add_convert_fusion.1
  161.7 11.6 %shard_map.191 = (f32[384,384]{1,0:T(8,128)}, bf16[2,1152,384]{2,1,0:T(8,128)(2,1)}) custom-call(bf16[3,384,384]{2,1,0:T(8,128)(2,1)} %fusion.59.qp_ref.kp_ref.vp_ref.refs_0_, bf16[2,1152,384]{2,1,0:T(8,128)(2,1)} %pad_maximum_fusion.refs_1_.refs_2_, bf16[2,1152,384]{2,1,0:T(8,128)(2,1)} %pad_maximum_fusion.refs_1_.refs_2_, ...), custom_call_target="tpu_custom_call" | custom-call | flops 2211840 | bytes 9216 | tf_op jit(solution)/shard_map/pallas_call | solution.py:310
  173.3 3.1 %fusion.116 = (f32[768]{0:T(1024)S(1)}, bf16[1152,768]{1,0:T(8,128)(2,1)S(1)}, f32[1152,768]{1,0:T(8,128)S(1)}) fusion(bf16[2,1152,384]{2,1,0:T(8,128)(2,1)} %get-tuple-element.115, bf16[3,768,384]{2,1,0:T(8,128)(2,1)S(1)} %copy-done.82), kind=kOutput, calls=%fused_computation.299 | convolution fusion | flops 1360723200 | bytes 8260608 | tf_op jit(solution)/shard_map/cne,cde->nd/dot_general | solution.py:621
  179.3 2.4 collective-permute-start.12
  182.3 14.8 %shard_map.192 = bf16[3,896,384]{2,1,0:T(8,128)(2,1)} custom-call(bf16[3,384,384]{2,1,0:T(8,128)(2,1)} %fusion.59.qp_ref.kp_ref.vp_ref.refs_0_, bf16[3,384,384]{2,1,0:T(8,128)(2,1)} %fusion.59.qp_ref.kp_ref.vp_ref.refs_0_, bf16[3,384,384]{2,1,0:T(8,128)(2,1)} %fusion.59.qp_ref.kp_ref.vp_ref.refs_0_, ...), custom_call_target="tpu_custom_call" | custom-call | flops 3031040 | bytes 5120 | tf_op jit(solution)/shard_map/pallas_call | solution.py:351
  197.4 2.4 convolution_convert_fusion.11
  207.5 2.0 bitcast_convert_fusion
  214.6 1.5 collective-permute-start.15
  216.1 2.9 %collective-permute-done.19 = bf16[2,48,1536]{2,1,0:T(8,128)(2,1)S(1)} collective-permute-done((bf16[2,48,1536]{2,1,0:T(8,128)(2,1)S(1)}, bf16[2,48,1536]{2,1,0:T(8,128)(2,1)S(1)}, u32[]{:S(2)}, u32[]{:S(2)}) %collective-permute-start.19) | collective-permute-done | bytes 294944 | tf_op jit(solution)/shard_map/ppermute | solution.py:364
  220.0 6.3 %collective-permute-done.16 = bf16[2,192,768]{2,1,0:T(8,128)(2,1)S(1)} collective-permute-done((bf16[2,192,768]{2,1,0:T(8,128)(2,1)S(1)}, bf16[2,192,768]{2,1,0:T(8,128)(2,1)S(1)}, u32[]{:S(2)}, u32[]{:S(2)}) %collective-permute-start.16) | collective-permute-done | bytes 589856 | tf_op jit(solution)/shard_map/ppermute | solution.py:364
  227.3 2.5 collective-permute-start.18
  229.8 2.5 fusion.81
  232.3 9.1 %collective-permute-done.18 = bf16[1,192,768]{2,1,0:T(8,128)(2,1)S(1)} collective-permute-done((bf16[1,192,768]{2,1,0:T(8,128)(2,1)S(1)}, bf16[1,192,768]{2,1,0:T(8,128)(2,1)S(1)}, u32[]{:S(2)}, u32[]{:S(2)}) %collective-permute-start.18) | collective-permute-done | bytes 294944 | tf_op jit(solution)/shard_map/ppermute | solution.py:364
  244.7 1.9 convolution_convert_fusion.9
  247.1 2.6 collective-permute-start.25
  249.8 1.9 collective-permute-start.26
  254.2 1.6 slice_bitcast_fusion
  256.9 1.6 fusion.82
  258.6 3.3 %collective-permute-done.25 = bf16[208,384]{1,0:T(8,128)(2,1)S(1)} collective-permute-done((bf16[208,384]{1,0:T(8,128)(2,1)S(1)}, bf16[208,384]{1,0:T(8,128)(2,1)S(1)}, u32[]{:S(2)}, u32[]{:S(2)}) %collective-permute-start.25) | collective-permute-done | bytes 159776 | tf_op jit(solution)/shard_map/ppermute | solution.py:721
  263.9 1.9 collective-permute-done.23
  268.7 1.9 collective-permute-done.28
  275.0 2.1 slice.227
  (349 shorter events, 63.0 us)
Async XLA Ops:
  0.6 93.5 %copy-start = (bf16[768,1536]{1,0:T(8,128)(2,1)S(1)}, bf16[768,1536]{1,0:T(8,128)(2,1)}, u32[]{:S(2)}) copy-start(bf16[768,1536]{1,0:T(8,128)(2,1)} %param.18) | copy-start | bytes 7077892
  0.7 9.5 %copy-start.4 = (bf16[1,1,512,768]{3,2,1,0:T(8,128)(2,1)S(1)}, bf16[1,1,512,768]{3,2,1,0:T(8,128)(2,1)}, u32[]{:S(2)}) copy-start(bf16[1,1,512,768]{3,2,1,0:T(8,128)(2,1)} %param.12) | copy-start | bytes 2359300
  0.7 10.4 %copy-start.74 = (bf16[2,768]{1,0:T(2,128)(2,1)S(1)}, bf16[2,768]{1,0:T(2,128)(2,1)}, u32[]{:S(2)}) copy-start(bf16[2,768]{1,0:T(2,128)(2,1)} %param.20) | copy-start | bytes 9220
  0.7 10.4 %copy-start.75 = (bf16[2,768]{1,0:T(2,128)(2,1)S(1)}, bf16[2,768]{1,0:T(2,128)(2,1)}, u32[]{:S(2)}) copy-start(bf16[2,768]{1,0:T(2,128)(2,1)} %param.21) | copy-start | bytes 9220
  2.5 29.7 %collective-permute-start.2 = (bf16[192,768]{1,0:T(8,128)(2,1)}, bf16[192,768]{1,0:T(8,128)(2,1)S(1)}, u32[]{:S(2)}, u32[]{:S(2)}) collective-permute-start(bf16[192,768]{1,0:T(8,128)(2,1)} %dynamic-slice_bitcast_fusion.7), channel_id=1, source_target_pairs={{0,6},{2,4},{4,2},{6,0},{1,7},{3,5},{5,3},{7,1},{8,14},{10,12},{12... | collective-permute-start | bytes 884744 | tf_op jit(solution)/shard_map/ppermute | solution.py:507
  7.6 25.4 %collective-permute-start.1 = (bf16[192,768]{1,0:T(8,128)(2,1)}, bf16[192,768]{1,0:T(8,128)(2,1)}, u32[]{:S(2)}, u32[]{:S(2)}) collective-permute-start(bf16[192,768]{1,0:T(8,128)(2,1)} %dynamic-slice_bitcast_fusion.7), channel_id=1, source_target_pairs={{0,4},{2,6},{4,0},{6,2},{1,5},{3,7},{5,1},{7,3},{8,12},{10,14},{12... | collective-permute-start | bytes 884744 | tf_op jit(solution)/shard_map/ppermute | solution.py:507
  7.6 25.4 %collective-permute-start = (bf16[192,768]{1,0:T(8,128)(2,1)}, bf16[192,768]{1,0:T(8,128)(2,1)}, u32[]{:S(2)}, u32[]{:S(2)}) collective-permute-start(bf16[192,768]{1,0:T(8,128)(2,1)} %dynamic-slice_bitcast_fusion.7), channel_id=1, source_target_pairs={{0,2},{2,0},{4,6},{6,4},{1,3},{3,1},{5,7},{7,5},{8,10},{10,8},{12,... | collective-permute-start | bytes 884744 | tf_op jit(solution)/shard_map/ppermute | solution.py:507
  10.7 4.5 %copy-start.66 = (f32[512]{0:T(512)}, f32[512]{0:T(512)S(1)}, u32[]{:S(2)}) copy-start(f32[512]{0:T(512)S(1)} %add_rsqrt_fusion.5) | copy-start | bytes 6148
  11.3 82.0 %copy-start.60 = (f32[768]{0:T(1024)}, f32[768]{0:T(1024)S(1)}, u32[]{:S(2)}) copy-start(f32[768]{0:T(1024)S(1)} %get-tuple-element.172) | copy-start | bytes 9220
  21.0 11.1 %copy-start.7 = (bf16[1,384,768]{2,1,0:T(8,128)(2,1)S(1)}, bf16[1,384,768]{2,1,0:T(8,128)(2,1)}, u32[]{:S(2)}) copy-start(bf16[1,384,768]{2,1,0:T(8,128)(2,1)} %param.11) | copy-start | bytes 1769476
  34.2 20.8 %collective-permute-start.3 = (bf16[576,768]{1,0:T(8,128)(2,1)S(1)}, bf16[576,768]{1,0:T(8,128)(2,1)S(1)}, u32[]{:S(2)}, u32[]{:S(2)}) collective-permute-start(bf16[576,768]{1,0:T(8,128)(2,1)S(1)} %pad_maximum_fusion.4), channel_id=1, source_target_pairs={{0,1},{1,0},{2,3},{3,2},{4,5},{5,4},{6,7},{7,6},{8,9},{9,8},{10,11... | collective-permute-start | bytes 2654216 | tf_op jit(solution)/shard_map/ppermute | solution.py:364
  59.4 7.6 %copy-start.21 = (bf16[384,768]{1,0:T(8,128)(2,1)S(1)}, bf16[384,768]{1,0:T(8,128)(2,1)}, u32[]{:S(2)}) copy-start(bf16[384,768]{1,0:T(8,128)(2,1)} %param.17) | copy-start | bytes 1769476
  69.4 20.7 %collective-permute-start.4 = (bf16[512,768]{1,0:T(8,128)(2,1)}, bf16[512,768]{1,0:T(8,128)(2,1)}, u32[]{:S(2)}, u32[]{:S(2)}) collective-permute-start(bf16[512,768]{1,0:T(8,128)(2,1)} %convolution_convert_fusion.8), channel_id=1, source_target_pairs={{0,1},{1,0},{2,3},{3,2},{4,5},{5,4},{6,7},{7,6},{8,9},{9,8},{10,11... | collective-permute-start | bytes 2359304 | tf_op jit(solution)/shard_map/ppermute | solution.py:364
  71.0 8.4 %copy-start.9 = (bf16[2,576,384]{2,1,0:T(8,128)(2,1)S(1)}, bf16[2,576,384]{2,1,0:T(8,128)(2,1)}, u32[]{:S(2)}) copy-start(bf16[2,576,384]{2,1,0:T(8,128)(2,1)} %fusion.66.refs_1_.refs_2_) | copy-start | bytes 2654212
  71.0 8.4 %copy-start.16 = (bf16[2,576,384]{2,1,0:T(8,128)(2,1)S(1)}, bf16[2,576,384]{2,1,0:T(8,128)(2,1)}, u32[]{:S(2)}) copy-start(bf16[2,576,384]{2,1,0:T(8,128)(2,1)} %fusion.65.k_ref.v_ref) | copy-start | bytes 2654212
  78.8 23.9 %collective-permute-start.5 = (bf16[384,768]{1,0:T(8,128)(2,1)S(1)}, bf16[384,768]{1,0:T(8,128)(2,1)S(1)}, u32[]{:S(2)}, u32[]{:S(2)}) collective-permute-start(bf16[384,768]{1,0:T(8,128)(2,1)S(1)} %convolution_convert_fusion.12), channel_id=1, source_target_pairs={{0,1},{1,0},{2,3},{3,2},{4,5},{5,4},{6,7},{7,6},{8,9},{9,8},{10,11... | collective-permute-start | bytes 1769480 | tf_op jit(solution)/shard_map/ppermute | solution.py:364
  97.0 11.4 %copy-start.38 = (bf16[512,1536]{1,0:T(8,128)(2,1)}, bf16[512,1536]{1,0:T(8,128)(2,1)S(1)}, u32[]{:S(2)}) copy-start(bf16[512,1536]{1,0:T(8,128)(2,1)S(1)} %get-tuple-element.111) | copy-start | bytes 4718596
  98.5 4.5 %copy-start.28 = (bf16[512,768]{1,0:T(8,128)(2,1)}, bf16[512,768]{1,0:T(8,128)(2,1)S(1)}, u32[]{:S(2)}) copy-start(bf16[512,768]{1,0:T(8,128)(2,1)S(1)} %convolution_convert_fusion.7) | copy-start | bytes 2359300
  98.5 4.8 %copy-start.61 = (f32[768]{0:T(1024)S(1)}, f32[768]{0:T(1024)}, u32[]{:S(2)}) copy-start(f32[768]{0:T(1024)} %copy-done.60) | copy-start | bytes 9220
  98.5 18.4 %collective-permute-start.7 = (bf16[512,768]{1,0:T(8,128)(2,1)S(1)}, bf16[512,768]{1,0:T(8,128)(2,1)S(1)}, u32[]{:S(2)}, u32[]{:S(2)}) collective-permute-start(bf16[512,768]{1,0:T(8,128)(2,1)S(1)} %convolution_convert_fusion.7), channel_id=1, source_target_pairs={{0,1},{1,0},{2,3},{3,2},{4,5},{5,4},{6,7},{7,6},{8,9},{9,8},{10,11... | collective-permute-start | bytes 2359304 | tf_op jit(solution)/shard_map/ppermute | solution.py:364
  108.4 8.5 %copy-start.14 = (bf16[768,1536]{1,0:T(8,128)(2,1)}, bf16[768,1536]{1,0:T(8,128)(2,1)S(1)}, u32[]{:S(2)}) copy-start(bf16[768,1536]{1,0:T(8,128)(2,1)S(1)} %convolution_convert_fusion.1) | copy-start | bytes 7077892
  111.6 5.3 %copy-start.15 = (bf16[768,1536]{1,0:T(8,128)(2,1)}, bf16[768,1536]{1,0:T(8,128)(2,1)S(1)}, u32[]{:S(2)}) copy-start(bf16[768,1536]{1,0:T(8,128)(2,1)S(1)} %convolution_convert_fusion) | copy-start | bytes 7077892
  118.6 4.9 %collective-permute-start.8 = (bf16[2,2,2,2,48,1536]{5,4,3,2,1,0:T(8,128)(2,1)}, bf16[2,2,2,2,48,1536]{5,4,3,2,1,0:T(8,128)(2,1)}, u32[]{:S(2)}, u32[]{:S(2)}) collective-permute-start(bf16[2,2,2,2,48,1536]{5,4,3,2,1,0:T(8,128)(2,1)} %fusion.21), channel_id=1, source_target_pairs={{0,8},{8,0},{16,24},{24,16},{1,9},{9,1},{17,25},{25,17},{2,10},{10... | collective-permute-start | bytes 7077896 | tf_op jit(solution)/shard_map/ppermute | solution.py:364
  118.6 7.9 %copy-start.3 = (f32[512,768]{1,0:T(8,128)S(1)}, f32[512,768]{1,0:T(8,128)}, u32[]{:S(2)}) copy-start(f32[512,768]{1,0:T(8,128)} %copy-done.2) | copy-start | bytes 4718596
  118.6 7.9 %copy-start.29 = (bf16[512,768]{1,0:T(8,128)(2,1)S(1)}, bf16[512,768]{1,0:T(8,128)(2,1)}, u32[]{:S(2)}) copy-start(bf16[512,768]{1,0:T(8,128)(2,1)} %copy-done.28) | copy-start | bytes 2359300
  118.7 7.9 %copy-start.31 = (bf16[512,768]{1,0:T(8,128)(2,1)S(1)}, bf16[512,768]{1,0:T(8,128)(2,1)}, u32[]{:S(2)}) copy-start(bf16[512,768]{1,0:T(8,128)(2,1)} %copy-done.30) | copy-start | bytes 2359300
  118.7 7.9 %copy-start.55 = (f32[512]{0:T(512)S(1)}, f32[512]{0:T(512)}, u32[]{:S(2)}) copy-start(f32[512]{0:T(512)} %copy-done.54) | copy-start | bytes 6148
  118.7 7.9 %copy-start.69 = (f32[512]{0:T(512)S(1)}, f32[512]{0:T(512)}, u32[]{:S(2)}) copy-start(f32[512]{0:T(512)} %copy-done.68) | copy-start | bytes 6148
  118.7 27.4 %collective-permute-start.6 = (bf16[384,768]{1,0:T(8,128)(2,1)}, bf16[384,768]{1,0:T(8,128)(2,1)S(1)}, u32[]{:S(2)}, u32[]{:S(2)}) collective-permute-start(bf16[384,768]{1,0:T(8,128)(2,1)} %convolution_convert_fusion.10), channel_id=1, source_target_pairs={{0,1},{1,0},{2,3},{3,2},{4,5},{5,4},{6,7},{7,6},{8,9},{9,8},{10,11... | collective-permute-start | bytes 1769480 | tf_op jit(solution)/shard_map/ppermute | solution.py:364
  127.7 29.4 %collective-permute-start.10 = (bf16[2,2,2,48,1536]{4,3,2,1,0:T(8,128)(2,1)S(1)}, bf16[2,2,2,48,1536]{4,3,2,1,0:T(8,128)(2,1)}, u32[]{:S(2)}, u32[]{:S(2)}) collective-permute-start(bf16[2,2,2,48,1536]{4,3,2,1,0:T(8,128)(2,1)S(1)} %get-tuple-element.188), channel_id=1, source_target_pairs={{0,16},{8,24},{16,0},{24,8},{1,17},{9,25},{17,1},{25,9},{2,18},{10... | collective-permute-start | bytes 3538952 | tf_op jit(solution)/shard_map/ppermute | solution.py:364
  155.5 26.8 %collective-permute-start.13 = (bf16[512,768]{1,0:T(8,128)(2,1)}, bf16[512,768]{1,0:T(8,128)(2,1)}, u32[]{:S(2)}, u32[]{:S(2)}) collective-permute-start(bf16[512,768]{1,0:T(8,128)(2,1)} %convolution_convert_fusion.6), channel_id=1, source_target_pairs={{0,1},{1,0},{2,3},{3,2},{4,5},{5,4},{6,7},{7,6},{8,9},{9,8},{10,11... | collective-permute-start | bytes 2359304 | tf_op jit(solution)/shard_map/ppermute | solution.py:364
  159.6 17.6 %collective-permute-start.11 = (bf16[2,2,48,1536]{3,2,0,1:T(8,128)(2,1)}, bf16[2,2,48,1536]{3,2,0,1:T(8,128)(2,1)}, u32[]{:S(2)}, u32[]{:S(2)}) collective-permute-start(bf16[2,2,48,1536]{3,2,0,1:T(8,128)(2,1)} %bitcast.223), channel_id=1, source_target_pairs={{0,2},{2,0},{4,6},{6,4},{1,3},{3,1},{5,7},{7,5},{8,10},{10,8},{12,... | collective-permute-start | bytes 1769480 | tf_op jit(solution)/shard_map/ppermute | solution.py:364
  161.7 11.6 %copy-start.82 = (bf16[3,768,384]{2,1,0:T(8,128)(2,1)S(1)}, bf16[3,768,384]{2,1,0:T(8,128)(2,1)}, u32[]{:S(2)}) copy-start(bf16[3,768,384]{2,1,0:T(8,128)(2,1)} %param.16) | copy-start | bytes 5308420
  176.5 20.9 %collective-permute-start.9 = (bf16[576,768]{1,0:T(8,128)(2,1)S(1)}, bf16[576,768]{1,0:T(8,128)(2,1)S(1)}, u32[]{:S(2)}, u32[]{:S(2)}) collective-permute-start(bf16[576,768]{1,0:T(8,128)(2,1)S(1)} %slice.215), channel_id=1, source_target_pairs={{0,1},{1,0},{2,3},{3,2},{4,5},{5,4},{6,7},{7,6},{8,9},{9,8},{10,11... | collective-permute-start | bytes 2654216 | tf_op jit(solution)/shard_map/ppermute | solution.py:364
  177.1 4.5 %copy-start.11 = (bf16[576,768]{1,0:T(8,128)(2,1)S(1)}, bf16[576,768]{1,0:T(8,128)(2,1)}, u32[]{:S(2)}) copy-start(bf16[576,768]{1,0:T(8,128)(2,1)} %copy-done.10) | copy-start | bytes 2654212
  177.1 4.5 %copy-start.13 = (bf16[576,768]{1,0:T(8,128)(2,1)S(1)}, bf16[576,768]{1,0:T(8,128)(2,1)}, u32[]{:S(2)}) copy-start(bf16[576,768]{1,0:T(8,128)(2,1)} %copy-done.12) | copy-start | bytes 2654212
  179.3 18.1 %collective-permute-start.12 = (bf16[2,48,1536]{2,1,0:T(8,128)(2,1)}, bf16[2,48,1536]{2,1,0:T(8,128)(2,1)S(1)}, u32[]{:S(2)}, u32[]{:S(2)}) collective-permute-start(bf16[2,48,1536]{2,1,0:T(8,128)(2,1)} %get-tuple-element.224), channel_id=1, source_target_pairs={{0,4},{2,6},{4,0},{6,2},{1,5},{3,7},{5,1},{7,3},{8,12},{10,14},{12... | collective-permute-start | bytes 884744 | tf_op jit(solution)/shard_map/ppermute | solution.py:364
  182.3 15.1 %copy-start.41 = (bf16[512,768]{1,0:T(8,128)(2,1)S(1)}, bf16[512,768]{1,0:T(8,128)(2,1)}, u32[]{:S(2)}) copy-start(bf16[512,768]{1,0:T(8,128)(2,1)} %copy-done.40) | copy-start | bytes 2359300
  206.3 12.9 %collective-permute-start.17 = (bf16[4,2,2,2,48,384]{5,4,2,1,0,3:T(8,128)(2,1)S(1)}, bf16[4,2,2,2,48,384]{5,4,2,1,0,3:T(8,128)(2,1)S(1)}, u32[]{:S(2)}, u32[]{:S(2)}) collective-permute-start(bf16[4,2,2,2,48,384]{5,4,2,1,0,3:T(8,128)(2,1)S(1)} %pad_maximum_fusion.3), channel_id=1, source_target_pairs={{0,8},{8,0},{16,24},{24,16},{1,9},{9,1},{17,25},{25,17},{2,10},{10... | collective-permute-start | bytes 3538952 | tf_op jit(solution)/shard_map/ppermute | solution.py:364
  210.7 8.3 %collective-permute-start.19 = (bf16[2,48,1536]{2,1,0:T(8,128)(2,1)S(1)}, bf16[2,48,1536]{2,1,0:T(8,128)(2,1)S(1)}, u32[]{:S(2)}, u32[]{:S(2)}) collective-permute-start(bf16[2,48,1536]{2,1,0:T(8,128)(2,1)S(1)} %add_convert_fusion.13), channel_id=1, source_target_pairs={{0,16},{8,24},{16,0},{24,8},{1,17},{9,25},{17,1},{25,9},{2,18},{10... | collective-permute-start | bytes 884744 | tf_op jit(solution)/shard_map/ppermute | solution.py:364
  212.0 14.4 %collective-permute-start.16 = (bf16[2,192,768]{2,1,0:T(8,128)(2,1)S(1)}, bf16[2,192,768]{2,1,0:T(8,128)(2,1)S(1)}, u32[]{:S(2)}, u32[]{:S(2)}) collective-permute-start(bf16[2,192,768]{2,1,0:T(8,128)(2,1)S(1)} %pad_maximum_fusion.5), channel_id=1, source_target_pairs={{0,2},{2,0},{4,6},{6,4},{1,3},{3,1},{5,7},{7,5},{8,10},{10,8},{12,... | collective-permute-start | bytes 1769480 | tf_op jit(solution)/shard_map/ppermute | solution.py:364
  214.0 27.8 %copy-start.17 = (bf16[528,768]{1,0:T(8,128)(2,1)}, bf16[528,768]{1,0:T(8,128)(2,1)S(1)}, u32[]{:S(2)}) copy-start(bf16[528,768]{1,0:T(8,128)(2,1)S(1)} %fusion.80) | copy-start | bytes 2433028
  214.0 27.7 %collective-permute-start.14 = (bf16[192,768]{1,0:T(8,128)(2,1)S(1)}, bf16[192,768]{1,0:T(8,128)(2,1)S(1)}, u32[]{:S(2)}, u32[]{:S(2)}) collective-permute-start(bf16[192,768]{1,0:T(8,128)(2,1)S(1)} %dynamic-slice_bitcast_fusion.4), channel_id=1, source_target_pairs={{0,1},{1,0},{2,3},{3,2},{4,5},{5,4},{6,7},{7,6},{8,9},{9,8},{10,11... | collective-permute-start | bytes 884744 | tf_op jit(solution)/shard_map/ppermute | solution.py:364
  214.6 27.1 %collective-permute-start.15 = (bf16[528,768]{1,0:T(8,128)(2,1)S(1)}, bf16[528,768]{1,0:T(8,128)(2,1)S(1)}, u32[]{:S(2)}, u32[]{:S(2)}) collective-permute-start(bf16[528,768]{1,0:T(8,128)(2,1)S(1)} %fusion.80), channel_id=1, source_target_pairs={{0,1},{1,0},{2,3},{3,2},{4,5},{5,4},{6,7},{7,6},{8,9},{9,8},{10,11... | collective-permute-start | bytes 2433032 | tf_op jit(solution)/shard_map/ppermute | solution.py:364
  219.1 22.6 %collective-permute-start.20 = (bf16[2,96,1536]{2,1,0:T(8,128)(2,1)S(1)}, bf16[2,96,1536]{2,1,0:T(8,128)(2,1)S(1)}, u32[]{:S(2)}, u32[]{:S(2)}) collective-permute-start(bf16[2,96,1536]{2,1,0:T(8,128)(2,1)S(1)} %pad_maximum_fusion.6), channel_id=1, source_target_pairs={{0,8},{8,0},{16,24},{24,16},{1,9},{9,1},{17,25},{25,17},{2,10},{10... | collective-permute-start | bytes 1769480 | tf_op jit(solution)/shard_map/ppermute | solution.py:364
  226.4 15.1 %collective-permute-start.21 = (bf16[4,2,2,48,384]{4,3,2,1,0:T(8,128)(2,1)S(1)}, bf16[4,2,2,48,384]{4,3,2,1,0:T(8,128)(2,1)S(1)}, u32[]{:S(2)}, u32[]{:S(2)}) collective-permute-start(bf16[4,2,2,48,384]{4,3,2,1,0:T(8,128)(2,1)S(1)} %get-tuple-element.194), channel_id=1, source_target_pairs={{0,16},{8,24},{16,0},{24,8},{1,17},{9,25},{17,1},{25,9},{2,18},{10... | collective-permute-start | bytes 1769480 | tf_op jit(solution)/shard_map/ppermute | solution.py:364
  227.3 14.1 %collective-permute-start.18 = (bf16[1,192,768]{2,1,0:T(8,128)(2,1)S(1)}, bf16[1,192,768]{2,1,0:T(8,128)(2,1)S(1)}, u32[]{:S(2)}, u32[]{:S(2)}) collective-permute-start(bf16[1,192,768]{2,1,0:T(8,128)(2,1)S(1)} %fusion.97), channel_id=1, source_target_pairs={{0,4},{2,6},{4,0},{6,2},{1,5},{3,7},{5,1},{7,3},{8,12},{10,14},{12... | collective-permute-start | bytes 884744 | tf_op jit(solution)/shard_map/ppermute | solution.py:364
  232.3 9.5 %copy-start.5 = (bf16[1,1,512,768]{3,2,1,0:T(8,128)(2,1)S(1)}, bf16[1,1,512,768]{3,2,1,0:T(8,128)(2,1)}, u32[]{:S(2)}) copy-start(bf16[1,1,512,768]{3,2,1,0:T(8,128)(2,1)} %param.12) | copy-start | bytes 2359300
  232.3 9.5 %copy-start.53 = (f32[512]{0:T(512)S(1)}, f32[512]{0:T(512)}, u32[]{:S(2)}) copy-start(f32[512]{0:T(512)} %copy-done.52) | copy-start | bytes 6148
  232.3 9.5 %copy-start.67 = (f32[512]{0:T(512)S(1)}, f32[512]{0:T(512)}, u32[]{:S(2)}) copy-start(f32[512]{0:T(512)} %copy-done.66) | copy-start | bytes 6148
  243.3 20.5 %collective-permute-start.22 = (bf16[192,768]{1,0:T(8,128)(2,1)}, bf16[192,768]{1,0:T(8,128)(2,1)}, u32[]{:S(2)}, u32[]{:S(2)}) collective-permute-start(bf16[192,768]{1,0:T(8,128)(2,1)} %fusion.99), channel_id=1, source_target_pairs={{0,1},{1,0},{2,3},{3,2},{4,5},{5,4},{6,7},{7,6},{8,9},{9,8},{10,11... | collective-permute-start | bytes 884744 | tf_op jit(solution)/shard_map/ppermute | solution.py:364
  246.8 4.8 %copy-start.49 = (bf16[384,768]{1,0:T(8,128)(2,1)S(1)}, bf16[384,768]{1,0:T(8,128)(2,1)}, u32[]{:S(2)}) copy-start(bf16[384,768]{1,0:T(8,128)(2,1)} %convolution_convert_fusion.9) | copy-start | bytes 1769476
  247.0 11.5 %collective-permute-start.24 = (bf16[208,384]{1,0:T(8,128)(2,1)S(1)}, bf16[208,384]{1,0:T(8,128)(2,1)S(1)}, u32[]{:S(2)}, u32[]{:S(2)}) collective-permute-start(bf16[208,384]{1,0:T(8,128)(2,1)S(1)} %pad_maximum_fusion.12), channel_id=1, source_target_pairs={{0,2},{2,0},{4,6},{6,4},{1,3},{3,1},{5,7},{7,5},{8,10},{10,8},{12,... | collective-permute-start | bytes 479240 | tf_op jit(solution)/shard_map/ppermute | solution.py:721
  247.1 14.8 %collective-permute-start.25 = (bf16[208,384]{1,0:T(8,128)(2,1)S(1)}, bf16[208,384]{1,0:T(8,128)(2,1)S(1)}, u32[]{:S(2)}, u32[]{:S(2)}) collective-permute-start(bf16[208,384]{1,0:T(8,128)(2,1)S(1)} %pad_maximum_fusion.13), channel_id=1, source_target_pairs={{0,4},{2,6},{4,0},{6,2},{1,5},{3,7},{5,1},{7,3},{8,12},{10,14},{12... | collective-permute-start | bytes 479240 | tf_op jit(solution)/shard_map/ppermute | solution.py:721
  249.8 12.1 %collective-permute-start.26 = (bf16[208,384]{1,0:T(8,128)(2,1)S(1)}, bf16[208,384]{1,0:T(8,128)(2,1)S(1)}, u32[]{:S(2)}, u32[]{:S(2)}) collective-permute-start(bf16[208,384]{1,0:T(8,128)(2,1)S(1)} %pad_maximum_fusion.14), channel_id=1, source_target_pairs={{0,6},{2,4},{4,2},{6,0},{1,7},{3,5},{5,3},{7,1},{8,14},{10,12},{12... | collective-permute-start | bytes 479240 | tf_op jit(solution)/shard_map/ppermute | solution.py:721
  251.6 14.1 %collective-permute-start.23 = (bf16[384,768]{1,0:T(8,128)(2,1)S(1)}, bf16[384,768]{1,0:T(8,128)(2,1)S(1)}, u32[]{:S(2)}, u32[]{:S(2)}) collective-permute-start(bf16[384,768]{1,0:T(8,128)(2,1)S(1)} %copy-done.49), channel_id=1, source_target_pairs={{0,1},{1,0},{2,3},{3,2},{4,5},{5,4},{6,7},{7,6},{8,9},{9,8},{10,11... | collective-permute-start | bytes 1769480 | tf_op jit(solution)/shard_map/ppermute | solution.py:364
  258.5 8.4 %copy-start.8 = (bf16[1,384,768]{2,1,0:T(8,128)(2,1)S(1)}, bf16[1,384,768]{2,1,0:T(8,128)(2,1)}, u32[]{:S(2)}) copy-start(bf16[1,384,768]{2,1,0:T(8,128)(2,1)} %param.11) | copy-start | bytes 1769476
  258.5 8.4 %copy-start.57 = (f32[384]{0:T(512)S(1)}, f32[384]{0:T(512)}, u32[]{:S(2)}) copy-start(f32[384]{0:T(512)} %copy-done.56) | copy-start | bytes 4612
  258.5 8.4 %copy-start.71 = (f32[384]{0:T(512)S(1)}, f32[384]{0:T(512)}, u32[]{:S(2)}) copy-start(f32[384]{0:T(512)} %copy-done.70) | copy-start | bytes 4612
  258.5 8.8 %copy-start.24 = (f32[384,768]{1,0:T(8,128)S(1)}, f32[384,768]{1,0:T(8,128)}, u32[]{:S(2)}) copy-start(f32[384,768]{1,0:T(8,128)} %get-tuple-element.175) | copy-start | bytes 3538948
  262.0 6.7 %collective-permute-start.29 = (bf16[208,384]{1,0:T(8,128)(2,1)S(1)}, bf16[208,384]{1,0:T(8,128)(2,1)S(1)}, u32[]{:S(2)}, u32[]{:S(2)}) collective-permute-start(bf16[208,384]{1,0:T(8,128)(2,1)S(1)} %add_convert_fusion.15), channel_id=1, source_target_pairs={{0,24},{8,16},{16,8},{24,0},{1,25},{9,17},{17,9},{25,1},{2,26},{10... | collective-permute-start | bytes 479240 | tf_op jit(solution)/shard_map/ppermute | solution.py:443
  262.0 8.6 %collective-permute-start.28 = (bf16[208,384]{1,0:T(8,128)(2,1)S(1)}, bf16[208,384]{1,0:T(8,128)(2,1)S(1)}, u32[]{:S(2)}, u32[]{:S(2)}) collective-permute-start(bf16[208,384]{1,0:T(8,128)(2,1)S(1)} %add_convert_fusion.15), channel_id=1, source_target_pairs={{0,16},{8,24},{16,0},{24,8},{1,17},{9,25},{17,1},{25,9},{2,18},{10... | collective-permute-start | bytes 479240 | tf_op jit(solution)/shard_map/ppermute | solution.py:443
  262.9 7.7 %collective-permute-start.27 = (bf16[208,384]{1,0:T(8,128)(2,1)S(1)}, bf16[208,384]{1,0:T(8,128)(2,1)S(1)}, u32[]{:S(2)}, u32[]{:S(2)}) collective-permute-start(bf16[208,384]{1,0:T(8,128)(2,1)S(1)} %add_convert_fusion.15), channel_id=1, source_target_pairs={{0,8},{8,0},{16,24},{24,16},{1,9},{9,1},{17,25},{25,17},{2,10},{10... | collective-permute-start | bytes 479240 | tf_op jit(solution)/shard_map/ppermute | solution.py:443
  272.6 4.6 %copy-start.1 = (bf16[768,1536]{1,0:T(8,128)(2,1)S(1)}, bf16[768,1536]{1,0:T(8,128)(2,1)}, u32[]{:S(2)}) copy-start(bf16[768,1536]{1,0:T(8,128)(2,1)} %param.18) | copy-start | bytes 7077892
  (53 other events, 114.9 us)

commit v8 on v7

--- a/solution.py
+++ b/solution.py
@@ -588,7 +588,6 @@
     in_grad = after(in_grad, second_other, terms_two_p)
     ffn_grad = cut(jnp.stack([in_grad, down_grad]))
     ffn_part = add_low(halve(ffn_grad, "grp", 0, seq_bits + 1))
-    second_other = after(second_other, ffn_part)
 
     def rest(cot, normed, inv, second):
         grad = cot.astype(F32) + norm_back(normed, inv, second, gains[1])
@@ -596,6 +595,7 @@
         return grad, low, back_dot(low, out_weight).astype(BF)
 
     second_c = terms_two_c.astype(F32) + second_other.astype(F32)
+    second_c = after(second_c, ffn_part)
     grad_c, dm_c, do_c = rest(cot_c, two_c, inv_two_c, second_c)
     for bit in range(1, grp_bits):
         ffn_pair = halve(ffn_part, "grp", bit, seq_bits + 1)

time: 282 us -> 281 us (level)
  no operation moved by 1% of the time
where the time goes in v8:
time: 281 us; the launch traced here: 276 us
  Pallas kernels  76.2 us (27%)
  other arithmetic  47 us (17%)
  matrix products  46.2 us (16%)
  waiting for transfers between devices  42.9 us (15%)
  starting transfers between devices  36.2 us (13%)
  local copies, waits for them, and re-layouts  24.2 us (9%)
  between operations  3.38 us (1%)
    ppermute x21, waiting for transfers between devices, swap(): return lax.ppermute(array, axis, [(j, j ^ 1 << bit) for j in range(count)])  36.8 us
    pallas_call x2, Pallas kernels, pull_far(): pl.pallas_call(functools.partial(pull_far_kernel, masked=masked, chunk=ch...  25.2 us
    ppermute x21, starting transfers between devices, swap(): return lax.ppermute(array, axis, [(j, j ^ 1 << bit) for j in range(count)])  24 us
    pallas_call x1, Pallas kernels, pull_near(): pl.pallas_call(pull_near_kernel, grid=(width // LANES,), in_specs=specs,...  14.8 us
    pallas_call x2, Pallas kernels, attend_far(): pl.pallas_call(functools.partial(far_kernel, masked=masked), grid=(width...  13.9 us
    dot_general x8, matrix products, rows_dot(): return jnp.einsum('nd,nf->df', left, right, preferred_element_type=F32)  13.8 us
    dot_general x6, matrix products, wide_dot(): return jnp.dot(left, right, preferred_element_type=F32)  11.3 us
    pallas_call x1, Pallas kernels, attend_near(): pl.pallas_call(near_kernel, grid=(width // LANES,), in_specs=[kind_spec(o...  11.1 us
  transfers between devices with their start and end apart: 30, of which 13 were waited for; matrix products, arithmetic and copies ran while one was open for 29% of the time, Pallas kernels for 25%

profile of v8, /device:TPU:0, one launch (start us, length us, event | category | flops | bytes accessed | tf_op | source)
XLA Modules:
  0.0 276.0 jit_solution(3551040638991415688)
XLA Ops:
  0.7 1.9 dynamic-slice_bitcast_fusion.7
  2.5 5.1 %collective-permute-start.2 = (bf16[192,768]{1,0:T(8,128)(2,1)}, bf16[192,768]{1,0:T(8,128)(2,1)S(1)}, u32[]{:S(2)}, u32[]{:S(2)}) collective-permute-start(bf16[192,768]{1,0:T(8,128)(2,1)} %dynamic-slice_bitcast_fusion.7), channel_id=1, source_target_pairs={{0,6},{2,4},{4,2},{6,0},{1,7},{3,5},{5,3},{7,1},{8,14},{10,12},{12... | collective-permute-start | bytes 884744 | tf_op jit(solution)/shard_map/ppermute | solution.py:507
  11.4 2.4 subtract_multiply_fusion.2
  13.7 1.5 fusion.34
  16.0 1.8 fusion.58.qp_ref.kp_ref.vp_ref.refs_0_
  17.8 2.2 fusion.47.qc_ref.kc_ref.vc_ref.refs_0_
  21.1 11.1 %shard_map.186 = (f32[384,384]{1,0:T(8,128)}, f32[3,8,384]{2,1,0:T(8,128)}, f32[512,384]{1,0:T(8,128)}, f32[3,8,512]{2,1,0:T(8,128)}) custom-call(bf16[3,384,384]{2,1,0:T(8,128)(2,1)} %fusion.58.qp_ref.kp_ref.vp_ref.refs_0_, bf16[3,384,384]{2,1,0:T(8,128)(2,1)} %fusion.58.qp_ref.kp_ref.vp_ref.refs_0_, ...), custom_call_target="tpu_custom_call" | custom-call | flops 1212416 | bytes 5120 | tf_op jit(solution)/shard_map/pallas_call | solution.py:122
  34.2 1.6 collective-permute-start.3
  37.3 1.8 fusion.64.k_ref.v_ref
  39.9 11.1 %shard_map.187 = (f32[384,384]{1,0:T(8,128)}, f32[3,8,384]{2,1,0:T(8,128)}, f32[512,384]{1,0:T(8,128)}, f32[3,8,512]{2,1,0:T(8,128)}) custom-call(bf16[2,576,384]{2,1,0:T(8,128)(2,1)} %fusion.64.k_ref.v_ref, bf16[2,576,384]{2,1,0:T(8,128)(2,1)} %fusion.64.k_ref.v_ref, f32[576,128]{1,0:T(8,128)} %broadcast_in_dim.37.bias_ref, ...), custom_call_target="tpu_custom_call" | custom-call | flops 1032192 | bytes 2304 | tf_op jit(solution)/shard_map/pallas_call | solution.py:176
  51.0 4.0 %collective-permute-done.3 = bf16[576,768]{1,0:T(8,128)(2,1)S(1)} collective-permute-done((bf16[576,768]{1,0:T(8,128)(2,1)S(1)}, bf16[576,768]{1,0:T(8,128)(2,1)S(1)}, u32[]{:S(2)}, u32[]{:S(2)}) %collective-permute-start.3) | collective-permute-done | bytes 884768 | tf_op jit(solution)/shard_map/ppermute | solution.py:364
  56.8 1.8 fusion.65.refs_1_.refs_2_
  59.4 7.5 %shard_map.188 = (bf16[512,384]{1,0:T(8,128)(2,1)}, f32[3,8,512]{2,1,0:T(8,128)}) custom-call(bf16[3,512,384]{2,1,0:T(8,128)(2,1)} %fusion.47.qc_ref.kc_ref.vc_ref.refs_0_, bf16[2,576,384]{2,1,0:T(8,128)(2,1)} %fusion.65.refs_1_.refs_2_, bf16[2,576,384]{2,1,0:T(8,128)(2,1)} %fusion.65.refs_1_.refs_2_, f32[576,128]{1,0:T(8,128)} %broadcast_in_dim.38.refs_3_, ...), custom_call_target="tpu_custom_call" | custom-call | flops 589824 | bytes 2304 | tf_op jit(solution)/shard_map/pallas_call | solution.py:222
  67.0 2.4 convolution_convert_fusion.8
  69.4 1.5 collective-permute-start.4
  70.9 6.4 %shard_map.189 = (bf16[384,384]{1,0:T(8,128)(2,1)}, f32[3,8,384]{2,1,0:T(8,128)}) custom-call(bf16[3,384,384]{2,1,0:T(8,128)(2,1)} %fusion.58.qp_ref.kp_ref.vp_ref.refs_0_, bf16[2,576,384]{2,1,0:T(8,128)(2,1)} %fusion.65.refs_1_.refs_2_, bf16[2,576,384]{2,1,0:T(8,128)(2,1)} %fusion.65.refs_1_.refs_2_, f32[384,384]{1,0:T(8,128)} %get-tuple-element.91.refs_3_, ...), custom_call_target="tpu_custom_call" | custom-call | flops 442368 | bytes 2304 | tf_op jit(solution)/shard_map/pallas_call | solution.py:222
  77.3 1.4 convolution_convert_fusion.12
  79.4 1.5 pad_maximum_fusion.refs_1_.refs_2_
  84.5 1.4 fusion.116
  85.9 4.2 %collective-permute-done.4 = bf16[512,768]{1,0:T(8,128)(2,1)} collective-permute-done((bf16[512,768]{1,0:T(8,128)(2,1)}, bf16[512,768]{1,0:T(8,128)(2,1)}, u32[]{:S(2)}, u32[]{:S(2)}) %collective-permute-start.4) | collective-permute-done | bytes 786464 | tf_op jit(solution)/shard_map/ppermute | solution.py:364
  91.2 1.7 fusion.112
  94.1 1.4 fusion.118
  95.5 1.5 multiply_convert_fusion
  97.0 1.4 convolution_convert_fusion.7
  98.5 1.6 collective-permute-start.7
  100.0 2.6 collective-permute-done.5
  103.5 1.9 multiply_convert_fusion.1
  105.5 2.9 %convolution_convert_fusion.1 = bf16[768,1536]{1,0:T(8,128)(2,1)S(1)} fusion(bf16[512,1536]{1,0:T(8,128)(2,1)S(1)} %get-tuple-element.185, bf16[384,1536]{1,0:T(8,128)(2,1)S(1)} %get-tuple-element.191, bf16[512,768]{1,0:T(8,128)(2,1)S(1)} %add_convert_fusion.5, bf16[384,768]{1,0:T(8,128)(2,1)S(1)} %add_convert_fusion.11), kind=kOutput, calls=%fused_computation.10 | convolution fusion | flops 2123366400 | bytes 6488064 | tf_op jit(solution)/shard_map/nd,nf->df/dot_general | solution.py:413
  108.4 3.1 %convolution_convert_fusion = bf16[768,1536]{1,0:T(8,128)(2,1)S(1)} fusion(bf16[512,1536]{1,0:T(8,128)(2,1)S(1)} %get-tuple-element.111, bf16[384,1536]{1,0:T(8,128)(2,1)S(1)} %get-tuple-element.136, bf16[512,768]{1,0:T(8,128)(2,1)S(1)} %bitcast.261, bf16[384,768]{1,0:T(8,128)(2,1)S(1)} %bitcast.271), kind=kOutput, calls=%fused_computation.9 | convolution fusion | flops 2123366400 | bytes 6488064 | tf_op jit(solution)/shard_map/nd,nf->df/dot_general | solution.py:413
  111.6 1.9 convolution_convert_fusion.10
  113.5 3.4 %collective-permute-done.7 = bf16[512,768]{1,0:T(8,128)(2,1)S(1)} collective-permute-done((bf16[512,768]{1,0:T(8,128)(2,1)S(1)}, bf16[512,768]{1,0:T(8,128)(2,1)S(1)}, u32[]{:S(2)}, u32[]{:S(2)}) %collective-permute-start.7) | collective-permute-done | bytes 786464 | tf_op jit(solution)/shard_map/ppermute | solution.py:364
  116.9 1.7 fusion.21
  118.6 1.6 collective-permute-start.6
  121.5 2.0 collective-permute-done.8
  123.5 2.7 fusion
  127.2 1.6 collective-permute-start.10
  128.7 1.8 fusion.110
  131.9 13.6 %shard_map.190 = (f32[512,384]{1,0:T(8,128)}, f32[2,1152,384]{2,1,0:T(8,128)}) custom-call(bf16[3,512,384]{2,1,0:T(8,128)(2,1)} %fusion.47.qc_ref.kc_ref.vc_ref.refs_0_, bf16[2,1152,384]{2,1,0:T(8,128)(2,1)} %pad_maximum_fusion.refs_1_.refs_2_, bf16[2,1152,384]{2,1,0:T(8,128)(2,1)} %pad_maximum_fusion.refs_1_.refs_2_, f32[1152,128]{1,0:T(8,128)} %broadcast_in_dim.39.refs_3_, ...), custom_call_target="tpu_custom_call" | custom-call | flops 2949120 | bytes 9216 | tf_op jit(solution)/shard_map/pallas_call | solution.py:310
  145.5 1.4 convert_add_fusion.2
  146.9 1.7 fusion.67
  148.8 1.5 fusion.109
  152.8 2.3 convolution_convert_fusion.6
  155.1 1.5 collective-permute-start.13
  160.1 11.6 %shard_map.191 = (f32[384,384]{1,0:T(8,128)}, bf16[2,1152,384]{2,1,0:T(8,128)(2,1)}) custom-call(bf16[3,384,384]{2,1,0:T(8,128)(2,1)} %fusion.58.qp_ref.kp_ref.vp_ref.refs_0_, bf16[2,1152,384]{2,1,0:T(8,128)(2,1)} %pad_maximum_fusion.refs_1_.refs_2_, bf16[2,1152,384]{2,1,0:T(8,128)(2,1)} %pad_maximum_fusion.refs_1_.refs_2_, ...), custom_call_target="tpu_custom_call" | custom-call | flops 2211840 | bytes 9216 | tf_op jit(solution)/shard_map/pallas_call | solution.py:310
  171.6 3.1 %fusion.114 = (f32[768]{0:T(1024)S(1)}, bf16[1152,768]{1,0:T(8,128)(2,1)S(1)}, f32[1152,768]{1,0:T(8,128)S(1)}) fusion(bf16[2,1152,384]{2,1,0:T(8,128)(2,1)} %get-tuple-element.115, bf16[3,768,384]{2,1,0:T(8,128)(2,1)S(1)} %copy-done.82), kind=kOutput, calls=%fused_computation.298 | convolution fusion | flops 1360723200 | bytes 8260608 | tf_op jit(solution)/shard_map/cne,cde->nd/dot_general | solution.py:621
  177.6 2.4 collective-permute-start.12
  180.6 14.8 %shard_map.192 = bf16[3,896,384]{2,1,0:T(8,128)(2,1)} custom-call(bf16[3,384,384]{2,1,0:T(8,128)(2,1)} %fusion.58.qp_ref.kp_ref.vp_ref.refs_0_, bf16[3,384,384]{2,1,0:T(8,128)(2,1)} %fusion.58.qp_ref.kp_ref.vp_ref.refs_0_, bf16[3,384,384]{2,1,0:T(8,128)(2,1)} %fusion.58.qp_ref.kp_ref.vp_ref.refs_0_, ...), custom_call_target="tpu_custom_call" | custom-call | flops 3031040 | bytes 5120 | tf_op jit(solution)/shard_map/pallas_call | solution.py:351
  195.7 2.4 convolution_convert_fusion.11
  205.8 2.0 bitcast_convert_fusion
  212.9 1.5 collective-permute-start.15
  214.4 2.9 %collective-permute-done.19 = bf16[2,48,1536]{2,1,0:T(8,128)(2,1)S(1)} collective-permute-done((bf16[2,48,1536]{2,1,0:T(8,128)(2,1)S(1)}, bf16[2,48,1536]{2,1,0:T(8,128)(2,1)S(1)}, u32[]{:S(2)}, u32[]{:S(2)}) %collective-permute-start.19) | collective-permute-done | bytes 294944 | tf_op jit(solution)/shard_map/ppermute | solution.py:364
  218.3 6.3 %collective-permute-done.16 = bf16[2,192,768]{2,1,0:T(8,128)(2,1)S(1)} collective-permute-done((bf16[2,192,768]{2,1,0:T(8,128)(2,1)S(1)}, bf16[2,192,768]{2,1,0:T(8,128)(2,1)S(1)}, u32[]{:S(2)}, u32[]{:S(2)}) %collective-permute-start.16) | collective-permute-done | bytes 589856 | tf_op jit(solution)/shard_map/ppermute | solution.py:364
  225.6 2.4 collective-permute-start.18
  228.0 2.5 fusion.79
  230.5 9.2 %collective-permute-done.18 = bf16[1,192,768]{2,1,0:T(8,128)(2,1)S(1)} collective-permute-done((bf16[1,192,768]{2,1,0:T(8,128)(2,1)S(1)}, bf16[1,192,768]{2,1,0:T(8,128)(2,1)S(1)}, u32[]{:S(2)}, u32[]{:S(2)}) %collective-permute-start.18) | collective-permute-done | bytes 294944 | tf_op jit(solution)/shard_map/ppermute | solution.py:364
  243.0 1.9 convolution_convert_fusion.9
  245.4 2.6 collective-permute-start.25
  248.0 1.9 collective-permute-start.26
  252.6 1.6 slice_bitcast_fusion
  255.2 1.6 fusion.80
  256.9 3.3 %collective-permute-done.25 = bf16[208,384]{1,0:T(8,128)(2,1)S(1)} collective-permute-done((bf16[208,384]{1,0:T(8,128)(2,1)S(1)}, bf16[208,384]{1,0:T(8,128)(2,1)S(1)}, u32[]{:S(2)}, u32[]{:S(2)}) %collective-permute-start.25) | collective-permute-done | bytes 159776 | tf_op jit(solution)/shard_map/ppermute | solution.py:721
  262.2 1.9 collective-permute-done.23
  267.0 2.0 collective-permute-done.28
  273.4 2.1 slice.227
  (350 shorter events, 63.4 us)
Async XLA Ops:
  0.6 93.5 %copy-start = (bf16[768,1536]{1,0:T(8,128)(2,1)S(1)}, bf16[768,1536]{1,0:T(8,128)(2,1)}, u32[]{:S(2)}) copy-start(bf16[768,1536]{1,0:T(8,128)(2,1)} %param.18) | copy-start | bytes 7077892
  0.7 9.5 %copy-start.4 = (bf16[1,1,512,768]{3,2,1,0:T(8,128)(2,1)S(1)}, bf16[1,1,512,768]{3,2,1,0:T(8,128)(2,1)}, u32[]{:S(2)}) copy-start(bf16[1,1,512,768]{3,2,1,0:T(8,128)(2,1)} %param.12) | copy-start | bytes 2359300
  0.7 10.4 %copy-start.74 = (bf16[2,768]{1,0:T(2,128)(2,1)S(1)}, bf16[2,768]{1,0:T(2,128)(2,1)}, u32[]{:S(2)}) copy-start(bf16[2,768]{1,0:T(2,128)(2,1)} %param.20) | copy-start | bytes 9220
  0.7 10.4 %copy-start.75 = (bf16[2,768]{1,0:T(2,128)(2,1)S(1)}, bf16[2,768]{1,0:T(2,128)(2,1)}, u32[]{:S(2)}) copy-start(bf16[2,768]{1,0:T(2,128)(2,1)} %param.21) | copy-start | bytes 9220
  2.5 29.7 %collective-permute-start.2 = (bf16[192,768]{1,0:T(8,128)(2,1)}, bf16[192,768]{1,0:T(8,128)(2,1)S(1)}, u32[]{:S(2)}, u32[]{:S(2)}) collective-permute-start(bf16[192,768]{1,0:T(8,128)(2,1)} %dynamic-slice_bitcast_fusion.7), channel_id=1, source_target_pairs={{0,6},{2,4},{4,2},{6,0},{1,7},{3,5},{5,3},{7,1},{8,14},{10,12},{12... | collective-permute-start | bytes 884744 | tf_op jit(solution)/shard_map/ppermute | solution.py:507
  7.6 25.4 %collective-permute-start.1 = (bf16[192,768]{1,0:T(8,128)(2,1)}, bf16[192,768]{1,0:T(8,128)(2,1)}, u32[]{:S(2)}, u32[]{:S(2)}) collective-permute-start(bf16[192,768]{1,0:T(8,128)(2,1)} %dynamic-slice_bitcast_fusion.7), channel_id=1, source_target_pairs={{0,4},{2,6},{4,0},{6,2},{1,5},{3,7},{5,1},{7,3},{8,12},{10,14},{12... | collective-permute-start | bytes 884744 | tf_op jit(solution)/shard_map/ppermute | solution.py:507
  7.6 25.4 %collective-permute-start = (bf16[192,768]{1,0:T(8,128)(2,1)}, bf16[192,768]{1,0:T(8,128)(2,1)}, u32[]{:S(2)}, u32[]{:S(2)}) collective-permute-start(bf16[192,768]{1,0:T(8,128)(2,1)} %dynamic-slice_bitcast_fusion.7), channel_id=1, source_target_pairs={{0,2},{2,0},{4,6},{6,4},{1,3},{3,1},{5,7},{7,5},{8,10},{10,8},{12,... | collective-permute-start | bytes 884744 | tf_op jit(solution)/shard_map/ppermute | solution.py:507
  10.7 4.5 %copy-start.66 = (f32[512]{0:T(512)}, f32[512]{0:T(512)S(1)}, u32[]{:S(2)}) copy-start(f32[512]{0:T(512)S(1)} %add_rsqrt_fusion.5) | copy-start | bytes 6148
  11.3 81.9 %copy-start.60 = (f32[768]{0:T(1024)}, f32[768]{0:T(1024)S(1)}, u32[]{:S(2)}) copy-start(f32[768]{0:T(1024)S(1)} %get-tuple-element.172) | copy-start | bytes 9220
  21.1 11.1 %copy-start.7 = (bf16[1,384,768]{2,1,0:T(8,128)(2,1)S(1)}, bf16[1,384,768]{2,1,0:T(8,128)(2,1)}, u32[]{:S(2)}) copy-start(bf16[1,384,768]{2,1,0:T(8,128)(2,1)} %param.11) | copy-start | bytes 1769476
  34.2 20.8 %collective-permute-start.3 = (bf16[576,768]{1,0:T(8,128)(2,1)S(1)}, bf16[576,768]{1,0:T(8,128)(2,1)S(1)}, u32[]{:S(2)}, u32[]{:S(2)}) collective-permute-start(bf16[576,768]{1,0:T(8,128)(2,1)S(1)} %pad_maximum_fusion.4), channel_id=1, source_target_pairs={{0,1},{1,0},{2,3},{3,2},{4,5},{5,4},{6,7},{7,6},{8,9},{9,8},{10,11... | collective-permute-start | bytes 2654216 | tf_op jit(solution)/shard_map/ppermute | solution.py:364
  59.4 7.5 %copy-start.22 = (bf16[384,768]{1,0:T(8,128)(2,1)S(1)}, bf16[384,768]{1,0:T(8,128)(2,1)}, u32[]{:S(2)}) copy-start(bf16[384,768]{1,0:T(8,128)(2,1)} %param.17) | copy-start | bytes 1769476
  69.4 20.7 %collective-permute-start.4 = (bf16[512,768]{1,0:T(8,128)(2,1)}, bf16[512,768]{1,0:T(8,128)(2,1)}, u32[]{:S(2)}, u32[]{:S(2)}) collective-permute-start(bf16[512,768]{1,0:T(8,128)(2,1)} %convolution_convert_fusion.8), channel_id=1, source_target_pairs={{0,1},{1,0},{2,3},{3,2},{4,5},{5,4},{6,7},{7,6},{8,9},{9,8},{10,11... | collective-permute-start | bytes 2359304 | tf_op jit(solution)/shard_map/ppermute | solution.py:364
  70.9 8.4 %copy-start.9 = (bf16[2,576,384]{2,1,0:T(8,128)(2,1)S(1)}, bf16[2,576,384]{2,1,0:T(8,128)(2,1)}, u32[]{:S(2)}) copy-start(bf16[2,576,384]{2,1,0:T(8,128)(2,1)} %fusion.65.refs_1_.refs_2_) | copy-start | bytes 2654212
  70.9 8.4 %copy-start.17 = (bf16[2,576,384]{2,1,0:T(8,128)(2,1)S(1)}, bf16[2,576,384]{2,1,0:T(8,128)(2,1)}, u32[]{:S(2)}) copy-start(bf16[2,576,384]{2,1,0:T(8,128)(2,1)} %fusion.64.k_ref.v_ref) | copy-start | bytes 2654212
  78.8 23.9 %collective-permute-start.5 = (bf16[384,768]{1,0:T(8,128)(2,1)S(1)}, bf16[384,768]{1,0:T(8,128)(2,1)S(1)}, u32[]{:S(2)}, u32[]{:S(2)}) collective-permute-start(bf16[384,768]{1,0:T(8,128)(2,1)S(1)} %convolution_convert_fusion.12), channel_id=1, source_target_pairs={{0,1},{1,0},{2,3},{3,2},{4,5},{5,4},{6,7},{7,6},{8,9},{9,8},{10,11... | collective-permute-start | bytes 1769480 | tf_op jit(solution)/shard_map/ppermute | solution.py:364
  97.0 11.4 %copy-start.37 = (bf16[512,1536]{1,0:T(8,128)(2,1)}, bf16[512,1536]{1,0:T(8,128)(2,1)S(1)}, u32[]{:S(2)}) copy-start(bf16[512,1536]{1,0:T(8,128)(2,1)S(1)} %get-tuple-element.111) | copy-start | bytes 4718596
  98.4 4.5 %copy-start.29 = (bf16[512,768]{1,0:T(8,128)(2,1)}, bf16[512,768]{1,0:T(8,128)(2,1)S(1)}, u32[]{:S(2)}) copy-start(bf16[512,768]{1,0:T(8,128)(2,1)S(1)} %convolution_convert_fusion.7) | copy-start | bytes 2359300
  98.4 4.8 %copy-start.61 = (f32[768]{0:T(1024)S(1)}, f32[768]{0:T(1024)}, u32[]{:S(2)}) copy-start(f32[768]{0:T(1024)} %copy-done.60) | copy-start | bytes 9220
  98.5 18.4 %collective-permute-start.7 = (bf16[512,768]{1,0:T(8,128)(2,1)S(1)}, bf16[512,768]{1,0:T(8,128)(2,1)S(1)}, u32[]{:S(2)}, u32[]{:S(2)}) collective-permute-start(bf16[512,768]{1,0:T(8,128)(2,1)S(1)} %convolution_convert_fusion.7), channel_id=1, source_target_pairs={{0,1},{1,0},{2,3},{3,2},{4,5},{5,4},{6,7},{7,6},{8,9},{9,8},{10,11... | collective-permute-start | bytes 2359304 | tf_op jit(solution)/shard_map/ppermute | solution.py:364
  108.4 8.5 %copy-start.14 = (bf16[768,1536]{1,0:T(8,128)(2,1)}, bf16[768,1536]{1,0:T(8,128)(2,1)S(1)}, u32[]{:S(2)}) copy-start(bf16[768,1536]{1,0:T(8,128)(2,1)S(1)} %convolution_convert_fusion.1) | copy-start | bytes 7077892
  111.6 5.3 %copy-start.16 = (bf16[768,1536]{1,0:T(8,128)(2,1)}, bf16[768,1536]{1,0:T(8,128)(2,1)S(1)}, u32[]{:S(2)}) copy-start(bf16[768,1536]{1,0:T(8,128)(2,1)S(1)} %convolution_convert_fusion) | copy-start | bytes 7077892
  118.6 4.9 %collective-permute-start.8 = (bf16[2,2,2,2,48,1536]{5,4,3,2,1,0:T(8,128)(2,1)}, bf16[2,2,2,2,48,1536]{5,4,3,2,1,0:T(8,128)(2,1)}, u32[]{:S(2)}, u32[]{:S(2)}) collective-permute-start(bf16[2,2,2,2,48,1536]{5,4,3,2,1,0:T(8,128)(2,1)} %fusion.21), channel_id=1, source_target_pairs={{0,8},{8,0},{16,24},{24,16},{1,9},{9,1},{17,25},{25,17},{2,10},{10... | collective-permute-start | bytes 7077896 | tf_op jit(solution)/shard_map/ppermute | solution.py:364
  118.6 4.9 %copy-start.15 = (bf16[768,1536]{1,0:T(8,128)(2,1)S(1)}, bf16[768,1536]{1,0:T(8,128)(2,1)}, u32[]{:S(2)}) copy-start(bf16[768,1536]{1,0:T(8,128)(2,1)} %copy-done.14) | copy-start | bytes 7077892
  118.6 26.9 %collective-permute-start.6 = (bf16[384,768]{1,0:T(8,128)(2,1)}, bf16[384,768]{1,0:T(8,128)(2,1)}, u32[]{:S(2)}, u32[]{:S(2)}) collective-permute-start(bf16[384,768]{1,0:T(8,128)(2,1)} %convolution_convert_fusion.10), channel_id=1, source_target_pairs={{0,1},{1,0},{2,3},{3,2},{4,5},{5,4},{6,7},{7,6},{8,9},{9,8},{10,11... | collective-permute-start | bytes 1769480 | tf_op jit(solution)/shard_map/ppermute | solution.py:364
  121.5 4.7 %copy-start.3 = (f32[512,768]{1,0:T(8,128)S(1)}, f32[512,768]{1,0:T(8,128)}, u32[]{:S(2)}) copy-start(f32[512,768]{1,0:T(8,128)} %copy-done.2) | copy-start | bytes 4718596
  121.5 4.7 %copy-start.55 = (f32[512]{0:T(512)S(1)}, f32[512]{0:T(512)}, u32[]{:S(2)}) copy-start(f32[512]{0:T(512)} %copy-done.54) | copy-start | bytes 6148
  121.5 4.7 %copy-start.69 = (f32[512]{0:T(512)S(1)}, f32[512]{0:T(512)}, u32[]{:S(2)}) copy-start(f32[512]{0:T(512)} %copy-done.68) | copy-start | bytes 6148
  127.2 29.4 %collective-permute-start.10 = (bf16[2,2,2,48,1536]{4,3,2,1,0:T(8,128)(2,1)S(1)}, bf16[2,2,2,48,1536]{4,3,2,1,0:T(8,128)(2,1)S(1)}, u32[]{:S(2)}, u32[]{:S(2)}) collective-permute-start(bf16[2,2,2,48,1536]{4,3,2,1,0:T(8,128)(2,1)S(1)} %get-tuple-element.188), channel_id=1, source_target_pairs={{0,16},{8,24},{16,0},{24,8},{1,17},{9,25},{17,1},{25,9},{2,18},{10... | collective-permute-start | bytes 3538952 | tf_op jit(solution)/shard_map/ppermute | solution.py:364
  155.1 25.5 %collective-permute-start.13 = (bf16[512,768]{1,0:T(8,128)(2,1)}, bf16[512,768]{1,0:T(8,128)(2,1)}, u32[]{:S(2)}, u32[]{:S(2)}) collective-permute-start(bf16[512,768]{1,0:T(8,128)(2,1)} %convolution_convert_fusion.6), channel_id=1, source_target_pairs={{0,1},{1,0},{2,3},{3,2},{4,5},{5,4},{6,7},{7,6},{8,9},{9,8},{10,11... | collective-permute-start | bytes 2359304 | tf_op jit(solution)/shard_map/ppermute | solution.py:364
  157.9 17.6 %collective-permute-start.11 = (bf16[2,2,48,1536]{3,2,0,1:T(8,128)(2,1)}, bf16[2,2,48,1536]{3,2,0,1:T(8,128)(2,1)}, u32[]{:S(2)}, u32[]{:S(2)}) collective-permute-start(bf16[2,2,48,1536]{3,2,0,1:T(8,128)(2,1)} %bitcast.223), channel_id=1, source_target_pairs={{0,2},{2,0},{4,6},{6,4},{1,3},{3,1},{5,7},{7,5},{8,10},{10,8},{12,... | collective-permute-start | bytes 1769480 | tf_op jit(solution)/shard_map/ppermute | solution.py:364
  160.0 11.6 %copy-start.82 = (bf16[3,768,384]{2,1,0:T(8,128)(2,1)S(1)}, bf16[3,768,384]{2,1,0:T(8,128)(2,1)}, u32[]{:S(2)}) copy-start(bf16[3,768,384]{2,1,0:T(8,128)(2,1)} %param.16) | copy-start | bytes 5308420
  174.8 20.9 %collective-permute-start.9 = (bf16[576,768]{1,0:T(8,128)(2,1)S(1)}, bf16[576,768]{1,0:T(8,128)(2,1)S(1)}, u32[]{:S(2)}, u32[]{:S(2)}) collective-permute-start(bf16[576,768]{1,0:T(8,128)(2,1)S(1)} %slice.215), channel_id=1, source_target_pairs={{0,1},{1,0},{2,3},{3,2},{4,5},{5,4},{6,7},{7,6},{8,9},{9,8},{10,11... | collective-permute-start | bytes 2654216 | tf_op jit(solution)/shard_map/ppermute | solution.py:364
  175.4 4.5 %copy-start.11 = (bf16[576,768]{1,0:T(8,128)(2,1)S(1)}, bf16[576,768]{1,0:T(8,128)(2,1)}, u32[]{:S(2)}) copy-start(bf16[576,768]{1,0:T(8,128)(2,1)} %copy-done.10) | copy-start | bytes 2654212
  175.4 4.5 %copy-start.13 = (bf16[576,768]{1,0:T(8,128)(2,1)S(1)}, bf16[576,768]{1,0:T(8,128)(2,1)}, u32[]{:S(2)}) copy-start(bf16[576,768]{1,0:T(8,128)(2,1)} %copy-done.12) | copy-start | bytes 2654212
  175.4 4.5 %copy-start.63 = (f32[576]{0:T(1024)S(1)}, f32[576]{0:T(1024)}, u32[]{:S(2)}) copy-start(f32[576]{0:T(1024)} %copy-done.62) | copy-start | bytes 6916
  177.6 18.1 %collective-permute-start.12 = (bf16[2,48,1536]{2,1,0:T(8,128)(2,1)}, bf16[2,48,1536]{2,1,0:T(8,128)(2,1)S(1)}, u32[]{:S(2)}, u32[]{:S(2)}) collective-permute-start(bf16[2,48,1536]{2,1,0:T(8,128)(2,1)} %get-tuple-element.224), channel_id=1, source_target_pairs={{0,4},{2,6},{4,0},{6,2},{1,5},{3,7},{5,1},{7,3},{8,12},{10,14},{12... | collective-permute-start | bytes 884744 | tf_op jit(solution)/shard_map/ppermute | solution.py:364
  180.6 15.1 %copy-start.40 = (bf16[512,768]{1,0:T(8,128)(2,1)S(1)}, bf16[512,768]{1,0:T(8,128)(2,1)}, u32[]{:S(2)}) copy-start(bf16[512,768]{1,0:T(8,128)(2,1)} %copy-done.39) | copy-start | bytes 2359300
  204.6 12.9 %collective-permute-start.17 = (bf16[4,2,2,2,48,384]{5,4,2,1,0,3:T(8,128)(2,1)S(1)}, bf16[4,2,2,2,48,384]{5,4,2,1,0,3:T(8,128)(2,1)S(1)}, u32[]{:S(2)}, u32[]{:S(2)}) collective-permute-start(bf16[4,2,2,2,48,384]{5,4,2,1,0,3:T(8,128)(2,1)S(1)} %pad_maximum_fusion.3), channel_id=1, source_target_pairs={{0,8},{8,0},{16,24},{24,16},{1,9},{9,1},{17,25},{25,17},{2,10},{10... | collective-permute-start | bytes 3538952 | tf_op jit(solution)/shard_map/ppermute | solution.py:364
  209.0 8.3 %collective-permute-start.19 = (bf16[2,48,1536]{2,1,0:T(8,128)(2,1)S(1)}, bf16[2,48,1536]{2,1,0:T(8,128)(2,1)S(1)}, u32[]{:S(2)}, u32[]{:S(2)}) collective-permute-start(bf16[2,48,1536]{2,1,0:T(8,128)(2,1)S(1)} %add_convert_fusion.13), channel_id=1, source_target_pairs={{0,16},{8,24},{16,0},{24,8},{1,17},{9,25},{17,1},{25,9},{2,18},{10... | collective-permute-start | bytes 884744 | tf_op jit(solution)/shard_map/ppermute | solution.py:364
  210.3 14.4 %collective-permute-start.16 = (bf16[2,192,768]{2,1,0:T(8,128)(2,1)S(1)}, bf16[2,192,768]{2,1,0:T(8,128)(2,1)S(1)}, u32[]{:S(2)}, u32[]{:S(2)}) collective-permute-start(bf16[2,192,768]{2,1,0:T(8,128)(2,1)S(1)} %pad_maximum_fusion.5), channel_id=1, source_target_pairs={{0,2},{2,0},{4,6},{6,4},{1,3},{3,1},{5,7},{7,5},{8,10},{10,8},{12,... | collective-permute-start | bytes 1769480 | tf_op jit(solution)/shard_map/ppermute | solution.py:364
  212.2 27.8 %copy-start.18 = (bf16[528,768]{1,0:T(8,128)(2,1)}, bf16[528,768]{1,0:T(8,128)(2,1)S(1)}, u32[]{:S(2)}) copy-start(bf16[528,768]{1,0:T(8,128)(2,1)S(1)} %fusion.78) | copy-start | bytes 2433028
  212.3 27.7 %collective-permute-start.14 = (bf16[192,768]{1,0:T(8,128)(2,1)S(1)}, bf16[192,768]{1,0:T(8,128)(2,1)S(1)}, u32[]{:S(2)}, u32[]{:S(2)}) collective-permute-start(bf16[192,768]{1,0:T(8,128)(2,1)S(1)} %dynamic-slice_bitcast_fusion.4), channel_id=1, source_target_pairs={{0,1},{1,0},{2,3},{3,2},{4,5},{5,4},{6,7},{7,6},{8,9},{9,8},{10,11... | collective-permute-start | bytes 884744 | tf_op jit(solution)/shard_map/ppermute | solution.py:364
  212.9 27.1 %collective-permute-start.15 = (bf16[528,768]{1,0:T(8,128)(2,1)S(1)}, bf16[528,768]{1,0:T(8,128)(2,1)S(1)}, u32[]{:S(2)}, u32[]{:S(2)}) collective-permute-start(bf16[528,768]{1,0:T(8,128)(2,1)S(1)} %fusion.78), channel_id=1, source_target_pairs={{0,1},{1,0},{2,3},{3,2},{4,5},{5,4},{6,7},{7,6},{8,9},{9,8},{10,11... | collective-permute-start | bytes 2433032 | tf_op jit(solution)/shard_map/ppermute | solution.py:364
  217.4 22.6 %collective-permute-start.20 = (bf16[2,96,1536]{2,1,0:T(8,128)(2,1)S(1)}, bf16[2,96,1536]{2,1,0:T(8,128)(2,1)S(1)}, u32[]{:S(2)}, u32[]{:S(2)}) collective-permute-start(bf16[2,96,1536]{2,1,0:T(8,128)(2,1)S(1)} %pad_maximum_fusion.6), channel_id=1, source_target_pairs={{0,8},{8,0},{16,24},{24,16},{1,9},{9,1},{17,25},{25,17},{2,10},{10... | collective-permute-start | bytes 1769480 | tf_op jit(solution)/shard_map/ppermute | solution.py:364
  224.6 15.2 %collective-permute-start.21 = (bf16[4,2,2,48,384]{4,3,2,1,0:T(8,128)(2,1)S(1)}, bf16[4,2,2,48,384]{4,3,2,1,0:T(8,128)(2,1)S(1)}, u32[]{:S(2)}, u32[]{:S(2)}) collective-permute-start(bf16[4,2,2,48,384]{4,3,2,1,0:T(8,128)(2,1)S(1)} %get-tuple-element.194), channel_id=1, source_target_pairs={{0,16},{8,24},{16,0},{24,8},{1,17},{9,25},{17,1},{25,9},{2,18},{10... | collective-permute-start | bytes 1769480 | tf_op jit(solution)/shard_map/ppermute | solution.py:364
  225.6 14.1 %collective-permute-start.18 = (bf16[1,192,768]{2,1,0:T(8,128)(2,1)S(1)}, bf16[1,192,768]{2,1,0:T(8,128)(2,1)S(1)}, u32[]{:S(2)}, u32[]{:S(2)}) collective-permute-start(bf16[1,192,768]{2,1,0:T(8,128)(2,1)S(1)} %fusion.95), channel_id=1, source_target_pairs={{0,4},{2,6},{4,0},{6,2},{1,5},{3,7},{5,1},{7,3},{8,12},{10,14},{12... | collective-permute-start | bytes 884744 | tf_op jit(solution)/shard_map/ppermute | solution.py:364
  230.5 9.6 %copy-start.5 = (bf16[1,1,512,768]{3,2,1,0:T(8,128)(2,1)S(1)}, bf16[1,1,512,768]{3,2,1,0:T(8,128)(2,1)}, u32[]{:S(2)}) copy-start(bf16[1,1,512,768]{3,2,1,0:T(8,128)(2,1)} %param.12) | copy-start | bytes 2359300
  230.5 9.6 %copy-start.53 = (f32[512]{0:T(512)S(1)}, f32[512]{0:T(512)}, u32[]{:S(2)}) copy-start(f32[512]{0:T(512)} %copy-done.52) | copy-start | bytes 6148
  230.5 9.6 %copy-start.67 = (f32[512]{0:T(512)S(1)}, f32[512]{0:T(512)}, u32[]{:S(2)}) copy-start(f32[512]{0:T(512)} %copy-done.66) | copy-start | bytes 6148
  241.7 20.6 %collective-permute-start.22 = (bf16[192,768]{1,0:T(8,128)(2,1)}, bf16[192,768]{1,0:T(8,128)(2,1)}, u32[]{:S(2)}, u32[]{:S(2)}) collective-permute-start(bf16[192,768]{1,0:T(8,128)(2,1)} %fusion.97), channel_id=1, source_target_pairs={{0,1},{1,0},{2,3},{3,2},{4,5},{5,4},{6,7},{7,6},{8,9},{9,8},{10,11... | collective-permute-start | bytes 884744 | tf_op jit(solution)/shard_map/ppermute | solution.py:364
  245.1 4.8 %copy-start.49 = (bf16[384,768]{1,0:T(8,128)(2,1)S(1)}, bf16[384,768]{1,0:T(8,128)(2,1)}, u32[]{:S(2)}) copy-start(bf16[384,768]{1,0:T(8,128)(2,1)} %convolution_convert_fusion.9) | copy-start | bytes 1769476
  245.3 11.5 %collective-permute-start.24 = (bf16[208,384]{1,0:T(8,128)(2,1)S(1)}, bf16[208,384]{1,0:T(8,128)(2,1)S(1)}, u32[]{:S(2)}, u32[]{:S(2)}) collective-permute-start(bf16[208,384]{1,0:T(8,128)(2,1)S(1)} %pad_maximum_fusion.12), channel_id=1, source_target_pairs={{0,2},{2,0},{4,6},{6,4},{1,3},{3,1},{5,7},{7,5},{8,10},{10,8},{12,... | collective-permute-start | bytes 479240 | tf_op jit(solution)/shard_map/ppermute | solution.py:721
  245.4 14.8 %collective-permute-start.25 = (bf16[208,384]{1,0:T(8,128)(2,1)S(1)}, bf16[208,384]{1,0:T(8,128)(2,1)S(1)}, u32[]{:S(2)}, u32[]{:S(2)}) collective-permute-start(bf16[208,384]{1,0:T(8,128)(2,1)S(1)} %pad_maximum_fusion.13), channel_id=1, source_target_pairs={{0,4},{2,6},{4,0},{6,2},{1,5},{3,7},{5,1},{7,3},{8,12},{10,14},{12... | collective-permute-start | bytes 479240 | tf_op jit(solution)/shard_map/ppermute | solution.py:721
  248.0 12.2 %collective-permute-start.26 = (bf16[208,384]{1,0:T(8,128)(2,1)S(1)}, bf16[208,384]{1,0:T(8,128)(2,1)S(1)}, u32[]{:S(2)}, u32[]{:S(2)}) collective-permute-start(bf16[208,384]{1,0:T(8,128)(2,1)S(1)} %pad_maximum_fusion.14), channel_id=1, source_target_pairs={{0,6},{2,4},{4,2},{6,0},{1,7},{3,5},{5,3},{7,1},{8,14},{10,12},{12... | collective-permute-start | bytes 479240 | tf_op jit(solution)/shard_map/ppermute | solution.py:721
  250.0 14.1 %collective-permute-start.23 = (bf16[384,768]{1,0:T(8,128)(2,1)S(1)}, bf16[384,768]{1,0:T(8,128)(2,1)S(1)}, u32[]{:S(2)}, u32[]{:S(2)}) collective-permute-start(bf16[384,768]{1,0:T(8,128)(2,1)S(1)} %copy-done.49), channel_id=1, source_target_pairs={{0,1},{1,0},{2,3},{3,2},{4,5},{5,4},{6,7},{7,6},{8,9},{9,8},{10,11... | collective-permute-start | bytes 1769480 | tf_op jit(solution)/shard_map/ppermute | solution.py:364
  256.8 8.4 %copy-start.8 = (bf16[1,384,768]{2,1,0:T(8,128)(2,1)S(1)}, bf16[1,384,768]{2,1,0:T(8,128)(2,1)}, u32[]{:S(2)}) copy-start(bf16[1,384,768]{2,1,0:T(8,128)(2,1)} %param.11) | copy-start | bytes 1769476
  256.8 8.4 %copy-start.57 = (f32[384]{0:T(512)S(1)}, f32[384]{0:T(512)}, u32[]{:S(2)}) copy-start(f32[384]{0:T(512)} %copy-done.56) | copy-start | bytes 4612
  256.8 8.4 %copy-start.71 = (f32[384]{0:T(512)S(1)}, f32[384]{0:T(512)}, u32[]{:S(2)}) copy-start(f32[384]{0:T(512)} %copy-done.70) | copy-start | bytes 4612
  256.8 8.8 %copy-start.25 = (f32[384,768]{1,0:T(8,128)S(1)}, f32[384,768]{1,0:T(8,128)}, u32[]{:S(2)}) copy-start(f32[384,768]{1,0:T(8,128)} %get-tuple-element.175) | copy-start | bytes 3538948
  260.3 6.7 %collective-permute-start.29 = (bf16[208,384]{1,0:T(8,128)(2,1)S(1)}, bf16[208,384]{1,0:T(8,128)(2,1)S(1)}, u32[]{:S(2)}, u32[]{:S(2)}) collective-permute-start(bf16[208,384]{1,0:T(8,128)(2,1)S(1)} %add_convert_fusion.15), channel_id=1, source_target_pairs={{0,24},{8,16},{16,8},{24,0},{1,25},{9,17},{17,9},{25,1},{2,26},{10... | collective-permute-start | bytes 479240 | tf_op jit(solution)/shard_map/ppermute | solution.py:443
  260.4 8.6 %collective-permute-start.28 = (bf16[208,384]{1,0:T(8,128)(2,1)S(1)}, bf16[208,384]{1,0:T(8,128)(2,1)S(1)}, u32[]{:S(2)}, u32[]{:S(2)}) collective-permute-start(bf16[208,384]{1,0:T(8,128)(2,1)S(1)} %add_convert_fusion.15), channel_id=1, source_target_pairs={{0,16},{8,24},{16,0},{24,8},{1,17},{9,25},{17,1},{25,9},{2,18},{10... | collective-permute-start | bytes 479240 | tf_op jit(solution)/shard_map/ppermute | solution.py:443
  261.3 7.7 %collective-permute-start.27 = (bf16[208,384]{1,0:T(8,128)(2,1)S(1)}, bf16[208,384]{1,0:T(8,128)(2,1)S(1)}, u32[]{:S(2)}, u32[]{:S(2)}) collective-permute-start(bf16[208,384]{1,0:T(8,128)(2,1)S(1)} %add_convert_fusion.15), channel_id=1, source_target_pairs={{0,8},{8,0},{16,24},{24,16},{1,9},{9,1},{17,25},{25,17},{2,10},{10... | collective-permute-start | bytes 479240 | tf_op jit(solution)/shard_map/ppermute | solution.py:443
  271.0 4.6 %copy-start.1 = (bf16[768,1536]{1,0:T(8,128)(2,1)S(1)}, bf16[768,1536]{1,0:T(8,128)(2,1)}, u32[]{:S(2)}) copy-start(bf16[768,1536]{1,0:T(8,128)(2,1)} %param.18) | copy-start | bytes 7077892
  (53 other events, 114.0 us)
